TPU v7x, 128 devices: a whole 4x4x4 slice. The times are simulated.
128 devices in a mesh: member: 2 (over y_hi), gridy: 8 (over x, core), gridx: 8 (over z, y_lo).
Axes of the slice: x: 4, y: 4 (y_hi: 2, y_lo: 2; y = y_hi * 2 + y_lo), z: 4, core: 2. Of those that a mesh axis runs over, the one named last changes fastest.
Arguments:
- temp: float32 [4, 4, 512, 2048], P('member', None, 'gridy', 'gridx'), may hold values from -6 to 6
- salt: float32 [4, 4, 512, 2048], P('member', None, 'gridy', 'gridx'), may hold values from -6 to 6
- uvel: float32 [4, 4, 512, 2048], P('member', None, 'gridy', 'gridx'), may hold values from -3 to 3
- vvel: float32 [4, 4, 512, 2048], P('member', None, 'gridy', 'gridx'), may hold values from -3 to 3
- eta: float32 [4, 512, 2048], P('member', 'gridy', 'gridx'), may hold values from -6 to 6
- land_mask: int32 [512, 2048], P('gridy', 'gridx'), may hold values 0 or 1
- clone_source: int32 [4], P('member'), may hold values from 0 to 3
Outputs:
- new_temp: float32 [4, 4, 512, 2048], P('member', None, 'gridy', 'gridx')
- new_salt: float32 [4, 4, 512, 2048], P('member', None, 'gridy', 'gridx')
- new_uvel: float32 [4, 4, 512, 2048], P('member', None, 'gridy', 'gridx')
- new_vvel: float32 [4, 4, 512, 2048], P('member', None, 'gridy', 'gridx')
- new_eta: float32 [4, 512, 2048], P('member', 'gridy', 'gridx')
- overturning: float32 [4, 4, 512], P('member', None, 'gridy')
- clone_weight: float32 [4], P('member')
All inputs are finite; a program needn't handle non-finite values. No bound on the sum of `land_mask` on one device may be relied on, other than what follows from the above.
Results may differ from a plain program's by a relative error of at most 0.0001.
Values sent between devices are 32-bit elements; how exact they have to be, the bound alone decides.
A program may use at most 128 MiB of HBM per device.

v0:
```python
import functools

import jax
import jax.numpy as jnp
from jax import lax
from jax.experimental import pallas as pl
from jax.experimental.pallas import tpu as pltpu
from jax.sharding import PartitionSpec as P

STEPS = 2
ITERS = 3


ALPHA_T = 0.8
BETA_S = 0.6
PRESS_K = 0.25
STEP_DT = 0.1
KAPPA = 0.1
VISCOSITY = 0.1
DRAG_K = 0.05
CORI_K = 1.0
SURF_C = 4.0
DIV_K = 0.5
GRAV_K = 0.5


def tree_sum(values, axes):
    for axis in axes:
        count = lax.axis_size(axis)
        step = 1
        while step < count:
            pairs = [(i, i ^ step) for i in range(count)]
            values = values + lax.ppermute(values, axis, pairs)
            step *= 2
    return values


def gather_sum_kernel(ny, nx, x_ref, o_ref, recv_y, recv_x, part, send_y, rsem_y, send_x, rsem_x):
    mesh_id = pl.DeviceIdType.MESH
    member = lax.axis_index("member")
    my = lax.axis_index("gridy")
    mx = lax.axis_index("gridx")
    barrier = pltpu.get_barrier_semaphore()
    for d in range(1, ny):
        pl.semaphore_signal(barrier, 1, device_id=(member, (my + d) % ny, mx), device_id_type=mesh_id)
    for d in range(1, nx):
        pl.semaphore_signal(barrier, 1, device_id=(member, my, (mx + d) % nx), device_id_type=mesh_id)
    pl.semaphore_wait(barrier, (ny - 1) + (nx - 1))

    def phase(src, recv, send_sem, recv_sem, count, me, device):
        recv[me] = src[...]
        sent = []
        for d in range(1, count):
            peer = (me + d) % count
            copy = pltpu.make_async_remote_copy(
                src_ref=src,
                dst_ref=recv.at[me],
                send_sem=send_sem.at[peer],
                recv_sem=recv_sem.at[me],
                device_id=device(peer),
                device_id_type=mesh_id,
            )
            copy.start()
            sent.append(copy)
        for d in range(1, count):
            peer = (me + d) % count
            pltpu.make_async_remote_copy(
                src_ref=src,
                dst_ref=recv.at[peer],
                send_sem=send_sem.at[peer],
                recv_sem=recv_sem.at[peer],
                device_id=device(peer),
                device_id_type=mesh_id,
            ).wait_recv()
        for copy in sent:
            copy.wait_send()
        total = recv[0]
        for j in range(1, count):
            total = total + recv[j]
        return total

    part[...] = phase(x_ref, recv_y, send_y, rsem_y, ny, my, lambda p: (member, p, mx))
    o_ref[...] = phase(part, recv_x, send_x, rsem_x, nx, mx, lambda p: (member, my, p))


def grid_sum(values):
    ny = lax.axis_size("gridy")
    nx = lax.axis_size("gridx")
    shape = values.shape
    return pl.pallas_call(
        functools.partial(gather_sum_kernel, ny, nx),
        out_shape=jax.ShapeDtypeStruct(shape, values.dtype),
        in_specs=[pl.BlockSpec(memory_space=pltpu.VMEM)],
        out_specs=pl.BlockSpec(memory_space=pltpu.VMEM),
        scratch_shapes=[
            pltpu.VMEM((ny,) + shape, values.dtype),
            pltpu.VMEM((nx,) + shape, values.dtype),
            pltpu.VMEM(shape, values.dtype),
            pltpu.SemaphoreType.DMA((ny,)),
            pltpu.SemaphoreType.DMA((ny,)),
            pltpu.SemaphoreType.DMA((nx,)),
            pltpu.SemaphoreType.DMA((nx,)),
        ],
        compiler_params=pltpu.CompilerParams(collective_id=0, has_side_effects=True),
    )(values)


def ring(axis):
    count = lax.axis_size(axis)
    forward = [(i, (i + 1) % count) for i in range(count)]
    backward = [((i + 1) % count, i) for i in range(count)]
    return forward, backward


def exchange(block, ydim, xdim, south_keep, north_keep):
    fwd_y, bwd_y = ring("gridy")
    fwd_x, bwd_x = ring("gridx")
    rows = block.shape[ydim]
    cols = block.shape[xdim]
    north = lax.ppermute(lax.slice_in_dim(block, 0, 1, axis=ydim), "gridy", bwd_y) * north_keep
    south = lax.ppermute(lax.slice_in_dim(block, rows - 1, rows, axis=ydim), "gridy", fwd_y) * south_keep
    east = lax.ppermute(lax.slice_in_dim(block, 0, 1, axis=xdim), "gridx", bwd_x)
    west = lax.ppermute(lax.slice_in_dim(block, cols - 1, cols, axis=xdim), "gridx", fwd_x)
    return (east, west, north, south)


def sides(field, rims, ydim, xdim):
    east, west, north, south = rims
    rows = field.shape[ydim]
    cols = field.shape[xdim]
    east_side = jnp.concatenate([lax.slice_in_dim(field, 1, cols, axis=xdim), east], axis=xdim)
    west_side = jnp.concatenate([west, lax.slice_in_dim(field, 0, cols - 1, axis=xdim)], axis=xdim)
    north_side = jnp.concatenate([lax.slice_in_dim(field, 1, rows, axis=ydim), north], axis=ydim)
    south_side = jnp.concatenate([south, lax.slice_in_dim(field, 0, rows - 1, axis=ydim)], axis=ydim)
    return (east_side, west_side, north_side, south_side)


def pressure(temp, salt):
    return PRESS_K * jnp.cumsum(BETA_S * salt - ALPHA_T * temp, axis=-3)


def surface_apply(field, rims):
    east_side, west_side, north_side, south_side = sides(field, rims, 1, 2)
    return (1.0 + 4.0 * SURF_C) * field - SURF_C * (east_side + west_side + north_side + south_side)


def member_total(values):
    return jnp.sum(values, axis=(1, 2))


def widen(values):
    return values[:, None, None]


def combine(a, fa, b, fb):
    def one(u, v):
        left = u if a is None else widen(a) * u
        return left + (v if b is None else widen(b) * v)

    return one(fa[0], fb[0]), tuple(one(u, v) for u, v in zip(fa[1], fb[1]))


def scaled(a, fa):
    return widen(a) * fa[0], tuple(widen(a) * u for u in fa[1])


def padded_2(block, sides_of, width):
    for axis, dim in sides_of:
        count = lax.axis_size(axis)
        forward = [(i, (i + 1) % count) for i in range(count)]
        backward = [((i + 1) % count, i) for i in range(count)]
        size = block.shape[dim]
        low = lax.ppermute(lax.slice_in_dim(block, size - width, size, axis=dim), axis, forward)
        high = lax.ppermute(lax.slice_in_dim(block, 0, width, axis=dim), axis, backward)
        block = jnp.concatenate([low, block, high], axis=dim)
    return block


def crop(field, by):
    if by == 0:
        return field
    return field[..., by:-by, by:-by]


def around(field):
    return (
        field[..., 1:-1, 1:-1],
        field[..., 1:-1, 2:],
        field[..., 1:-1, :-2],
        field[..., 2:, 1:-1],
        field[..., :-2, 1:-1],
    )


def rows_at(inside, full, want):
    cut = full - want
    return inside if cut == 0 else inside[cut:-cut]


def apply_wide(field, inside):
    centre, east, west, north, south = around(field)
    return ((1.0 + 4.0 * SURF_C) * centre - SURF_C * (east + west + north + south)) * inside


def surface_solve(rhs, inside, width, full):
    residual, wide_r = rhs, width
    gamma_prev = None
    alpha_prev = None
    for count in range(ITERS):
        image_res = apply_wide(residual, rows_at(inside, full, wide_r - 1))
        own_res = crop(residual, wide_r)
        own_img = crop(image_res, wide_r - 1)
        dots = grid_sum(jnp.stack([member_total(own_res * own_res), member_total(own_res * own_img)]))
        gamma, delta = dots[0], dots[1]
        if count == 0:
            alpha = gamma / delta
            direction, wide_p = residual, wide_r
            image_dir, wide_s = image_res, wide_r - 1
            solution, wide_x = widen(alpha) * direction, wide_r
        else:
            beta = gamma / gamma_prev
            alpha = gamma / (delta - beta * gamma / alpha_prev)
            direction = residual + widen(beta) * crop(direction, wide_p - wide_r)
            wide_p = wide_r
            image_dir = image_res + widen(beta) * crop(image_dir, wide_s - (wide_r - 1))
            wide_s = wide_r - 1
            solution = crop(solution, wide_x - wide_r) + widen(alpha) * direction
            wide_x = wide_r
        if count < ITERS - 1:
            residual = crop(residual, 1) - widen(alpha) * image_dir
            wide_r -= 1
        gamma_prev = gamma
        alpha_prev = alpha
    return solution


def shards(temp, salt, uvel, vvel, eta, land_mask, clone_source):
    levels = temp.shape[1]
    rows = temp.shape[2]
    cols = temp.shape[3]
    ocean = land_mask.astype(jnp.float32)
    tile_row = lax.axis_index("gridy")
    tile_count = lax.axis_size("gridy")
    total_rows = rows * tile_count
    total_cols = cols * lax.axis_size("gridx")
    south_keep = (tile_row > 0).astype(jnp.float32)
    north_keep = (tile_row < tile_count - 1).astype(jnp.float32)
    latitude = (tile_row * rows + jnp.arange(rows, dtype=jnp.int32)).astype(jnp.float32) + 0.5
    coriolis = (CORI_K * (2.0 * latitude / total_rows - 1.0))[:, None]
    wide_rows = tile_row * rows - (ITERS + 1) + jnp.arange(rows + 2 * (ITERS + 1), dtype=jnp.int32)
    inside = ((wide_rows >= 0) & (wide_rows < total_rows)).astype(jnp.float32)[:, None]
    for count in range(STEPS):
        press = pressure(temp, salt)
        volume = jnp.stack((temp, salt, uvel, vvel, press))
        east_side, west_side, north_side, south_side = sides(
            volume, exchange(volume, 3, 4, south_keep, north_keep), 3, 4
        )
        lap_temp = east_side[0] + west_side[0] + north_side[0] + south_side[0] - 4.0 * temp
        lap_salt = east_side[1] + west_side[1] + north_side[1] + south_side[1] - 4.0 * salt
        lap_uvel = east_side[2] + west_side[2] + north_side[2] + south_side[2] - 4.0 * uvel
        lap_vvel = east_side[3] + west_side[3] + north_side[3] + south_side[3] - 4.0 * vvel
        temp_next = ocean * (
            temp
            - STEP_DT
            * 0.5
            * (uvel * (east_side[0] - west_side[0]) + vvel * (north_side[0] - south_side[0]))
            + KAPPA * lap_temp
        )
        salt_next = ocean * (
            salt
            - STEP_DT
            * 0.5
            * (uvel * (east_side[1] - west_side[1]) + vvel * (north_side[1] - south_side[1]))
            + KAPPA * lap_salt
        )
        ustar = ocean * (
            uvel
            + STEP_DT * (coriolis * vvel - 0.5 * (east_side[4] - west_side[4]) - DRAG_K * uvel)
            + VISCOSITY * lap_uvel
        )
        vstar = ocean * (
            vvel
            + STEP_DT * (-coriolis * uvel - 0.5 * (north_side[4] - south_side[4]) - DRAG_K * vvel)
            + VISCOSITY * lap_vvel
        )
        halo = ITERS + 1
        surface = padded_2(
            jnp.stack((jnp.sum(ustar, axis=1), jnp.sum(vstar, axis=1), eta)),
            (("gridy", 2), ("gridx", 3)),
            halo,
        ) * inside
        centre, east_t, west_t, north_t, south_t = around(surface)
        rhs = (centre[2] - DIV_K * 0.5 * (east_t[0] - west_t[0] + (north_t[1] - south_t[1]))) * rows_at(
            inside, halo, halo - 1
        )
        wide_eta = surface_solve(rhs, inside, halo - 1, halo)
        eta, east_e, west_e, north_e, south_e = around(wide_eta)
        uvel = ocean * (ustar - GRAV_K * 0.5 * (east_e - west_e)[:, None])
        vvel = ocean * (vstar - GRAV_K * 0.5 * (north_e - south_e)[:, None])
        temp = temp_next
        salt = salt_next
    zonal_scale = 1.0 / jnp.sqrt(jnp.float32(total_cols))
    score_scale = 1.0 / jnp.sqrt(jnp.float32(levels * total_rows))
    lat_weight = latitude / total_rows
    zonal_local = jnp.sum(vvel, axis=3)
    zonal_whole = tree_sum(zonal_local, ("gridx",))
    overturn = jnp.cumsum(zonal_whole, axis=1) * zonal_scale
    score = tree_sum(jnp.sum(overturn * lat_weight, axis=(1, 2)) * score_scale, ("gridy",))
    state_stack = jnp.stack((temp, salt, uvel, vvel))
    every_state, every_eta, every_score = (
        lax.all_gather(state_stack, "member", axis=1, tiled=True),
        lax.all_gather(eta, "member", axis=0, tiled=True),
        lax.all_gather(score, "member", axis=0, tiled=True),
    )
    picked = jnp.take(every_state, clone_source, axis=1)
    new_eta = jnp.take(every_eta, clone_source, axis=0)
    clone_weight = jnp.take(every_score, clone_source, axis=0) - jnp.mean(every_score)
    return (picked[0], picked[1], picked[2], picked[3], new_eta, overturn, clone_weight)


def solution(mesh):
    in_specs = (
        P("member", None, "gridy", "gridx"),
        P("member", None, "gridy", "gridx"),
        P("member", None, "gridy", "gridx"),
        P("member", None, "gridy", "gridx"),
        P("member", "gridy", "gridx"),
        P("gridy", "gridx"),
        P("member"),
    )
    out_specs = (
        P("member", None, "gridy", "gridx"),
        P("member", None, "gridy", "gridx"),
        P("member", None, "gridy", "gridx"),
        P("member", None, "gridy", "gridx"),
        P("member", "gridy", "gridx"),
        P("member", None, "gridy"),
        P("member"),
    )
    return jax.shard_map(shards, mesh=mesh, in_specs=in_specs, out_specs=out_specs, check_vma=False)
```

profile of v0, /device:TPU:0, one launch (start us, length us, event | category | flops | bytes accessed | tf_op | source)
XLA Modules:
  0.0 270.9 jit_solution(8752358808770804465)
XLA Ops:
  11.0 2.9 %collective-permute-start.2 = (f32[5,2,4,1,256]{4,3,2,1,0:T(1,128)S(1)}, f32[5,2,4,1,256]{4,3,2,1,0:T(1,128)S(1)}, u32[]{:S(2)}, u32[]{:S(2)}) collective-permute-start(f32[5,2,4,1,256]{4,3,2,1,0:T(1,128)S(1)} %get-tuple-element.57), channel_id=1, source_target_pairs={{8,0},{16,8},{24,16},{32,24},{40,32},{48,40},{56,48},{0,56},{9,1},... | collective-permute-start | bytes 122888 | tf_op jit(solution)/shard_map/ppermute | solution.py:120
  21.1 3.5 %collective-permute-start = (f32[5,2,4,64,1]{3,2,4,1,0:T(4,128)S(1)}, f32[5,2,4,64,1]{3,2,4,1,0:T(4,128)S(1)}, u32[]{:S(2)}, u32[]{:S(2)}) collective-permute-start(f32[5,2,4,64,1]{3,2,4,1,0:T(4,128)S(1)} %copy.14), channel_id=1, source_target_pairs={{1,0},{2,1},{3,2},{4,3},{5,4},{6,5},{7,6},{0,7},{9,8},{10,9},{11,1... | collective-permute-start | bytes 30728 | tf_op jit(solution)/shard_map/ppermute | solution.py:122
  24.7 2.8 %fusion.231 = (f32[5,2,4,63,256]{4,3,2,1,0:T(8,128)}, f32[5,2,4,63,256]{4,3,2,1,0:T(8,128)}) fusion(f32[5,2,4,64,256]{4,3,2,1,0:T(8,128)S(1)} %constant_dynamic-update-slice_fusion), kind=kLoop, calls=%fused_computation.423 | loop fusion | bytes 10321920 | tf_op jit(solution)/shard_map/slice | solution.py:133
  27.5 3.4 %fusion.229 = (f32[5,2,4,64,255]{4,3,2,1,0:T(8,128)}, f32[5,2,4,64,255]{4,3,2,1,0:T(8,128)}) fusion(f32[5,2,4,64,256]{4,3,2,1,0:T(8,128)S(1)} %constant_dynamic-update-slice_fusion), kind=kLoop, calls=%fused_computation.421 | loop fusion | bytes 10444800 | tf_op jit(solution)/shard_map/slice | solution.py:131
  34.5 3.7 %fusion.219 = (f32[2,64,256]{2,1,0:T(8,128)S(1)}, f32[2,4,64,256]{3,2,1,0:T(8,128)}) fusion(f32[2,4,64,256]{3,2,1,0:T(8,128)} %param.9, f32[5,2,4,63,256]{4,3,2,1,0:T(8,128)} %get-tuple-element.56, f32[5,2,4,1,256]{4,3,2,1,0:T(1,128)S(1)} %broadcast_multiply_fusion.1, f32[5,2,4,1,256]{4,3,2,1,0:T(1,128)S(1)} %broadcast_multiply_fusion.3, ...), kind=kLoop, calls=%fused_computation.415 | loop fusion | flops 2981888 | bytes 12255488 | tf_op jit(solution)/shard_map/reduce_sum | solution.py:288
  43.4 2.5 collective-permute-done.4
  49.5 3.8 %collective-permute-done.7 = f32[3,2,72,4]{3,2,1,0:T(8,128)S(1)} collective-permute-done((f32[3,2,72,4]{3,2,1,0:T(8,128)S(1)}, f32[3,2,72,4]{3,2,1,0:T(8,128)S(1)}, u32[]{:S(2)}, u32[]{:S(2)}) %collective-permute-start.7) | collective-permute-done | bytes 6944 | tf_op jit(solution)/shard_map/ppermute | solution.py:174
  53.3 3.8 %collective-permute-done.6 = f32[3,2,72,4]{3,2,1,0:T(8,128)S(1)} collective-permute-done((f32[3,2,72,4]{3,2,1,0:T(8,128)S(1)}, f32[3,2,72,4]{3,2,1,0:T(8,128)S(1)}, u32[]{:S(2)}, u32[]{:S(2)}) %collective-permute-start.6) | collective-permute-done | bytes 6944 | tf_op jit(solution)/shard_map/ppermute | solution.py:173
  59.0 11.9 %shard_map.126 = f32[2,2]{1,0:T(2,128)} custom-call(f32[2,2]{1,0:T(2,128)} %pad_maximum_fusion.17.x_ref), custom_call_target="tpu_custom_call" | custom-call | tf_op jit(solution)/shard_map/pallas_call | solution.py:90
  73.1 10.6 %shard_map.127 = f32[2,2]{1,0:T(2,128)} custom-call(f32[2,2]{1,0:T(2,128)} %pad_maximum_fusion.18.x_ref), custom_call_target="tpu_custom_call" | custom-call | tf_op jit(solution)/shard_map/pallas_call | solution.py:90
  87.7 11.2 %shard_map.128 = f32[2,2]{1,0:T(2,128)} custom-call(f32[2,2]{1,0:T(2,128)} %pad_maximum_fusion.19.x_ref), custom_call_target="tpu_custom_call" | custom-call | tf_op jit(solution)/shard_map/pallas_call | solution.py:90
  102.3 2.9 %fusion.227 = (f32[5,2,4,63,256]{4,3,2,1,0:T(8,128)}, f32[5,2,4,63,256]{4,3,2,1,0:T(8,128)}) fusion(f32[5,2,4,64,256]{4,3,2,1,0:T(8,128)S(1)} %constant_dynamic-update-slice_fusion.1), kind=kLoop, calls=%fused_computation.419 | loop fusion | bytes 10321920 | tf_op jit(solution)/shard_map/slice | solution.py:133
  107.2 2.4 copy.20
  110.3 2.4 copy.18
  112.7 3.4 %collective-permute-start.8 = (f32[5,2,4,64,1]{3,2,4,1,0:T(4,128)}, f32[5,2,4,64,1]{3,2,4,1,0:T(4,128)}, u32[]{:S(2)}, u32[]{:S(2)}) collective-permute-start(f32[5,2,4,64,1]{3,2,4,1,0:T(4,128)} %copy.18), channel_id=1, source_target_pairs={{1,0},{2,1},{3,2},{4,3},{5,4},{6,5},{7,6},{0,7},{9,8},{10,9},{11,1... | collective-permute-start | bytes 30728 | tf_op jit(solution)/shard_map/ppermute | solution.py:122
  116.1 3.3 %fusion.225 = (f32[5,2,4,64,255]{4,3,2,1,0:T(8,128)}, f32[5,2,4,64,255]{4,3,2,1,0:T(8,128)}) fusion(f32[5,2,4,64,256]{4,3,2,1,0:T(8,128)S(1)} %constant_dynamic-update-slice_fusion.1), kind=kLoop, calls=%fused_computation.417 | loop fusion | bytes 10444800 | tf_op jit(solution)/shard_map/slice | solution.py:131
  119.4 2.4 collective-permute-start.10
  128.1 3.4 %fusion.217 = (f32[2,64,256]{2,1,0:T(8,128)S(1)}, f32[2,4,64,256]{3,2,1,0:T(8,128)}) fusion(f32[5,2,4,63,256]{4,3,2,1,0:T(8,128)} %get-tuple-element.48, f32[5,2,4,1,256]{4,3,2,1,0:T(1,128)S(1)} %broadcast_multiply_fusion, f32[5,2,4,1,256]{4,3,2,1,0:T(1,128)S(1)} %broadcast_multiply_fusion.2, f32[5,2,4,63,256]{4,3,2,1,0:T(8,128)S(1)} %copy-done.5, ...), kind=kLoop, calls=%fused_computation.414 | loop fusion | flops 3506176 | bytes 12517632 | tf_op jit(solution)/shard_map/reduce_sum | solution.py:288
  136.4 2.9 %collective-permute-done.12 = f32[3,2,4,256]{3,2,1,0:T(4,128)S(1)} collective-permute-done((f32[3,2,4,256]{3,2,1,0:T(4,128)S(1)}, f32[3,2,4,256]{3,2,1,0:T(4,128)S(1)}, u32[]{:S(2)}, u32[]{:S(2)}) %collective-permute-start.12) | collective-permute-done | bytes 24608 | tf_op jit(solution)/shard_map/ppermute | solution.py:173
  143.0 3.4 %collective-permute-done.15 = f32[3,2,72,4]{3,2,1,0:T(8,128)S(1)} collective-permute-done((f32[3,2,72,4]{3,2,1,0:T(8,128)S(1)}, f32[3,2,72,4]{3,2,1,0:T(8,128)S(1)}, u32[]{:S(2)}, u32[]{:S(2)}) %collective-permute-start.15) | collective-permute-done | bytes 6944 | tf_op jit(solution)/shard_map/ppermute | solution.py:174
  146.4 2.4 collective-permute-done.14
  150.7 12.2 %shard_map.129 = f32[2,2]{1,0:T(2,128)} custom-call(f32[2,2]{1,0:T(2,128)} %pad_maximum_fusion.20.x_ref), custom_call_target="tpu_custom_call" | custom-call | tf_op jit(solution)/shard_map/pallas_call | solution.py:90
  165.1 10.6 %shard_map.130 = f32[2,2]{1,0:T(2,128)} custom-call(f32[2,2]{1,0:T(2,128)} %pad_maximum_fusion.21.x_ref), custom_call_target="tpu_custom_call" | custom-call | tf_op jit(solution)/shard_map/pallas_call | solution.py:90
  179.7 11.2 %shard_map.131 = f32[2,2]{1,0:T(2,128)} custom-call(f32[2,2]{1,0:T(2,128)} %pad_maximum_fusion.22.x_ref), custom_call_target="tpu_custom_call" | custom-call | tf_op jit(solution)/shard_map/pallas_call | solution.py:90
  193.8 3.4 %fusion.142 = (f32[2,4,64]{2,1,0:T(4,128)}, f32[1,2,4,64,256]{4,3,2,1,0:T(8,128)S(1)}, f32[1,2,4,64,256]{4,3,2,1,0:T(8,128)S(1)}, f32[1,2,4,64,256]{4,3,2,1,0:T(8,128)S(1)}) fusion(f32[2,4,64,256]{3,2,1,0:T(8,128)} %get-tuple-element.29, f32[2,64,256]{2,1,0:T(8,128)S(1)} %get-tuple-element.75, f32[64,256]{1,0:T(8,128)S(1)} %convert_element_type.31, ...), kind=kLoop, calls=%fused_computation.247 | loop fusion | flops 3669504 | bytes 15271936 | tf_op jit(solution)/shard_map/reduce_sum | solution.py:305
  199.5 3.0 %collective-permute-done.16 = f32[2,4,64]{2,1,0:T(4,128)S(1)} collective-permute-done((f32[2,4,64]{2,1,0:T(4,128)S(1)}, f32[2,4,64]{2,1,0:T(4,128)S(1)}, u32[]{:S(2)}, u32[]{:S(2)}) %collective-permute-start.16) | collective-permute-done | bytes 2080 | tf_op jit(solution)/shard_map/ppermute | solution.py:33
  207.6 9.7 %all_gather.10 = f32[4,64,256]{2,1,0:T(8,128)S(1)} all-gather(f32[2,64,256]{2,1,0:T(8,128)S(1)} %copy-done.34), channel_id=1, replica_groups=mesh['member'=2,'gridy'=8,'gridx'=8] {'member'}, dimensions={0}, use_global_device_ids=true | all-gather | bytes 393216 | tf_op jit(solution)/shard_map/all_gather | solution.py:312
  219.8 2.8 %collective-permute-done.20 = f32[2]{0:T(128)S(1)} collective-permute-done((f32[2]{0:T(128)S(1)}, f32[2]{0:T(128)S(1)}, u32[]{:S(2)}, u32[]{:S(2)}) %collective-permute-start.20) | collective-permute-done | bytes 40 | tf_op jit(solution)/shard_map/ppermute | solution.py:33
  223.5 4.2 %collective-permute-done.21 = f32[2]{0:T(128)S(1)} collective-permute-done((f32[2]{0:T(128)S(1)}, f32[2]{0:T(128)S(1)}, u32[]{:S(2)}, u32[]{:S(2)}) %collective-permute-start.21) | collective-permute-done | bytes 40 | tf_op jit(solution)/shard_map/ppermute | solution.py:33
  228.3 6.5 %all-reduce = f32[4]{0:T(128)S(1)} all-reduce(f32[4]{0:T(128)S(1)} %add_dynamic-update-slice_fusion), channel_id=1, replica_groups=mesh['member'=2,'gridy'=8,'gridx'=8] {'member'}, use_global_device_ids=true, to_apply=%add | all-reduce | flops 4 | bytes 32
  237.9 21.6 %all-gather.2.cloned.1.call-done = f32[4,4,4,64,256]{4,3,2,1,0:T(8,128)} async-done(((f32[4,2,4,64,256]{4,3,2,1,0:T(8,128)}), f32[4,4,4,64,256]{4,3,2,1,0:T(8,128)}) %all-gather.2.cloned.1.call-update) | async-done | bytes 4194320 | tf_op jit(solution)/shard_map/all_gather | solution.py:311
  259.5 2.9 %gather_fusion = f32[2,4,4,64,256]{4,3,2,1,0:T(8,128)S(1)} fusion(f32[4,4,4,64,256]{4,3,2,1,0:T(8,128)} %all-gather.2.cloned.1.call-done, s32[1024]{0:T(1024)S(1)} %pad_clamp_fusion), kind=kCustom, calls=%fused_computation | custom fusion | bytes 4194312 | tf_op jit(solution)/shard_map/jit(_take)/gather | solution.py:315
  (243 shorter events, 77.5 us)
Async XLA Ops:
  7.2 252.3 %all-gather.2.cloned.1.call-start = ((), (), s32[]{:S(2)}) async-start(), calls=%async_computation | async-start | bytes 6291456 | tf_op jit(solution)/shard_map/all_gather | solution.py:311
  11.0 23.4 %collective-permute-start.3 = (f32[5,2,4,1,256]{4,3,2,1,0:T(1,128)S(1)}, f32[5,2,4,1,256]{4,3,2,1,0:T(1,128)S(1)}, u32[]{:S(2)}, u32[]{:S(2)}) collective-permute-start(f32[5,2,4,1,256]{4,3,2,1,0:T(1,128)S(1)} %get-tuple-element.58), channel_id=1, source_target_pairs={{0,8},{8,16},{16,24},{24,32},{32,40},{40,48},{48,56},{56,0},{1,9},... | collective-permute-start | bytes 122888 | tf_op jit(solution)/shard_map/ppermute | solution.py:121
  11.0 23.4 %collective-permute-start.2 = (f32[5,2,4,1,256]{4,3,2,1,0:T(1,128)S(1)}, f32[5,2,4,1,256]{4,3,2,1,0:T(1,128)S(1)}, u32[]{:S(2)}, u32[]{:S(2)}) collective-permute-start(f32[5,2,4,1,256]{4,3,2,1,0:T(1,128)S(1)} %get-tuple-element.57), channel_id=1, source_target_pairs={{8,0},{16,8},{24,16},{32,24},{40,32},{48,40},{56,48},{0,56},{9,1},... | collective-permute-start | bytes 122888 | tf_op jit(solution)/shard_map/ppermute | solution.py:120
  17.7 13.6 %collective-permute-start.1 = (f32[5,2,4,64,1]{3,2,4,1,0:T(4,128)S(1)}, f32[5,2,4,64,1]{3,2,4,1,0:T(4,128)S(1)}, u32[]{:S(2)}, u32[]{:S(2)}) collective-permute-start(f32[5,2,4,64,1]{3,2,4,1,0:T(4,128)S(1)} %copy.16), channel_id=1, source_target_pairs={{0,1},{1,2},{2,3},{3,4},{4,5},{5,6},{6,7},{7,0},{8,9},{9,10},{10,1... | collective-permute-start | bytes 30728 | tf_op jit(solution)/shard_map/ppermute | solution.py:123
  21.1 11.6 %collective-permute-start = (f32[5,2,4,64,1]{3,2,4,1,0:T(4,128)S(1)}, f32[5,2,4,64,1]{3,2,4,1,0:T(4,128)S(1)}, u32[]{:S(2)}, u32[]{:S(2)}) collective-permute-start(f32[5,2,4,64,1]{3,2,4,1,0:T(4,128)S(1)} %copy.14), channel_id=1, source_target_pairs={{1,0},{2,1},{3,2},{4,3},{5,4},{6,5},{7,6},{0,7},{9,8},{10,9},{11,1... | collective-permute-start | bytes 30728 | tf_op jit(solution)/shard_map/ppermute | solution.py:122
  30.9 26.2 %copy-start.47 = (f32[72]{0:T(128)}, f32[72]{0:T(128)S(1)}, u32[]{:S(2)}) copy-start(f32[72]{0:T(128)S(1)} %and_convert_fusion) | copy-start | bytes 868
  31.0 26.5 %copy-start.45 = (f32[70]{0:T(128)}, f32[70]{0:T(128)S(1)}, u32[]{:S(2)}) copy-start(f32[70]{0:T(128)S(1)} %slice.535) | copy-start | bytes 844
  31.0 40.7 %copy-start.39 = (f32[68]{0:T(128)}, f32[68]{0:T(128)S(1)}, u32[]{:S(2)}) copy-start(f32[68]{0:T(128)S(1)} %slice.542) | copy-start | bytes 820
  31.1 54.4 %copy-start.37 = (f32[66]{0:T(128)}, f32[66]{0:T(128)S(1)}, u32[]{:S(2)}) copy-start(f32[66]{0:T(128)S(1)} %slice.553) | copy-start | bytes 796
  31.2 55.6 %copy-start.52 = (f32[64]{0:T(128)}, f32[64]{0:T(128)S(1)}, u32[]{:S(2)}) copy-start(f32[64]{0:T(128)S(1)} %slice.564) | copy-start | bytes 772
  41.4 2.0 collective-permute-start.5
  41.5 4.5 %collective-permute-start.4 = (f32[3,2,4,256]{3,2,1,0:T(4,128)S(1)}, f32[3,2,4,256]{3,2,1,0:T(4,128)S(1)}, u32[]{:S(2)}, u32[]{:S(2)}) collective-permute-start(f32[3,2,4,256]{3,2,1,0:T(4,128)S(1)} %get-tuple-element.71), channel_id=1, source_target_pairs={{0,8},{8,16},{16,24},{24,32},{32,40},{40,48},{48,56},{56,0},{1,9},... | collective-permute-start | bytes 73736 | tf_op jit(solution)/shard_map/ppermute | solution.py:173
  46.1 7.2 %collective-permute-start.7 = (f32[3,2,72,4]{3,2,1,0:T(8,128)S(1)}, f32[3,2,72,4]{3,2,1,0:T(8,128)S(1)}, u32[]{:S(2)}, u32[]{:S(2)}) collective-permute-start(f32[3,2,72,4]{3,2,1,0:T(8,128)S(1)} %get-tuple-element.68), channel_id=1, source_target_pairs={{1,0},{2,1},{3,2},{4,3},{5,4},{6,5},{7,6},{0,7},{9,8},{10,9},{11,1... | collective-permute-start | bytes 20744 | tf_op jit(solution)/shard_map/ppermute | solution.py:174
  48.2 8.9 %collective-permute-start.6 = (f32[3,2,72,4]{3,2,1,0:T(8,128)S(1)}, f32[3,2,72,4]{3,2,1,0:T(8,128)S(1)}, u32[]{:S(2)}, u32[]{:S(2)}) collective-permute-start(f32[3,2,72,4]{3,2,1,0:T(8,128)S(1)} %get-tuple-element.67), channel_id=1, source_target_pairs={{0,1},{1,2},{2,3},{3,4},{4,5},{5,6},{6,7},{7,0},{8,9},{9,10},{10,1... | collective-permute-start | bytes 20744 | tf_op jit(solution)/shard_map/ppermute | solution.py:173
  83.8 15.2 %copy-start.42 = (f32[2,2]{1,0:T(2,128)S(1)}, f32[2,2]{1,0:T(2,128)}, u32[]{:S(2)}) copy-start(f32[2,2]{1,0:T(2,128)} %shard_map.127) | copy-start | bytes 52
  101.9 39.8 %copy-start.20 = (f32[2,64,256]{2,1,0:T(8,128)}, f32[2,64,256]{2,1,0:T(8,128)S(1)}, u32[]{:S(2)}) copy-start(f32[2,64,256]{2,1,0:T(8,128)S(1)} %get-tuple-element.79) | copy-start | bytes 393220
  101.9 39.8 %copy-start.21 = (f32[2,64,256]{2,1,0:T(8,128)}, f32[2,64,256]{2,1,0:T(8,128)S(1)}, u32[]{:S(2)}) copy-start(f32[2,64,256]{2,1,0:T(8,128)S(1)} %get-tuple-element.80) | copy-start | bytes 393220
  107.2 19.1 %collective-permute-start.11 = (f32[5,2,4,1,256]{4,3,2,1,0:T(1,128)S(1)}, f32[5,2,4,1,256]{4,3,2,1,0:T(1,128)}, u32[]{:S(2)}, u32[]{:S(2)}) collective-permute-start(f32[5,2,4,1,256]{4,3,2,1,0:T(1,128)S(1)} %get-tuple-element.50), channel_id=1, source_target_pairs={{0,8},{8,16},{16,24},{24,32},{32,40},{40,48},{48,56},{56,0},{1,9},... | collective-permute-start | bytes 122888 | tf_op jit(solution)/shard_map/ppermute | solution.py:121
  109.6 12.2 %collective-permute-start.9 = (f32[5,2,4,64,1]{3,2,4,1,0:T(4,128)}, f32[5,2,4,64,1]{3,2,4,1,0:T(4,128)}, u32[]{:S(2)}, u32[]{:S(2)}) collective-permute-start(f32[5,2,4,64,1]{3,2,4,1,0:T(4,128)} %copy.20), channel_id=1, source_target_pairs={{0,1},{1,2},{2,3},{3,4},{4,5},{5,6},{6,7},{7,0},{8,9},{9,10},{10,1... | collective-permute-start | bytes 30728 | tf_op jit(solution)/shard_map/ppermute | solution.py:123
  112.7 11.4 %collective-permute-start.8 = (f32[5,2,4,64,1]{3,2,4,1,0:T(4,128)}, f32[5,2,4,64,1]{3,2,4,1,0:T(4,128)}, u32[]{:S(2)}, u32[]{:S(2)}) collective-permute-start(f32[5,2,4,64,1]{3,2,4,1,0:T(4,128)} %copy.18), channel_id=1, source_target_pairs={{1,0},{2,1},{3,2},{4,3},{5,4},{6,5},{7,6},{0,7},{9,8},{10,9},{11,1... | collective-permute-start | bytes 30728 | tf_op jit(solution)/shard_map/ppermute | solution.py:122
  119.4 7.8 %collective-permute-start.10 = (f32[5,2,4,1,256]{4,3,2,1,0:T(1,128)S(1)}, f32[5,2,4,1,256]{4,3,2,1,0:T(1,128)}, u32[]{:S(2)}, u32[]{:S(2)}) collective-permute-start(f32[5,2,4,1,256]{4,3,2,1,0:T(1,128)S(1)} %get-tuple-element.49), channel_id=1, source_target_pairs={{8,0},{16,8},{24,16},{32,24},{40,32},{48,40},{56,48},{0,56},{9,1},... | collective-permute-start | bytes 122888 | tf_op jit(solution)/shard_map/ppermute | solution.py:120
  134.7 1.7 collective-permute-start.13
  134.9 4.5 %collective-permute-start.12 = (f32[3,2,4,256]{3,2,1,0:T(4,128)S(1)}, f32[3,2,4,256]{3,2,1,0:T(4,128)S(1)}, u32[]{:S(2)}, u32[]{:S(2)}) collective-permute-start(f32[3,2,4,256]{3,2,1,0:T(4,128)S(1)} %get-tuple-element.69), channel_id=1, source_target_pairs={{0,8},{8,16},{16,24},{24,32},{32,40},{40,48},{48,56},{56,0},{1,9},... | collective-permute-start | bytes 73736 | tf_op jit(solution)/shard_map/ppermute | solution.py:173
  139.5 6.9 %collective-permute-start.15 = (f32[3,2,72,4]{3,2,1,0:T(8,128)S(1)}, f32[3,2,72,4]{3,2,1,0:T(8,128)S(1)}, u32[]{:S(2)}, u32[]{:S(2)}) collective-permute-start(f32[3,2,72,4]{3,2,1,0:T(8,128)S(1)} %get-tuple-element.66), channel_id=1, source_target_pairs={{1,0},{2,1},{3,2},{4,3},{5,4},{6,5},{7,6},{0,7},{9,8},{10,9},{11,1... | collective-permute-start | bytes 20744 | tf_op jit(solution)/shard_map/ppermute | solution.py:174
  139.9 8.9 %collective-permute-start.14 = (f32[3,2,72,4]{3,2,1,0:T(8,128)S(1)}, f32[3,2,72,4]{3,2,1,0:T(8,128)S(1)}, u32[]{:S(2)}, u32[]{:S(2)}) collective-permute-start(f32[3,2,72,4]{3,2,1,0:T(8,128)S(1)} %get-tuple-element.65), channel_id=1, source_target_pairs={{0,1},{1,2},{2,3},{3,4},{4,5},{5,6},{6,7},{7,0},{8,9},{9,10},{10,1... | collective-permute-start | bytes 20744 | tf_op jit(solution)/shard_map/ppermute | solution.py:173
  143.0 21.0 %copy-start.38 = (f32[66]{0:T(128)S(1)}, f32[66]{0:T(128)}, u32[]{:S(2)}) copy-start(f32[66]{0:T(128)} %copy-done.37) | copy-start | bytes 796
  198.8 3.7 %collective-permute-start.16 = (f32[2,4,64]{2,1,0:T(4,128)S(1)}, f32[2,4,64]{2,1,0:T(4,128)S(1)}, u32[]{:S(2)}, u32[]{:S(2)}) collective-permute-start(f32[2,4,64]{2,1,0:T(4,128)S(1)} %copy-done.36), channel_id=1, source_target_pairs={{0,1},{1,0},{2,3},{3,2},{4,5},{5,4},{6,7},{7,6},{8,9},{9,8},{10,11... | collective-permute-start | bytes 6152 | tf_op jit(solution)/shard_map/ppermute | solution.py:33
  202.5 3.6 %collective-permute-start.17 = (f32[2,4,64]{2,1,0:T(4,128)S(1)}, f32[2,4,64]{2,1,0:T(4,128)S(1)}, u32[]{:S(2)}, u32[]{:S(2)}) collective-permute-start(f32[2,4,64]{2,1,0:T(4,128)S(1)} %add.411), channel_id=1, source_target_pairs={{0,2},{1,3},{2,0},{3,1},{4,6},{5,7},{6,4},{7,5},{8,10},{9,11},{10,... | collective-permute-start | bytes 6152 | tf_op jit(solution)/shard_map/ppermute | solution.py:33
  206.1 11.2 %collective-permute-start.18 = (f32[2,4,64]{2,1,0:T(4,128)S(1)}, f32[2,4,64]{2,1,0:T(4,128)S(1)}, u32[]{:S(2)}, u32[]{:S(2)}) collective-permute-start(f32[2,4,64]{2,1,0:T(4,128)S(1)} %add.412), channel_id=1, source_target_pairs={{0,4},{1,5},{2,6},{3,7},{4,0},{5,1},{6,2},{7,3},{8,12},{9,13},{10,... | collective-permute-start | bytes 6152 | tf_op jit(solution)/shard_map/ppermute | solution.py:33
  217.9 1.1 collective-permute-start.19
  219.1 3.5 %collective-permute-start.20 = (f32[2]{0:T(128)S(1)}, f32[2]{0:T(128)S(1)}, u32[]{:S(2)}, u32[]{:S(2)}) collective-permute-start(f32[2]{0:T(128)S(1)} %fusion.213), channel_id=1, source_target_pairs={{0,16},{8,24},{16,0},{24,8},{32,48},{40,56},{48,32},{56,40},{1,17}... | collective-permute-start | bytes 32 | tf_op jit(solution)/shard_map/ppermute | solution.py:33
  222.6 5.0 %collective-permute-start.21 = (f32[2]{0:T(128)S(1)}, f32[2]{0:T(128)S(1)}, u32[]{:S(2)}, u32[]{:S(2)}) collective-permute-start(f32[2]{0:T(128)S(1)} %add.415), channel_id=1, source_target_pairs={{0,32},{8,40},{16,48},{24,56},{32,0},{40,8},{48,16},{56,24},{1,33}... | collective-permute-start | bytes 32 | tf_op jit(solution)/shard_map/ppermute | solution.py:33
  (47 other events, 295.0 us)
Sparse Core Ops, SparseCore 0:
  198.9 60.5 all-gather.1
where the time goes:
time: 273 us; the launch traced here: 271 us
  Pallas kernels  67.8 us (25%)
  waiting for transfers between devices  54.3 us (20%)
  local copies, waits for them, and re-layouts  46.1 us (17%)
  other arithmetic  45.7 us (17%)
  starting transfers between devices  24.6 us (9%)
  blocking collectives  16.2 us (6%)
  between operations  16.2 us (6%)
    pallas_call x6, Pallas kernels, grid_sum(): pl.pallas_call(functools.partial(gather_sum_kernel, ny, nx), out_shape=ja...  67.8 us
    all_gather x1, waiting for transfers between devices, shards(): lax.all_gather(state_stack, 'member', axis=1, tiled=True)  21.6 us
    ppermute x6, waiting for transfers between devices, tree_sum(): values = values + lax.ppermute(values, axis, pairs)  12.6 us
    ppermute x4, waiting for transfers between devices, padded_2(): lax.ppermute(lax.slice_in_dim(block, size - width, size, axis=dim), axis,...  11.7 us
    all_gather x1, blocking collectives, shards(): lax.all_gather(eta, 'member', axis=0, tiled=True)  9.67 us
    ppermute x4, waiting for transfers between devices, padded_2(): lax.ppermute(lax.slice_in_dim(block, 0, width, axis=dim), axis, backward)  8.33 us
    slice x4, local copies, waits for them, and re-layouts, exchange(): lax.slice_in_dim(block, 0, 1, axis=xdim)  8.04 us
    unnamed x118, local copies, waits for them, and re-layouts  7.84 us
  transfers between devices with their start and end apart: 23, of which 13 were waited for; matrix products, arithmetic and copies ran while one was open for 14% of the time, Pallas kernels for 0%

commit v1 on v0

--- a/solution.py
+++ b/solution.py
@@ -105,6 +105,147 @@
     )(values)
 
 
+def exchange_sum(k, vec, ny, nx, bufs, device_ids):
+    send_y, recv_y, send_x, recv_x, sy, ry, sx, rx = bufs
+    my, mx, along_y, along_x = device_ids
+    mesh_id = pl.DeviceIdType.MESH
+
+    def phase(value, send_buf, recv, send_sem, recv_sem, count, me, device):
+        send_buf[k] = value
+        recv[k, me] = value
+        sent = []
+        for d in range(1, count):
+            peer = (me + d) % count
+            copy = pltpu.make_async_remote_copy(
+                src_ref=send_buf.at[k],
+                dst_ref=recv.at[k, me],
+                send_sem=send_sem.at[k, peer],
+                recv_sem=recv_sem.at[k, me],
+                device_id=device(peer),
+                device_id_type=mesh_id,
+            )
+            copy.start()
+            sent.append(copy)
+        for d in range(1, count):
+            peer = (me + d) % count
+            pltpu.make_async_remote_copy(
+                src_ref=send_buf.at[k],
+                dst_ref=recv.at[k, peer],
+                send_sem=send_sem.at[k, peer],
+                recv_sem=recv_sem.at[k, peer],
+                device_id=device(peer),
+                device_id_type=mesh_id,
+            ).wait_recv()
+        for copy in sent:
+            copy.wait_send()
+        total = recv[k, 0]
+        for j in range(1, count):
+            total = total + recv[k, j]
+        return total
+
+    partial = phase(vec, send_y, recv_y, sy, ry, ny, my, along_y)
+    return phase(partial, send_x, recv_x, sx, rx, nx, mx, along_x)
+
+
+def solve_kernel(ny, nx, rhs_ref, inside_ref, own_ref, out_ref, *bufs):
+    mesh_id = pl.DeviceIdType.MESH
+    member = lax.axis_index("member")
+    my = lax.axis_index("gridy")
+    mx = lax.axis_index("gridx")
+    along_y = lambda p: (member, p, mx)
+    along_x = lambda p: (member, my, p)
+    barrier = pltpu.get_barrier_semaphore()
+    for d in range(1, ny):
+        pl.semaphore_signal(barrier, 1, device_id=along_y((my + d) % ny), device_id_type=mesh_id)
+    for d in range(1, nx):
+        pl.semaphore_signal(barrier, 1, device_id=along_x((mx + d) % nx), device_id_type=mesh_id)
+    pl.semaphore_wait(barrier, (ny - 1) + (nx - 1))
+
+    members = rhs_ref.shape[0]
+    rows, cols = rhs_ref.shape[1], rhs_ref.shape[2]
+    inside = inside_ref[...]
+    own = own_ref[...] > 0.5
+
+    def east(f):
+        return pltpu.roll(f, cols - 1, 1)
+
+    def west(f):
+        return pltpu.roll(f, 1, 1)
+
+    def north(f):
+        return pltpu.roll(f, rows - 1, 0)
+
+    def south(f):
+        return pltpu.roll(f, 1, 0)
+
+    def apply(f):
+        return ((1.0 + 4.0 * SURF_C) * f - SURF_C * (east(f) + west(f) + north(f) + south(f))) * inside
+
+    def total(f):
+        return jnp.sum(jnp.where(own, f, 0.0), axis=(0, 1), keepdims=True)
+
+    lane = lax.broadcasted_iota(jnp.int32, (8, 128), 1)
+    residual = [rhs_ref[m] for m in range(members)]
+    direction = [None] * members
+    image_dir = [None] * members
+    solution = [None] * members
+    gamma_prev = [None] * members
+    alpha_prev = [None] * members
+    for count in range(ITERS):
+        image_res = [apply(residual[m]) for m in range(members)]
+        vec = jnp.zeros((8, 128), jnp.float32)
+        for m in range(members):
+            vec = jnp.where(lane == 2 * m, total(residual[m] * residual[m]), vec)
+            vec = jnp.where(lane == 2 * m + 1, total(residual[m] * image_res[m]), vec)
+        sums = exchange_sum(count, vec, ny, nx, bufs, (my, mx, along_y, along_x))
+        for m in range(members):
+            gamma = sums[0:1, 2 * m : 2 * m + 1]
+            delta = sums[0:1, 2 * m + 1 : 2 * m + 2]
+            if count == 0:
+                alpha = gamma / delta
+                direction[m] = residual[m]
+                image_dir[m] = image_res[m]
+                solution[m] = alpha * direction[m]
+            else:
+                beta = gamma / gamma_prev[m]
+                alpha = gamma / (delta - beta * gamma / alpha_prev[m])
+                direction[m] = residual[m] + beta * direction[m]
+                image_dir[m] = image_res[m] + beta * image_dir[m]
+                solution[m] = solution[m] + alpha * direction[m]
+            if count < ITERS - 1:
+                residual[m] = residual[m] - alpha * image_dir[m]
+            gamma_prev[m] = gamma
+            alpha_prev[m] = alpha
+    for m in range(members):
+        x = solution[m]
+        out_ref[0, m] = x
+        out_ref[1, m] = east(x) - west(x)
+        out_ref[2, m] = north(x) - south(x)
+
+
+def surface_kernel_solve(rhs, inside, own):
+    ny = lax.axis_size("gridy")
+    nx = lax.axis_size("gridx")
+    shape = rhs.shape
+    return pl.pallas_call(
+        functools.partial(solve_kernel, ny, nx),
+        out_shape=jax.ShapeDtypeStruct((3,) + shape, jnp.float32),
+        in_specs=[pl.BlockSpec(memory_space=pltpu.VMEM)] * 3,
+        out_specs=pl.BlockSpec(memory_space=pltpu.VMEM),
+        scratch_shapes=[
+            pltpu.VMEM((ITERS, 8, 128), jnp.float32),
+            pltpu.VMEM((ITERS, ny, 8, 128), jnp.float32),
+            pltpu.VMEM((ITERS, 8, 128), jnp.float32),
+            pltpu.VMEM((ITERS, nx, 8, 128), jnp.float32),
+            pltpu.SemaphoreType.DMA((ITERS, ny)),
+            pltpu.SemaphoreType.DMA((ITERS, ny)),
+            pltpu.SemaphoreType.DMA((ITERS, nx)),
+            pltpu.SemaphoreType.DMA((ITERS, nx)),
+        ],
+        compiler_params=pltpu.CompilerParams(collective_id=1, has_side_effects=True),
+    )(rhs, inside, own)
+
+
 def ring(axis):
     count = lax.axis_size(axis)
     forward = [(i, (i + 1) % count) for i in range(count)]
@@ -249,6 +390,14 @@
     coriolis = (CORI_K * (2.0 * latitude / total_rows - 1.0))[:, None]
     wide_rows = tile_row * rows - (ITERS + 1) + jnp.arange(rows + 2 * (ITERS + 1), dtype=jnp.int32)
     inside = ((wide_rows >= 0) & (wide_rows < total_rows)).astype(jnp.float32)[:, None]
+    halo = ITERS + 1
+    lanes = 128 * ((cols + 2 * halo + 127) // 128)
+    wide_inside = jnp.broadcast_to(inside, (rows + 2 * halo, lanes))
+    row_at = lax.broadcasted_iota(jnp.int32, (rows + 2 * halo, lanes), 0)
+    col_at = lax.broadcasted_iota(jnp.int32, (rows + 2 * halo, lanes), 1)
+    own_mask = (
+        (row_at >= halo) & (row_at < halo + rows) & (col_at >= halo) & (col_at < halo + cols)
+    ).astype(jnp.float32)
     for count in range(STEPS):
         press = pressure(temp, salt)
         volume = jnp.stack((temp, salt, uvel, vvel, press))
@@ -293,10 +442,14 @@
         rhs = (centre[2] - DIV_K * 0.5 * (east_t[0] - west_t[0] + (north_t[1] - south_t[1]))) * rows_at(
             inside, halo, halo - 1
         )
-        wide_eta = surface_solve(rhs, inside, halo - 1, halo)
-        eta, east_e, west_e, north_e, south_e = around(wide_eta)
-        uvel = ocean * (ustar - GRAV_K * 0.5 * (east_e - west_e)[:, None])
-        vvel = ocean * (vstar - GRAV_K * 0.5 * (north_e - south_e)[:, None])
+        lanes = 128 * ((cols + 2 * halo + 127) // 128)
+        rhs_tile = jnp.pad(rhs, ((0, 0), (1, 1), (1, lanes - cols - 2 * halo + 1)))
+        solved = surface_kernel_solve(rhs_tile, wide_inside, own_mask)
+        eta = solved[0, :, halo : halo + rows, halo : halo + cols]
+        east_west = solved[1, :, halo : halo + rows, halo : halo + cols]
+        north_south = solved[2, :, halo : halo + rows, halo : halo + cols]
+        uvel = ocean * (ustar - GRAV_K * 0.5 * east_west[:, None])
+        vvel = ocean * (vstar - GRAV_K * 0.5 * north_south[:, None])
         temp = temp_next
         salt = salt_next
     zonal_scale = 1.0 / jnp.sqrt(jnp.float32(total_cols))

time: 273 us -> 252 us (0.923)
  other arithmetic: 45.7 us -> 30.7 us
  Pallas kernels: 67.8 us -> 59.7 us
  local copies, waits for them, and re-layouts: 46.1 us -> 49 us
    pallas_call x6 -> x2, Pallas kernels: 67.8 us -> 59.7 us  [surface_kernel_solve(): pl.pallas_call(functools.partial(solve_kernel, ny, nx), out_shape=jax.Sha...]
    div x6 -> x0, other arithmetic: 4.59 us -> none  [the longest x4 3.1 us: surface_solve(): alpha = gamma / (delta - beta * gamma / alpha_prev)]
    another operation x7 -> x0, other arithmetic: 4.34 us -> none  [the longest x6 3.47 us: surface_solve(): jnp.stack([member_total(own_res * own_res), member_total(own_res * own_im...]
    add x4 -> x0, other arithmetic: 4.32 us -> none  [the longest x2 2.48 us: surface_solve(): solution = crop(solution, wide_x - wide_r) + widen(alpha) * direction]
    sub x4 -> x0, other arithmetic: 3.24 us -> none  [surface_solve(): residual = crop(residual, 1) - widen(alpha) * image_dir]
    slice x1 -> x2, other arithmetic: 0.86 us -> 4.05 us  [shards(): eta = solved[0, :, halo:halo + rows, halo:halo + cols]]
    unnamed x118 -> x84, local copies, waits for them, and re-layouts: 7.84 us -> 8.55 us
  transfers between devices with their start and end apart: 23 -> 23, of which waited for: 13 -> 13; matrix products, arithmetic and copies ran while one was open for 14% -> 15% of each run, Pallas kernels for 0% -> 0%
where the time goes in v1:
time: 252 us; the launch traced here: 250 us
  Pallas kernels  59.7 us (24%)
  waiting for transfers between devices  54.6 us (22%)
  local copies, waits for them, and re-layouts  49 us (19%)
  other arithmetic  30.7 us (12%)
  starting transfers between devices  24.2 us (10%)
  blocking collectives  16.3 us (6%)
  between operations  16 us (6%)
    pallas_call x2, Pallas kernels, surface_kernel_solve(): pl.pallas_call(functools.partial(solve_kernel, ny, nx), out_shape=jax.Sha...  59.7 us
    all_gather x1, waiting for transfers between devices, shards(): lax.all_gather(state_stack, 'member', axis=1, tiled=True)  21.6 us
    ppermute x6, waiting for transfers between devices, tree_sum(): values = values + lax.ppermute(values, axis, pairs)  13.1 us
    ppermute x4, waiting for transfers between devices, padded_2(): lax.ppermute(lax.slice_in_dim(block, size - width, size, axis=dim), axis,...  11.5 us
    all_gather x1, blocking collectives, shards(): lax.all_gather(eta, 'member', axis=0, tiled=True)  9.75 us
    unnamed x84, local copies, waits for them, and re-layouts  8.55 us
    ppermute x4, waiting for transfers between devices, padded_2(): lax.ppermute(lax.slice_in_dim(block, 0, width, axis=dim), axis, backward)  8.35 us
    slice x4, local copies, waits for them, and re-layouts, exchange(): lax.slice_in_dim(block, 0, 1, axis=xdim)  7.98 us
  transfers between devices with their start and end apart: 23, of which 13 were waited for; matrix products, arithmetic and copies ran while one was open for 15% of the time, Pallas kernels for 0%

profile of v1, /device:TPU:0, one launch (start us, length us, event | category | flops | bytes accessed | tf_op | source)
XLA Modules:
  0.0 250.4 jit_solution(5329602145819950775)
XLA Ops:
  11.0 2.9 %collective-permute-start.2 = (f32[5,2,4,1,256]{4,3,2,1,0:T(1,128)S(1)}, f32[5,2,4,1,256]{4,3,2,1,0:T(1,128)S(1)}, u32[]{:S(2)}, u32[]{:S(2)}) collective-permute-start(f32[5,2,4,1,256]{4,3,2,1,0:T(1,128)S(1)} %get-tuple-element.35), channel_id=1, source_target_pairs={{8,0},{16,8},{24,16},{32,24},{40,32},{48,40},{56,48},{0,56},{9,1},... | collective-permute-start | bytes 122888 | tf_op jit(solution)/shard_map/ppermute | solution.py:261
  21.1 3.5 %collective-permute-start = (f32[5,2,4,64,1]{3,2,4,1,0:T(4,128)S(1)}, f32[5,2,4,64,1]{3,2,4,1,0:T(4,128)S(1)}, u32[]{:S(2)}, u32[]{:S(2)}) collective-permute-start(f32[5,2,4,64,1]{3,2,4,1,0:T(4,128)S(1)} %copy.14), channel_id=1, source_target_pairs={{1,0},{2,1},{3,2},{4,3},{5,4},{6,5},{7,6},{0,7},{9,8},{10,9},{11,1... | collective-permute-start | bytes 30728 | tf_op jit(solution)/shard_map/ppermute | solution.py:263
  24.6 2.8 %fusion.181 = (f32[5,2,4,63,256]{4,3,2,1,0:T(8,128)}, f32[5,2,4,63,256]{4,3,2,1,0:T(8,128)}) fusion(f32[5,2,4,64,256]{4,3,2,1,0:T(8,128)S(1)} %constant_dynamic-update-slice_fusion), kind=kLoop, calls=%fused_computation.319 | loop fusion | bytes 10321920 | tf_op jit(solution)/shard_map/slice | solution.py:274
  27.4 3.4 %fusion.179 = (f32[5,2,4,64,255]{4,3,2,1,0:T(8,128)}, f32[5,2,4,64,255]{4,3,2,1,0:T(8,128)}) fusion(f32[5,2,4,64,256]{4,3,2,1,0:T(8,128)S(1)} %constant_dynamic-update-slice_fusion), kind=kLoop, calls=%fused_computation.317 | loop fusion | bytes 10444800 | tf_op jit(solution)/shard_map/slice | solution.py:272
  35.0 3.1 %fusion.169 = (f32[2,64,256]{2,1,0:T(8,128)S(1)}, f32[2,4,64,256]{3,2,1,0:T(8,128)S(1)}) fusion(f32[2,4,64,256]{3,2,1,0:T(8,128)} %param.9, f32[5,2,4,63,256]{4,3,2,1,0:T(8,128)} %get-tuple-element.34, f32[5,2,4,1,256]{4,3,2,1,0:T(1,128)S(1)} %broadcast_multiply_fusion.1, f32[5,2,4,1,256]{4,3,2,1,0:T(1,128)S(1)} %broadcast_multiply_fusion.3, ...), kind=kLoop, calls=%fused_computation.311 | loop fusion | flops 2981888 | bytes 12255488 | tf_op jit(solution)/shard_map/reduce_sum | solution.py:437
  44.0 2.5 %collective-permute-done.4 = f32[3,2,4,256]{3,2,1,0:T(4,128)S(1)} collective-permute-done((f32[3,2,4,256]{3,2,1,0:T(4,128)S(1)}, f32[3,2,4,256]{3,2,1,0:T(4,128)S(1)}, u32[]{:S(2)}, u32[]{:S(2)}) %collective-permute-start.4) | collective-permute-done | bytes 24608 | tf_op jit(solution)/shard_map/ppermute | solution.py:314
  46.7 2.1 collective-permute-start.7
  50.1 3.8 %collective-permute-done.7 = f32[3,2,72,4]{3,2,1,0:T(8,128)S(1)} collective-permute-done((f32[3,2,72,4]{3,2,1,0:T(8,128)S(1)}, f32[3,2,72,4]{3,2,1,0:T(8,128)S(1)}, u32[]{:S(2)}, u32[]{:S(2)}) %collective-permute-start.7) | collective-permute-done | bytes 6944 | tf_op jit(solution)/shard_map/ppermute | solution.py:315
  53.9 3.8 %collective-permute-done.6 = f32[3,2,72,4]{3,2,1,0:T(8,128)S(1)} collective-permute-done((f32[3,2,72,4]{3,2,1,0:T(8,128)S(1)}, f32[3,2,72,4]{3,2,1,0:T(8,128)S(1)}, u32[]{:S(2)}, u32[]{:S(2)}) %collective-permute-start.6) | collective-permute-done | bytes 6944 | tf_op jit(solution)/shard_map/ppermute | solution.py:314
  60.0 29.7 %shard_map.126 = f32[3,2,72,384]{3,2,1,0:T(8,128)} custom-call(f32[2,72,384]{2,1,0:T(8,128)} %pad.7.rhs_ref, f32[72,384]{1,0:T(8,128)} %broadcast_in_dim.20.inside_ref, f32[72,384]{1,0:T(8,128)} %and_convert_fusion.own_ref), custom_call_target="tpu_custom_call" | custom-call | tf_op jit(solution)/shard_map/pallas_call | solution.py:230
  89.7 2.1 fusion.183
  93.2 2.9 %fusion.177 = (f32[5,2,4,63,256]{4,3,2,1,0:T(8,128)}, f32[5,2,4,63,256]{4,3,2,1,0:T(8,128)}) fusion(f32[5,2,4,64,256]{4,3,2,1,0:T(8,128)S(1)} %constant_dynamic-update-slice_fusion.1), kind=kLoop, calls=%fused_computation.315 | loop fusion | bytes 10321920 | tf_op jit(solution)/shard_map/slice | solution.py:274
  98.1 2.4 copy.20
  101.2 2.4 copy.18
  103.5 3.4 %collective-permute-start.8 = (f32[5,2,4,64,1]{3,2,4,1,0:T(4,128)}, f32[5,2,4,64,1]{3,2,4,1,0:T(4,128)}, u32[]{:S(2)}, u32[]{:S(2)}) collective-permute-start(f32[5,2,4,64,1]{3,2,4,1,0:T(4,128)} %copy.18), channel_id=1, source_target_pairs={{1,0},{2,1},{3,2},{4,3},{5,4},{6,5},{7,6},{0,7},{9,8},{10,9},{11,1... | collective-permute-start | bytes 30728 | tf_op jit(solution)/shard_map/ppermute | solution.py:263
  107.0 3.3 %fusion.175 = (f32[5,2,4,64,255]{4,3,2,1,0:T(8,128)}, f32[5,2,4,64,255]{4,3,2,1,0:T(8,128)}) fusion(f32[5,2,4,64,256]{4,3,2,1,0:T(8,128)S(1)} %constant_dynamic-update-slice_fusion.1), kind=kLoop, calls=%fused_computation.313 | loop fusion | bytes 10444800 | tf_op jit(solution)/shard_map/slice | solution.py:272
  110.3 2.4 collective-permute-start.10
  112.7 2.3 copy.21
  115.0 2.3 copy.19
  119.0 3.4 %fusion.167 = (f32[2,64,256]{2,1,0:T(8,128)S(1)}, f32[2,4,64,256]{3,2,1,0:T(8,128)}) fusion(f32[5,2,4,63,256]{4,3,2,1,0:T(8,128)} %get-tuple-element.26, f32[5,2,4,1,256]{4,3,2,1,0:T(1,128)S(1)} %broadcast_multiply_fusion, f32[5,2,4,1,256]{4,3,2,1,0:T(1,128)S(1)} %broadcast_multiply_fusion.2, f32[5,2,4,63,256]{4,3,2,1,0:T(8,128)S(1)} %copy-done.5, ...), kind=kLoop, calls=%fused_computation.310 | loop fusion | flops 3506176 | bytes 12517632 | tf_op jit(solution)/shard_map/reduce_sum | solution.py:437
  127.4 2.9 %collective-permute-done.12 = f32[3,2,4,256]{3,2,1,0:T(4,128)S(1)} collective-permute-done((f32[3,2,4,256]{3,2,1,0:T(4,128)S(1)}, f32[3,2,4,256]{3,2,1,0:T(4,128)S(1)}, u32[]{:S(2)}, u32[]{:S(2)}) %collective-permute-start.12) | collective-permute-done | bytes 24608 | tf_op jit(solution)/shard_map/ppermute | solution.py:314
  133.9 3.4 %collective-permute-done.15 = f32[3,2,72,4]{3,2,1,0:T(8,128)S(1)} collective-permute-done((f32[3,2,72,4]{3,2,1,0:T(8,128)S(1)}, f32[3,2,72,4]{3,2,1,0:T(8,128)S(1)}, u32[]{:S(2)}, u32[]{:S(2)}) %collective-permute-start.15) | collective-permute-done | bytes 6944 | tf_op jit(solution)/shard_map/ppermute | solution.py:315
  137.3 2.2 collective-permute-done.14
  141.1 30.1 %shard_map.127 = f32[3,2,72,384]{3,2,1,0:T(8,128)} custom-call(f32[2,72,384]{2,1,0:T(8,128)} %pad.8.rhs_ref, f32[72,384]{1,0:T(8,128)} %broadcast_in_dim.20.inside_ref, f32[72,384]{1,0:T(8,128)} %and_convert_fusion.own_ref), custom_call_target="tpu_custom_call" | custom-call | tf_op jit(solution)/shard_map/pallas_call | solution.py:230
  173.2 3.4 %fusion.142 = (f32[2,4,64]{2,1,0:T(4,128)}, f32[1,2,4,64,256]{4,3,2,1,0:T(8,128)S(1)}, f32[1,2,4,64,256]{4,3,2,1,0:T(8,128)S(1)}, f32[1,2,4,64,256]{4,3,2,1,0:T(8,128)S(1)}) fusion(f32[2,4,64,256]{3,2,1,0:T(8,128)} %get-tuple-element.12, f32[2,64,256]{2,1,0:T(8,128)S(1)} %get-tuple-element.44, f32[64,256]{1,0:T(8,128)S(1)} %convert_element_type.43, ...), kind=kLoop, calls=%fused_computation.247 | loop fusion | flops 3669504 | bytes 15271936 | tf_op jit(solution)/shard_map/reduce_sum | solution.py:458
  178.9 2.9 %collective-permute-done.16 = f32[2,4,64]{2,1,0:T(4,128)S(1)} collective-permute-done((f32[2,4,64]{2,1,0:T(4,128)S(1)}, f32[2,4,64]{2,1,0:T(4,128)S(1)}, u32[]{:S(2)}, u32[]{:S(2)}) %collective-permute-start.16) | collective-permute-done | bytes 2080 | tf_op jit(solution)/shard_map/ppermute | solution.py:33
  187.0 9.8 %all-gather = f32[1,4,64,256]{3,2,0,1:T(8,128)S(1)} all-gather(f32[1,2,64,256]{3,2,0,1:T(8,128)S(1)} %copy-done.27), channel_id=2, replica_groups=mesh['member'=2,'gridy'=8,'gridx'=8] {'member'}, dimensions={1}, use_global_device_ids=true | all-gather | bytes 393216 | tf_op jit(solution)/shard_map/all_gather | solution.py:465
  198.8 3.3 %collective-permute-done.20 = f32[2]{0:T(128)S(1)} collective-permute-done((f32[2]{0:T(128)S(1)}, f32[2]{0:T(128)S(1)}, u32[]{:S(2)}, u32[]{:S(2)}) %collective-permute-start.20) | collective-permute-done | bytes 40 | tf_op jit(solution)/shard_map/ppermute | solution.py:33
  202.9 4.2 %collective-permute-done.21 = f32[2]{0:T(128)S(1)} collective-permute-done((f32[2]{0:T(128)S(1)}, f32[2]{0:T(128)S(1)}, u32[]{:S(2)}, u32[]{:S(2)}) %collective-permute-start.21) | collective-permute-done | bytes 40 | tf_op jit(solution)/shard_map/ppermute | solution.py:33
  207.8 6.5 %all-reduce.2 = f32[4]{0:T(128)S(1)} all-reduce(f32[4]{0:T(128)S(1)} %add_dynamic-update-slice_fusion), channel_id=1, replica_groups=mesh['member'=2,'gridy'=8,'gridx'=8] {'member'}, use_global_device_ids=true, to_apply=%add.2 | all-reduce | flops 4 | bytes 32
  217.5 21.6 %all-gather.3.cloned.1.call-done = f32[4,4,4,64,256]{4,3,2,1,0:T(8,128)} async-done(((f32[4,2,4,64,256]{4,3,2,1,0:T(8,128)}), f32[4,4,4,64,256]{4,3,2,1,0:T(8,128)}) %all-gather.3.cloned.1.call-update) | async-done | bytes 4194320 | tf_op jit(solution)/shard_map/all_gather | solution.py:464
  239.0 2.9 %gather_fusion = f32[2,4,4,64,256]{4,3,2,1,0:T(8,128)S(1)} fusion(f32[4,4,4,64,256]{4,3,2,1,0:T(8,128)} %all-gather.3.cloned.1.call-done, s32[1024]{0:T(1024)S(1)} %pad_clamp_fusion), kind=kCustom, calls=%fused_computation | custom fusion | bytes 4194312 | tf_op jit(solution)/shard_map/jit(_take)/gather | solution.py:468
  (178 shorter events, 56.8 us)
Async XLA Ops:
  7.2 231.9 %all-gather.3.cloned.1.call-start = ((), (), s32[]{:S(2)}) async-start(), calls=%async_computation | async-start | bytes 6291456 | tf_op jit(solution)/shard_map/all_gather | solution.py:464
  11.0 23.9 %collective-permute-start.3 = (f32[5,2,4,1,256]{4,3,2,1,0:T(1,128)S(1)}, f32[5,2,4,1,256]{4,3,2,1,0:T(1,128)S(1)}, u32[]{:S(2)}, u32[]{:S(2)}) collective-permute-start(f32[5,2,4,1,256]{4,3,2,1,0:T(1,128)S(1)} %get-tuple-element.36), channel_id=1, source_target_pairs={{0,8},{8,16},{16,24},{24,32},{32,40},{40,48},{48,56},{56,0},{1,9},... | collective-permute-start | bytes 122888 | tf_op jit(solution)/shard_map/ppermute | solution.py:262
  11.0 23.9 %collective-permute-start.2 = (f32[5,2,4,1,256]{4,3,2,1,0:T(1,128)S(1)}, f32[5,2,4,1,256]{4,3,2,1,0:T(1,128)S(1)}, u32[]{:S(2)}, u32[]{:S(2)}) collective-permute-start(f32[5,2,4,1,256]{4,3,2,1,0:T(1,128)S(1)} %get-tuple-element.35), channel_id=1, source_target_pairs={{8,0},{16,8},{24,16},{32,24},{40,32},{48,40},{56,48},{0,56},{9,1},... | collective-permute-start | bytes 122888 | tf_op jit(solution)/shard_map/ppermute | solution.py:261
  17.6 14.1 %collective-permute-start.1 = (f32[5,2,4,64,1]{3,2,4,1,0:T(4,128)S(1)}, f32[5,2,4,64,1]{3,2,4,1,0:T(4,128)S(1)}, u32[]{:S(2)}, u32[]{:S(2)}) collective-permute-start(f32[5,2,4,64,1]{3,2,4,1,0:T(4,128)S(1)} %copy.16), channel_id=1, source_target_pairs={{0,1},{1,2},{2,3},{3,4},{4,5},{5,6},{6,7},{7,0},{8,9},{9,10},{10,1... | collective-permute-start | bytes 30728 | tf_op jit(solution)/shard_map/ppermute | solution.py:264
  21.1 12.2 %collective-permute-start = (f32[5,2,4,64,1]{3,2,4,1,0:T(4,128)S(1)}, f32[5,2,4,64,1]{3,2,4,1,0:T(4,128)S(1)}, u32[]{:S(2)}, u32[]{:S(2)}) collective-permute-start(f32[5,2,4,64,1]{3,2,4,1,0:T(4,128)S(1)} %copy.14), channel_id=1, source_target_pairs={{1,0},{2,1},{3,2},{4,3},{5,4},{6,5},{7,6},{0,7},{9,8},{10,9},{11,1... | collective-permute-start | bytes 30728 | tf_op jit(solution)/shard_map/ppermute | solution.py:263
  30.8 7.3 %copy-start.34 = (f32[64]{0:T(128)}, f32[64]{0:T(128)S(1)}, u32[]{:S(2)}) copy-start(f32[64]{0:T(128)S(1)} %get-tuple-element.61) | copy-start | bytes 772
  30.9 7.3 %copy-start.36 = (f32[64]{0:T(128)}, f32[64]{0:T(128)S(1)}, u32[]{:S(2)}) copy-start(f32[64]{0:T(128)S(1)} %get-tuple-element.62) | copy-start | bytes 772
  31.6 27.7 %copy-start.30 = (f32[72]{0:T(128)}, f32[72]{0:T(128)S(1)}, u32[]{:S(2)}) copy-start(f32[72]{0:T(128)S(1)} %and_convert_fusion.1) | copy-start | bytes 868
  31.7 26.4 %copy-start.32 = (f32[70]{0:T(128)}, f32[70]{0:T(128)S(1)}, u32[]{:S(2)}) copy-start(f32[70]{0:T(128)S(1)} %slice.326) | copy-start | bytes 844
  42.1 2.0 collective-permute-start.5
  42.1 4.5 %collective-permute-start.4 = (f32[3,2,4,256]{3,2,1,0:T(4,128)S(1)}, f32[3,2,4,256]{3,2,1,0:T(4,128)S(1)}, u32[]{:S(2)}, u32[]{:S(2)}) collective-permute-start(f32[3,2,4,256]{3,2,1,0:T(4,128)S(1)} %get-tuple-element.55), channel_id=1, source_target_pairs={{0,8},{8,16},{16,24},{24,32},{32,40},{40,48},{48,56},{56,0},{1,9},... | collective-permute-start | bytes 73736 | tf_op jit(solution)/shard_map/ppermute | solution.py:314
  46.7 7.2 %collective-permute-start.7 = (f32[3,2,72,4]{3,2,1,0:T(8,128)S(1)}, f32[3,2,72,4]{3,2,1,0:T(8,128)S(1)}, u32[]{:S(2)}, u32[]{:S(2)}) collective-permute-start(f32[3,2,72,4]{3,2,1,0:T(8,128)S(1)} %get-tuple-element.52), channel_id=1, source_target_pairs={{1,0},{2,1},{3,2},{4,3},{5,4},{6,5},{7,6},{0,7},{9,8},{10,9},{11,1... | collective-permute-start | bytes 20744 | tf_op jit(solution)/shard_map/ppermute | solution.py:315
  48.8 8.9 %collective-permute-start.6 = (f32[3,2,72,4]{3,2,1,0:T(8,128)S(1)}, f32[3,2,72,4]{3,2,1,0:T(8,128)S(1)}, u32[]{:S(2)}, u32[]{:S(2)}) collective-permute-start(f32[3,2,72,4]{3,2,1,0:T(8,128)S(1)} %get-tuple-element.51), channel_id=1, source_target_pairs={{0,1},{1,2},{2,3},{3,4},{4,5},{5,6},{6,7},{7,0},{8,9},{9,10},{10,1... | collective-permute-start | bytes 20744 | tf_op jit(solution)/shard_map/ppermute | solution.py:314
  98.1 19.2 %collective-permute-start.11 = (f32[5,2,4,1,256]{4,3,2,1,0:T(1,128)S(1)}, f32[5,2,4,1,256]{4,3,2,1,0:T(1,128)}, u32[]{:S(2)}, u32[]{:S(2)}) collective-permute-start(f32[5,2,4,1,256]{4,3,2,1,0:T(1,128)S(1)} %get-tuple-element.28), channel_id=1, source_target_pairs={{0,8},{8,16},{16,24},{24,32},{32,40},{40,48},{48,56},{56,0},{1,9},... | collective-permute-start | bytes 122888 | tf_op jit(solution)/shard_map/ppermute | solution.py:262
  100.5 12.2 %collective-permute-start.9 = (f32[5,2,4,64,1]{3,2,4,1,0:T(4,128)}, f32[5,2,4,64,1]{3,2,4,1,0:T(4,128)}, u32[]{:S(2)}, u32[]{:S(2)}) collective-permute-start(f32[5,2,4,64,1]{3,2,4,1,0:T(4,128)} %copy.20), channel_id=1, source_target_pairs={{0,1},{1,2},{2,3},{3,4},{4,5},{5,6},{6,7},{7,0},{8,9},{9,10},{10,1... | collective-permute-start | bytes 30728 | tf_op jit(solution)/shard_map/ppermute | solution.py:264
  103.5 11.4 %collective-permute-start.8 = (f32[5,2,4,64,1]{3,2,4,1,0:T(4,128)}, f32[5,2,4,64,1]{3,2,4,1,0:T(4,128)}, u32[]{:S(2)}, u32[]{:S(2)}) collective-permute-start(f32[5,2,4,64,1]{3,2,4,1,0:T(4,128)} %copy.18), channel_id=1, source_target_pairs={{1,0},{2,1},{3,2},{4,3},{5,4},{6,5},{7,6},{0,7},{9,8},{10,9},{11,1... | collective-permute-start | bytes 30728 | tf_op jit(solution)/shard_map/ppermute | solution.py:263
  110.3 8.7 %copy-start.5 = (f32[5,2,4,63,256]{4,3,2,1,0:T(8,128)S(1)}, f32[5,2,4,63,256]{4,3,2,1,0:T(8,128)}, u32[]{:S(2)}) copy-start(f32[5,2,4,63,256]{4,3,2,1,0:T(8,128)} %get-tuple-element.25) | copy-start | bytes 7741444
  110.3 7.8 %collective-permute-start.10 = (f32[5,2,4,1,256]{4,3,2,1,0:T(1,128)S(1)}, f32[5,2,4,1,256]{4,3,2,1,0:T(1,128)}, u32[]{:S(2)}, u32[]{:S(2)}) collective-permute-start(f32[5,2,4,1,256]{4,3,2,1,0:T(1,128)S(1)} %get-tuple-element.27), channel_id=1, source_target_pairs={{8,0},{16,8},{24,16},{32,24},{40,32},{48,40},{56,48},{0,56},{9,1},... | collective-permute-start | bytes 122888 | tf_op jit(solution)/shard_map/ppermute | solution.py:261
  124.2 8.4 %copy-start.19 = (f32[2,4,64,256]{3,2,1,0:T(8,128)S(1)}, f32[2,4,64,256]{3,2,1,0:T(8,128)}, u32[]{:S(2)}) copy-start(f32[2,4,64,256]{3,2,1,0:T(8,128)} %get-tuple-element.18) | copy-start | bytes 1572868
  125.7 1.7 collective-permute-start.13
  125.8 4.5 %collective-permute-start.12 = (f32[3,2,4,256]{3,2,1,0:T(4,128)S(1)}, f32[3,2,4,256]{3,2,1,0:T(4,128)S(1)}, u32[]{:S(2)}, u32[]{:S(2)}) collective-permute-start(f32[3,2,4,256]{3,2,1,0:T(4,128)S(1)} %get-tuple-element.53), channel_id=1, source_target_pairs={{0,8},{8,16},{16,24},{24,32},{32,40},{40,48},{48,56},{56,0},{1,9},... | collective-permute-start | bytes 73736 | tf_op jit(solution)/shard_map/ppermute | solution.py:314
  130.5 6.9 %collective-permute-start.15 = (f32[3,2,72,4]{3,2,1,0:T(8,128)S(1)}, f32[3,2,72,4]{3,2,1,0:T(8,128)S(1)}, u32[]{:S(2)}, u32[]{:S(2)}) collective-permute-start(f32[3,2,72,4]{3,2,1,0:T(8,128)S(1)} %get-tuple-element.50), channel_id=1, source_target_pairs={{1,0},{2,1},{3,2},{4,3},{5,4},{6,5},{7,6},{0,7},{9,8},{10,9},{11,1... | collective-permute-start | bytes 20744 | tf_op jit(solution)/shard_map/ppermute | solution.py:315
  130.8 8.7 %copy-start.31 = (f32[72]{0:T(128)S(1)}, f32[72]{0:T(128)}, u32[]{:S(2)}) copy-start(f32[72]{0:T(128)} %copy-done.30) | copy-start | bytes 868
  130.8 9.1 %copy-start.33 = (f32[70]{0:T(128)S(1)}, f32[70]{0:T(128)}, u32[]{:S(2)}) copy-start(f32[70]{0:T(128)} %copy-done.32) | copy-start | bytes 844
  130.8 8.7 %collective-permute-start.14 = (f32[3,2,72,4]{3,2,1,0:T(8,128)S(1)}, f32[3,2,72,4]{3,2,1,0:T(8,128)S(1)}, u32[]{:S(2)}, u32[]{:S(2)}) collective-permute-start(f32[3,2,72,4]{3,2,1,0:T(8,128)S(1)} %get-tuple-element.49), channel_id=1, source_target_pairs={{0,1},{1,2},{2,3},{3,4},{4,5},{5,6},{6,7},{7,0},{8,9},{9,10},{10,1... | collective-permute-start | bytes 20744 | tf_op jit(solution)/shard_map/ppermute | solution.py:314
  176.6 10.4 %copy-start.27 = (f32[1,2,64,256]{3,2,0,1:T(8,128)S(1)}, f32[1,2,64,256]{3,2,0,1:T(8,128)}, u32[]{:S(2)}) copy-start(f32[1,2,64,256]{3,2,0,1:T(8,128)} %get-tuple-element.43) | copy-start | bytes 393220
  178.2 3.7 %collective-permute-start.16 = (f32[2,4,64]{2,1,0:T(4,128)S(1)}, f32[2,4,64]{2,1,0:T(4,128)S(1)}, u32[]{:S(2)}, u32[]{:S(2)}) collective-permute-start(f32[2,4,64]{2,1,0:T(4,128)S(1)} %copy-done.29), channel_id=1, source_target_pairs={{0,1},{1,0},{2,3},{3,2},{4,5},{5,4},{6,7},{7,6},{8,9},{9,8},{10,11... | collective-permute-start | bytes 6152 | tf_op jit(solution)/shard_map/ppermute | solution.py:33
  181.9 3.6 %collective-permute-start.17 = (f32[2,4,64]{2,1,0:T(4,128)S(1)}, f32[2,4,64]{2,1,0:T(4,128)S(1)}, u32[]{:S(2)}, u32[]{:S(2)}) collective-permute-start(f32[2,4,64]{2,1,0:T(4,128)S(1)} %add.307), channel_id=1, source_target_pairs={{0,2},{1,3},{2,0},{3,1},{4,6},{5,7},{6,4},{7,5},{8,10},{9,11},{10,... | collective-permute-start | bytes 6152 | tf_op jit(solution)/shard_map/ppermute | solution.py:33
  185.5 11.2 %collective-permute-start.18 = (f32[2,4,64]{2,1,0:T(4,128)S(1)}, f32[2,4,64]{2,1,0:T(4,128)S(1)}, u32[]{:S(2)}, u32[]{:S(2)}) collective-permute-start(f32[2,4,64]{2,1,0:T(4,128)S(1)} %add.308), channel_id=1, source_target_pairs={{0,4},{1,5},{2,6},{3,7},{4,0},{5,1},{6,2},{7,3},{8,12},{9,13},{10,... | collective-permute-start | bytes 6152 | tf_op jit(solution)/shard_map/ppermute | solution.py:33
  197.4 1.1 collective-permute-start.19
  198.6 3.5 %collective-permute-start.20 = (f32[2]{0:T(128)S(1)}, f32[2]{0:T(128)S(1)}, u32[]{:S(2)}, u32[]{:S(2)}) collective-permute-start(f32[2]{0:T(128)S(1)} %fusion.163), channel_id=1, source_target_pairs={{0,16},{8,24},{16,0},{24,8},{32,48},{40,56},{48,32},{56,40},{1,17}... | collective-permute-start | bytes 32 | tf_op jit(solution)/shard_map/ppermute | solution.py:33
  202.1 5.0 %collective-permute-start.21 = (f32[2]{0:T(128)S(1)}, f32[2]{0:T(128)S(1)}, u32[]{:S(2)}, u32[]{:S(2)}) collective-permute-start(f32[2]{0:T(128)S(1)} %add.311), channel_id=1, source_target_pairs={{0,32},{8,40},{16,48},{24,56},{32,0},{40,8},{48,16},{56,24},{1,33}... | collective-permute-start | bytes 32 | tf_op jit(solution)/shard_map/ppermute | solution.py:33
  (30 other events, 116.6 us)
Sparse Core Ops, SparseCore 0:
  178.3 60.6 all-gather.2

commit v2 on v1

--- a/solution.py
+++ b/solution.py
@@ -450,25 +450,55 @@
         north_south = solved[2, :, halo : halo + rows, halo : halo + cols]
         uvel = ocean * (ustar - GRAV_K * 0.5 * east_west[:, None])
         vvel = ocean * (vstar - GRAV_K * 0.5 * north_south[:, None])
+        if count == STEPS - 1:
+            tracers_other = lax.ppermute(jnp.stack((temp_next, salt_next)), "member", [(0, 1), (1, 0)])
         temp = temp_next
         salt = salt_next
     zonal_scale = 1.0 / jnp.sqrt(jnp.float32(total_cols))
     score_scale = 1.0 / jnp.sqrt(jnp.float32(levels * total_rows))
     lat_weight = latitude / total_rows
+    members = temp.shape[0]
     zonal_local = jnp.sum(vvel, axis=3)
-    zonal_whole = tree_sum(zonal_local, ("gridx",))
+    depth_weight = (levels - jnp.arange(levels, dtype=jnp.int32)).astype(jnp.float32)
+    score_local = jnp.sum(zonal_local * depth_weight[None, :, None] * lat_weight[None, None, :], axis=(1, 2))
+    slot = lax.broadcasted_iota(jnp.int32, (tile_count, 1, 1, 1), 0) == tile_row
+    zonal_slots = jnp.where(slot, zonal_local[None], 0.0).reshape(-1, 128)
+    score_row = jnp.zeros((8, 128), jnp.float32).at[0, :members].set(score_local)
+    summed = grid_sum(jnp.concatenate([zonal_slots, score_row], axis=0))
+    zonal_whole = summed[: zonal_slots.shape[0]].reshape((tile_count,) + zonal_local.shape)
+    zonal_whole = jnp.sum(jnp.where(slot, zonal_whole, 0.0), axis=0)
     overturn = jnp.cumsum(zonal_whole, axis=1) * zonal_scale
-    score = tree_sum(jnp.sum(overturn * lat_weight, axis=(1, 2)) * score_scale, ("gridy",))
-    state_stack = jnp.stack((temp, salt, uvel, vvel))
-    every_state, every_eta, every_score = (
-        lax.all_gather(state_stack, "member", axis=1, tiled=True),
-        lax.all_gather(eta, "member", axis=0, tiled=True),
-        lax.all_gather(score, "member", axis=0, tiled=True),
+    score = summed[zonal_slots.shape[0], :members] * (zonal_scale * score_scale)
+    swap = [(0, 1), (1, 0)]
+    mine = lax.axis_index("member")
+    flows = jnp.concatenate([uvel, vvel, eta[:, None]], axis=1)
+    flows_other = lax.ppermute(flows, "member", swap)
+    score_other = lax.ppermute(score, "member", swap)
+    every_score = jnp.where(
+        mine == 0, jnp.concatenate([score, score_other]), jnp.concatenate([score_other, score])
     )
-    picked = jnp.take(every_state, clone_source, axis=1)
-    new_eta = jnp.take(every_eta, clone_source, axis=0)
+    here = (clone_source // members) == mine
+    local_at = clone_source % members
+
+    def pick(local, other):
+        chosen_local = jnp.take(local, local_at, axis=0)
+        chosen_other = jnp.take(other, local_at, axis=0)
+        keep = here.reshape((-1,) + (1,) * (local.ndim - 1))
+        return jnp.where(keep, chosen_local, chosen_other)
+
+    new_temp = pick(temp, tracers_other[0])
+    new_salt = pick(salt, tracers_other[1])
+    new_flows = pick(flows, flows_other)
     clone_weight = jnp.take(every_score, clone_source, axis=0) - jnp.mean(every_score)
-    return (picked[0], picked[1], picked[2], picked[3], new_eta, overturn, clone_weight)
+    return (
+        new_temp,
+        new_salt,
+        new_flows[:, :levels],
+        new_flows[:, levels : 2 * levels],
+        new_flows[:, 2 * levels],
+        overturn,
+        clone_weight,
+    )
 
 
 def solution(mesh):

time: 252 us -> 259 us (1.028)
  Pallas kernels: 59.7 us -> 108 us
  waiting for transfers between devices: 54.6 us -> 20.7 us
  blocking collectives: 16.3 us -> 0 us
  between operations: 16 us -> 2.02 us
  local copies, waits for them, and re-layouts: 49 us -> 60.9 us
  other arithmetic: 30.7 us -> 41.4 us
    pallas_call x0 -> x1, Pallas kernels: none -> 50.4 us  [grid_sum(): pl.pallas_call(functools.partial(gather_sum_kernel, ny, nx), out_shape=ja...]
    all_gather x1 -> x0, waiting for transfers between devices: 21.6 us -> none  [shards(): lax.all_gather(state_stack, 'member', axis=1, tiled=True)]
    ppermute x6 -> x3, waiting for transfers between devices: 13.1 us -> 2.91 us  [the longest x1 2.9 us: shards(): score_other = lax.ppermute(score, 'member', swap)]
    all_gather x1 -> x0, blocking collectives: 9.75 us -> none  [shards(): lax.all_gather(eta, 'member', axis=0, tiled=True)]
    gather x2 -> x6, local copies, waits for them, and re-layouts: 3.42 us -> 11.5 us  [the longest x3 6.72 us: pick(): chosen_other = jnp.take(other, local_at, axis=0)]
    slice x0 -> x5, local copies, waits for them, and re-layouts: none -> 7.97 us  [the longest x1 3.32 us: sides(): lax.slice_in_dim(field, 0, cols - 1, axis=xdim)]
    mul x2 -> x4, other arithmetic: 0.01 us -> 7.95 us  [the longest x2 4.16 us: shards(): uvel = ocean * (ustar - GRAV_K * 0.5 * east_west[:, None])]
    unnamed x1 -> x0, blocking collectives: 6.5 us -> none
  transfers between devices with their start and end apart: 23 -> 19, of which waited for: 13 -> 8; matrix products, arithmetic and copies ran while one was open for 15% -> 22% of each run, Pallas kernels for 0% -> 20%
where the time goes in v2:
time: 259 us; the launch traced here: 258 us
  Pallas kernels  108 us (42%)
  local copies, waits for them, and re-layouts  60.9 us (24%)
  other arithmetic  41.4 us (16%)
  starting transfers between devices  24.8 us (10%)
  waiting for transfers between devices  20.7 us (8%)
    pallas_call x2, Pallas kernels, surface_kernel_solve(): pl.pallas_call(functools.partial(solve_kernel, ny, nx), out_shape=jax.Sha...  57.8 us
    pallas_call x1, Pallas kernels, grid_sum(): pl.pallas_call(functools.partial(gather_sum_kernel, ny, nx), out_shape=ja...  50.4 us
    ppermute x4, waiting for transfers between devices, padded_2(): lax.ppermute(lax.slice_in_dim(block, size - width, size, axis=dim), axis,...  12.4 us
    ppermute x4, starting transfers between devices, padded_2(): lax.ppermute(lax.slice_in_dim(block, 0, width, axis=dim), axis, backward)  8.59 us
    unnamed x94, local copies, waits for them, and re-layouts  7.97 us
    reduce_sum x2, other arithmetic, shards(): jnp.sum(ustar, axis=1)  6.79 us
    gather x3, local copies, waits for them, and re-layouts, pick(): chosen_other = jnp.take(other, local_at, axis=0)  6.72 us
    slice x3, local copies, waits for them, and re-layouts, exchange(): lax.slice_in_dim(block, cols - 1, cols, axis=xdim)  6.06 us
  transfers between devices with their start and end apart: 19, of which 8 were waited for; matrix products, arithmetic and copies ran while one was open for 22% of the time, Pallas kernels for 20%

profile of v2, /device:TPU:0, one launch (start us, length us, event | category | flops | bytes accessed | tf_op | source)
XLA Modules:
  0.0 258.0 jit_solution(9693953631912686888)
XLA Ops:
  4.4 2.9 %collective-permute-start.2 = (f32[5,2,4,1,256]{4,3,2,1,0:T(1,128)S(1)}, f32[5,2,4,1,256]{4,3,2,1,0:T(1,128)S(1)}, u32[]{:S(2)}, u32[]{:S(2)}) collective-permute-start(f32[5,2,4,1,256]{4,3,2,1,0:T(1,128)S(1)} %get-tuple-element.60), channel_id=1, source_target_pairs={{8,0},{16,8},{24,16},{32,24},{40,32},{48,40},{56,48},{0,56},{9,1},... | collective-permute-start | bytes 122888 | tf_op jit(solution)/shard_map/ppermute | solution.py:261
  14.5 3.5 %collective-permute-start = (f32[5,2,4,64,1]{3,2,4,1,0:T(4,128)S(1)}, f32[5,2,4,64,1]{3,2,4,1,0:T(4,128)S(1)}, u32[]{:S(2)}, u32[]{:S(2)}) collective-permute-start(f32[5,2,4,64,1]{3,2,4,1,0:T(4,128)S(1)} %copy.18), channel_id=1, source_target_pairs={{1,0},{2,1},{3,2},{4,3},{5,4},{6,5},{7,6},{0,7},{9,8},{10,9},{11,1... | collective-permute-start | bytes 30728 | tf_op jit(solution)/shard_map/ppermute | solution.py:263
  18.1 2.8 %fusion.180 = (f32[5,2,4,63,256]{4,3,2,1,0:T(8,128)}, f32[5,2,4,63,256]{4,3,2,1,0:T(8,128)}) fusion(f32[5,2,4,64,256]{4,3,2,1,0:T(8,128)S(1)} %constant_dynamic-update-slice_fusion), kind=kLoop, calls=%fused_computation.336 | loop fusion | bytes 10321920 | tf_op jit(solution)/shard_map/slice | solution.py:274
  20.9 3.4 %fusion.178 = (f32[5,2,4,64,255]{4,3,2,1,0:T(8,128)}, f32[5,2,4,64,255]{4,3,2,1,0:T(8,128)}) fusion(f32[5,2,4,64,256]{4,3,2,1,0:T(8,128)S(1)} %constant_dynamic-update-slice_fusion), kind=kLoop, calls=%fused_computation.334 | loop fusion | bytes 10444800 | tf_op jit(solution)/shard_map/slice | solution.py:272
  31.4 3.1 %fusion.168 = (f32[2,64,256]{2,1,0:T(8,128)S(1)}, f32[2,4,64,256]{3,2,1,0:T(8,128)S(1)}) fusion(f32[2,4,64,256]{3,2,1,0:T(8,128)} %param.15, f32[5,2,4,63,256]{4,3,2,1,0:T(8,128)} %get-tuple-element.59, f32[5,2,4,1,256]{4,3,2,1,0:T(1,128)S(1)} %broadcast_multiply_fusion.1, f32[5,2,4,1,256]{4,3,2,1,0:T(1,128)S(1)} %broadcast_multiply_fusion.3, ...), kind=kLoop, calls=%fused_computation.328 | loop fusion | flops 2981888 | bytes 12255488 | tf_op jit(solution)/shard_map/reduce_sum | solution.py:437
  40.4 2.5 collective-permute-done.4
  43.1 2.1 collective-permute-start.7
  46.5 3.8 %collective-permute-done.7 = f32[3,2,72,4]{3,2,1,0:T(8,128)S(1)} collective-permute-done((f32[3,2,72,4]{3,2,1,0:T(8,128)S(1)}, f32[3,2,72,4]{3,2,1,0:T(8,128)S(1)}, u32[]{:S(2)}, u32[]{:S(2)}) %collective-permute-start.7) | collective-permute-done | bytes 6944 | tf_op jit(solution)/shard_map/ppermute | solution.py:315
  50.3 3.8 %collective-permute-done.6 = f32[3,2,72,4]{3,2,1,0:T(8,128)S(1)} collective-permute-done((f32[3,2,72,4]{3,2,1,0:T(8,128)S(1)}, f32[3,2,72,4]{3,2,1,0:T(8,128)S(1)}, u32[]{:S(2)}, u32[]{:S(2)}) %collective-permute-start.6) | collective-permute-done | bytes 6944 | tf_op jit(solution)/shard_map/ppermute | solution.py:314
  56.4 29.7 %shard_map.126 = f32[3,2,72,384]{3,2,1,0:T(8,128)} custom-call(f32[2,72,384]{2,1,0:T(8,128)} %pad.12.rhs_ref, f32[72,384]{1,0:T(8,128)} %broadcast_in_dim.71.inside_ref, f32[72,384]{1,0:T(8,128)} %and_convert_fusion.own_ref), custom_call_target="tpu_custom_call" | custom-call | tf_op jit(solution)/shard_map/pallas_call | solution.py:230
  89.6 2.8 %fusion.177 = (f32[5,2,4,63,256]{4,3,2,1,0:T(8,128)}, f32[5,2,4,63,256]{4,3,2,1,0:T(8,128)}) fusion(f32[5,2,4,64,256]{4,3,2,1,0:T(8,128)S(1)} %constant_dynamic-update-slice_fusion.1), kind=kLoop, calls=%fused_computation.333 | loop fusion | bytes 10321920 | tf_op jit(solution)/shard_map/slice | solution.py:275
  94.6 2.4 copy.22
  99.0 2.4 copy.24
  101.4 3.3 %fusion.175 = (f32[5,2,4,64,255]{4,3,2,1,0:T(8,128)}, f32[5,2,4,64,255]{4,3,2,1,0:T(8,128)}) fusion(f32[5,2,4,64,256]{4,3,2,1,0:T(8,128)S(1)} %constant_dynamic-update-slice_fusion.1), kind=kLoop, calls=%fused_computation.331 | loop fusion | bytes 10444800 | tf_op jit(solution)/shard_map/slice | solution.py:273
  104.7 2.4 copy.23
  107.6 2.3 copy.25
  111.6 3.7 %fusion.164 = (f32[2,64,256]{2,1,0:T(8,128)S(1)}, f32[2,4,64,256]{3,2,1,0:T(8,128)}) fusion(f32[5,2,4,63,256]{4,3,2,1,0:T(8,128)S(1)} %copy-done.5, f32[5,2,4,1,256]{4,3,2,1,0:T(1,128)S(1)} %broadcast_multiply_fusion, f32[5,2,4,1,256]{4,3,2,1,0:T(1,128)S(1)} %broadcast_multiply_fusion.2, f32[5,2,4,63,256]{4,3,2,1,0:T(8,128)} %get-tuple-element.53, ...), kind=kLoop, calls=%fused_computation.326 | loop fusion | flops 3506176 | bytes 12517632 | tf_op jit(solution)/shard_map/reduce_sum | solution.py:437
  119.3 2.4 collective-permute-start.14
  123.4 3.0 %collective-permute-done.13 = f32[3,2,4,256]{3,2,1,0:T(4,128)} collective-permute-done((f32[3,2,4,256]{3,2,1,0:T(4,128)}, f32[3,2,4,256]{3,2,1,0:T(4,128)}, u32[]{:S(2)}, u32[]{:S(2)}) %collective-permute-start.13) | collective-permute-done | bytes 24608 | tf_op jit(solution)/shard_map/ppermute | solution.py:314
  128.3 4.1 %collective-permute-start.16 = (f32[3,2,72,4]{3,2,1,0:T(8,128)}, f32[3,2,72,4]{3,2,1,0:T(8,128)}, u32[]{:S(2)}, u32[]{:S(2)}) collective-permute-start(f32[3,2,72,4]{3,2,1,0:T(8,128)} %get-tuple-element.73), channel_id=1, source_target_pairs={{1,0},{2,1},{3,2},{4,3},{5,4},{6,5},{7,6},{0,7},{9,8},{10,9},{11,1... | collective-permute-start | bytes 20744 | tf_op jit(solution)/shard_map/ppermute | solution.py:315
  132.5 3.1 %fusion.104 = f32[2,4,64,256]{3,2,1,0:T(8,128)} fusion(f32[2,4,64,256]{3,2,1,0:T(8,128)} %get-tuple-element.43, f32[5,2,4,1,256]{4,3,2,1,0:T(1,128)S(1)} %broadcast_multiply_fusion.2, f32[5,2,4,63,256]{4,3,2,1,0:T(8,128)} %get-tuple-element.53, f32[5,2,4,63,256]{4,3,2,1,0:T(8,128)S(1)} %copy-done.5, f32[5,2,4,1,256]{4,3,2,1,0:T(1,128)S(1)} %broadcast_multiply_fusion, ...), kind=kLoop, calls=%fused_computation.193 | loop fusion | flops 3014656 | bytes 12910592 | tf_op jit(solution)/shard_map/mul | solution.py:418
  135.6 2.5 gather_fusion.3
  138.1 3.0 %collective-permute-done.15 = f32[3,2,72,4]{3,2,1,0:T(8,128)} collective-permute-done((f32[3,2,72,4]{3,2,1,0:T(8,128)}, f32[3,2,72,4]{3,2,1,0:T(8,128)}, u32[]{:S(2)}, u32[]{:S(2)}) %collective-permute-start.15) | collective-permute-done | bytes 6944 | tf_op jit(solution)/shard_map/ppermute | solution.py:314
  144.5 28.1 %shard_map.127 = f32[3,2,72,384]{3,2,1,0:T(8,128)} custom-call(f32[2,72,384]{2,1,0:T(8,128)} %pad.13.rhs_ref, f32[72,384]{1,0:T(8,128)} %broadcast_in_dim.71.inside_ref, f32[72,384]{1,0:T(8,128)} %and_convert_fusion.own_ref), custom_call_target="tpu_custom_call" | custom-call | tf_op jit(solution)/shard_map/pallas_call | solution.py:230
  174.0 2.8 %subtract_multiply_fusion.1 = (f32[2,4,64,256]{3,2,1,0:T(8,128)S(1)}, f32[2,4,64,256]{3,2,1,0:T(8,128)S(1)}, f32[2,4,64]{2,1,0:T(4,128)S(1)}, f32[2,4,64,256]{3,2,1,0:T(8,128)S(1)}) fusion(f32[2,4,64,256]{3,2,1,0:T(8,128)} %get-tuple-element.33, f32[2,64,256]{2,1,0:T(8,128)S(1)} %get-tuple-element.66, f32[64,256]{1,0:T(8,128)S(1)} %convert_element_type.50, ...), kind=kLoop, calls=%fused_computation.241 | loop fusion | flops 3669504 | bytes 15271936 | tf_op jit(solution)/shard_map/mul | solution.py:451
  178.0 3.2 %collective-permute-start.12 = (f32[2,2,4,64,256]{4,3,2,1,0:T(8,128)}, f32[2,2,4,64,256]{4,3,2,1,0:T(8,128)}, u32[]{:S(2)}, u32[]{:S(2)}) collective-permute-start(f32[2,2,4,64,256]{4,3,2,1,0:T(8,128)} %pad_maximum_fusion.1), channel_id=1, source_target_pairs={{0,64},{64,0},{1,65},{65,1},{2,66},{66,2},{3,67},{67,3},{4,68},{68... | collective-permute-start | bytes 3145736 | tf_op jit(solution)/shard_map/ppermute | solution.py:454
  182.7 50.4 %shard_map.128 = f32[40,128]{1,0:T(8,128)} custom-call(f32[40,128]{1,0:T(8,128)} %select_maximum_fusion.x_ref), custom_call_target="tpu_custom_call" | custom-call | tf_op jit(solution)/shard_map/pallas_call | solution.py:90
  239.2 2.9 %collective-permute-done.18 = f32[2]{0:T(128)S(1)} collective-permute-done((f32[2]{0:T(128)S(1)}, f32[2]{0:T(128)S(1)}, u32[]{:S(2)}, u32[]{:S(2)}) %collective-permute-start.18) | collective-permute-done | bytes 40 | tf_op jit(solution)/shard_map/ppermute | solution.py:476
  244.7 2.3 slice_bitcast_fusion
  247.0 2.4 gather_fusion.4
  249.4 2.4 gather_fusion.2
  251.8 2.4 select_select_fusion.1
  (190 shorter events, 64.0 us)
Async XLA Ops:
  4.4 26.9 %collective-permute-start.3 = (f32[5,2,4,1,256]{4,3,2,1,0:T(1,128)S(1)}, f32[5,2,4,1,256]{4,3,2,1,0:T(1,128)S(1)}, u32[]{:S(2)}, u32[]{:S(2)}) collective-permute-start(f32[5,2,4,1,256]{4,3,2,1,0:T(1,128)S(1)} %get-tuple-element.61), channel_id=1, source_target_pairs={{0,8},{8,16},{16,24},{24,32},{32,40},{40,48},{48,56},{56,0},{1,9},... | collective-permute-start | bytes 122888 | tf_op jit(solution)/shard_map/ppermute | solution.py:262
  4.4 26.9 %collective-permute-start.2 = (f32[5,2,4,1,256]{4,3,2,1,0:T(1,128)S(1)}, f32[5,2,4,1,256]{4,3,2,1,0:T(1,128)S(1)}, u32[]{:S(2)}, u32[]{:S(2)}) collective-permute-start(f32[5,2,4,1,256]{4,3,2,1,0:T(1,128)S(1)} %get-tuple-element.60), channel_id=1, source_target_pairs={{8,0},{16,8},{24,16},{32,24},{40,32},{48,40},{56,48},{0,56},{9,1},... | collective-permute-start | bytes 122888 | tf_op jit(solution)/shard_map/ppermute | solution.py:261
  11.1 17.0 %collective-permute-start.1 = (f32[5,2,4,64,1]{3,2,4,1,0:T(4,128)S(1)}, f32[5,2,4,64,1]{3,2,4,1,0:T(4,128)S(1)}, u32[]{:S(2)}, u32[]{:S(2)}) collective-permute-start(f32[5,2,4,64,1]{3,2,4,1,0:T(4,128)S(1)} %copy.20), channel_id=1, source_target_pairs={{0,1},{1,2},{2,3},{3,4},{4,5},{5,6},{6,7},{7,0},{8,9},{9,10},{10,1... | collective-permute-start | bytes 30728 | tf_op jit(solution)/shard_map/ppermute | solution.py:264
  14.5 15.1 %collective-permute-start = (f32[5,2,4,64,1]{3,2,4,1,0:T(4,128)S(1)}, f32[5,2,4,64,1]{3,2,4,1,0:T(4,128)S(1)}, u32[]{:S(2)}, u32[]{:S(2)}) collective-permute-start(f32[5,2,4,64,1]{3,2,4,1,0:T(4,128)S(1)} %copy.18), channel_id=1, source_target_pairs={{1,0},{2,1},{3,2},{4,3},{5,4},{6,5},{7,6},{0,7},{9,8},{10,9},{11,1... | collective-permute-start | bytes 30728 | tf_op jit(solution)/shard_map/ppermute | solution.py:263
  20.9 7.1 %copy-start.31 = (s32[64,256]{1,0:T(8,128)S(1)}, s32[64,256]{1,0:T(8,128)}, u32[]{:S(2)}) copy-start(s32[64,256]{1,0:T(8,128)} %param.18) | copy-start | bytes 196612
  24.3 7.1 %copy-start = (f32[5,2,4,63,256]{4,3,2,1,0:T(8,128)S(1)}, f32[5,2,4,63,256]{4,3,2,1,0:T(8,128)}, u32[]{:S(2)}) copy-start(f32[5,2,4,63,256]{4,3,2,1,0:T(8,128)} %get-tuple-element.58) | copy-start | bytes 7741444
  24.3 10.2 %copy-start.39 = (f32[64]{0:T(128)}, f32[64]{0:T(128)S(1)}, u32[]{:S(2)}) copy-start(f32[64]{0:T(128)S(1)} %get-tuple-element.87) | copy-start | bytes 772
  24.3 10.2 %copy-start.37 = (f32[64]{0:T(128)}, f32[64]{0:T(128)S(1)}, u32[]{:S(2)}) copy-start(f32[64]{0:T(128)S(1)} %get-tuple-element.88) | copy-start | bytes 772
  28.0 27.7 %copy-start.33 = (f32[72]{0:T(128)}, f32[72]{0:T(128)S(1)}, u32[]{:S(2)}) copy-start(f32[72]{0:T(128)S(1)} %and_convert_fusion.1) | copy-start | bytes 868
  28.1 26.4 %copy-start.36 = (f32[70]{0:T(128)}, f32[70]{0:T(128)S(1)}, u32[]{:S(2)}) copy-start(f32[70]{0:T(128)S(1)} %slice.351) | copy-start | bytes 844
  38.4 2.0 collective-permute-start.5
  38.5 4.5 %collective-permute-start.4 = (f32[3,2,4,256]{3,2,1,0:T(4,128)S(1)}, f32[3,2,4,256]{3,2,1,0:T(4,128)S(1)}, u32[]{:S(2)}, u32[]{:S(2)}) collective-permute-start(f32[3,2,4,256]{3,2,1,0:T(4,128)S(1)} %get-tuple-element.78), channel_id=1, source_target_pairs={{0,8},{8,16},{16,24},{24,32},{32,40},{40,48},{48,56},{56,0},{1,9},... | collective-permute-start | bytes 73736 | tf_op jit(solution)/shard_map/ppermute | solution.py:314
  43.1 7.2 %collective-permute-start.7 = (f32[3,2,72,4]{3,2,1,0:T(8,128)S(1)}, f32[3,2,72,4]{3,2,1,0:T(8,128)S(1)}, u32[]{:S(2)}, u32[]{:S(2)}) collective-permute-start(f32[3,2,72,4]{3,2,1,0:T(8,128)S(1)} %get-tuple-element.75), channel_id=1, source_target_pairs={{1,0},{2,1},{3,2},{4,3},{5,4},{6,5},{7,6},{0,7},{9,8},{10,9},{11,1... | collective-permute-start | bytes 20744 | tf_op jit(solution)/shard_map/ppermute | solution.py:315
  45.2 8.9 %collective-permute-start.6 = (f32[3,2,72,4]{3,2,1,0:T(8,128)S(1)}, f32[3,2,72,4]{3,2,1,0:T(8,128)S(1)}, u32[]{:S(2)}, u32[]{:S(2)}) collective-permute-start(f32[3,2,72,4]{3,2,1,0:T(8,128)S(1)} %get-tuple-element.74), channel_id=1, source_target_pairs={{0,1},{1,2},{2,3},{3,4},{4,5},{5,6},{6,7},{7,0},{8,9},{9,10},{10,1... | collective-permute-start | bytes 20744 | tf_op jit(solution)/shard_map/ppermute | solution.py:314
  94.4 15.5 %collective-permute-start.10 = (f32[5,2,4,1,256]{4,3,2,1,0:T(1,128)S(1)}, f32[5,2,4,1,256]{4,3,2,1,0:T(1,128)}, u32[]{:S(2)}, u32[]{:S(2)}) collective-permute-start(f32[5,2,4,1,256]{4,3,2,1,0:T(1,128)S(1)} %get-tuple-element.51), channel_id=1, source_target_pairs={{8,0},{16,8},{24,16},{32,24},{40,32},{48,40},{56,48},{0,56},{9,1},... | collective-permute-start | bytes 122888 | tf_op jit(solution)/shard_map/ppermute | solution.py:261
  97.0 7.7 %collective-permute-start.8 = (f32[5,2,4,64,1]{3,2,4,1,0:T(4,128)}, f32[5,2,4,64,1]{3,2,4,1,0:T(4,128)}, u32[]{:S(2)}, u32[]{:S(2)}) collective-permute-start(f32[5,2,4,64,1]{3,2,4,1,0:T(4,128)} %copy.22), channel_id=1, source_target_pairs={{1,0},{2,1},{3,2},{4,3},{5,4},{6,5},{7,6},{0,7},{9,8},{10,9},{11,1... | collective-permute-start | bytes 30728 | tf_op jit(solution)/shard_map/ppermute | solution.py:263
  101.4 6.2 %collective-permute-start.9 = (f32[5,2,4,64,1]{3,2,4,1,0:T(4,128)}, f32[5,2,4,64,1]{3,2,4,1,0:T(4,128)}, u32[]{:S(2)}, u32[]{:S(2)}) collective-permute-start(f32[5,2,4,64,1]{3,2,4,1,0:T(4,128)} %copy.24), channel_id=1, source_target_pairs={{0,1},{1,2},{2,3},{3,4},{4,5},{5,6},{6,7},{7,0},{8,9},{9,10},{10,1... | collective-permute-start | bytes 30728 | tf_op jit(solution)/shard_map/ppermute | solution.py:264
  104.7 6.8 %copy-start.5 = (f32[5,2,4,63,256]{4,3,2,1,0:T(8,128)S(1)}, f32[5,2,4,63,256]{4,3,2,1,0:T(8,128)}, u32[]{:S(2)}) copy-start(f32[5,2,4,63,256]{4,3,2,1,0:T(8,128)} %get-tuple-element.52) | copy-start | bytes 7741444
  104.7 6.0 %collective-permute-start.11 = (f32[5,2,4,1,256]{4,3,2,1,0:T(1,128)S(1)}, f32[5,2,4,1,256]{4,3,2,1,0:T(1,128)}, u32[]{:S(2)}, u32[]{:S(2)}) collective-permute-start(f32[5,2,4,1,256]{4,3,2,1,0:T(1,128)S(1)} %get-tuple-element.50), channel_id=1, source_target_pairs={{0,8},{8,16},{16,24},{24,32},{32,40},{40,48},{48,56},{56,0},{1,9},... | collective-permute-start | bytes 122888 | tf_op jit(solution)/shard_map/ppermute | solution.py:262
  119.3 4.1 %collective-permute-start.14 = (f32[3,2,4,256]{3,2,1,0:T(4,128)}, f32[3,2,4,256]{3,2,1,0:T(4,128)}, u32[]{:S(2)}, u32[]{:S(2)}) collective-permute-start(f32[3,2,4,256]{3,2,1,0:T(4,128)} %get-tuple-element.77), channel_id=1, source_target_pairs={{8,0},{16,8},{24,16},{32,24},{40,32},{48,40},{56,48},{0,56},{9,1},... | collective-permute-start | bytes 73736 | tf_op jit(solution)/shard_map/ppermute | solution.py:315
  121.6 4.8 %collective-permute-start.13 = (f32[3,2,4,256]{3,2,1,0:T(4,128)}, f32[3,2,4,256]{3,2,1,0:T(4,128)}, u32[]{:S(2)}, u32[]{:S(2)}) collective-permute-start(f32[3,2,4,256]{3,2,1,0:T(4,128)} %get-tuple-element.76), channel_id=1, source_target_pairs={{0,8},{8,16},{16,24},{24,32},{32,40},{40,48},{48,56},{56,0},{1,9},... | collective-permute-start | bytes 73736 | tf_op jit(solution)/shard_map/ppermute | solution.py:314
  122.1 10.3 %copy-start.10 = (f32[5,2,4,64,1]{4,3,2,1,0:T(8,128)S(1)}, f32[5,2,4,64,1]{4,3,2,1,0:T(8,128)}, u32[]{:S(2)}) copy-start(f32[5,2,4,64,1]{4,3,2,1,0:T(8,128)} %copy.23) | copy-start | bytes 30724
  128.3 9.8 %collective-permute-start.16 = (f32[3,2,72,4]{3,2,1,0:T(8,128)}, f32[3,2,72,4]{3,2,1,0:T(8,128)}, u32[]{:S(2)}, u32[]{:S(2)}) collective-permute-start(f32[3,2,72,4]{3,2,1,0:T(8,128)} %get-tuple-element.73), channel_id=1, source_target_pairs={{1,0},{2,1},{3,2},{4,3},{5,4},{6,5},{7,6},{0,7},{9,8},{10,9},{11,1... | collective-permute-start | bytes 20744 | tf_op jit(solution)/shard_map/ppermute | solution.py:315
  132.5 8.6 %collective-permute-start.15 = (f32[3,2,72,4]{3,2,1,0:T(8,128)}, f32[3,2,72,4]{3,2,1,0:T(8,128)}, u32[]{:S(2)}, u32[]{:S(2)}) collective-permute-start(f32[3,2,72,4]{3,2,1,0:T(8,128)} %get-tuple-element.72), channel_id=1, source_target_pairs={{0,1},{1,2},{2,3},{3,4},{4,5},{5,6},{6,7},{7,0},{8,9},{9,10},{10,1... | collective-permute-start | bytes 20744 | tf_op jit(solution)/shard_map/ppermute | solution.py:314
  176.9 57.7 %copy-start.32 = (s32[1024]{0:T(1024)S(1)}, s32[1024]{0:T(1024)}, u32[]{:S(2)}) copy-start(s32[1024]{0:T(1024)} %pad_clamp_fusion.1) | copy-start | bytes 12292
  178.0 66.7 %collective-permute-start.12 = (f32[2,2,4,64,256]{4,3,2,1,0:T(8,128)}, f32[2,2,4,64,256]{4,3,2,1,0:T(8,128)}, u32[]{:S(2)}, u32[]{:S(2)}) collective-permute-start(f32[2,2,4,64,256]{4,3,2,1,0:T(8,128)} %pad_maximum_fusion.1), channel_id=1, source_target_pairs={{0,64},{64,0},{1,65},{65,1},{2,66},{66,2},{3,67},{67,3},{4,68},{68... | collective-permute-start | bytes 3145736 | tf_op jit(solution)/shard_map/ppermute | solution.py:454
  181.3 62.9 %copy-start.42 = (s32[2]{0:T(128)S(1)}, s32[2]{0:T(128)}, u32[]{:S(2)}) copy-start(s32[2]{0:T(128)} %param.19) | copy-start | bytes 28
  181.3 72.9 %collective-permute-start.17 = (f32[2,9,64,256]{3,2,1,0:T(8,128)S(1)}, f32[2,9,64,256]{3,2,1,0:T(8,128)}, u32[]{:S(2)}, u32[]{:S(2)}) collective-permute-start(f32[2,9,64,256]{3,2,1,0:T(8,128)S(1)} %pad_maximum_fusion), channel_id=1, source_target_pairs={{0,64},{64,0},{1,65},{65,1},{2,66},{66,2},{3,67},{67,3},{4,68},{68... | collective-permute-start | bytes 3538952 | tf_op jit(solution)/shard_map/ppermute | solution.py:475
  236.9 14.9 %copy-start.29 = (f32[2,4,64,256]{3,2,1,0:T(8,128)S(1)}, f32[2,4,64,256]{3,2,1,0:T(8,128)}, u32[]{:S(2)}) copy-start(f32[2,4,64,256]{3,2,1,0:T(8,128)} %gather_fusion.3) | copy-start | bytes 1572868
  236.9 14.9 %copy-start.34 = (pred[2]{0:T(512)(128)(4,1)S(1)}, pred[2]{0:T(512)(128)(4,1)}, u32[]{:S(2)}) copy-start(pred[2]{0:T(512)(128)(4,1)} %get-tuple-element.36) | copy-start | bytes 10
  236.9 14.9 %copy-start.35 = (pred[2]{0:T(512)(128)(4,1)S(1)}, pred[2]{0:T(512)(128)(4,1)}, u32[]{:S(2)}) copy-start(pred[2]{0:T(512)(128)(4,1)} %get-tuple-element.86) | copy-start | bytes 10
  237.0 5.1 %collective-permute-start.18 = (f32[2]{0:T(128)S(1)}, f32[2]{0:T(128)S(1)}, u32[]{:S(2)}, u32[]{:S(2)}) collective-permute-start(f32[2]{0:T(128)S(1)} %multiply_bitcast_fusion.4), channel_id=1, source_target_pairs={{0,64},{64,0},{1,65},{65,1},{2,66},{66,2},{3,67},{67,3},{4,68},{68... | collective-permute-start | bytes 32 | tf_op jit(solution)/shard_map/ppermute | solution.py:476
  (32 other events, 126.5 us)

commit v3 on v2

--- a/solution.py
+++ b/solution.py
@@ -471,9 +471,10 @@
     score = summed[zonal_slots.shape[0], :members] * (zonal_scale * score_scale)
     swap = [(0, 1), (1, 0)]
     mine = lax.axis_index("member")
-    flows = jnp.concatenate([uvel, vvel, eta[:, None]], axis=1)
+    score_slab = jnp.zeros((members, 1) + eta.shape[1:], jnp.float32).at[:, 0, 0, 0].set(score)
+    flows = jnp.concatenate([uvel, vvel, eta[:, None], score_slab], axis=1)
     flows_other = lax.ppermute(flows, "member", swap)
-    score_other = lax.ppermute(score, "member", swap)
+    score_other = flows_other[:, 2 * levels + 1, 0, 0]
     every_score = jnp.where(
         mine == 0, jnp.concatenate([score, score_other]), jnp.concatenate([score_other, score])
     )
@@ -481,14 +482,16 @@
     local_at = clone_source % members
 
     def pick(local, other):
-        chosen_local = jnp.take(local, local_at, axis=0)
-        chosen_other = jnp.take(other, local_at, axis=0)
-        keep = here.reshape((-1,) + (1,) * (local.ndim - 1))
-        return jnp.where(keep, chosen_local, chosen_other)
+        chosen = []
+        for place in range(members):
+            from_here = lax.dynamic_index_in_dim(local, local_at[place], 0, keepdims=False)
+            from_other = lax.dynamic_index_in_dim(other, local_at[place], 0, keepdims=False)
+            chosen.append(jnp.where(here[place], from_here, from_other))
+        return jnp.stack(chosen)
 
     new_temp = pick(temp, tracers_other[0])
     new_salt = pick(salt, tracers_other[1])
-    new_flows = pick(flows, flows_other)
+    new_flows = pick(flows[:, : 2 * levels + 1], flows_other[:, : 2 * levels + 1])
     clone_weight = jnp.take(every_score, clone_source, axis=0) - jnp.mean(every_score)
     return (
         new_temp,

time: 259 us -> 250 us (0.965)
  Pallas kernels: 108 us -> 83.5 us
  waiting for transfers between devices: 20.7 us -> 37.8 us
  local copies, waits for them, and re-layouts: 60.9 us -> 50.6 us
  other arithmetic: 41.4 us -> 46.4 us
  between operations: 2.02 us -> 6.01 us
    pallas_call x1, Pallas kernels: 50.4 us -> 24.7 us  [grid_sum(): pl.pallas_call(functools.partial(gather_sum_kernel, ny, nx), out_shape=ja...]
    ppermute x1, waiting for transfers between devices: 0.01 us -> 21.6 us  [shards(): flows_other = lax.ppermute(flows, 'member', swap)]
    gather x6 -> x0, local copies, waits for them, and re-layouts: 11.5 us -> none  [the longest x3 6.72 us: pick(): chosen_other = jnp.take(other, local_at, axis=0)]
    slice x1 -> x5, local copies, waits for them, and re-layouts: 1.03 us -> 4.63 us  [the longest x1 1.35 us: shards(): new_flows = pick(flows[:, :2 * levels + 1], flows_other[:, :2 * levels + 1])]
    squeeze x2 -> x0, local copies, waits for them, and re-layouts: 2.93 us -> none  [the longest x1 2.26 us: shards(): new_salt = pick(salt, tracers_other[1])]
    ppermute x1 -> x0, waiting for transfers between devices: 2.9 us -> none  [shards(): score_other = lax.ppermute(score, 'member', swap)]
    another operation x0 -> x3, other arithmetic: none -> 2.7 us  [pick(): return jnp.stack(chosen)]
    ppermute x4, waiting for transfers between devices: 12.4 us -> 9.77 us  [padded_2(): lax.ppermute(lax.slice_in_dim(block, size - width, size, axis=dim), axis,...]
  transfers between devices with their start and end apart: 19 -> 18, of which waited for: 8 -> 8; matrix products, arithmetic and copies ran while one was open for 22% -> 20% of each run, Pallas kernels for 20% -> 10%
where the time goes in v3:
time: 250 us; the launch traced here: 249 us
  Pallas kernels  83.5 us (33%)
  local copies, waits for them, and re-layouts  50.6 us (20%)
  other arithmetic  46.4 us (19%)
  waiting for transfers between devices  37.8 us (15%)
  starting transfers between devices  24.8 us (10%)
  between operations  6.01 us (2%)
    pallas_call x2, Pallas kernels, surface_kernel_solve(): pl.pallas_call(functools.partial(solve_kernel, ny, nx), out_shape=jax.Sha...  58.8 us
    pallas_call x1, Pallas kernels, grid_sum(): pl.pallas_call(functools.partial(gather_sum_kernel, ny, nx), out_shape=ja...  24.7 us
    ppermute x1, waiting for transfers between devices, shards(): flows_other = lax.ppermute(flows, 'member', swap)  21.6 us
    ppermute x4, waiting for transfers between devices, padded_2(): lax.ppermute(lax.slice_in_dim(block, size - width, size, axis=dim), axis,...  9.77 us
    ppermute x4, starting transfers between devices, padded_2(): lax.ppermute(lax.slice_in_dim(block, 0, width, axis=dim), axis, backward)  8.97 us
    unnamed x109, local copies, waits for them, and re-layouts  8.09 us
    reduce_sum x2, other arithmetic, shards(): jnp.sum(ustar, axis=1)  6.79 us
    ppermute x4, waiting for transfers between devices, padded_2(): lax.ppermute(lax.slice_in_dim(block, 0, width, axis=dim), axis, backward)  6.37 us
  transfers between devices with their start and end apart: 18, of which 8 were waited for; matrix products, arithmetic and copies ran while one was open for 20% of the time, Pallas kernels for 10%

profile of v3, /device:TPU:0, one launch (start us, length us, event | category | flops | bytes accessed | tf_op | source)
XLA Modules:
  0.0 249.2 jit_solution(13906068484213023649)
XLA Ops:
  4.5 2.9 %collective-permute-start.2 = (f32[5,2,4,1,256]{4,2,3,1,0:T(4,128)S(1)}, f32[5,2,4,1,256]{4,2,3,1,0:T(4,128)S(1)}, u32[]{:S(2)}, u32[]{:S(2)}) collective-permute-start(f32[5,2,4,1,256]{4,2,3,1,0:T(4,128)S(1)} %copy.168), channel_id=1, source_target_pairs={{8,0},{16,8},{24,16},{32,24},{40,32},{48,40},{56,48},{0,56},{9,1},... | collective-permute-start | bytes 122888 | tf_op jit(solution)/shard_map/ppermute | solution.py:261
  7.4 1.9 fusion.186
  14.6 3.5 %collective-permute-start = (f32[5,2,4,64,1]{3,2,4,1,0:T(4,128)S(1)}, f32[5,2,4,64,1]{3,2,4,1,0:T(4,128)S(1)}, u32[]{:S(2)}, u32[]{:S(2)}) collective-permute-start(f32[5,2,4,64,1]{3,2,4,1,0:T(4,128)S(1)} %copy.164), channel_id=1, source_target_pairs={{1,0},{2,1},{3,2},{4,3},{5,4},{6,5},{7,6},{0,7},{9,8},{10,9},{11,1... | collective-permute-start | bytes 30728 | tf_op jit(solution)/shard_map/ppermute | solution.py:263
  18.1 2.8 %fusion.187 = (f32[5,2,4,63,256]{4,3,2,1,0:T(8,128)}, f32[5,2,4,63,256]{4,3,2,1,0:T(8,128)}) fusion(f32[5,2,4,64,256]{4,3,2,1,0:T(8,128)S(1)} %constant_dynamic-update-slice_fusion), kind=kLoop, calls=%fused_computation.344 | loop fusion | bytes 10321920 | tf_op jit(solution)/shard_map/slice | solution.py:274
  20.9 3.4 %fusion.185 = (f32[5,2,4,64,255]{4,3,2,1,0:T(8,128)}, f32[5,2,4,64,255]{4,3,2,1,0:T(8,128)}) fusion(f32[5,2,4,64,256]{4,3,2,1,0:T(8,128)S(1)} %constant_dynamic-update-slice_fusion), kind=kLoop, calls=%fused_computation.342 | loop fusion | bytes 10444800 | tf_op jit(solution)/shard_map/slice | solution.py:272
  31.4 3.1 %fusion.175 = (f32[2,64,256]{2,1,0:T(8,128)S(1)}, f32[2,4,64,256]{3,2,1,0:T(8,128)S(1)}) fusion(f32[2,4,64,256]{3,2,1,0:T(8,128)} %param.13, f32[5,2,4,63,256]{4,3,2,1,0:T(8,128)} %get-tuple-element.88, f32[5,2,4,1,256]{4,3,2,1,0:T(1,128)S(1)} %copy_multiply_fusion.2, f32[5,2,4,1,256]{4,3,2,1,0:T(1,128)S(1)} %copy_multiply_fusion.3, ...), kind=kLoop, calls=%fused_computation.336 | loop fusion | flops 2981888 | bytes 12255488 | tf_op jit(solution)/shard_map/reduce_sum | solution.py:437
  40.3 2.5 %collective-permute-done.4 = f32[3,2,4,256]{3,2,1,0:T(4,128)S(1)} collective-permute-done((f32[3,2,4,256]{3,2,1,0:T(4,128)S(1)}, f32[3,2,4,256]{3,2,1,0:T(4,128)S(1)}, u32[]{:S(2)}, u32[]{:S(2)}) %collective-permute-start.4) | collective-permute-done | bytes 24608 | tf_op jit(solution)/shard_map/ppermute | solution.py:314
  43.0 2.1 collective-permute-start.7
  46.4 3.8 %collective-permute-done.7 = f32[3,2,72,4]{3,2,1,0:T(8,128)S(1)} collective-permute-done((f32[3,2,72,4]{3,2,1,0:T(8,128)S(1)}, f32[3,2,72,4]{3,2,1,0:T(8,128)S(1)}, u32[]{:S(2)}, u32[]{:S(2)}) %collective-permute-start.7) | collective-permute-done | bytes 6944 | tf_op jit(solution)/shard_map/ppermute | solution.py:315
  50.2 3.8 %collective-permute-done.6 = f32[3,2,72,4]{3,2,1,0:T(8,128)S(1)} collective-permute-done((f32[3,2,72,4]{3,2,1,0:T(8,128)S(1)}, f32[3,2,72,4]{3,2,1,0:T(8,128)S(1)}, u32[]{:S(2)}, u32[]{:S(2)}) %collective-permute-start.6) | collective-permute-done | bytes 6944 | tf_op jit(solution)/shard_map/ppermute | solution.py:314
  56.3 29.7 %shard_map.126 = f32[3,2,72,384]{3,2,1,0:T(8,128)} custom-call(f32[2,72,384]{2,1,0:T(8,128)} %pad.16.rhs_ref, f32[72,384]{1,0:T(8,128)} %broadcast_in_dim.22.inside_ref, f32[72,384]{1,0:T(8,128)} %and_convert_fusion.own_ref), custom_call_target="tpu_custom_call" | custom-call | tf_op jit(solution)/shard_map/pallas_call | solution.py:230
  86.0 2.1 fusion.190
  89.6 2.8 %fusion.184 = (f32[5,2,4,63,256]{4,3,2,1,0:T(8,128)}, f32[5,2,4,63,256]{4,3,2,1,0:T(8,128)}) fusion(f32[5,2,4,64,256]{4,3,2,1,0:T(8,128)S(1)} %constant_dynamic-update-slice_fusion.1), kind=kLoop, calls=%fused_computation.341 | loop fusion | bytes 10321920 | tf_op jit(solution)/shard_map/slice | solution.py:275
  92.4 1.9 fusion.181
  95.2 2.4 copy.178
  97.5 2.0 collective-permute-start.8
  99.5 2.4 copy.180
  101.9 3.3 %fusion.182 = (f32[5,2,4,64,255]{4,3,2,1,0:T(8,128)}, f32[5,2,4,64,255]{4,3,2,1,0:T(8,128)}) fusion(f32[5,2,4,64,256]{4,3,2,1,0:T(8,128)S(1)} %constant_dynamic-update-slice_fusion.1), kind=kLoop, calls=%fused_computation.339 | loop fusion | bytes 10444800 | tf_op jit(solution)/shard_map/slice | solution.py:273
  105.8 2.5 copy.179
  108.3 2.3 copy.181
  111.7 3.7 %fusion.171 = (f32[2,64,256]{2,1,0:T(8,128)S(1)}, f32[2,4,64,256]{3,2,1,0:T(8,128)}) fusion(f32[5,2,4,63,256]{4,3,2,1,0:T(8,128)S(1)} %copy-done.5, f32[5,2,4,1,256]{4,3,2,1,0:T(1,128)S(1)} %copy_multiply_fusion, f32[5,2,4,1,256]{4,3,2,1,0:T(1,128)S(1)} %copy_multiply_fusion.1, f32[5,2,4,63,256]{4,3,2,1,0:T(8,128)} %get-tuple-element.82, ...), kind=kLoop, calls=%fused_computation.334 | loop fusion | flops 3506176 | bytes 12517632 | tf_op jit(solution)/shard_map/reduce_sum | solution.py:437
  119.3 2.7 %collective-permute-start.14 = (f32[3,2,4,256]{3,2,1,0:T(4,128)}, f32[3,2,4,256]{3,2,1,0:T(4,128)}, u32[]{:S(2)}, u32[]{:S(2)}) collective-permute-start(f32[3,2,4,256]{3,2,1,0:T(4,128)} %get-tuple-element.112), channel_id=1, source_target_pairs={{8,0},{16,8},{24,16},{32,24},{40,32},{48,40},{56,48},{0,56},{9,1},... | collective-permute-start | bytes 73736 | tf_op jit(solution)/shard_map/ppermute | solution.py:315
  128.1 4.2 %collective-permute-start.16 = (f32[3,2,72,4]{3,2,1,0:T(8,128)S(1)}, f32[3,2,72,4]{3,2,1,0:T(8,128)S(1)}, u32[]{:S(2)}, u32[]{:S(2)}) collective-permute-start(f32[3,2,72,4]{3,2,1,0:T(8,128)S(1)} %get-tuple-element.108), channel_id=1, source_target_pairs={{1,0},{2,1},{3,2},{4,3},{5,4},{6,5},{7,6},{0,7},{9,8},{10,9},{11,1... | collective-permute-start | bytes 20744 | tf_op jit(solution)/shard_map/ppermute | solution.py:315
  132.4 3.2 %fusion.106 = f32[2,4,64,256]{3,2,1,0:T(8,128)} fusion(f32[2,4,64,256]{3,2,1,0:T(8,128)} %get-tuple-element.72, f32[5,2,4,1,256]{4,3,2,1,0:T(1,128)S(1)} %copy_multiply_fusion.1, f32[5,2,4,63,256]{4,3,2,1,0:T(8,128)} %get-tuple-element.82, f32[5,2,4,63,256]{4,3,2,1,0:T(8,128)S(1)} %copy-done.5, f32[5,2,4,1,256]{4,3,2,1,0:T(1,128)S(1)} %copy_multiply_fusion, ...), kind=kLoop, calls=%fused_computation.196 | loop fusion | flops 3014656 | bytes 12910592 | tf_op jit(solution)/shard_map/mul | solution.py:418
  135.6 2.6 %collective-permute-done.16 = f32[3,2,72,4]{3,2,1,0:T(8,128)S(1)} collective-permute-done((f32[3,2,72,4]{3,2,1,0:T(8,128)S(1)}, f32[3,2,72,4]{3,2,1,0:T(8,128)S(1)}, u32[]{:S(2)}, u32[]{:S(2)}) %collective-permute-start.16) | collective-permute-done | bytes 6944 | tf_op jit(solution)/shard_map/ppermute | solution.py:315
  138.2 3.1 %collective-permute-done.15 = f32[3,2,72,4]{3,2,1,0:T(8,128)S(1)} collective-permute-done((f32[3,2,72,4]{3,2,1,0:T(8,128)S(1)}, f32[3,2,72,4]{3,2,1,0:T(8,128)S(1)}, u32[]{:S(2)}, u32[]{:S(2)}) %collective-permute-start.15) | collective-permute-done | bytes 6944 | tf_op jit(solution)/shard_map/ppermute | solution.py:314
  143.6 29.1 %shard_map.127 = f32[3,2,72,384]{3,2,1,0:T(8,128)} custom-call(f32[2,72,384]{2,1,0:T(8,128)} %pad.17.rhs_ref, f32[72,384]{1,0:T(8,128)} %broadcast_in_dim.22.inside_ref, f32[72,384]{1,0:T(8,128)} %and_convert_fusion.own_ref), custom_call_target="tpu_custom_call" | custom-call | tf_op jit(solution)/shard_map/pallas_call | solution.py:230
  172.7 2.0 multiply_bitcast_fusion.1
  174.7 3.7 %subtract_multiply_fusion.1 = (f32[2,4,64,256]{3,2,1,0:T(8,128)}, f32[2,4,64,256]{3,2,1,0:T(8,128)S(1)}, f32[2,4,64]{2,1,0:T(4,128)S(1)}, f32[2,4,64,256]{3,2,1,0:T(8,128)}) fusion(f32[2,4,64,256]{3,2,1,0:T(8,128)} %get-tuple-element.64, f32[2,64,256]{2,1,0:T(8,128)S(1)} %get-tuple-element.101, f32[64,256]{1,0:T(8,128)S(1)} %convert_element_type.50, ...), kind=kLoop, calls=%fused_computation.242 | loop fusion | flops 3669504 | bytes 15271936 | tf_op jit(solution)/shard_map/mul | solution.py:451
  179.6 3.2 %collective-permute-start.12 = (f32[2,2,4,64,256]{4,3,2,1,0:T(8,128)}, f32[2,2,4,64,256]{4,3,2,1,0:T(8,128)}, u32[]{:S(2)}, u32[]{:S(2)}) collective-permute-start(f32[2,2,4,64,256]{4,3,2,1,0:T(8,128)} %pad_maximum_fusion.1), channel_id=1, source_target_pairs={{0,64},{64,0},{1,65},{65,1},{2,66},{66,2},{3,67},{67,3},{4,68},{68... | collective-permute-start | bytes 3145736 | tf_op jit(solution)/shard_map/ppermute | solution.py:454
  184.4 24.7 %shard_map.128 = f32[40,128]{1,0:T(8,128)} custom-call(f32[40,128]{1,0:T(8,128)} %select_maximum_fusion.1.x_ref), custom_call_target="tpu_custom_call" | custom-call | tf_op jit(solution)/shard_map/pallas_call | solution.py:90
  219.8 21.6 %collective-permute-done.17 = f32[2,10,64,256]{3,2,1,0:T(8,128)} collective-permute-done((f32[2,10,64,256]{3,2,1,0:T(8,128)S(1)}, f32[2,10,64,256]{3,2,1,0:T(8,128)}, u32[]{:S(2)}, u32[]{:S(2)}) %collective-permute-start.17) | collective-permute-done | bytes 1310752 | tf_op jit(solution)/shard_map/ppermute | solution.py:476
  (208 shorter events, 58.2 us)
Async XLA Ops:
  4.4 26.7 %collective-permute-start.3 = (f32[5,2,4,1,256]{4,2,3,1,0:T(4,128)S(1)}, f32[5,2,4,1,256]{4,2,3,1,0:T(4,128)S(1)}, u32[]{:S(2)}, u32[]{:S(2)}) collective-permute-start(f32[5,2,4,1,256]{4,2,3,1,0:T(4,128)S(1)} %copy.171), channel_id=1, source_target_pairs={{0,8},{8,16},{16,24},{24,32},{32,40},{40,48},{48,56},{56,0},{1,9},... | collective-permute-start | bytes 122888 | tf_op jit(solution)/shard_map/ppermute | solution.py:262
  4.5 26.7 %collective-permute-start.2 = (f32[5,2,4,1,256]{4,2,3,1,0:T(4,128)S(1)}, f32[5,2,4,1,256]{4,2,3,1,0:T(4,128)S(1)}, u32[]{:S(2)}, u32[]{:S(2)}) collective-permute-start(f32[5,2,4,1,256]{4,2,3,1,0:T(4,128)S(1)} %copy.168), channel_id=1, source_target_pairs={{8,0},{16,8},{24,16},{32,24},{40,32},{48,40},{56,48},{0,56},{9,1},... | collective-permute-start | bytes 122888 | tf_op jit(solution)/shard_map/ppermute | solution.py:261
  11.1 16.9 %collective-permute-start.1 = (f32[5,2,4,64,1]{3,2,4,1,0:T(4,128)S(1)}, f32[5,2,4,64,1]{3,2,4,1,0:T(4,128)S(1)}, u32[]{:S(2)}, u32[]{:S(2)}) collective-permute-start(f32[5,2,4,64,1]{3,2,4,1,0:T(4,128)S(1)} %copy.166), channel_id=1, source_target_pairs={{0,1},{1,2},{2,3},{3,4},{4,5},{5,6},{6,7},{7,0},{8,9},{9,10},{10,1... | collective-permute-start | bytes 30728 | tf_op jit(solution)/shard_map/ppermute | solution.py:264
  14.6 15.0 %collective-permute-start = (f32[5,2,4,64,1]{3,2,4,1,0:T(4,128)S(1)}, f32[5,2,4,64,1]{3,2,4,1,0:T(4,128)S(1)}, u32[]{:S(2)}, u32[]{:S(2)}) collective-permute-start(f32[5,2,4,64,1]{3,2,4,1,0:T(4,128)S(1)} %copy.164), channel_id=1, source_target_pairs={{1,0},{2,1},{3,2},{4,3},{5,4},{6,5},{7,6},{0,7},{9,8},{10,9},{11,1... | collective-permute-start | bytes 30728 | tf_op jit(solution)/shard_map/ppermute | solution.py:263
  24.9 9.5 %copy-start.46 = (f32[64]{0:T(128)}, f32[64]{0:T(128)S(1)}, u32[]{:S(2)}) copy-start(f32[64]{0:T(128)S(1)} %get-tuple-element.127) | copy-start | bytes 772
  24.9 9.5 %copy-start.44 = (f32[64]{0:T(128)}, f32[64]{0:T(128)S(1)}, u32[]{:S(2)}) copy-start(f32[64]{0:T(128)S(1)} %get-tuple-element.128) | copy-start | bytes 772
  27.9 27.7 %copy-start.40 = (f32[72]{0:T(128)}, f32[72]{0:T(128)S(1)}, u32[]{:S(2)}) copy-start(f32[72]{0:T(128)S(1)} %and_convert_fusion.1) | copy-start | bytes 868
  28.0 26.5 %copy-start.42 = (f32[70]{0:T(128)}, f32[70]{0:T(128)S(1)}, u32[]{:S(2)}) copy-start(f32[70]{0:T(128)S(1)} %slice.410) | copy-start | bytes 844
  38.4 2.0 collective-permute-start.5
  38.4 4.5 %collective-permute-start.4 = (f32[3,2,4,256]{3,2,1,0:T(4,128)S(1)}, f32[3,2,4,256]{3,2,1,0:T(4,128)S(1)}, u32[]{:S(2)}, u32[]{:S(2)}) collective-permute-start(f32[3,2,4,256]{3,2,1,0:T(4,128)S(1)} %get-tuple-element.113), channel_id=1, source_target_pairs={{0,8},{8,16},{16,24},{24,32},{32,40},{40,48},{48,56},{56,0},{1,9},... | collective-permute-start | bytes 73736 | tf_op jit(solution)/shard_map/ppermute | solution.py:314
  43.0 7.2 %collective-permute-start.7 = (f32[3,2,72,4]{3,2,1,0:T(8,128)S(1)}, f32[3,2,72,4]{3,2,1,0:T(8,128)S(1)}, u32[]{:S(2)}, u32[]{:S(2)}) collective-permute-start(f32[3,2,72,4]{3,2,1,0:T(8,128)S(1)} %get-tuple-element.110), channel_id=1, source_target_pairs={{1,0},{2,1},{3,2},{4,3},{5,4},{6,5},{7,6},{0,7},{9,8},{10,9},{11,1... | collective-permute-start | bytes 20744 | tf_op jit(solution)/shard_map/ppermute | solution.py:315
  45.1 8.9 %collective-permute-start.6 = (f32[3,2,72,4]{3,2,1,0:T(8,128)S(1)}, f32[3,2,72,4]{3,2,1,0:T(8,128)S(1)}, u32[]{:S(2)}, u32[]{:S(2)}) collective-permute-start(f32[3,2,72,4]{3,2,1,0:T(8,128)S(1)} %get-tuple-element.109), channel_id=1, source_target_pairs={{0,1},{1,2},{2,3},{3,4},{4,5},{5,6},{6,7},{7,0},{8,9},{9,10},{10,1... | collective-permute-start | bytes 20744 | tf_op jit(solution)/shard_map/ppermute | solution.py:314
  94.9 15.7 %collective-permute-start.10 = (f32[5,2,4,1,256]{4,2,3,1,0:T(4,128)}, f32[5,2,4,1,256]{4,2,3,1,0:T(4,128)S(1)}, u32[]{:S(2)}, u32[]{:S(2)}) collective-permute-start(f32[5,2,4,1,256]{4,2,3,1,0:T(4,128)} %copy.182), channel_id=1, source_target_pairs={{8,0},{16,8},{24,16},{32,24},{40,32},{48,40},{56,48},{0,56},{9,1},... | collective-permute-start | bytes 122888 | tf_op jit(solution)/shard_map/ppermute | solution.py:261
  97.5 8.3 %collective-permute-start.8 = (f32[5,2,4,64,1]{3,2,4,1,0:T(4,128)}, f32[5,2,4,64,1]{3,2,4,1,0:T(4,128)}, u32[]{:S(2)}, u32[]{:S(2)}) collective-permute-start(f32[5,2,4,64,1]{3,2,4,1,0:T(4,128)} %copy.178), channel_id=1, source_target_pairs={{1,0},{2,1},{3,2},{4,3},{5,4},{6,5},{7,6},{0,7},{9,8},{10,9},{11,1... | collective-permute-start | bytes 30728 | tf_op jit(solution)/shard_map/ppermute | solution.py:263
  101.9 6.4 %collective-permute-start.9 = (f32[5,2,4,64,1]{3,2,4,1,0:T(4,128)}, f32[5,2,4,64,1]{3,2,4,1,0:T(4,128)}, u32[]{:S(2)}, u32[]{:S(2)}) collective-permute-start(f32[5,2,4,64,1]{3,2,4,1,0:T(4,128)} %copy.180), channel_id=1, source_target_pairs={{0,1},{1,2},{2,3},{3,4},{4,5},{5,6},{6,7},{7,0},{8,9},{9,10},{10,1... | collective-permute-start | bytes 30728 | tf_op jit(solution)/shard_map/ppermute | solution.py:264
  105.8 5.0 %collective-permute-start.11 = (f32[5,2,4,1,256]{4,2,3,1,0:T(4,128)}, f32[5,2,4,1,256]{4,2,3,1,0:T(4,128)}, u32[]{:S(2)}, u32[]{:S(2)}) collective-permute-start(f32[5,2,4,1,256]{4,2,3,1,0:T(4,128)} %copy.185), channel_id=1, source_target_pairs={{0,8},{8,16},{16,24},{24,32},{32,40},{40,48},{48,56},{56,0},{1,9},... | collective-permute-start | bytes 122888 | tf_op jit(solution)/shard_map/ppermute | solution.py:262
  119.3 7.2 %collective-permute-start.14 = (f32[3,2,4,256]{3,2,1,0:T(4,128)}, f32[3,2,4,256]{3,2,1,0:T(4,128)}, u32[]{:S(2)}, u32[]{:S(2)}) collective-permute-start(f32[3,2,4,256]{3,2,1,0:T(4,128)} %get-tuple-element.112), channel_id=1, source_target_pairs={{8,0},{16,8},{24,16},{32,24},{40,32},{48,40},{56,48},{0,56},{9,1},... | collective-permute-start | bytes 73736 | tf_op jit(solution)/shard_map/ppermute | solution.py:315
  122.0 4.8 %collective-permute-start.13 = (f32[3,2,4,256]{3,2,1,0:T(4,128)}, f32[3,2,4,256]{3,2,1,0:T(4,128)}, u32[]{:S(2)}, u32[]{:S(2)}) collective-permute-start(f32[3,2,4,256]{3,2,1,0:T(4,128)} %get-tuple-element.111), channel_id=1, source_target_pairs={{0,8},{8,16},{16,24},{24,32},{32,40},{40,48},{48,56},{56,0},{1,9},... | collective-permute-start | bytes 73736 | tf_op jit(solution)/shard_map/ppermute | solution.py:314
  128.1 10.1 %collective-permute-start.16 = (f32[3,2,72,4]{3,2,1,0:T(8,128)S(1)}, f32[3,2,72,4]{3,2,1,0:T(8,128)S(1)}, u32[]{:S(2)}, u32[]{:S(2)}) collective-permute-start(f32[3,2,72,4]{3,2,1,0:T(8,128)S(1)} %get-tuple-element.108), channel_id=1, source_target_pairs={{1,0},{2,1},{3,2},{4,3},{5,4},{6,5},{7,6},{0,7},{9,8},{10,9},{11,1... | collective-permute-start | bytes 20744 | tf_op jit(solution)/shard_map/ppermute | solution.py:315
  132.3 9.0 %copy-start.31 = (f32[2,64,256]{2,1,0:T(8,128)S(1)}, f32[2,64,256]{2,1,0:T(8,128)}, u32[]{:S(2)}) copy-start(f32[2,64,256]{2,1,0:T(8,128)} %copy-done.30) | copy-start | bytes 393220
  132.3 9.0 %copy-start.33 = (f32[2,64,256]{2,1,0:T(8,128)S(1)}, f32[2,64,256]{2,1,0:T(8,128)}, u32[]{:S(2)}) copy-start(f32[2,64,256]{2,1,0:T(8,128)} %copy-done.32) | copy-start | bytes 393220
  132.3 9.0 %copy-start.35 = (f32[1,2,64,256]{3,2,1,0:T(8,128)S(1)}, f32[1,2,64,256]{3,2,1,0:T(8,128)}, u32[]{:S(2)}) copy-start(f32[1,2,64,256]{3,2,1,0:T(8,128)} %get-tuple-element.104) | copy-start | bytes 393220
  132.3 9.0 %copy-start.41 = (f32[72]{0:T(128)S(1)}, f32[72]{0:T(128)}, u32[]{:S(2)}) copy-start(f32[72]{0:T(128)} %copy-done.40) | copy-start | bytes 868
  132.3 10.1 %copy-start.43 = (f32[70]{0:T(128)S(1)}, f32[70]{0:T(128)}, u32[]{:S(2)}) copy-start(f32[70]{0:T(128)} %copy-done.42) | copy-start | bytes 844
  132.3 9.0 %collective-permute-start.15 = (f32[3,2,72,4]{3,2,1,0:T(8,128)S(1)}, f32[3,2,72,4]{3,2,1,0:T(8,128)S(1)}, u32[]{:S(2)}, u32[]{:S(2)}) collective-permute-start(f32[3,2,72,4]{3,2,1,0:T(8,128)S(1)} %get-tuple-element.107), channel_id=1, source_target_pairs={{0,1},{1,2},{2,3},{3,4},{4,5},{5,6},{6,7},{7,0},{8,9},{9,10},{10,1... | collective-permute-start | bytes 20744 | tf_op jit(solution)/shard_map/ppermute | solution.py:314
  178.4 31.5 %copy-start.28 = (f32[2,4,64,256]{3,2,1,0:T(8,128)S(1)}, f32[2,4,64,256]{3,2,1,0:T(8,128)}, u32[]{:S(2)}) copy-start(f32[2,4,64,256]{3,2,1,0:T(8,128)} %get-tuple-element.115) | copy-start | bytes 1572868
  178.4 31.5 %copy-start.29 = (f32[2,4,64,256]{3,2,1,0:T(8,128)S(1)}, f32[2,4,64,256]{3,2,1,0:T(8,128)}, u32[]{:S(2)}) copy-start(f32[2,4,64,256]{3,2,1,0:T(8,128)} %get-tuple-element.118) | copy-start | bytes 1572868
  178.4 34.1 %copy-start.49 = (s32[2]{0:T(128)S(1)}, s32[2]{0:T(128)}, u32[]{:S(2)}) copy-start(s32[2]{0:T(128)} %get-tuple-element.121) | copy-start | bytes 28
  178.5 34.9 %copy-start.48 = (pred[8]{0:T(512)(128)(4,1)S(1)}, pred[8]{0:T(512)(128)(4,1)}, u32[]{:S(2)}) copy-start(pred[8]{0:T(512)(128)(4,1)} %iota_compare_fusion.4) | copy-start | bytes 28
  178.5 35.1 %copy-start.36 = (f32[2,1,64,256]{3,2,1,0:T(8,128)S(1)}, f32[2,1,64,256]{3,2,1,0:T(8,128)}, u32[]{:S(2)}) copy-start(f32[2,1,64,256]{3,2,1,0:T(8,128)} %get-tuple-element.102) | copy-start | bytes 393220
  179.6 34.7 %collective-permute-start.12 = (f32[2,2,4,64,256]{4,3,2,1,0:T(8,128)}, f32[2,2,4,64,256]{4,3,2,1,0:T(8,128)}, u32[]{:S(2)}, u32[]{:S(2)}) collective-permute-start(f32[2,2,4,64,256]{4,3,2,1,0:T(8,128)} %pad_maximum_fusion.1), channel_id=1, source_target_pairs={{0,64},{64,0},{1,65},{65,1},{2,66},{66,2},{3,67},{67,3},{4,68},{68... | collective-permute-start | bytes 3145736 | tf_op jit(solution)/shard_map/ppermute | solution.py:454
  211.0 30.4 %collective-permute-start.17 = (f32[2,10,64,256]{3,2,1,0:T(8,128)S(1)}, f32[2,10,64,256]{3,2,1,0:T(8,128)}, u32[]{:S(2)}, u32[]{:S(2)}) collective-permute-start(f32[2,10,64,256]{3,2,1,0:T(8,128)S(1)} %select_maximum_fusion), channel_id=1, source_target_pairs={{0,64},{64,0},{1,65},{65,1},{2,66},{66,2},{3,67},{67,3},{4,68},{68... | collective-permute-start | bytes 3932168 | tf_op jit(solution)/shard_map/ppermute | solution.py:476
  (38 other events, 160.5 us)

commit v4 on v3

--- a/solution.py
+++ b/solution.py
@@ -246,6 +246,93 @@
     )(rhs, inside, own)
 
 
+def volume_kernel(temp_ref, salt_ref, uvel_ref, vvel_ref, ocean_ref, cor_ref, n_ref, s_ref, e_ref, w_ref,
+                  tn_ref, sn_ref, us_ref, vs_ref, tu_ref, tv_ref):
+    levels, rows, cols = temp_ref.shape[1], temp_ref.shape[2], temp_ref.shape[3]
+    row = lax.broadcasted_iota(jnp.int32, (rows, cols), 0)
+    col = lax.broadcasted_iota(jnp.int32, (rows, cols), 1)
+    top = row == rows - 1
+    bottom = row == 0
+    right = col == cols - 1
+    left = col == 0
+    ocean = ocean_ref[...]
+    cor = cor_ref[...]
+
+    def around(f, rims):
+        n, s, e, w = rims
+        return (
+            jnp.where(right, e, pltpu.roll(f, cols - 1, 1)),
+            jnp.where(left, w, pltpu.roll(f, 1, 1)),
+            jnp.where(top, n, pltpu.roll(f, rows - 1, 0)),
+            jnp.where(bottom, s, pltpu.roll(f, 1, 0)),
+        )
+
+    def rims_of(k, l):
+        return (n_ref[k, 0, l], s_ref[k, 0, l], e_ref[k, 0, l], w_ref[k, 0, l])
+
+    running = None
+    running_rims = None
+    tu = None
+    tv = None
+    for l in range(levels):
+        t = temp_ref[0, l]
+        s = salt_ref[0, l]
+        u = uvel_ref[0, l]
+        v = vvel_ref[0, l]
+        rt, rs, ru, rv = rims_of(0, l), rims_of(1, l), rims_of(2, l), rims_of(3, l)
+        layer = BETA_S * s - ALPHA_T * t
+        layer_rims = tuple(BETA_S * b - ALPHA_T * a for a, b in zip(rt, rs))
+        if running is None:
+            running, running_rims = layer, layer_rims
+        else:
+            running = running + layer
+            running_rims = tuple(a + b for a, b in zip(running_rims, layer_rims))
+        press = PRESS_K * running
+        press_rims = tuple(PRESS_K * a for a in running_rims)
+        te, tw, tn, ts = around(t, rt)
+        se, sw, sn, ss = around(s, rs)
+        ue, uw, un, us = around(u, ru)
+        ve, vw, vn, vs = around(v, rv)
+        pe, pw, pn, ps = around(press, press_rims)
+        tn_ref[0, l] = ocean * (
+            t - STEP_DT * 0.5 * (u * (te - tw) + v * (tn - ts)) + KAPPA * (te + tw + tn + ts - 4.0 * t)
+        )
+        sn_ref[0, l] = ocean * (
+            s - STEP_DT * 0.5 * (u * (se - sw) + v * (sn - ss)) + KAPPA * (se + sw + sn + ss - 4.0 * s)
+        )
+        ustar = ocean * (
+            u + STEP_DT * (cor * v - 0.5 * (pe - pw) - DRAG_K * u) + VISCOSITY * (ue + uw + un + us - 4.0 * u)
+        )
+        vstar = ocean * (
+            v + STEP_DT * (-cor * u - 0.5 * (pn - ps) - DRAG_K * v) + VISCOSITY * (ve + vw + vn + vs - 4.0 * v)
+        )
+        us_ref[0, l] = ustar
+        vs_ref[0, l] = vstar
+        tu = ustar if tu is None else tu + ustar
+        tv = vstar if tv is None else tv + vstar
+    tu_ref[0] = tu
+    tv_ref[0] = tv
+
+
+def volume_step(temp, salt, uvel, vvel, ocean, cor_tile, rims):
+    members, levels, rows, cols = temp.shape
+    field = pl.BlockSpec((1, levels, rows, cols), lambda m: (m, 0, 0, 0))
+    plane = pl.BlockSpec((rows, cols), lambda m: (0, 0))
+    north, south, east, west = rims
+    row_rim = pl.BlockSpec((4, 1, levels, 1, cols), lambda m: (0, m, 0, 0, 0))
+    col_rim = pl.BlockSpec((4, 1, levels, rows, 1), lambda m: (0, m, 0, 0, 0))
+    surface = pl.BlockSpec((1, rows, cols), lambda m: (m, 0, 0))
+    volume_shape = jax.ShapeDtypeStruct(temp.shape, jnp.float32)
+    surface_shape = jax.ShapeDtypeStruct((members, rows, cols), jnp.float32)
+    return pl.pallas_call(
+        volume_kernel,
+        grid=(members,),
+        in_specs=[field] * 4 + [plane, plane, row_rim, row_rim, col_rim, col_rim],
+        out_specs=[field] * 4 + [surface] * 2,
+        out_shape=[volume_shape] * 4 + [surface_shape] * 2,
+    )(temp, salt, uvel, vvel, ocean, cor_tile, north, south, east, west)
+
+
 def ring(axis):
     count = lax.axis_size(axis)
     forward = [(i, (i + 1) % count) for i in range(count)]
@@ -263,6 +350,16 @@
     east = lax.ppermute(lax.slice_in_dim(block, 0, 1, axis=xdim), "gridx", bwd_x)
     west = lax.ppermute(lax.slice_in_dim(block, cols - 1, cols, axis=xdim), "gridx", fwd_x)
     return (east, west, north, south)
+
+
+def exchange_fields(fields, south_keep, north_keep):
+    fwd_y, bwd_y = ring("gridy")
+    fwd_x, bwd_x = ring("gridx")
+    north = lax.ppermute(jnp.stack([f[..., :1, :] for f in fields]), "gridy", bwd_y) * north_keep
+    south = lax.ppermute(jnp.stack([f[..., -1:, :] for f in fields]), "gridy", fwd_y) * south_keep
+    east = lax.ppermute(jnp.stack([f[..., :, :1] for f in fields]), "gridx", bwd_x)
+    west = lax.ppermute(jnp.stack([f[..., :, -1:] for f in fields]), "gridx", fwd_x)
+    return (north, south, east, west)
 
 
 def sides(field, rims, ydim, xdim):
@@ -388,6 +485,7 @@
     north_keep = (tile_row < tile_count - 1).astype(jnp.float32)
     latitude = (tile_row * rows + jnp.arange(rows, dtype=jnp.int32)).astype(jnp.float32) + 0.5
     coriolis = (CORI_K * (2.0 * latitude / total_rows - 1.0))[:, None]
+    cor_tile = jnp.broadcast_to(coriolis, (rows, cols))
     wide_rows = tile_row * rows - (ITERS + 1) + jnp.arange(rows + 2 * (ITERS + 1), dtype=jnp.int32)
     inside = ((wide_rows >= 0) & (wide_rows < total_rows)).astype(jnp.float32)[:, None]
     halo = ITERS + 1
@@ -399,42 +497,14 @@
         (row_at >= halo) & (row_at < halo + rows) & (col_at >= halo) & (col_at < halo + cols)
     ).astype(jnp.float32)
     for count in range(STEPS):
-        press = pressure(temp, salt)
-        volume = jnp.stack((temp, salt, uvel, vvel, press))
-        east_side, west_side, north_side, south_side = sides(
-            volume, exchange(volume, 3, 4, south_keep, north_keep), 3, 4
-        )
-        lap_temp = east_side[0] + west_side[0] + north_side[0] + south_side[0] - 4.0 * temp
-        lap_salt = east_side[1] + west_side[1] + north_side[1] + south_side[1] - 4.0 * salt
-        lap_uvel = east_side[2] + west_side[2] + north_side[2] + south_side[2] - 4.0 * uvel
-        lap_vvel = east_side[3] + west_side[3] + north_side[3] + south_side[3] - 4.0 * vvel
-        temp_next = ocean * (
-            temp
-            - STEP_DT
-            * 0.5
-            * (uvel * (east_side[0] - west_side[0]) + vvel * (north_side[0] - south_side[0]))
-            + KAPPA * lap_temp
-        )
-        salt_next = ocean * (
-            salt
-            - STEP_DT
-            * 0.5
-            * (uvel * (east_side[1] - west_side[1]) + vvel * (north_side[1] - south_side[1]))
-            + KAPPA * lap_salt
-        )
-        ustar = ocean * (
-            uvel
-            + STEP_DT * (coriolis * vvel - 0.5 * (east_side[4] - west_side[4]) - DRAG_K * uvel)
-            + VISCOSITY * lap_uvel
-        )
-        vstar = ocean * (
-            vvel
-            + STEP_DT * (-coriolis * uvel - 0.5 * (north_side[4] - south_side[4]) - DRAG_K * vvel)
-            + VISCOSITY * lap_vvel
+        fields = (temp, salt, uvel, vvel)
+        rims = exchange_fields(fields, south_keep, north_keep)
+        temp_next, salt_next, ustar, vstar, trans_u, trans_v = volume_step(
+            temp, salt, uvel, vvel, ocean, cor_tile, rims
         )
         halo = ITERS + 1
         surface = padded_2(
-            jnp.stack((jnp.sum(ustar, axis=1), jnp.sum(vstar, axis=1), eta)),
+            jnp.stack((trans_u, trans_v, eta)),
             (("gridy", 2), ("gridx", 3)),
             halo,
         ) * inside

time: 250 us -> 219 us (0.88)
  local copies, waits for them, and re-layouts: 50.6 us -> 25.6 us
  other arithmetic: 46.4 us -> 28.8 us
  starting transfers between devices: 24.8 us -> 35.7 us
  Pallas kernels: 83.5 us -> 93 us
  waiting for transfers between devices: 37.8 us -> 29.3 us
    slice x16 -> x8, local copies, waits for them, and re-layouts: 25.8 us -> 5.84 us  [exchange_fields(): f[..., :, -1:]]
    pallas_call x1, Pallas kernels: 24.7 us -> 12.5 us  [grid_sum(): pl.pallas_call(functools.partial(gather_sum_kernel, ny, nx), out_shape=ja...]
    pallas_call x2, Pallas kernels: 58.8 us -> 70.5 us  [surface_kernel_solve(): pl.pallas_call(functools.partial(solve_kernel, ny, nx), out_shape=jax.Sha...]
    pallas_call x0 -> x2, Pallas kernels: none -> 9.92 us  [volume_step(): pl.pallas_call(volume_kernel, grid=(members,), in_specs=[field] * 4 + [pl...]
    reduce_sum x4 -> x1, other arithmetic: 9.67 us -> 0.17 us  [shards(): zonal_local = jnp.sum(vvel, axis=3)]
    unnamed x109 -> x48, local copies, waits for them, and re-layouts: 8.09 us -> 0.12 us
    ppermute x4, starting transfers between devices: 8.97 us -> 14.1 us  [padded_2(): lax.ppermute(lax.slice_in_dim(block, 0, width, axis=dim), axis, backward)]
    ppermute x4, waiting for transfers between devices: 6.37 us -> 1.47 us  [padded_2(): lax.ppermute(lax.slice_in_dim(block, 0, width, axis=dim), axis, backward)]
  transfers between devices with their start and end apart: 18 -> 18, of which waited for: 8 -> 5; matrix products, arithmetic and copies ran while one was open for 20% -> 16% of each run, Pallas kernels for 10% -> 24%
where the time goes in v4:
time: 219 us; the launch traced here: 218 us
  Pallas kernels  93 us (42%)
  starting transfers between devices  35.7 us (16%)
  waiting for transfers between devices  29.3 us (13%)
  other arithmetic  28.8 us (13%)
  local copies, waits for them, and re-layouts  25.6 us (12%)
  between operations  5.9 us (3%)
    pallas_call x2, Pallas kernels, surface_kernel_solve(): pl.pallas_call(functools.partial(solve_kernel, ny, nx), out_shape=jax.Sha...  70.5 us
    ppermute x1, waiting for transfers between devices, shards(): flows_other = lax.ppermute(flows, 'member', swap)  19.4 us
    ppermute x4, starting transfers between devices, padded_2(): lax.ppermute(lax.slice_in_dim(block, 0, width, axis=dim), axis, backward)  14.1 us
    pallas_call x1, Pallas kernels, grid_sum(): pl.pallas_call(functools.partial(gather_sum_kernel, ny, nx), out_shape=ja...  12.5 us
    pallas_call x2, Pallas kernels, volume_step(): pl.pallas_call(volume_kernel, grid=(members,), in_specs=[field] * 4 + [pl...  9.92 us
    ppermute x2, starting transfers between devices, exchange_fields(): lax.ppermute(jnp.stack([f[..., :, :1] for f in fields]), 'gridx', bwd_x)  8.12 us
    ppermute x4, waiting for transfers between devices, padded_2(): lax.ppermute(lax.slice_in_dim(block, size - width, size, axis=dim), axis,...  7.28 us
    ppermute x2, starting transfers between devices, exchange_fields(): lax.ppermute(jnp.stack([f[..., :1, :] for f in fields]), 'gridy', bwd_y)  5.89 us
  transfers between devices with their start and end apart: 18, of which 5 were waited for; matrix products, arithmetic and copies ran while one was open for 16% of the time, Pallas kernels for 24%

profile of v4, /device:TPU:0, one launch (start us, length us, event | category | flops | bytes accessed | tf_op | source)
XLA Modules:
  0.0 218.4 jit_solution(8948491387089179461)
XLA Ops:
  2.8 2.9 %collective-permute-start = (f32[4,2,4,1,256]{4,3,2,1,0:T(1,128)S(1)}, f32[4,2,4,1,256]{4,3,2,1,0:T(1,128)S(1)}, u32[]{:S(2)}, u32[]{:S(2)}) collective-permute-start(f32[4,2,4,1,256]{4,3,2,1,0:T(1,128)S(1)} %pad_maximum_fusion.7), channel_id=1, source_target_pairs={{8,0},{16,8},{24,16},{32,24},{40,32},{48,40},{56,48},{0,56},{9,1},... | collective-permute-start | bytes 98312 | tf_op jit(solution)/shard_map/ppermute | solution.py:358
  5.8 1.4 slice_reduce_fusion.10
  7.1 1.4 slice_reduce_fusion.9
  9.2 5.2 %collective-permute-start.2 = (f32[4,2,4,64,1]{3,2,4,1,0:T(4,128)S(1)}, f32[4,2,4,64,1]{3,2,4,1,0:T(4,128)S(1)}, u32[]{:S(2)}, u32[]{:S(2)}) collective-permute-start(f32[4,2,4,64,1]{3,2,4,1,0:T(4,128)S(1)} %pad_maximum_fusion.17), channel_id=1, source_target_pairs={{1,0},{2,1},{3,2},{4,3},{5,4},{6,5},{7,6},{0,7},{9,8},{10,9},{11,1... | collective-permute-start | bytes 24584 | tf_op jit(solution)/shard_map/ppermute | solution.py:360
  17.8 1.4 copy.225.e_ref
  20.3 1.4 copy.226.w_ref
  23.6 5.0 %shard_map.126 = (f32[2,4,64,256]{3,2,1,0:T(8,128)}, f32[2,4,64,256]{3,2,1,0:T(8,128)}, f32[2,4,64,256]{3,2,1,0:T(8,128)}, f32[2,4,64,256]{3,2,1,0:T(8,128)}, f3...) custom-call(f32[2,4,64,256]{3,2,1,0:T(8,128)} %temp_ref.1, f32[2,4,64,256]{3,2,1,0:T(8,128)} %salt_ref.1, ...), custom_call_target="tpu_custom_call" | custom-call | tf_op jit(solution)/shard_map/pallas_call | solution.py:327
  29.5 2.9 %collective-permute-start.5 = (f32[3,2,4,256]{3,2,1,0:T(4,128)S(1)}, f32[3,2,4,256]{3,2,1,0:T(4,128)S(1)}, u32[]{:S(2)}, u32[]{:S(2)}) collective-permute-start(f32[3,2,4,256]{3,2,1,0:T(4,128)S(1)} %get-tuple-element.142), channel_id=1, source_target_pairs={{8,0},{16,8},{24,16},{32,24},{40,32},{48,40},{56,48},{0,56},{9,1},... | collective-permute-start | bytes 73736 | tf_op jit(solution)/shard_map/ppermute | solution.py:412
  34.2 1.4 slice_reduce_fusion.5
  36.9 4.1 %collective-permute-start.7 = (f32[3,2,72,4]{3,2,1,0:T(8,128)S(1)}, f32[3,2,72,4]{3,2,1,0:T(8,128)S(1)}, u32[]{:S(2)}, u32[]{:S(2)}) collective-permute-start(f32[3,2,72,4]{3,2,1,0:T(8,128)S(1)} %get-tuple-element.138), channel_id=1, source_target_pairs={{1,0},{2,1},{3,2},{4,3},{5,4},{6,5},{7,6},{0,7},{9,8},{10,9},{11,1... | collective-permute-start | bytes 20744 | tf_op jit(solution)/shard_map/ppermute | solution.py:412
  41.4 4.9 %collective-permute-done.6 = f32[3,2,72,4]{3,2,1,0:T(8,128)S(1)} collective-permute-done((f32[3,2,72,4]{3,2,1,0:T(8,128)S(1)}, f32[3,2,72,4]{3,2,1,0:T(8,128)S(1)}, u32[]{:S(2)}, u32[]{:S(2)}) %collective-permute-start.6) | collective-permute-done | bytes 6944 | tf_op jit(solution)/shard_map/ppermute | solution.py:411
  48.6 31.5 %shard_map.127 = f32[3,2,72,384]{3,2,1,0:T(8,128)} custom-call(f32[2,72,384]{2,1,0:T(8,128)} %pad.16.rhs_ref, f32[72,384]{1,0:T(8,128)} %broadcast_in_dim.25.inside_ref, f32[72,384]{1,0:T(8,128)} %and_convert_fusion.own_ref), custom_call_target="tpu_custom_call" | custom-call | tf_op jit(solution)/shard_map/pallas_call | solution.py:230
  80.1 1.3 fusion.21
  82.4 1.3 collective-permute-start.11
  83.7 2.9 %collective-permute-start.10 = (f32[4,2,4,64,1]{3,2,4,1,0:T(4,128)S(1)}, f32[4,2,4,64,1]{3,2,4,1,0:T(4,128)S(1)}, u32[]{:S(2)}, u32[]{:S(2)}) collective-permute-start(f32[4,2,4,64,1]{3,2,4,1,0:T(4,128)S(1)} %pad_maximum_fusion.19), channel_id=1, source_target_pairs={{1,0},{2,1},{3,2},{4,3},{5,4},{6,5},{7,6},{0,7},{9,8},{10,9},{11,1... | collective-permute-start | bytes 24584 | tf_op jit(solution)/shard_map/ppermute | solution.py:360
  86.7 2.9 %collective-permute-start.8 = (f32[4,2,4,1,256]{4,3,2,1,0:T(1,128)S(1)}, f32[4,2,4,1,256]{4,3,2,1,0:T(1,128)S(1)}, u32[]{:S(2)}, u32[]{:S(2)}) collective-permute-start(f32[4,2,4,1,256]{4,3,2,1,0:T(1,128)S(1)} %pad_maximum_fusion.9), channel_id=1, source_target_pairs={{8,0},{16,8},{24,16},{32,24},{40,32},{48,40},{56,48},{0,56},{9,1},... | collective-permute-start | bytes 98312 | tf_op jit(solution)/shard_map/ppermute | solution.py:358
  89.6 1.4 copy.240.w_ref
  91.0 1.4 copy.239.e_ref
  93.7 5.0 %shard_map.128 = (f32[2,4,64,256]{3,2,1,0:T(8,128)}, f32[2,4,64,256]{3,2,1,0:T(8,128)}, f32[2,4,64,256]{3,2,1,0:T(8,128)}, f32[2,4,64,256]{3,2,1,0:T(8,128)}, f3...) custom-call(f32[2,4,64,256]{3,2,1,0:T(8,128)} %get-tuple-element.43.temp_ref, f32[2,4,64,256]{3,2,1,0:T(8,128)} %get-tuple-element.44.salt_ref, ...), custom_call_target="tpu_custom_call" | custom-call | tf_op jit(solution)/shard_map/pallas_call | solution.py:327
  99.6 2.9 %collective-permute-start.14 = (f32[3,2,4,256]{3,2,1,0:T(4,128)S(1)}, f32[3,2,4,256]{3,2,1,0:T(4,128)S(1)}, u32[]{:S(2)}, u32[]{:S(2)}) collective-permute-start(f32[3,2,4,256]{3,2,1,0:T(4,128)S(1)} %get-tuple-element.140), channel_id=1, source_target_pairs={{8,0},{16,8},{24,16},{32,24},{40,32},{48,40},{56,48},{0,56},{9,1},... | collective-permute-start | bytes 73736 | tf_op jit(solution)/shard_map/ppermute | solution.py:412
  107.9 4.1 %collective-permute-start.16 = (f32[3,2,72,4]{3,2,1,0:T(8,128)S(1)}, f32[3,2,72,4]{3,2,1,0:T(8,128)S(1)}, u32[]{:S(2)}, u32[]{:S(2)}) collective-permute-start(f32[3,2,72,4]{3,2,1,0:T(8,128)S(1)} %get-tuple-element.136), channel_id=1, source_target_pairs={{1,0},{2,1},{3,2},{4,3},{5,4},{6,5},{7,6},{0,7},{9,8},{10,9},{11,1... | collective-permute-start | bytes 20744 | tf_op jit(solution)/shard_map/ppermute | solution.py:412
  113.1 2.9 %collective-permute-start.12 = (f32[2,2,4,64,256]{4,3,2,1,0:T(8,128)}, f32[2,2,4,64,256]{4,3,2,1,0:T(8,128)}, u32[]{:S(2)}, u32[]{:S(2)}) collective-permute-start(f32[2,2,4,64,256]{4,3,2,1,0:T(8,128)} %pad_maximum_fusion.1), channel_id=1, source_target_pairs={{0,64},{64,0},{1,65},{65,1},{2,66},{66,2},{3,67},{67,3},{4,68},{68... | collective-permute-start | bytes 3145736 | tf_op jit(solution)/shard_map/ppermute | solution.py:524
  116.0 2.4 %collective-permute-done.15 = f32[3,2,72,4]{3,2,1,0:T(8,128)S(1)} collective-permute-done((f32[3,2,72,4]{3,2,1,0:T(8,128)S(1)}, f32[3,2,72,4]{3,2,1,0:T(8,128)S(1)}, u32[]{:S(2)}, u32[]{:S(2)}) %collective-permute-start.15) | collective-permute-done | bytes 6944 | tf_op jit(solution)/shard_map/ppermute | solution.py:411
  118.4 1.5 collective-permute-done.16
  121.4 39.0 %shard_map.129 = f32[3,2,72,384]{3,2,1,0:T(8,128)} custom-call(f32[2,72,384]{2,1,0:T(8,128)} %pad.17.rhs_ref, f32[72,384]{1,0:T(8,128)} %broadcast_in_dim.25.inside_ref, f32[72,384]{1,0:T(8,128)} %and_convert_fusion.own_ref), custom_call_target="tpu_custom_call" | custom-call | tf_op jit(solution)/shard_map/pallas_call | solution.py:230
  160.4 2.0 multiply_bitcast_fusion.1
  163.5 12.5 %shard_map.130 = f32[40,128]{1,0:T(8,128)} custom-call(f32[40,128]{1,0:T(8,128)} %select_maximum_fusion.1.x_ref), custom_call_target="tpu_custom_call" | custom-call | tf_op jit(solution)/shard_map/pallas_call | solution.py:90
  179.1 3.0 %collective-permute-start.17 = (f32[2,10,64,256]{3,2,1,0:T(8,128)S(1)}, f32[2,10,64,256]{3,2,1,0:T(8,128)}, u32[]{:S(2)}, u32[]{:S(2)}) collective-permute-start(f32[2,10,64,256]{3,2,1,0:T(8,128)S(1)} %select_maximum_fusion), channel_id=1, source_target_pairs={{0,64},{64,0},{1,65},{65,1},{2,66},{66,2},{3,67},{67,3},{4,68},{68... | collective-permute-start | bytes 3932168 | tf_op jit(solution)/shard_map/ppermute | solution.py:546
  185.6 1.3 fusion.20
  191.1 19.4 %collective-permute-done.17 = f32[2,10,64,256]{3,2,1,0:T(8,128)} collective-permute-done((f32[2,10,64,256]{3,2,1,0:T(8,128)S(1)}, f32[2,10,64,256]{3,2,1,0:T(8,128)}, u32[]{:S(2)}, u32[]{:S(2)}) %collective-permute-start.17) | collective-permute-done | bytes 1310752 | tf_op jit(solution)/shard_map/ppermute | solution.py:546
  210.5 1.3 slice.384
  211.9 1.3 dynamic-slice_select_fusion
  (148 shorter events, 39.0 us)
Async XLA Ops:
  0.7 13.9 %copy-start.22 = (s32[2]{0:T(128)S(1)}, s32[2]{0:T(128)}, u32[]{:S(2)}) copy-start(s32[2]{0:T(128)} %param.17) | copy-start | bytes 28
  1.7 15.4 %copy-start.19 = (s32[64,256]{1,0:T(8,128)S(1)}, s32[64,256]{1,0:T(8,128)}, u32[]{:S(2)}) copy-start(s32[64,256]{1,0:T(8,128)} %param.16) | copy-start | bytes 196612
  2.8 18.9 %collective-permute-start.1 = (f32[4,2,4,1,256]{4,3,2,1,0:T(1,128)S(1)}, f32[4,2,4,1,256]{4,3,2,1,0:T(1,128)S(1)}, u32[]{:S(2)}, u32[]{:S(2)}) collective-permute-start(f32[4,2,4,1,256]{4,3,2,1,0:T(1,128)S(1)} %pad_maximum_fusion.8), channel_id=1, source_target_pairs={{0,8},{8,16},{16,24},{24,32},{32,40},{40,48},{48,56},{56,0},{1,9},... | collective-permute-start | bytes 98312 | tf_op jit(solution)/shard_map/ppermute | solution.py:359
  2.8 19.5 %collective-permute-start = (f32[4,2,4,1,256]{4,3,2,1,0:T(1,128)S(1)}, f32[4,2,4,1,256]{4,3,2,1,0:T(1,128)S(1)}, u32[]{:S(2)}, u32[]{:S(2)}) collective-permute-start(f32[4,2,4,1,256]{4,3,2,1,0:T(1,128)S(1)} %pad_maximum_fusion.7), channel_id=1, source_target_pairs={{8,0},{16,8},{24,16},{32,24},{40,32},{48,40},{56,48},{0,56},{9,1},... | collective-permute-start | bytes 98312 | tf_op jit(solution)/shard_map/ppermute | solution.py:358
  9.2 8.5 %collective-permute-start.2 = (f32[4,2,4,64,1]{3,2,4,1,0:T(4,128)S(1)}, f32[4,2,4,64,1]{3,2,4,1,0:T(4,128)S(1)}, u32[]{:S(2)}, u32[]{:S(2)}) collective-permute-start(f32[4,2,4,64,1]{3,2,4,1,0:T(4,128)S(1)} %pad_maximum_fusion.17), channel_id=1, source_target_pairs={{1,0},{2,1},{3,2},{4,3},{5,4},{6,5},{7,6},{0,7},{9,8},{10,9},{11,1... | collective-permute-start | bytes 24584 | tf_op jit(solution)/shard_map/ppermute | solution.py:360
  14.4 5.8 %collective-permute-start.3 = (f32[4,2,4,64,1]{3,2,4,1,0:T(4,128)S(1)}, f32[4,2,4,64,1]{3,2,4,1,0:T(4,128)S(1)}, u32[]{:S(2)}, u32[]{:S(2)}) collective-permute-start(f32[4,2,4,64,1]{3,2,4,1,0:T(4,128)S(1)} %pad_maximum_fusion.18), channel_id=1, source_target_pairs={{0,1},{1,2},{2,3},{3,4},{4,5},{5,6},{6,7},{7,0},{8,9},{9,10},{10,1... | collective-permute-start | bytes 24584 | tf_op jit(solution)/shard_map/ppermute | solution.py:361
  14.5 148.1 %copy-start.20 = (pred[8]{0:T(512)(128)(4,1)}, pred[8]{0:T(512)(128)(4,1)S(1)}, u32[]{:S(2)}) copy-start(pred[8]{0:T(512)(128)(4,1)S(1)} %iota_compare_fusion.4) | copy-start | bytes 28
  28.6 12.4 %copy-start.4 = (f32[2,4,64,256]{3,2,1,0:T(8,128)S(1)}, f32[2,4,64,256]{3,2,1,0:T(8,128)}, u32[]{:S(2)}) copy-start(f32[2,4,64,256]{3,2,1,0:T(8,128)} %get-tuple-element.44.salt_ref) | copy-start | bytes 1572868
  29.5 6.2 %collective-permute-start.4 = (f32[3,2,4,256]{3,2,1,0:T(4,128)S(1)}, f32[3,2,4,256]{3,2,1,0:T(4,128)S(1)}, u32[]{:S(2)}, u32[]{:S(2)}) collective-permute-start(f32[3,2,4,256]{3,2,1,0:T(4,128)S(1)} %get-tuple-element.141), channel_id=1, source_target_pairs={{0,8},{8,16},{16,24},{24,32},{32,40},{40,48},{48,56},{56,0},{1,9},... | collective-permute-start | bytes 73736 | tf_op jit(solution)/shard_map/ppermute | solution.py:411
  29.5 6.2 %collective-permute-start.5 = (f32[3,2,4,256]{3,2,1,0:T(4,128)S(1)}, f32[3,2,4,256]{3,2,1,0:T(4,128)S(1)}, u32[]{:S(2)}, u32[]{:S(2)}) collective-permute-start(f32[3,2,4,256]{3,2,1,0:T(4,128)S(1)} %get-tuple-element.142), channel_id=1, source_target_pairs={{8,0},{16,8},{24,16},{32,24},{40,32},{48,40},{56,48},{0,56},{9,1},... | collective-permute-start | bytes 73736 | tf_op jit(solution)/shard_map/ppermute | solution.py:412
  36.8 9.5 %collective-permute-start.6 = (f32[3,2,72,4]{3,2,1,0:T(8,128)S(1)}, f32[3,2,72,4]{3,2,1,0:T(8,128)S(1)}, u32[]{:S(2)}, u32[]{:S(2)}) collective-permute-start(f32[3,2,72,4]{3,2,1,0:T(8,128)S(1)} %get-tuple-element.137), channel_id=1, source_target_pairs={{0,1},{1,2},{2,3},{3,4},{4,5},{5,6},{6,7},{7,0},{8,9},{9,10},{10,1... | collective-permute-start | bytes 20744 | tf_op jit(solution)/shard_map/ppermute | solution.py:411
  36.9 9.4 %collective-permute-start.7 = (f32[3,2,72,4]{3,2,1,0:T(8,128)S(1)}, f32[3,2,72,4]{3,2,1,0:T(8,128)S(1)}, u32[]{:S(2)}, u32[]{:S(2)}) collective-permute-start(f32[3,2,72,4]{3,2,1,0:T(8,128)S(1)} %get-tuple-element.138), channel_id=1, source_target_pairs={{1,0},{2,1},{3,2},{4,3},{5,4},{6,5},{7,6},{0,7},{9,8},{10,9},{11,1... | collective-permute-start | bytes 20744 | tf_op jit(solution)/shard_map/ppermute | solution.py:412
  47.0 34.4 %copy-start.7 = (f32[64,256]{1,0:T(8,128)S(1)}, f32[64,256]{1,0:T(8,128)}, u32[]{:S(2)}) copy-start(f32[64,256]{1,0:T(8,128)} %convert_element_type.46.ocean_ref) | copy-start | bytes 196612
  47.0 34.4 %copy-start.17 = (f32[2,4,64,256]{3,2,1,0:T(8,128)S(1)}, f32[2,4,64,256]{3,2,1,0:T(8,128)}, u32[]{:S(2)}) copy-start(f32[2,4,64,256]{3,2,1,0:T(8,128)} %get-tuple-element.45) | copy-start | bytes 1572868
  47.0 34.4 %copy-start.18 = (f32[2,4,64,256]{3,2,1,0:T(8,128)S(1)}, f32[2,4,64,256]{3,2,1,0:T(8,128)}, u32[]{:S(2)}) copy-start(f32[2,4,64,256]{3,2,1,0:T(8,128)} %get-tuple-element.48) | copy-start | bytes 1572868
  82.4 7.3 %collective-permute-start.11 = (f32[4,2,4,64,1]{3,2,4,1,0:T(4,128)S(1)}, f32[4,2,4,64,1]{3,2,4,1,0:T(4,128)S(1)}, u32[]{:S(2)}, u32[]{:S(2)}) collective-permute-start(f32[4,2,4,64,1]{3,2,4,1,0:T(4,128)S(1)} %pad_maximum_fusion.20), channel_id=1, source_target_pairs={{0,1},{1,2},{2,3},{3,4},{4,5},{5,6},{6,7},{7,0},{8,9},{9,10},{10,1... | collective-permute-start | bytes 24584 | tf_op jit(solution)/shard_map/ppermute | solution.py:361
  83.7 7.4 %collective-permute-start.10 = (f32[4,2,4,64,1]{3,2,4,1,0:T(4,128)S(1)}, f32[4,2,4,64,1]{3,2,4,1,0:T(4,128)S(1)}, u32[]{:S(2)}, u32[]{:S(2)}) collective-permute-start(f32[4,2,4,64,1]{3,2,4,1,0:T(4,128)S(1)} %pad_maximum_fusion.19), channel_id=1, source_target_pairs={{1,0},{2,1},{3,2},{4,3},{5,4},{6,5},{7,6},{0,7},{9,8},{10,9},{11,1... | collective-permute-start | bytes 24584 | tf_op jit(solution)/shard_map/ppermute | solution.py:360
  86.6 5.8 %collective-permute-start.9 = (f32[4,2,4,1,256]{4,3,2,1,0:T(1,128)S(1)}, f32[4,2,4,1,256]{4,3,2,1,0:T(1,128)S(1)}, u32[]{:S(2)}, u32[]{:S(2)}) collective-permute-start(f32[4,2,4,1,256]{4,3,2,1,0:T(1,128)S(1)} %pad_maximum_fusion.10), channel_id=1, source_target_pairs={{0,8},{8,16},{16,24},{24,32},{32,40},{40,48},{48,56},{56,0},{1,9},... | collective-permute-start | bytes 98312 | tf_op jit(solution)/shard_map/ppermute | solution.py:359
  86.7 6.4 %collective-permute-start.8 = (f32[4,2,4,1,256]{4,3,2,1,0:T(1,128)S(1)}, f32[4,2,4,1,256]{4,3,2,1,0:T(1,128)S(1)}, u32[]{:S(2)}, u32[]{:S(2)}) collective-permute-start(f32[4,2,4,1,256]{4,3,2,1,0:T(1,128)S(1)} %pad_maximum_fusion.9), channel_id=1, source_target_pairs={{8,0},{16,8},{24,16},{32,24},{40,32},{48,40},{56,48},{0,56},{9,1},... | collective-permute-start | bytes 98312 | tf_op jit(solution)/shard_map/ppermute | solution.py:358
  98.7 13.4 %copy-start.5 = (f32[2,4,64,256]{3,2,1,0:T(8,128)S(1)}, f32[2,4,64,256]{3,2,1,0:T(8,128)}, u32[]{:S(2)}) copy-start(f32[2,4,64,256]{3,2,1,0:T(8,128)} %get-tuple-element.49) | copy-start | bytes 1572868
  98.7 13.4 %copy-start.6 = (f32[2,4,64,256]{3,2,1,0:T(8,128)S(1)}, f32[2,4,64,256]{3,2,1,0:T(8,128)}, u32[]{:S(2)}) copy-start(f32[2,4,64,256]{3,2,1,0:T(8,128)} %get-tuple-element.50) | copy-start | bytes 1572868
  99.5 6.9 %collective-permute-start.13 = (f32[3,2,4,256]{3,2,1,0:T(4,128)S(1)}, f32[3,2,4,256]{3,2,1,0:T(4,128)S(1)}, u32[]{:S(2)}, u32[]{:S(2)}) collective-permute-start(f32[3,2,4,256]{3,2,1,0:T(4,128)S(1)} %get-tuple-element.139), channel_id=1, source_target_pairs={{0,8},{8,16},{16,24},{24,32},{32,40},{40,48},{48,56},{56,0},{1,9},... | collective-permute-start | bytes 73736 | tf_op jit(solution)/shard_map/ppermute | solution.py:411
  99.6 6.9 %collective-permute-start.14 = (f32[3,2,4,256]{3,2,1,0:T(4,128)S(1)}, f32[3,2,4,256]{3,2,1,0:T(4,128)S(1)}, u32[]{:S(2)}, u32[]{:S(2)}) collective-permute-start(f32[3,2,4,256]{3,2,1,0:T(4,128)S(1)} %get-tuple-element.140), channel_id=1, source_target_pairs={{8,0},{16,8},{24,16},{32,24},{40,32},{48,40},{56,48},{0,56},{9,1},... | collective-permute-start | bytes 73736 | tf_op jit(solution)/shard_map/ppermute | solution.py:412
  107.5 12.3 %copy-start.11 = (f32[2,64,256]{2,1,0:T(8,128)S(1)}, f32[2,64,256]{2,1,0:T(8,128)}, u32[]{:S(2)}) copy-start(f32[2,64,256]{2,1,0:T(8,128)} %get-tuple-element.52) | copy-start | bytes 393220
  107.5 12.3 %copy-start.12 = (f32[2,64,256]{2,1,0:T(8,128)S(1)}, f32[2,64,256]{2,1,0:T(8,128)}, u32[]{:S(2)}) copy-start(f32[2,64,256]{2,1,0:T(8,128)} %get-tuple-element.53) | copy-start | bytes 393220
  107.7 10.7 %collective-permute-start.15 = (f32[3,2,72,4]{3,2,1,0:T(8,128)S(1)}, f32[3,2,72,4]{3,2,1,0:T(8,128)S(1)}, u32[]{:S(2)}, u32[]{:S(2)}) collective-permute-start(f32[3,2,72,4]{3,2,1,0:T(8,128)S(1)} %get-tuple-element.135), channel_id=1, source_target_pairs={{0,1},{1,2},{2,3},{3,4},{4,5},{5,6},{6,7},{7,0},{8,9},{9,10},{10,1... | collective-permute-start | bytes 20744 | tf_op jit(solution)/shard_map/ppermute | solution.py:411
  107.9 11.9 %collective-permute-start.16 = (f32[3,2,72,4]{3,2,1,0:T(8,128)S(1)}, f32[3,2,72,4]{3,2,1,0:T(8,128)S(1)}, u32[]{:S(2)}, u32[]{:S(2)}) collective-permute-start(f32[3,2,72,4]{3,2,1,0:T(8,128)S(1)} %get-tuple-element.136), channel_id=1, source_target_pairs={{1,0},{2,1},{3,2},{4,3},{5,4},{6,5},{7,6},{0,7},{9,8},{10,9},{11,1... | collective-permute-start | bytes 20744 | tf_op jit(solution)/shard_map/ppermute | solution.py:412
  113.1 72.4 %collective-permute-start.12 = (f32[2,2,4,64,256]{4,3,2,1,0:T(8,128)}, f32[2,2,4,64,256]{4,3,2,1,0:T(8,128)}, u32[]{:S(2)}, u32[]{:S(2)}) collective-permute-start(f32[2,2,4,64,256]{4,3,2,1,0:T(8,128)} %pad_maximum_fusion.1), channel_id=1, source_target_pairs={{0,64},{64,0},{1,65},{65,1},{2,66},{66,2},{3,67},{67,3},{4,68},{68... | collective-permute-start | bytes 3145736 | tf_op jit(solution)/shard_map/ppermute | solution.py:524
  120.6 41.8 %copy-start.8 = (f32[64,256]{1,0:T(8,128)S(1)}, f32[64,256]{1,0:T(8,128)}, u32[]{:S(2)}) copy-start(f32[64,256]{1,0:T(8,128)} %convert_element_type.46.ocean_ref) | copy-start | bytes 196612
  120.6 41.8 %copy-start.15 = (f32[2,4,64,256]{3,2,1,0:T(8,128)S(1)}, f32[2,4,64,256]{3,2,1,0:T(8,128)}, u32[]{:S(2)}) copy-start(f32[2,4,64,256]{3,2,1,0:T(8,128)} %get-tuple-element.51) | copy-start | bytes 1572868
  120.6 41.8 %copy-start.16 = (f32[2,4,64,256]{3,2,1,0:T(8,128)S(1)}, f32[2,4,64,256]{3,2,1,0:T(8,128)}, u32[]{:S(2)}) copy-start(f32[2,4,64,256]{3,2,1,0:T(8,128)} %get-tuple-element.54) | copy-start | bytes 1572868
  179.1 31.4 %collective-permute-start.17 = (f32[2,10,64,256]{3,2,1,0:T(8,128)S(1)}, f32[2,10,64,256]{3,2,1,0:T(8,128)}, u32[]{:S(2)}, u32[]{:S(2)}) collective-permute-start(f32[2,10,64,256]{3,2,1,0:T(8,128)S(1)} %select_maximum_fusion), channel_id=1, source_target_pairs={{0,64},{64,0},{1,65},{65,1},{2,66},{66,2},{3,67},{67,3},{4,68},{68... | collective-permute-start | bytes 3932168 | tf_op jit(solution)/shard_map/ppermute | solution.py:546
  (11 other events, 86.8 us)

commit v5 on v4

--- a/solution.py
+++ b/solution.py
@@ -147,7 +147,7 @@
     return phase(partial, send_x, recv_x, sx, rx, nx, mx, along_x)
 
 
-def solve_kernel(ny, nx, rhs_ref, inside_ref, own_ref, out_ref, *bufs):
+def solve_kernel(ny, nx, surf_ref, inside_ref, own_ref, out_ref, frame, hsend, hrecv, *bufs):
     mesh_id = pl.DeviceIdType.MESH
     member = lax.axis_index("member")
     my = lax.axis_index("gridy")
@@ -159,21 +159,48 @@
         pl.semaphore_signal(barrier, 1, device_id=along_y((my + d) % ny), device_id_type=mesh_id)
     for d in range(1, nx):
         pl.semaphore_signal(barrier, 1, device_id=along_x((mx + d) % nx), device_id_type=mesh_id)
+    rows, cols = surf_ref.shape[2], surf_ref.shape[3]
+    wide_rows, wide_cols = frame.shape[2], frame.shape[3]
+    band = (wide_rows - rows) // 2
+    block = (wide_cols - cols) // 2
+    frame[:, :, 0:rows, 0:cols] = surf_ref[...]
     pl.semaphore_wait(barrier, (ny - 1) + (nx - 1))
 
-    members = rhs_ref.shape[0]
-    rows, cols = rhs_ref.shape[1], rhs_ref.shape[2]
+    def halo_copies(first, moves):
+        started = []
+        for slot, (src, dst, device) in enumerate(moves, start=first):
+            copy = pltpu.make_async_remote_copy(
+                src_ref=src, dst_ref=dst, send_sem=hsend.at[slot], recv_sem=hrecv.at[slot],
+                device_id=device, device_id_type=mesh_id,
+            )
+            copy.start()
+            started.append(copy)
+        for copy in started:
+            copy.wait()
+
+    halo_copies(0, [
+        (frame.at[:, :, 0:band, 0:cols], frame.at[:, :, rows : rows + band, 0:cols], along_y((my + ny - 1) % ny)),
+        (frame.at[:, :, rows - band : rows, 0:cols], frame.at[:, :, rows + band : wide_rows, 0:cols],
+         along_y((my + 1) % ny)),
+    ])
+    halo_copies(2, [
+        (frame.at[:, :, :, 0:block], frame.at[:, :, :, cols : cols + block], along_x((mx + nx - 1) % nx)),
+        (frame.at[:, :, :, cols - block : cols], frame.at[:, :, :, cols + block : wide_cols],
+         along_x((mx + 1) % nx)),
+    ])
+
+    members = surf_ref.shape[1]
     inside = inside_ref[...]
     own = own_ref[...] > 0.5
 
     def east(f):
-        return pltpu.roll(f, cols - 1, 1)
+        return pltpu.roll(f, wide_cols - 1, 1)
 
     def west(f):
         return pltpu.roll(f, 1, 1)
 
     def north(f):
-        return pltpu.roll(f, rows - 1, 0)
+        return pltpu.roll(f, wide_rows - 1, 0)
 
     def south(f):
         return pltpu.roll(f, 1, 0)
@@ -184,8 +211,15 @@
     def total(f):
         return jnp.sum(jnp.where(own, f, 0.0), axis=(0, 1), keepdims=True)
 
+    residual = []
+    for m in range(members):
+        trans_u = frame[0, m] * inside
+        trans_v = frame[1, m] * inside
+        level = frame[2, m] * inside
+        residual.append(
+            (level - DIV_K * 0.5 * (east(trans_u) - west(trans_u) + (north(trans_v) - south(trans_v)))) * inside
+        )
     lane = lax.broadcasted_iota(jnp.int32, (8, 128), 1)
-    residual = [rhs_ref[m] for m in range(members)]
     direction = [None] * members
     image_dir = [None] * members
     solution = [None] * members
@@ -218,21 +252,24 @@
             alpha_prev[m] = alpha
     for m in range(members):
         x = solution[m]
-        out_ref[0, m] = x
-        out_ref[1, m] = east(x) - west(x)
-        out_ref[2, m] = north(x) - south(x)
-
-
-def surface_kernel_solve(rhs, inside, own):
+        out_ref[0, m] = x[0:rows, 0:cols]
+        out_ref[1, m] = (east(x) - west(x))[0:rows, 0:cols]
+        out_ref[2, m] = (north(x) - south(x))[0:rows, 0:cols]
+
+
+def surface_kernel_solve(surf, inside, own):
     ny = lax.axis_size("gridy")
     nx = lax.axis_size("gridx")
-    shape = rhs.shape
+    fields, members, rows, cols = surf.shape
     return pl.pallas_call(
         functools.partial(solve_kernel, ny, nx),
-        out_shape=jax.ShapeDtypeStruct((3,) + shape, jnp.float32),
+        out_shape=jax.ShapeDtypeStruct((3, members, rows, cols), jnp.float32),
         in_specs=[pl.BlockSpec(memory_space=pltpu.VMEM)] * 3,
         out_specs=pl.BlockSpec(memory_space=pltpu.VMEM),
         scratch_shapes=[
+            pltpu.VMEM((fields, members) + inside.shape, jnp.float32),
+            pltpu.SemaphoreType.DMA((4,)),
+            pltpu.SemaphoreType.DMA((4,)),
             pltpu.VMEM((ITERS, 8, 128), jnp.float32),
             pltpu.VMEM((ITERS, ny, 8, 128), jnp.float32),
             pltpu.VMEM((ITERS, 8, 128), jnp.float32),
@@ -243,7 +280,7 @@
             pltpu.SemaphoreType.DMA((ITERS, nx)),
         ],
         compiler_params=pltpu.CompilerParams(collective_id=1, has_side_effects=True),
-    )(rhs, inside, own)
+    )(surf, inside, own)
 
 
 def volume_kernel(temp_ref, salt_ref, uvel_ref, vvel_ref, ocean_ref, cor_ref, n_ref, s_ref, e_ref, w_ref,
@@ -486,38 +523,25 @@
     latitude = (tile_row * rows + jnp.arange(rows, dtype=jnp.int32)).astype(jnp.float32) + 0.5
     coriolis = (CORI_K * (2.0 * latitude / total_rows - 1.0))[:, None]
     cor_tile = jnp.broadcast_to(coriolis, (rows, cols))
-    wide_rows = tile_row * rows - (ITERS + 1) + jnp.arange(rows + 2 * (ITERS + 1), dtype=jnp.int32)
-    inside = ((wide_rows >= 0) & (wide_rows < total_rows)).astype(jnp.float32)[:, None]
-    halo = ITERS + 1
-    lanes = 128 * ((cols + 2 * halo + 127) // 128)
-    wide_inside = jnp.broadcast_to(inside, (rows + 2 * halo, lanes))
-    row_at = lax.broadcasted_iota(jnp.int32, (rows + 2 * halo, lanes), 0)
-    col_at = lax.broadcasted_iota(jnp.int32, (rows + 2 * halo, lanes), 1)
-    own_mask = (
-        (row_at >= halo) & (row_at < halo + rows) & (col_at >= halo) & (col_at < halo + cols)
-    ).astype(jnp.float32)
+    band = 8
+    block = 128
+    frame_rows = rows + 2 * band
+    frame_cols = cols + 2 * block
+    row_at = lax.broadcasted_iota(jnp.int32, (frame_rows, frame_cols), 0)
+    col_at = lax.broadcasted_iota(jnp.int32, (frame_rows, frame_cols), 1)
+    global_row = tile_row * rows + jnp.where(row_at < rows + band, row_at, row_at - frame_rows)
+    wide_inside = ((global_row >= 0) & (global_row < total_rows)).astype(jnp.float32)
+    own_mask = ((row_at < rows) & (col_at < cols)).astype(jnp.float32)
     for count in range(STEPS):
         fields = (temp, salt, uvel, vvel)
         rims = exchange_fields(fields, south_keep, north_keep)
         temp_next, salt_next, ustar, vstar, trans_u, trans_v = volume_step(
             temp, salt, uvel, vvel, ocean, cor_tile, rims
         )
-        halo = ITERS + 1
-        surface = padded_2(
-            jnp.stack((trans_u, trans_v, eta)),
-            (("gridy", 2), ("gridx", 3)),
-            halo,
-        ) * inside
-        centre, east_t, west_t, north_t, south_t = around(surface)
-        rhs = (centre[2] - DIV_K * 0.5 * (east_t[0] - west_t[0] + (north_t[1] - south_t[1]))) * rows_at(
-            inside, halo, halo - 1
-        )
-        lanes = 128 * ((cols + 2 * halo + 127) // 128)
-        rhs_tile = jnp.pad(rhs, ((0, 0), (1, 1), (1, lanes - cols - 2 * halo + 1)))
-        solved = surface_kernel_solve(rhs_tile, wide_inside, own_mask)
-        eta = solved[0, :, halo : halo + rows, halo : halo + cols]
-        east_west = solved[1, :, halo : halo + rows, halo : halo + cols]
-        north_south = solved[2, :, halo : halo + rows, halo : halo + cols]
+        solved = surface_kernel_solve(jnp.stack((trans_u, trans_v, eta)), wide_inside, own_mask)
+        eta = solved[0]
+        east_west = solved[1]
+        north_south = solved[2]
         uvel = ocean * (ustar - GRAV_K * 0.5 * east_west[:, None])
         vvel = ocean * (vstar - GRAV_K * 0.5 * north_south[:, None])
         if count == STEPS - 1:

time: 219 us -> 220 us (level)
  Pallas kernels: 93 us -> 126 us
  starting transfers between devices: 35.7 us -> 20.2 us
  waiting for transfers between devices: 29.3 us -> 18.7 us
  local copies, waits for them, and re-layouts: 25.6 us -> 21.4 us
    pallas_call x2, Pallas kernels: 70.5 us -> 89.8 us  [surface_kernel_solve(): pl.pallas_call(functools.partial(solve_kernel, ny, nx), out_shape=jax.Sha...]
    ppermute x8 -> x0, starting transfers between devices: 14.5 us -> none  [the longest x4 14.1 us: padded_2(): lax.ppermute(lax.slice_in_dim(block, 0, width, axis=dim), axis, backward)]
    pallas_call x1, Pallas kernels: 12.5 us -> 26.5 us  [grid_sum(): pl.pallas_call(functools.partial(gather_sum_kernel, ny, nx), out_shape=ja...]
    ppermute x8 -> x0, waiting for transfers between devices: 8.75 us -> none  [the longest x4 7.28 us: padded_2(): lax.ppermute(lax.slice_in_dim(block, size - width, size, axis=dim), axis,...]
    another operation x0 -> x2, other arithmetic: none -> 3.66 us  [shards(): jnp.stack((trans_u, trans_v, eta))]
  transfers between devices with their start and end apart: 18 -> 10, of which waited for: 5 -> 1; matrix products, arithmetic and copies ran while one was open for 16% -> 12% of each run, Pallas kernels for 24% -> 12%
where the time goes in v5:
time: 220 us; the launch traced here: 219 us
  Pallas kernels  126 us (57%)
  other arithmetic  26.6 us (12%)
  local copies, waits for them, and re-layouts  21.4 us (10%)
  starting transfers between devices  20.2 us (9%)
  waiting for transfers between devices  18.7 us (8%)
  between operations  5.75 us (3%)
    pallas_call x2, Pallas kernels, surface_kernel_solve(): pl.pallas_call(functools.partial(solve_kernel, ny, nx), out_shape=jax.Sha...  89.8 us
    pallas_call x1, Pallas kernels, grid_sum(): pl.pallas_call(functools.partial(gather_sum_kernel, ny, nx), out_shape=ja...  26.5 us
    ppermute x1, waiting for transfers between devices, shards(): flows_other = lax.ppermute(flows, 'member', swap)  18.6 us
    pallas_call x2, Pallas kernels, volume_step(): pl.pallas_call(volume_kernel, grid=(members,), in_specs=[field] * 4 + [pl...  9.92 us
    ppermute x2, starting transfers between devices, exchange_fields(): lax.ppermute(jnp.stack([f[..., :, :1] for f in fields]), 'gridx', bwd_x)  7.92 us
    ppermute x2, starting transfers between devices, exchange_fields(): lax.ppermute(jnp.stack([f[..., :1, :] for f in fields]), 'gridy', bwd_y)  5.89 us
    slice x8, local copies, waits for them, and re-layouts, exchange_fields(): f[..., :, -1:]  4.77 us
    select_n x3, other arithmetic, pick(): chosen.append(jnp.where(here[place], from_here, from_other))  4.44 us
  transfers between devices with their start and end apart: 10, of which 1 were waited for; matrix products, arithmetic and copies ran while one was open for 12% of the time, Pallas kernels for 12%

profile of v5, /device:TPU:0, one launch (start us, length us, event | category | flops | bytes accessed | tf_op | source)
XLA Modules:
  0.0 218.7 jit_solution(8087816659770711916)
XLA Ops:
  0.7 1.0 slice_bitcast_fusion.11
  2.8 2.9 %collective-permute-start = (f32[4,2,4,1,256]{4,3,2,1,0:T(1,128)S(1)}, f32[4,2,4,1,256]{4,3,2,1,0:T(1,128)S(1)}, u32[]{:S(2)}, u32[]{:S(2)}) collective-permute-start(f32[4,2,4,1,256]{4,3,2,1,0:T(1,128)S(1)} %pad_maximum_fusion.7), channel_id=1, source_target_pairs={{8,0},{16,8},{24,16},{32,24},{40,32},{48,40},{56,48},{0,56},{9,1},... | collective-permute-start | bytes 98312 | tf_op jit(solution)/shard_map/ppermute | solution.py:395
  5.8 1.4 slice_reduce_fusion.10
  7.1 1.4 slice_reduce_fusion.9
  9.2 5.2 %collective-permute-start.2 = (f32[4,2,4,64,1]{3,2,4,1,0:T(4,128)S(1)}, f32[4,2,4,64,1]{3,2,4,1,0:T(4,128)S(1)}, u32[]{:S(2)}, u32[]{:S(2)}) collective-permute-start(f32[4,2,4,64,1]{3,2,4,1,0:T(4,128)S(1)} %pad_maximum_fusion.11), channel_id=1, source_target_pairs={{1,0},{2,1},{3,2},{4,3},{5,4},{6,5},{7,6},{0,7},{9,8},{10,9},{11,1... | collective-permute-start | bytes 24584 | tf_op jit(solution)/shard_map/ppermute | solution.py:397
  21.7 1.4 copy.225.e_ref
  23.1 1.4 copy.226.w_ref
  26.5 5.0 %shard_map.126 = (f32[2,4,64,256]{3,2,1,0:T(8,128)}, f32[2,4,64,256]{3,2,1,0:T(8,128)}, f32[2,4,64,256]{3,2,1,0:T(8,128)}, f32[2,4,64,256]{3,2,1,0:T(8,128)}, f3...) custom-call(f32[2,4,64,256]{3,2,1,0:T(8,128)} %temp_ref.1, f32[2,4,64,256]{3,2,1,0:T(8,128)} %salt_ref.1, ...), custom_call_target="tpu_custom_call" | custom-call | tf_op jit(solution)/shard_map/pallas_call | solution.py:364
  31.5 1.8 pad_maximum_fusion.4.surf_ref
  33.3 46.4 %shard_map.127 = f32[3,2,64,256]{3,2,1,0:T(8,128)} custom-call(f32[3,2,64,256]{3,2,1,0:T(8,128)} %pad_maximum_fusion.4.surf_ref, f32[80,512]{1,0:T(8,128)} %get-tuple-element.150.inside_ref, f32[80,512]{1,0:T(8,128)} %get-tuple-element.151.own_ref), custom_call_target="tpu_custom_call" | custom-call | tf_op jit(solution)/shard_map/pallas_call | solution.py:264
  79.7 1.1 fusion.15
  82.8 1.5 collective-permute-start.7
  84.3 2.7 %collective-permute-start.6 = (f32[4,2,4,64,1]{3,2,4,1,0:T(4,128)S(1)}, f32[4,2,4,64,1]{3,2,4,1,0:T(4,128)S(1)}, u32[]{:S(2)}, u32[]{:S(2)}) collective-permute-start(f32[4,2,4,64,1]{3,2,4,1,0:T(4,128)S(1)} %pad_maximum_fusion.13), channel_id=1, source_target_pairs={{1,0},{2,1},{3,2},{4,3},{5,4},{6,5},{7,6},{0,7},{9,8},{10,9},{11,1... | collective-permute-start | bytes 24584 | tf_op jit(solution)/shard_map/ppermute | solution.py:397
  87.1 2.9 %collective-permute-start.4 = (f32[4,2,4,1,256]{4,3,2,1,0:T(1,128)S(1)}, f32[4,2,4,1,256]{4,3,2,1,0:T(1,128)S(1)}, u32[]{:S(2)}, u32[]{:S(2)}) collective-permute-start(f32[4,2,4,1,256]{4,3,2,1,0:T(1,128)S(1)} %pad_maximum_fusion.9), channel_id=1, source_target_pairs={{8,0},{16,8},{24,16},{32,24},{40,32},{48,40},{56,48},{0,56},{9,1},... | collective-permute-start | bytes 98312 | tf_op jit(solution)/shard_map/ppermute | solution.py:395
  90.1 1.4 copy.240.w_ref
  91.5 1.4 copy.239.e_ref
  94.2 5.0 %shard_map.128 = (f32[2,4,64,256]{3,2,1,0:T(8,128)}, f32[2,4,64,256]{3,2,1,0:T(8,128)}, f32[2,4,64,256]{3,2,1,0:T(8,128)}, f32[2,4,64,256]{3,2,1,0:T(8,128)}, f3...) custom-call(f32[2,4,64,256]{3,2,1,0:T(8,128)} %get-tuple-element.43.temp_ref, f32[2,4,64,256]{3,2,1,0:T(8,128)} %get-tuple-element.44.salt_ref, ...), custom_call_target="tpu_custom_call" | custom-call | tf_op jit(solution)/shard_map/pallas_call | solution.py:364
  99.2 1.8 pad_maximum_fusion.5.surf_ref
  101.0 43.4 %shard_map.129 = f32[3,2,64,256]{3,2,1,0:T(8,128)} custom-call(f32[3,2,64,256]{3,2,1,0:T(8,128)} %pad_maximum_fusion.5.surf_ref, f32[80,512]{1,0:T(8,128)} %get-tuple-element.150.inside_ref, f32[80,512]{1,0:T(8,128)} %get-tuple-element.151.own_ref), custom_call_target="tpu_custom_call" | custom-call | tf_op jit(solution)/shard_map/pallas_call | solution.py:264
  144.4 1.1 multiply_bitcast_fusion.1
  146.7 1.1 pad_maximum_fusion.1
  147.8 2.9 %collective-permute-start.8 = (f32[2,2,4,64,256]{4,3,2,1,0:T(8,128)}, f32[2,2,4,64,256]{4,3,2,1,0:T(8,128)}, u32[]{:S(2)}, u32[]{:S(2)}) collective-permute-start(f32[2,2,4,64,256]{4,3,2,1,0:T(8,128)} %pad_maximum_fusion.1), channel_id=1, source_target_pairs={{0,64},{64,0},{1,65},{65,1},{2,66},{66,2},{3,67},{67,3},{4,68},{68... | collective-permute-start | bytes 3145736 | tf_op jit(solution)/shard_map/ppermute | solution.py:548
  151.5 26.5 %shard_map.130 = f32[40,128]{1,0:T(8,128)} custom-call(f32[40,128]{1,0:T(8,128)} %select_maximum_fusion.1.x_ref), custom_call_target="tpu_custom_call" | custom-call | tf_op jit(solution)/shard_map/pallas_call | solution.py:90
  177.9 1.3 fusion.10
  180.7 1.9 collective-permute-start.9
  182.6 1.3 pad_clamp_fusion
  186.1 1.3 fusion.14
  187.4 1.4 bitcast_select_fusion.1
  188.8 1.4 bitcast_select_fusion.3
  192.0 18.6 %collective-permute-done.9 = f32[2,10,64,256]{3,2,1,0:T(8,128)} collective-permute-done((f32[2,10,64,256]{3,2,1,0:T(8,128)S(1)}, f32[2,10,64,256]{3,2,1,0:T(8,128)}, u32[]{:S(2)}, u32[]{:S(2)}) %collective-permute-start.9) | collective-permute-done | bytes 1310752 | tf_op jit(solution)/shard_map/ppermute | solution.py:570
  210.6 1.3 slice.272
  212.0 1.6 dynamic-slice_select_fusion
  (113 shorter events, 22.1 us)
Async XLA Ops:
  0.6 8.2 %copy-start.2 = (f32[2,4,64,256]{3,2,1,0:T(8,128)S(1)}, f32[2,4,64,256]{3,2,1,0:T(8,128)}, u32[]{:S(2)}) copy-start(f32[2,4,64,256]{3,2,1,0:T(8,128)} %temp_ref.1) | copy-start | bytes 1572868
  0.6 7.9 %copy-start.3 = (f32[2,4,64,256]{3,2,1,0:T(8,128)S(1)}, f32[2,4,64,256]{3,2,1,0:T(8,128)}, u32[]{:S(2)}) copy-start(f32[2,4,64,256]{3,2,1,0:T(8,128)} %vvel_ref.1) | copy-start | bytes 1572868
  0.7 13.9 %copy-start.18 = (s32[2]{0:T(128)S(1)}, s32[2]{0:T(128)}, u32[]{:S(2)}) copy-start(s32[2]{0:T(128)} %param.17) | copy-start | bytes 28
  2.7 21.8 %collective-permute-start.1 = (f32[4,2,4,1,256]{4,3,2,1,0:T(1,128)S(1)}, f32[4,2,4,1,256]{4,3,2,1,0:T(1,128)S(1)}, u32[]{:S(2)}, u32[]{:S(2)}) collective-permute-start(f32[4,2,4,1,256]{4,3,2,1,0:T(1,128)S(1)} %pad_maximum_fusion.8), channel_id=1, source_target_pairs={{0,8},{8,16},{16,24},{24,32},{32,40},{40,48},{48,56},{56,0},{1,9},... | collective-permute-start | bytes 98312 | tf_op jit(solution)/shard_map/ppermute | solution.py:396
  2.8 16.9 %copy-start.15 = (s32[64,256]{1,0:T(8,128)S(1)}, s32[64,256]{1,0:T(8,128)}, u32[]{:S(2)}) copy-start(s32[64,256]{1,0:T(8,128)} %param.16) | copy-start | bytes 196612
  2.8 22.4 %collective-permute-start = (f32[4,2,4,1,256]{4,3,2,1,0:T(1,128)S(1)}, f32[4,2,4,1,256]{4,3,2,1,0:T(1,128)S(1)}, u32[]{:S(2)}, u32[]{:S(2)}) collective-permute-start(f32[4,2,4,1,256]{4,3,2,1,0:T(1,128)S(1)} %pad_maximum_fusion.7), channel_id=1, source_target_pairs={{8,0},{16,8},{24,16},{32,24},{40,32},{48,40},{56,48},{0,56},{9,1},... | collective-permute-start | bytes 98312 | tf_op jit(solution)/shard_map/ppermute | solution.py:395
  9.2 12.5 %collective-permute-start.2 = (f32[4,2,4,64,1]{3,2,4,1,0:T(4,128)S(1)}, f32[4,2,4,64,1]{3,2,4,1,0:T(4,128)S(1)}, u32[]{:S(2)}, u32[]{:S(2)}) collective-permute-start(f32[4,2,4,64,1]{3,2,4,1,0:T(4,128)S(1)} %pad_maximum_fusion.11), channel_id=1, source_target_pairs={{1,0},{2,1},{3,2},{4,3},{5,4},{6,5},{7,6},{0,7},{9,8},{10,9},{11,1... | collective-permute-start | bytes 24584 | tf_op jit(solution)/shard_map/ppermute | solution.py:397
  14.4 8.7 %collective-permute-start.3 = (f32[4,2,4,64,1]{3,2,4,1,0:T(4,128)S(1)}, f32[4,2,4,64,1]{3,2,4,1,0:T(4,128)S(1)}, u32[]{:S(2)}, u32[]{:S(2)}) collective-permute-start(f32[4,2,4,64,1]{3,2,4,1,0:T(4,128)S(1)} %pad_maximum_fusion.12), channel_id=1, source_target_pairs={{0,1},{1,2},{2,3},{3,4},{4,5},{5,6},{6,7},{7,0},{8,9},{9,10},{10,1... | collective-permute-start | bytes 24584 | tf_op jit(solution)/shard_map/ppermute | solution.py:398
  14.5 131.2 %copy-start.16 = (pred[8]{0:T(512)(128)(4,1)}, pred[8]{0:T(512)(128)(4,1)S(1)}, u32[]{:S(2)}) copy-start(pred[8]{0:T(512)(128)(4,1)S(1)} %iota_compare_fusion.4) | copy-start | bytes 28
  26.5 5.0 %copy-start.14 = (f32[2,64,256]{2,1,0:T(8,128)S(1)}, f32[2,64,256]{2,1,0:T(8,128)}, u32[]{:S(2)}) copy-start(f32[2,64,256]{2,1,0:T(8,128)} %param.15) | copy-start | bytes 393220
  31.5 49.3 %copy-start.8 = (f32[64,256]{1,0:T(8,128)S(1)}, f32[64,256]{1,0:T(8,128)}, u32[]{:S(2)}) copy-start(f32[64,256]{1,0:T(8,128)} %convert_element_type.35.ocean_ref) | copy-start | bytes 196612
  31.5 49.3 %copy-start.12 = (f32[2,4,64,256]{3,2,1,0:T(8,128)S(1)}, f32[2,4,64,256]{3,2,1,0:T(8,128)}, u32[]{:S(2)}) copy-start(f32[2,4,64,256]{3,2,1,0:T(8,128)} %get-tuple-element.45) | copy-start | bytes 1572868
  31.5 49.3 %copy-start.13 = (f32[2,4,64,256]{3,2,1,0:T(8,128)S(1)}, f32[2,4,64,256]{3,2,1,0:T(8,128)}, u32[]{:S(2)}) copy-start(f32[2,4,64,256]{3,2,1,0:T(8,128)} %get-tuple-element.48) | copy-start | bytes 1572868
  80.8 1.1 copy-start.4
  80.9 10.6 %copy-start = (f32[2,4,64,256]{3,2,1,0:T(8,128)}, f32[2,4,64,256]{3,2,1,0:T(8,128)S(1)}, u32[]{:S(2)}) copy-start(f32[2,4,64,256]{3,2,1,0:T(8,128)S(1)} %get-tuple-element.136.vvel_ref) | copy-start | bytes 1572868
  81.0 10.6 %copy-start.1 = (f32[2,4,64,256]{3,2,1,0:T(8,128)}, f32[2,4,64,256]{3,2,1,0:T(8,128)S(1)}, u32[]{:S(2)}) copy-start(f32[2,4,64,256]{3,2,1,0:T(8,128)S(1)} %get-tuple-element.137.uvel_ref) | copy-start | bytes 1572868
  81.0 1.5 copy-start.5
  82.8 7.3 %collective-permute-start.7 = (f32[4,2,4,64,1]{3,2,4,1,0:T(4,128)S(1)}, f32[4,2,4,64,1]{3,2,4,1,0:T(4,128)S(1)}, u32[]{:S(2)}, u32[]{:S(2)}) collective-permute-start(f32[4,2,4,64,1]{3,2,4,1,0:T(4,128)S(1)} %pad_maximum_fusion.14), channel_id=1, source_target_pairs={{0,1},{1,2},{2,3},{3,4},{4,5},{5,6},{6,7},{7,0},{8,9},{9,10},{10,1... | collective-permute-start | bytes 24584 | tf_op jit(solution)/shard_map/ppermute | solution.py:398
  84.3 7.2 %collective-permute-start.6 = (f32[4,2,4,64,1]{3,2,4,1,0:T(4,128)S(1)}, f32[4,2,4,64,1]{3,2,4,1,0:T(4,128)S(1)}, u32[]{:S(2)}, u32[]{:S(2)}) collective-permute-start(f32[4,2,4,64,1]{3,2,4,1,0:T(4,128)S(1)} %pad_maximum_fusion.13), channel_id=1, source_target_pairs={{1,0},{2,1},{3,2},{4,3},{5,4},{6,5},{7,6},{0,7},{9,8},{10,9},{11,1... | collective-permute-start | bytes 24584 | tf_op jit(solution)/shard_map/ppermute | solution.py:397
  87.0 5.9 %collective-permute-start.5 = (f32[4,2,4,1,256]{4,3,2,1,0:T(1,128)S(1)}, f32[4,2,4,1,256]{4,3,2,1,0:T(1,128)S(1)}, u32[]{:S(2)}, u32[]{:S(2)}) collective-permute-start(f32[4,2,4,1,256]{4,3,2,1,0:T(1,128)S(1)} %pad_maximum_fusion.10), channel_id=1, source_target_pairs={{0,8},{8,16},{16,24},{24,32},{32,40},{40,48},{48,56},{56,0},{1,9},... | collective-permute-start | bytes 98312 | tf_op jit(solution)/shard_map/ppermute | solution.py:396
  87.1 6.4 %collective-permute-start.4 = (f32[4,2,4,1,256]{4,3,2,1,0:T(1,128)S(1)}, f32[4,2,4,1,256]{4,3,2,1,0:T(1,128)S(1)}, u32[]{:S(2)}, u32[]{:S(2)}) collective-permute-start(f32[4,2,4,1,256]{4,3,2,1,0:T(1,128)S(1)} %pad_maximum_fusion.9), channel_id=1, source_target_pairs={{8,0},{16,8},{24,16},{32,24},{40,32},{48,40},{56,48},{0,56},{9,1},... | collective-permute-start | bytes 98312 | tf_op jit(solution)/shard_map/ppermute | solution.py:395
  99.1 46.4 %copy-start.9 = (f32[64,256]{1,0:T(8,128)S(1)}, f32[64,256]{1,0:T(8,128)}, u32[]{:S(2)}) copy-start(f32[64,256]{1,0:T(8,128)} %convert_element_type.35.ocean_ref) | copy-start | bytes 196612
  99.2 46.4 %copy-start.10 = (f32[2,4,64,256]{3,2,1,0:T(8,128)S(1)}, f32[2,4,64,256]{3,2,1,0:T(8,128)}, u32[]{:S(2)}) copy-start(f32[2,4,64,256]{3,2,1,0:T(8,128)} %get-tuple-element.51) | copy-start | bytes 1572868
  99.2 46.4 %copy-start.11 = (f32[2,4,64,256]{3,2,1,0:T(8,128)S(1)}, f32[2,4,64,256]{3,2,1,0:T(8,128)}, u32[]{:S(2)}) copy-start(f32[2,4,64,256]{3,2,1,0:T(8,128)} %get-tuple-element.54) | copy-start | bytes 1572868
  145.5 1.0 copy-start.6
  145.5 1.2 copy-start.7
  147.8 38.3 %collective-permute-start.8 = (f32[2,2,4,64,256]{4,3,2,1,0:T(8,128)}, f32[2,2,4,64,256]{4,3,2,1,0:T(8,128)}, u32[]{:S(2)}, u32[]{:S(2)}) collective-permute-start(f32[2,2,4,64,256]{4,3,2,1,0:T(8,128)} %pad_maximum_fusion.1), channel_id=1, source_target_pairs={{0,64},{64,0},{1,65},{65,1},{2,66},{66,2},{3,67},{67,3},{4,68},{68... | collective-permute-start | bytes 3145736 | tf_op jit(solution)/shard_map/ppermute | solution.py:548
  177.9 5.9 %slice-start = ((f32[40,128]{1,0:T(8,128)}), f32[32,128]{1,0:T(8,128)S(1)}, s32[]{:S(2)}) async-start(f32[40,128]{1,0:T(8,128)} %shard_map.130), calls=%async_computation | async-start | bytes 32768 | tf_op jit(solution)/shard_map/slice | solution.py:562
  180.7 30.0 %collective-permute-start.9 = (f32[2,10,64,256]{3,2,1,0:T(8,128)S(1)}, f32[2,10,64,256]{3,2,1,0:T(8,128)}, u32[]{:S(2)}, u32[]{:S(2)}) collective-permute-start(f32[2,10,64,256]{3,2,1,0:T(8,128)S(1)} %select_maximum_fusion), channel_id=1, source_target_pairs={{0,64},{64,0},{1,65},{65,1},{2,66},{66,2},{3,67},{67,3},{4,68},{68... | collective-permute-start | bytes 3932168 | tf_op jit(solution)/shard_map/ppermute | solution.py:570
  214.2 1.9 copy-start.17
  214.2 3.9 %copy-start.19 = (s32[2]{0:T(128)S(1)}, s32[2]{0:T(128)}, u32[]{:S(2)}) copy-start(s32[2]{0:T(128)} %param.17) | copy-start | bytes 28

commit v6 on v5

--- a/solution.py
+++ b/solution.py
@@ -159,12 +159,17 @@
         pl.semaphore_signal(barrier, 1, device_id=along_y((my + d) % ny), device_id_type=mesh_id)
     for d in range(1, nx):
         pl.semaphore_signal(barrier, 1, device_id=along_x((mx + d) % nx), device_id_type=mesh_id)
+    for dy in (1, ny - 1):
+        for dx in (1, nx - 1):
+            pl.semaphore_signal(
+                barrier, 1, device_id=(member, (my + dy) % ny, (mx + dx) % nx), device_id_type=mesh_id
+            )
     rows, cols = surf_ref.shape[2], surf_ref.shape[3]
     wide_rows, wide_cols = frame.shape[2], frame.shape[3]
     band = (wide_rows - rows) // 2
     block = (wide_cols - cols) // 2
     frame[:, :, 0:rows, 0:cols] = surf_ref[...]
-    pl.semaphore_wait(barrier, (ny - 1) + (nx - 1))
+    pl.semaphore_wait(barrier, (ny - 1) + (nx - 1) + 4)
 
     def halo_copies(first, moves):
         started = []
@@ -178,15 +183,27 @@
         for copy in started:
             copy.wait()
 
+    up, down = (my + 1) % ny, (my + ny - 1) % ny
+    right, left = (mx + 1) % nx, (mx + nx - 1) % nx
+    top_rows = slice(0, band)
+    low_rows = slice(rows - band, rows)
+    own_rows = slice(0, rows)
+    west_part = slice(0, block)
+    east_part = slice(cols - block, cols)
+    own_cols = slice(0, cols)
+    north_halo = slice(rows, rows + band)
+    south_halo = slice(rows + band, wide_rows)
+    east_halo = slice(cols, cols + block)
+    west_halo = slice(cols + block, wide_cols)
     halo_copies(0, [
-        (frame.at[:, :, 0:band, 0:cols], frame.at[:, :, rows : rows + band, 0:cols], along_y((my + ny - 1) % ny)),
-        (frame.at[:, :, rows - band : rows, 0:cols], frame.at[:, :, rows + band : wide_rows, 0:cols],
-         along_y((my + 1) % ny)),
-    ])
-    halo_copies(2, [
-        (frame.at[:, :, :, 0:block], frame.at[:, :, :, cols : cols + block], along_x((mx + nx - 1) % nx)),
-        (frame.at[:, :, :, cols - block : cols], frame.at[:, :, :, cols + block : wide_cols],
-         along_x((mx + 1) % nx)),
+        (frame.at[:, :, top_rows, own_cols], frame.at[:, :, north_halo, own_cols], (member, down, mx)),
+        (frame.at[:, :, low_rows, own_cols], frame.at[:, :, south_halo, own_cols], (member, up, mx)),
+        (frame.at[:, :, own_rows, west_part], frame.at[:, :, own_rows, east_halo], (member, my, left)),
+        (frame.at[:, :, own_rows, east_part], frame.at[:, :, own_rows, west_halo], (member, my, right)),
+        (frame.at[:, :, top_rows, west_part], frame.at[:, :, north_halo, east_halo], (member, down, left)),
+        (frame.at[:, :, top_rows, east_part], frame.at[:, :, north_halo, west_halo], (member, down, right)),
+        (frame.at[:, :, low_rows, west_part], frame.at[:, :, south_halo, east_halo], (member, up, left)),
+        (frame.at[:, :, low_rows, east_part], frame.at[:, :, south_halo, west_halo], (member, up, right)),
     ])
 
     members = surf_ref.shape[1]
@@ -268,8 +285,8 @@
         out_specs=pl.BlockSpec(memory_space=pltpu.VMEM),
         scratch_shapes=[
             pltpu.VMEM((fields, members) + inside.shape, jnp.float32),
-            pltpu.SemaphoreType.DMA((4,)),
-            pltpu.SemaphoreType.DMA((4,)),
+            pltpu.SemaphoreType.DMA((8,)),
+            pltpu.SemaphoreType.DMA((8,)),
             pltpu.VMEM((ITERS, 8, 128), jnp.float32),
             pltpu.VMEM((ITERS, ny, 8, 128), jnp.float32),
             pltpu.VMEM((ITERS, 8, 128), jnp.float32),

time: 220 us -> 216 us (0.982)
  Pallas kernels: 126 us -> 122 us
    pallas_call x2, Pallas kernels: 89.8 us -> 86.8 us  [surface_kernel_solve(): pl.pallas_call(functools.partial(solve_kernel, ny, nx), out_shape=jax.Sha...]
where the time goes in v6:
time: 216 us; the launch traced here: 215 us
  Pallas kernels  122 us (56%)
  other arithmetic  26.6 us (12%)
  local copies, waits for them, and re-layouts  21.4 us (10%)
  starting transfers between devices  20.2 us (9%)
  waiting for transfers between devices  18.7 us (9%)
  between operations  5.75 us (3%)
    pallas_call x2, Pallas kernels, surface_kernel_solve(): pl.pallas_call(functools.partial(solve_kernel, ny, nx), out_shape=jax.Sha...  86.8 us
    pallas_call x1, Pallas kernels, grid_sum(): pl.pallas_call(functools.partial(gather_sum_kernel, ny, nx), out_shape=ja...  25.7 us
    ppermute x1, waiting for transfers between devices, shards(): flows_other = lax.ppermute(flows, 'member', swap)  18.7 us
    pallas_call x2, Pallas kernels, volume_step(): pl.pallas_call(volume_kernel, grid=(members,), in_specs=[field] * 4 + [pl...  9.92 us
    ppermute x2, starting transfers between devices, exchange_fields(): lax.ppermute(jnp.stack([f[..., :, :1] for f in fields]), 'gridx', bwd_x)  8.68 us
    ppermute x2, starting transfers between devices, exchange_fields(): lax.ppermute(jnp.stack([f[..., :1, :] for f in fields]), 'gridy', bwd_y)  5.89 us
    slice x8, local copies, waits for them, and re-layouts, exchange_fields(): f[..., :, -1:]  4.77 us
    select_n x3, other arithmetic, pick(): chosen.append(jnp.where(here[place], from_here, from_other))  4.44 us
  transfers between devices with their start and end apart: 10, of which 1 were waited for; matrix products, arithmetic and copies ran while one was open for 12% of the time, Pallas kernels for 12%

profile of v6, /device:TPU:0, one launch (start us, length us, event | category | flops | bytes accessed | tf_op | source)
XLA Modules:
  0.0 215.0 jit_solution(10240101147754740377)
XLA Ops:
  0.7 1.0 slice_bitcast_fusion.11
  2.8 2.9 %collective-permute-start = (f32[4,2,4,1,256]{4,3,2,1,0:T(1,128)S(1)}, f32[4,2,4,1,256]{4,3,2,1,0:T(1,128)S(1)}, u32[]{:S(2)}, u32[]{:S(2)}) collective-permute-start(f32[4,2,4,1,256]{4,3,2,1,0:T(1,128)S(1)} %pad_maximum_fusion.7), channel_id=1, source_target_pairs={{8,0},{16,8},{24,16},{32,24},{40,32},{48,40},{56,48},{0,56},{9,1},... | collective-permute-start | bytes 98312 | tf_op jit(solution)/shard_map/ppermute | solution.py:412
  5.8 1.4 slice_reduce_fusion.10
  7.1 1.4 slice_reduce_fusion.9
  9.2 5.2 %collective-permute-start.2 = (f32[4,2,4,64,1]{3,2,4,1,0:T(4,128)S(1)}, f32[4,2,4,64,1]{3,2,4,1,0:T(4,128)S(1)}, u32[]{:S(2)}, u32[]{:S(2)}) collective-permute-start(f32[4,2,4,64,1]{3,2,4,1,0:T(4,128)S(1)} %pad_maximum_fusion.11), channel_id=1, source_target_pairs={{1,0},{2,1},{3,2},{4,3},{5,4},{6,5},{7,6},{0,7},{9,8},{10,9},{11,1... | collective-permute-start | bytes 24584 | tf_op jit(solution)/shard_map/ppermute | solution.py:414
  21.7 1.4 copy.225.e_ref
  23.1 1.4 copy.226.w_ref
  26.5 5.0 %shard_map.126 = (f32[2,4,64,256]{3,2,1,0:T(8,128)}, f32[2,4,64,256]{3,2,1,0:T(8,128)}, f32[2,4,64,256]{3,2,1,0:T(8,128)}, f32[2,4,64,256]{3,2,1,0:T(8,128)}, f3...) custom-call(f32[2,4,64,256]{3,2,1,0:T(8,128)} %temp_ref.1, f32[2,4,64,256]{3,2,1,0:T(8,128)} %salt_ref.1, ...), custom_call_target="tpu_custom_call" | custom-call | tf_op jit(solution)/shard_map/pallas_call | solution.py:381
  31.5 1.8 pad_maximum_fusion.4.surf_ref
  33.3 44.7 %shard_map.127 = f32[3,2,64,256]{3,2,1,0:T(8,128)} custom-call(f32[3,2,64,256]{3,2,1,0:T(8,128)} %pad_maximum_fusion.4.surf_ref, f32[80,512]{1,0:T(8,128)} %get-tuple-element.150.inside_ref, f32[80,512]{1,0:T(8,128)} %get-tuple-element.151.own_ref), custom_call_target="tpu_custom_call" | custom-call | tf_op jit(solution)/shard_map/pallas_call | solution.py:281
  78.0 1.1 fusion.15
  81.8 3.5 %collective-permute-start.6 = (f32[4,2,4,64,1]{3,2,4,1,0:T(4,128)S(1)}, f32[4,2,4,64,1]{3,2,4,1,0:T(4,128)S(1)}, u32[]{:S(2)}, u32[]{:S(2)}) collective-permute-start(f32[4,2,4,64,1]{3,2,4,1,0:T(4,128)S(1)} %pad_maximum_fusion.13), channel_id=1, source_target_pairs={{1,0},{2,1},{3,2},{4,3},{5,4},{6,5},{7,6},{0,7},{9,8},{10,9},{11,1... | collective-permute-start | bytes 24584 | tf_op jit(solution)/shard_map/ppermute | solution.py:414
  85.4 2.9 %collective-permute-start.4 = (f32[4,2,4,1,256]{4,3,2,1,0:T(1,128)S(1)}, f32[4,2,4,1,256]{4,3,2,1,0:T(1,128)S(1)}, u32[]{:S(2)}, u32[]{:S(2)}) collective-permute-start(f32[4,2,4,1,256]{4,3,2,1,0:T(1,128)S(1)} %pad_maximum_fusion.9), channel_id=1, source_target_pairs={{8,0},{16,8},{24,16},{32,24},{40,32},{48,40},{56,48},{0,56},{9,1},... | collective-permute-start | bytes 98312 | tf_op jit(solution)/shard_map/ppermute | solution.py:412
  88.4 1.4 copy.240.w_ref
  89.8 1.4 copy.239.e_ref
  92.5 5.0 %shard_map.128 = (f32[2,4,64,256]{3,2,1,0:T(8,128)}, f32[2,4,64,256]{3,2,1,0:T(8,128)}, f32[2,4,64,256]{3,2,1,0:T(8,128)}, f32[2,4,64,256]{3,2,1,0:T(8,128)}, f3...) custom-call(f32[2,4,64,256]{3,2,1,0:T(8,128)} %get-tuple-element.43.temp_ref, f32[2,4,64,256]{3,2,1,0:T(8,128)} %get-tuple-element.44.salt_ref, ...), custom_call_target="tpu_custom_call" | custom-call | tf_op jit(solution)/shard_map/pallas_call | solution.py:381
  97.5 1.8 pad_maximum_fusion.5.surf_ref
  99.3 42.1 %shard_map.129 = f32[3,2,64,256]{3,2,1,0:T(8,128)} custom-call(f32[3,2,64,256]{3,2,1,0:T(8,128)} %pad_maximum_fusion.5.surf_ref, f32[80,512]{1,0:T(8,128)} %get-tuple-element.150.inside_ref, f32[80,512]{1,0:T(8,128)} %get-tuple-element.151.own_ref), custom_call_target="tpu_custom_call" | custom-call | tf_op jit(solution)/shard_map/pallas_call | solution.py:281
  141.4 1.1 multiply_bitcast_fusion.1
  143.7 1.1 pad_maximum_fusion.1
  144.8 2.9 %collective-permute-start.8 = (f32[2,2,4,64,256]{4,3,2,1,0:T(8,128)}, f32[2,2,4,64,256]{4,3,2,1,0:T(8,128)}, u32[]{:S(2)}, u32[]{:S(2)}) collective-permute-start(f32[2,2,4,64,256]{4,3,2,1,0:T(8,128)} %pad_maximum_fusion.1), channel_id=1, source_target_pairs={{0,64},{64,0},{1,65},{65,1},{2,66},{66,2},{3,67},{67,3},{4,68},{68... | collective-permute-start | bytes 3145736 | tf_op jit(solution)/shard_map/ppermute | solution.py:565
  148.4 25.7 %shard_map.130 = f32[40,128]{1,0:T(8,128)} custom-call(f32[40,128]{1,0:T(8,128)} %select_maximum_fusion.1.x_ref), custom_call_target="tpu_custom_call" | custom-call | tf_op jit(solution)/shard_map/pallas_call | solution.py:90
  174.1 1.3 fusion.10
  176.9 1.9 collective-permute-start.9
  178.8 1.3 pad_clamp_fusion
  182.3 1.3 fusion.14
  183.6 1.4 bitcast_select_fusion.1
  185.1 1.4 bitcast_select_fusion.3
  188.2 18.7 %collective-permute-done.9 = f32[2,10,64,256]{3,2,1,0:T(8,128)} collective-permute-done((f32[2,10,64,256]{3,2,1,0:T(8,128)S(1)}, f32[2,10,64,256]{3,2,1,0:T(8,128)}, u32[]{:S(2)}, u32[]{:S(2)}) %collective-permute-start.9) | collective-permute-done | bytes 1310752 | tf_op jit(solution)/shard_map/ppermute | solution.py:587
  206.9 1.3 slice.272
  208.2 1.6 dynamic-slice_select_fusion
  210.5 1.0 fusion
  (113 shorter events, 21.8 us)
Async XLA Ops:
  0.6 8.2 %copy-start.2 = (f32[2,4,64,256]{3,2,1,0:T(8,128)S(1)}, f32[2,4,64,256]{3,2,1,0:T(8,128)}, u32[]{:S(2)}) copy-start(f32[2,4,64,256]{3,2,1,0:T(8,128)} %temp_ref.1) | copy-start | bytes 1572868
  0.6 7.9 %copy-start.3 = (f32[2,4,64,256]{3,2,1,0:T(8,128)S(1)}, f32[2,4,64,256]{3,2,1,0:T(8,128)}, u32[]{:S(2)}) copy-start(f32[2,4,64,256]{3,2,1,0:T(8,128)} %vvel_ref.1) | copy-start | bytes 1572868
  0.7 13.9 %copy-start.18 = (s32[2]{0:T(128)S(1)}, s32[2]{0:T(128)}, u32[]{:S(2)}) copy-start(s32[2]{0:T(128)} %param.17) | copy-start | bytes 28
  2.7 21.8 %collective-permute-start.1 = (f32[4,2,4,1,256]{4,3,2,1,0:T(1,128)S(1)}, f32[4,2,4,1,256]{4,3,2,1,0:T(1,128)S(1)}, u32[]{:S(2)}, u32[]{:S(2)}) collective-permute-start(f32[4,2,4,1,256]{4,3,2,1,0:T(1,128)S(1)} %pad_maximum_fusion.8), channel_id=1, source_target_pairs={{0,8},{8,16},{16,24},{24,32},{32,40},{40,48},{48,56},{56,0},{1,9},... | collective-permute-start | bytes 98312 | tf_op jit(solution)/shard_map/ppermute | solution.py:413
  2.8 16.9 %copy-start.15 = (s32[64,256]{1,0:T(8,128)S(1)}, s32[64,256]{1,0:T(8,128)}, u32[]{:S(2)}) copy-start(s32[64,256]{1,0:T(8,128)} %param.16) | copy-start | bytes 196612
  2.8 22.4 %collective-permute-start = (f32[4,2,4,1,256]{4,3,2,1,0:T(1,128)S(1)}, f32[4,2,4,1,256]{4,3,2,1,0:T(1,128)S(1)}, u32[]{:S(2)}, u32[]{:S(2)}) collective-permute-start(f32[4,2,4,1,256]{4,3,2,1,0:T(1,128)S(1)} %pad_maximum_fusion.7), channel_id=1, source_target_pairs={{8,0},{16,8},{24,16},{32,24},{40,32},{48,40},{56,48},{0,56},{9,1},... | collective-permute-start | bytes 98312 | tf_op jit(solution)/shard_map/ppermute | solution.py:412
  9.2 12.5 %collective-permute-start.2 = (f32[4,2,4,64,1]{3,2,4,1,0:T(4,128)S(1)}, f32[4,2,4,64,1]{3,2,4,1,0:T(4,128)S(1)}, u32[]{:S(2)}, u32[]{:S(2)}) collective-permute-start(f32[4,2,4,64,1]{3,2,4,1,0:T(4,128)S(1)} %pad_maximum_fusion.11), channel_id=1, source_target_pairs={{1,0},{2,1},{3,2},{4,3},{5,4},{6,5},{7,6},{0,7},{9,8},{10,9},{11,1... | collective-permute-start | bytes 24584 | tf_op jit(solution)/shard_map/ppermute | solution.py:414
  14.4 8.7 %collective-permute-start.3 = (f32[4,2,4,64,1]{3,2,4,1,0:T(4,128)S(1)}, f32[4,2,4,64,1]{3,2,4,1,0:T(4,128)S(1)}, u32[]{:S(2)}, u32[]{:S(2)}) collective-permute-start(f32[4,2,4,64,1]{3,2,4,1,0:T(4,128)S(1)} %pad_maximum_fusion.12), channel_id=1, source_target_pairs={{0,1},{1,2},{2,3},{3,4},{4,5},{5,6},{6,7},{7,0},{8,9},{9,10},{10,1... | collective-permute-start | bytes 24584 | tf_op jit(solution)/shard_map/ppermute | solution.py:415
  14.5 128.2 %copy-start.16 = (pred[8]{0:T(512)(128)(4,1)}, pred[8]{0:T(512)(128)(4,1)S(1)}, u32[]{:S(2)}) copy-start(pred[8]{0:T(512)(128)(4,1)S(1)} %iota_compare_fusion.4) | copy-start | bytes 28
  26.5 5.0 %copy-start.14 = (f32[2,64,256]{2,1,0:T(8,128)S(1)}, f32[2,64,256]{2,1,0:T(8,128)}, u32[]{:S(2)}) copy-start(f32[2,64,256]{2,1,0:T(8,128)} %param.15) | copy-start | bytes 393220
  31.5 47.6 %copy-start.8 = (f32[64,256]{1,0:T(8,128)S(1)}, f32[64,256]{1,0:T(8,128)}, u32[]{:S(2)}) copy-start(f32[64,256]{1,0:T(8,128)} %convert_element_type.35.ocean_ref) | copy-start | bytes 196612
  31.5 47.6 %copy-start.12 = (f32[2,4,64,256]{3,2,1,0:T(8,128)S(1)}, f32[2,4,64,256]{3,2,1,0:T(8,128)}, u32[]{:S(2)}) copy-start(f32[2,4,64,256]{3,2,1,0:T(8,128)} %get-tuple-element.45) | copy-start | bytes 1572868
  31.5 47.6 %copy-start.13 = (f32[2,4,64,256]{3,2,1,0:T(8,128)S(1)}, f32[2,4,64,256]{3,2,1,0:T(8,128)}, u32[]{:S(2)}) copy-start(f32[2,4,64,256]{3,2,1,0:T(8,128)} %get-tuple-element.48) | copy-start | bytes 1572868
  79.1 1.1 copy-start.4
  79.3 10.6 %copy-start = (f32[2,4,64,256]{3,2,1,0:T(8,128)}, f32[2,4,64,256]{3,2,1,0:T(8,128)S(1)}, u32[]{:S(2)}) copy-start(f32[2,4,64,256]{3,2,1,0:T(8,128)S(1)} %get-tuple-element.136.vvel_ref) | copy-start | bytes 1572868
  79.3 10.6 %copy-start.1 = (f32[2,4,64,256]{3,2,1,0:T(8,128)}, f32[2,4,64,256]{3,2,1,0:T(8,128)S(1)}, u32[]{:S(2)}) copy-start(f32[2,4,64,256]{3,2,1,0:T(8,128)S(1)} %get-tuple-element.137.uvel_ref) | copy-start | bytes 1572868
  79.3 1.5 copy-start.5
  81.1 7.3 %collective-permute-start.7 = (f32[4,2,4,64,1]{3,2,4,1,0:T(4,128)S(1)}, f32[4,2,4,64,1]{3,2,4,1,0:T(4,128)S(1)}, u32[]{:S(2)}, u32[]{:S(2)}) collective-permute-start(f32[4,2,4,64,1]{3,2,4,1,0:T(4,128)S(1)} %pad_maximum_fusion.14), channel_id=1, source_target_pairs={{0,1},{1,2},{2,3},{3,4},{4,5},{5,6},{6,7},{7,0},{8,9},{9,10},{10,1... | collective-permute-start | bytes 24584 | tf_op jit(solution)/shard_map/ppermute | solution.py:415
  81.8 8.0 %collective-permute-start.6 = (f32[4,2,4,64,1]{3,2,4,1,0:T(4,128)S(1)}, f32[4,2,4,64,1]{3,2,4,1,0:T(4,128)S(1)}, u32[]{:S(2)}, u32[]{:S(2)}) collective-permute-start(f32[4,2,4,64,1]{3,2,4,1,0:T(4,128)S(1)} %pad_maximum_fusion.13), channel_id=1, source_target_pairs={{1,0},{2,1},{3,2},{4,3},{5,4},{6,5},{7,6},{0,7},{9,8},{10,9},{11,1... | collective-permute-start | bytes 24584 | tf_op jit(solution)/shard_map/ppermute | solution.py:414
  85.4 5.9 %collective-permute-start.5 = (f32[4,2,4,1,256]{4,3,2,1,0:T(1,128)S(1)}, f32[4,2,4,1,256]{4,3,2,1,0:T(1,128)S(1)}, u32[]{:S(2)}, u32[]{:S(2)}) collective-permute-start(f32[4,2,4,1,256]{4,3,2,1,0:T(1,128)S(1)} %pad_maximum_fusion.10), channel_id=1, source_target_pairs={{0,8},{8,16},{16,24},{24,32},{32,40},{40,48},{48,56},{56,0},{1,9},... | collective-permute-start | bytes 98312 | tf_op jit(solution)/shard_map/ppermute | solution.py:413
  85.4 6.4 %collective-permute-start.4 = (f32[4,2,4,1,256]{4,3,2,1,0:T(1,128)S(1)}, f32[4,2,4,1,256]{4,3,2,1,0:T(1,128)S(1)}, u32[]{:S(2)}, u32[]{:S(2)}) collective-permute-start(f32[4,2,4,1,256]{4,3,2,1,0:T(1,128)S(1)} %pad_maximum_fusion.9), channel_id=1, source_target_pairs={{8,0},{16,8},{24,16},{32,24},{40,32},{48,40},{56,48},{0,56},{9,1},... | collective-permute-start | bytes 98312 | tf_op jit(solution)/shard_map/ppermute | solution.py:412
  97.5 45.0 %copy-start.9 = (f32[64,256]{1,0:T(8,128)S(1)}, f32[64,256]{1,0:T(8,128)}, u32[]{:S(2)}) copy-start(f32[64,256]{1,0:T(8,128)} %convert_element_type.35.ocean_ref) | copy-start | bytes 196612
  97.5 45.0 %copy-start.10 = (f32[2,4,64,256]{3,2,1,0:T(8,128)S(1)}, f32[2,4,64,256]{3,2,1,0:T(8,128)}, u32[]{:S(2)}) copy-start(f32[2,4,64,256]{3,2,1,0:T(8,128)} %get-tuple-element.51) | copy-start | bytes 1572868
  97.5 45.0 %copy-start.11 = (f32[2,4,64,256]{3,2,1,0:T(8,128)S(1)}, f32[2,4,64,256]{3,2,1,0:T(8,128)}, u32[]{:S(2)}) copy-start(f32[2,4,64,256]{3,2,1,0:T(8,128)} %get-tuple-element.54) | copy-start | bytes 1572868
  142.5 1.0 copy-start.6
  142.5 1.2 copy-start.7
  144.8 37.5 %collective-permute-start.8 = (f32[2,2,4,64,256]{4,3,2,1,0:T(8,128)}, f32[2,2,4,64,256]{4,3,2,1,0:T(8,128)}, u32[]{:S(2)}, u32[]{:S(2)}) collective-permute-start(f32[2,2,4,64,256]{4,3,2,1,0:T(8,128)} %pad_maximum_fusion.1), channel_id=1, source_target_pairs={{0,64},{64,0},{1,65},{65,1},{2,66},{66,2},{3,67},{67,3},{4,68},{68... | collective-permute-start | bytes 3145736 | tf_op jit(solution)/shard_map/ppermute | solution.py:565
  174.1 5.9 %slice-start = ((f32[40,128]{1,0:T(8,128)}), f32[32,128]{1,0:T(8,128)S(1)}, s32[]{:S(2)}) async-start(f32[40,128]{1,0:T(8,128)} %shard_map.130), calls=%async_computation | async-start | bytes 32768 | tf_op jit(solution)/shard_map/slice | solution.py:579
  176.9 30.0 %collective-permute-start.9 = (f32[2,10,64,256]{3,2,1,0:T(8,128)S(1)}, f32[2,10,64,256]{3,2,1,0:T(8,128)}, u32[]{:S(2)}, u32[]{:S(2)}) collective-permute-start(f32[2,10,64,256]{3,2,1,0:T(8,128)S(1)} %select_maximum_fusion), channel_id=1, source_target_pairs={{0,64},{64,0},{1,65},{65,1},{2,66},{66,2},{3,67},{67,3},{4,68},{68... | collective-permute-start | bytes 3932168 | tf_op jit(solution)/shard_map/ppermute | solution.py:587
  210.5 1.9 copy-start.17
  210.5 3.9 %copy-start.19 = (s32[2]{0:T(128)S(1)}, s32[2]{0:T(128)}, u32[]{:S(2)}) copy-start(s32[2]{0:T(128)} %param.17) | copy-start | bytes 28

commit v7 on v6

--- a/solution.py
+++ b/solution.py
@@ -147,7 +147,13 @@
     return phase(partial, send_x, recv_x, sx, rx, nx, mx, along_x)
 
 
-def solve_kernel(ny, nx, surf_ref, inside_ref, own_ref, out_ref, frame, hsend, hrecv, *bufs):
+def solve_kernel(ny, nx, carry, *refs):
+    if carry:
+        surf_ref, inside_ref, own_ref, cargo_ref, out_ref, cargo_out, frame, hsend, hrecv, csem = refs[:10]
+        bufs = refs[10:]
+    else:
+        surf_ref, inside_ref, own_ref, out_ref, frame, hsend, hrecv = refs[:7]
+        bufs = refs[7:]
     mesh_id = pl.DeviceIdType.MESH
     member = lax.axis_index("member")
     my = lax.axis_index("gridy")
@@ -169,7 +175,16 @@
     band = (wide_rows - rows) // 2
     block = (wide_cols - cols) // 2
     frame[:, :, 0:rows, 0:cols] = surf_ref[...]
-    pl.semaphore_wait(barrier, (ny - 1) + (nx - 1) + 4)
+    if carry:
+        partner = (lax.axis_index("member") + 1) % 2
+        pl.semaphore_signal(barrier, 1, device_id=(partner, my, mx), device_id_type=mesh_id)
+    pl.semaphore_wait(barrier, (ny - 1) + (nx - 1) + 4 + (1 if carry else 0))
+    if carry:
+        cargo_copy = pltpu.make_async_remote_copy(
+            src_ref=cargo_ref, dst_ref=cargo_out, send_sem=csem.at[0], recv_sem=csem.at[1],
+            device_id=(partner, my, mx), device_id_type=mesh_id,
+        )
+        cargo_copy.start()
 
     def halo_copies(first, moves):
         started = []
@@ -272,21 +287,31 @@
         out_ref[0, m] = x[0:rows, 0:cols]
         out_ref[1, m] = (east(x) - west(x))[0:rows, 0:cols]
         out_ref[2, m] = (north(x) - south(x))[0:rows, 0:cols]
-
-
-def surface_kernel_solve(surf, inside, own):
+    if carry:
+        cargo_copy.wait()
+
+
+def surface_kernel_solve(surf, inside, own, cargo=None):
     ny = lax.axis_size("gridy")
     nx = lax.axis_size("gridx")
     fields, members, rows, cols = surf.shape
-    return pl.pallas_call(
-        functools.partial(solve_kernel, ny, nx),
-        out_shape=jax.ShapeDtypeStruct((3, members, rows, cols), jnp.float32),
-        in_specs=[pl.BlockSpec(memory_space=pltpu.VMEM)] * 3,
-        out_specs=pl.BlockSpec(memory_space=pltpu.VMEM),
+    carry = cargo is not None
+    vmem = pl.BlockSpec(memory_space=pltpu.VMEM)
+    anywhere = pl.BlockSpec(memory_space=pl.ANY)
+    solved_shape = jax.ShapeDtypeStruct((3, members, rows, cols), jnp.float32)
+    operands = (surf, inside, own) + ((cargo,) if carry else ())
+    results = pl.pallas_call(
+        functools.partial(solve_kernel, ny, nx, carry),
+        out_shape=[solved_shape] + ([jax.ShapeDtypeStruct(cargo.shape, cargo.dtype)] if carry else []),
+        in_specs=[vmem] * 3 + ([anywhere] if carry else []),
+        out_specs=[vmem] + ([anywhere] if carry else []),
         scratch_shapes=[
             pltpu.VMEM((fields, members) + inside.shape, jnp.float32),
             pltpu.SemaphoreType.DMA((8,)),
             pltpu.SemaphoreType.DMA((8,)),
+        ]
+        + ([pltpu.SemaphoreType.DMA((2,))] if carry else [])
+        + [
             pltpu.VMEM((ITERS, 8, 128), jnp.float32),
             pltpu.VMEM((ITERS, ny, 8, 128), jnp.float32),
             pltpu.VMEM((ITERS, 8, 128), jnp.float32),
@@ -296,8 +321,9 @@
             pltpu.SemaphoreType.DMA((ITERS, nx)),
             pltpu.SemaphoreType.DMA((ITERS, nx)),
         ],
-        compiler_params=pltpu.CompilerParams(collective_id=1, has_side_effects=True),
-    )(surf, inside, own)
+        compiler_params=pltpu.CompilerParams(collective_id=2 if carry else 1, has_side_effects=True),
+    )(*operands)
+    return results if carry else (results[0], None)
 
 
 def volume_kernel(temp_ref, salt_ref, uvel_ref, vvel_ref, ocean_ref, cor_ref, n_ref, s_ref, e_ref, w_ref,
@@ -555,14 +581,16 @@
         temp_next, salt_next, ustar, vstar, trans_u, trans_v = volume_step(
             temp, salt, uvel, vvel, ocean, cor_tile, rims
         )
-        solved = surface_kernel_solve(jnp.stack((trans_u, trans_v, eta)), wide_inside, own_mask)
+        last = count == STEPS - 1
+        cargo = jnp.stack((temp_next, salt_next, ustar, vstar)) if last else None
+        solved, cargo_other = surface_kernel_solve(
+            jnp.stack((trans_u, trans_v, eta)), wide_inside, own_mask, cargo
+        )
         eta = solved[0]
         east_west = solved[1]
         north_south = solved[2]
         uvel = ocean * (ustar - GRAV_K * 0.5 * east_west[:, None])
         vvel = ocean * (vstar - GRAV_K * 0.5 * north_south[:, None])
-        if count == STEPS - 1:
-            tracers_other = lax.ppermute(jnp.stack((temp_next, salt_next)), "member", [(0, 1), (1, 0)])
         temp = temp_next
         salt = salt_next
     zonal_scale = 1.0 / jnp.sqrt(jnp.float32(total_cols))
@@ -583,9 +611,9 @@
     swap = [(0, 1), (1, 0)]
     mine = lax.axis_index("member")
     score_slab = jnp.zeros((members, 1) + eta.shape[1:], jnp.float32).at[:, 0, 0, 0].set(score)
-    flows = jnp.concatenate([uvel, vvel, eta[:, None], score_slab], axis=1)
-    flows_other = lax.ppermute(flows, "member", swap)
-    score_other = flows_other[:, 2 * levels + 1, 0, 0]
+    surface_last = jnp.concatenate([solved.transpose(1, 0, 2, 3), score_slab], axis=1)
+    surface_other = lax.ppermute(surface_last, "member", swap)
+    score_other = surface_other[:, 3, 0, 0]
     every_score = jnp.where(
         mine == 0, jnp.concatenate([score, score_other]), jnp.concatenate([score_other, score])
     )
@@ -600,19 +628,15 @@
             chosen.append(jnp.where(here[place], from_here, from_other))
         return jnp.stack(chosen)
 
-    new_temp = pick(temp, tracers_other[0])
-    new_salt = pick(salt, tracers_other[1])
-    new_flows = pick(flows[:, : 2 * levels + 1], flows_other[:, : 2 * levels + 1])
+    uvel_other = ocean * (cargo_other[2] - GRAV_K * 0.5 * surface_other[:, 1][:, None])
+    vvel_other = ocean * (cargo_other[3] - GRAV_K * 0.5 * surface_other[:, 2][:, None])
+    new_temp = pick(temp, cargo_other[0])
+    new_salt = pick(salt, cargo_other[1])
+    new_uvel = pick(uvel, uvel_other)
+    new_vvel = pick(vvel, vvel_other)
+    new_eta = pick(eta, surface_other[:, 0])
     clone_weight = jnp.take(every_score, clone_source, axis=0) - jnp.mean(every_score)
-    return (
-        new_temp,
-        new_salt,
-        new_flows[:, :levels],
-        new_flows[:, levels : 2 * levels],
-        new_flows[:, 2 * levels],
-        overturn,
-        clone_weight,
-    )
+    return (new_temp, new_salt, new_uvel, new_vvel, new_eta, overturn, clone_weight)
 
 
 def solution(mesh):

time: 216 us -> 236 us (1.093)
  Pallas kernels: 122 us -> 154 us
  waiting for transfers between devices: 18.7 us -> 2.12 us
  other arithmetic: 26.6 us -> 34.7 us
    pallas_call x2, Pallas kernels: 86.8 us -> 132 us  [surface_kernel_solve(): pl.pallas_call(functools.partial(solve_kernel, ny, nx, carry), out_shape=...]
    ppermute x2 -> x1, waiting for transfers between devices: 18.7 us -> 2.1 us  [shards(): surface_other = lax.ppermute(surface_last, 'member', swap)]
    pallas_call x1, Pallas kernels: 25.7 us -> 12.2 us  [grid_sum(): pl.pallas_call(functools.partial(gather_sum_kernel, ny, nx), out_shape=ja...]
    select_n x3 -> x5, other arithmetic: 4.44 us -> 8.02 us  [pick(): chosen.append(jnp.where(here[place], from_here, from_other))]
    another operation x3 -> x5, other arithmetic: 2.71 us -> 6.05 us  [pick(): return jnp.stack(chosen)]
    slice x3 -> x2, local copies, waits for them, and re-layouts: 3.46 us -> 0.9 us  [the longest x1 0.81 us: shards(): score_other = surface_other[:, 3, 0, 0]]
    ppermute x2 -> x1, starting transfers between devices: 4.82 us -> 2.9 us  [shards(): surface_other = lax.ppermute(surface_last, 'member', swap)]
  transfers between devices with their start and end apart: 10 -> 9, of which waited for: 1 -> 1; matrix products, arithmetic and copies ran while one was open for 12% -> 10% of each run, Pallas kernels for 12% -> 0%
where the time goes in v7:
time: 236 us
  Pallas kernels  154 us (65%)
  other arithmetic  34.7 us (15%)
  local copies, waits for them, and re-layouts  20.7 us (9%)
  starting transfers between devices  18.2 us (8%)
  between operations  5.69 us (2%)
    pallas_call x2, Pallas kernels, surface_kernel_solve(): pl.pallas_call(functools.partial(solve_kernel, ny, nx, carry), out_shape=...  132 us
    pallas_call x1, Pallas kernels, grid_sum(): pl.pallas_call(functools.partial(gather_sum_kernel, ny, nx), out_shape=ja...  12.2 us
    pallas_call x2, Pallas kernels, volume_step(): pl.pallas_call(volume_kernel, grid=(members,), in_specs=[field] * 4 + [pl...  9.91 us
    ppermute x2, starting transfers between devices, exchange_fields(): lax.ppermute(jnp.stack([f[..., :, :1] for f in fields]), 'gridx', bwd_x)  8.68 us
    select_n x5, other arithmetic, pick(): chosen.append(jnp.where(here[place], from_here, from_other))  8.02 us
    another operation x5, other arithmetic, pick(): return jnp.stack(chosen)  6.05 us
    ppermute x2, starting transfers between devices, exchange_fields(): lax.ppermute(jnp.stack([f[..., :1, :] for f in fields]), 'gridy', bwd_y)  5.89 us
    slice x8, local copies, waits for them, and re-layouts, exchange_fields(): f[..., :, -1:]  5.8 us
  transfers between devices with their start and end apart: 9, of which 1 were waited for; matrix products, arithmetic and copies ran while one was open for 10% of the time, Pallas kernels for 0%

profile of v7, /device:TPU:0, one launch (start us, length us, event | category | flops | bytes accessed | tf_op | source)
XLA Modules:
  0.0 235.6 jit_solution(6226716481833770996)
XLA Ops:
  2.8 2.9 %collective-permute-start = (f32[4,2,4,1,256]{4,3,2,1,0:T(1,128)S(1)}, f32[4,2,4,1,256]{4,3,2,1,0:T(1,128)S(1)}, u32[]{:S(2)}, u32[]{:S(2)}) collective-permute-start(f32[4,2,4,1,256]{4,3,2,1,0:T(1,128)S(1)} %pad_maximum_fusion.8), channel_id=1, source_target_pairs={{8,0},{16,8},{24,16},{32,24},{40,32},{48,40},{56,48},{0,56},{9,1},... | collective-permute-start | bytes 98312 | tf_op jit(solution)/shard_map/ppermute | solution.py:438
  5.7 1.4 slice_reduce_fusion.10
  7.1 1.4 slice_reduce_fusion.9
  8.5 1.4 slice_reduce_fusion.8
  10.2 5.2 %collective-permute-start.2 = (f32[4,2,4,64,1]{3,2,4,1,0:T(4,128)S(1)}, f32[4,2,4,64,1]{3,2,4,1,0:T(4,128)S(1)}, u32[]{:S(2)}, u32[]{:S(2)}) collective-permute-start(f32[4,2,4,64,1]{3,2,4,1,0:T(4,128)S(1)} %pad_maximum_fusion.12), channel_id=1, source_target_pairs={{1,0},{2,1},{3,2},{4,3},{5,4},{6,5},{7,6},{0,7},{9,8},{10,9},{11,1... | collective-permute-start | bytes 24584 | tf_op jit(solution)/shard_map/ppermute | solution.py:440
  22.1 1.4 copy.143.e_ref
  23.5 1.4 copy.144.w_ref
  26.9 5.0 %shard_map.126 = (f32[2,4,64,256]{3,2,1,0:T(8,128)}, f32[2,4,64,256]{3,2,1,0:T(8,128)}, f32[2,4,64,256]{3,2,1,0:T(8,128)}, f32[2,4,64,256]{3,2,1,0:T(8,128)}, f3...) custom-call(f32[2,4,64,256]{3,2,1,0:T(8,128)} %temp_ref.1, f32[2,4,64,256]{3,2,1,0:T(8,128)} %salt_ref.1, ...), custom_call_target="tpu_custom_call" | custom-call | tf_op jit(solution)/shard_map/pallas_call | solution.py:407
  31.9 1.8 pad_maximum_fusion.5.refs_0_
  33.8 44.7 %shard_map.127 = f32[3,2,64,256]{3,2,1,0:T(8,128)} custom-call(f32[3,2,64,256]{3,2,1,0:T(8,128)} %pad_maximum_fusion.5.refs_0_, f32[80,512]{1,0:T(8,128)} %get-tuple-element.133.refs_1_, f32[80,512]{1,0:T(8,128)} %get-tuple-element.134.refs_2_), custom_call_target="tpu_custom_call" | custom-call | tf_op jit(solution)/shard_map/pallas_call | solution.py:303
  78.5 1.1 multiply_bitcast_fusion.2
  82.0 3.5 %collective-permute-start.6 = (f32[4,2,4,64,1]{3,2,4,1,0:T(4,128)S(1)}, f32[4,2,4,64,1]{3,2,4,1,0:T(4,128)S(1)}, u32[]{:S(2)}, u32[]{:S(2)}) collective-permute-start(f32[4,2,4,64,1]{3,2,4,1,0:T(4,128)S(1)} %pad_maximum_fusion.14), channel_id=1, source_target_pairs={{1,0},{2,1},{3,2},{4,3},{5,4},{6,5},{7,6},{0,7},{9,8},{10,9},{11,1... | collective-permute-start | bytes 24584 | tf_op jit(solution)/shard_map/ppermute | solution.py:440
  85.6 2.9 %collective-permute-start.4 = (f32[4,2,4,1,256]{4,3,2,1,0:T(1,128)S(1)}, f32[4,2,4,1,256]{4,3,2,1,0:T(1,128)S(1)}, u32[]{:S(2)}, u32[]{:S(2)}) collective-permute-start(f32[4,2,4,1,256]{4,3,2,1,0:T(1,128)S(1)} %pad_maximum_fusion.10), channel_id=1, source_target_pairs={{8,0},{16,8},{24,16},{32,24},{40,32},{48,40},{56,48},{0,56},{9,1},... | collective-permute-start | bytes 98312 | tf_op jit(solution)/shard_map/ppermute | solution.py:438
  88.5 1.4 copy.156.w_ref
  90.0 1.4 copy.155.e_ref
  92.6 5.0 %shard_map.128 = (f32[2,4,64,256]{3,2,1,0:T(8,128)}, f32[2,4,64,256]{3,2,1,0:T(8,128)}, f32[2,4,64,256]{3,2,1,0:T(8,128)}, f32[2,4,64,256]{3,2,1,0:T(8,128)}, f3...) custom-call(f32[2,4,64,256]{3,2,1,0:T(8,128)} %get-tuple-element.45.temp_ref, f32[2,4,64,256]{3,2,1,0:T(8,128)} %get-tuple-element.46.salt_ref, ...), custom_call_target="tpu_custom_call" | custom-call | tf_op jit(solution)/shard_map/pallas_call | solution.py:407
  97.6 1.7 pad_maximum_fusion.6.refs_0_
  99.3 3.0 %pad_maximum_fusion.refs_3_ = f32[4,2,4,64,256]{4,3,2,1,0:T(8,128)} fusion(f32[1,2,4,64,256]{4,3,2,1,0:T(8,128)} %bitcast.136, f32[1,2,4,64,256]{4,3,2,1,0:T(8,128)} %bitcast.133, f32[1,2,4,64,256]{4,3,2,1,0:T(8,128)} %bitcast.135, f32[1,2,4,64,256]{4,3,2,1,0:T(8,128)} %bitcast.134), kind=kLoop, calls=%fused_computation.1 | loop fusion | flops 1572864 | bytes 4194304 | tf_op jit(solution)/shard_map/stack | solution.py:585
  102.4 87.3 %shard_map.129 = (f32[3,2,64,256]{3,2,1,0:T(8,128)}, f32[4,2,4,64,256]{4,3,2,1,0:T(8,128)}) custom-call(f32[3,2,64,256]{3,2,1,0:T(8,128)} %pad_maximum_fusion.6.refs_0_, f32[80,512]{1,0:T(8,128)} %get-tuple-element.133.refs_1_, f32[80,512]{1,0:T(8,128)} %get-tuple-element.134.refs_2_, f32[4,2,4,64,256]{4,3,2,1,0:T(8,128)} %pad_maximum_fusion.refs_3_), custom_call_target="tpu_custom_call" | custom-call | tf_op jit(solution)/shard_map/pallas_call | solution.py:303
  189.7 1.9 fusion.17
  191.6 1.8 copy.160
  194.5 12.2 %shard_map.130 = f32[40,128]{1,0:T(8,128)} custom-call(f32[40,128]{1,0:T(8,128)} %select_maximum_fusion.1.x_ref), custom_call_target="tpu_custom_call" | custom-call | tf_op jit(solution)/shard_map/pallas_call | solution.py:90
  208.2 1.9 select_maximum_fusion
  210.1 2.9 %collective-permute-start.8 = (f32[2,4,64,256]{3,2,1,0:T(8,128)}, f32[2,4,64,256]{3,2,1,0:T(8,128)}, u32[]{:S(2)}, u32[]{:S(2)}) collective-permute-start(f32[2,4,64,256]{3,2,1,0:T(8,128)} %select_maximum_fusion), channel_id=1, source_target_pairs={{0,64},{64,0},{1,65},{65,1},{2,66},{66,2},{3,67},{67,3},{4,68},{68... | collective-permute-start | bytes 1572872 | tf_op jit(solution)/shard_map/ppermute | solution.py:615
  214.1 2.0 bitcast_select_fusion.1
  216.1 2.1 bitcast_select_fusion.3
  218.3 1.8 pad_maximum_fusion.2
  220.2 1.9 pad_maximum_fusion.1
  222.7 2.1 collective-permute-done.8
  229.1 1.3 select_bitcast_fusion.1
  231.2 1.3 dynamic-slice_select_fusion.1
  233.4 1.3 dynamic-slice_select_fusion.3
  (112 shorter events, 21.4 us)
Async XLA Ops:
  0.6 9.2 %copy-start.4 = (f32[2,4,64,256]{3,2,1,0:T(8,128)S(1)}, f32[2,4,64,256]{3,2,1,0:T(8,128)}, u32[]{:S(2)}) copy-start(f32[2,4,64,256]{3,2,1,0:T(8,128)} %temp_ref.1) | copy-start | bytes 1572868
  0.6 14.9 %copy-start.18 = (s32[2]{0:T(128)S(1)}, s32[2]{0:T(128)}, u32[]{:S(2)}) copy-start(s32[2]{0:T(128)} %param.17) | copy-start | bytes 28
  0.7 19.5 %copy-start.17 = (s32[64,256]{1,0:T(8,128)S(1)}, s32[64,256]{1,0:T(8,128)}, u32[]{:S(2)}) copy-start(s32[64,256]{1,0:T(8,128)} %param.16) | copy-start | bytes 196612
  2.7 22.3 %collective-permute-start.1 = (f32[4,2,4,1,256]{4,3,2,1,0:T(1,128)S(1)}, f32[4,2,4,1,256]{4,3,2,1,0:T(1,128)S(1)}, u32[]{:S(2)}, u32[]{:S(2)}) collective-permute-start(f32[4,2,4,1,256]{4,3,2,1,0:T(1,128)S(1)} %pad_maximum_fusion.9), channel_id=1, source_target_pairs={{0,8},{8,16},{16,24},{24,32},{32,40},{40,48},{48,56},{56,0},{1,9},... | collective-permute-start | bytes 98312 | tf_op jit(solution)/shard_map/ppermute | solution.py:439
  2.8 22.8 %collective-permute-start = (f32[4,2,4,1,256]{4,3,2,1,0:T(1,128)S(1)}, f32[4,2,4,1,256]{4,3,2,1,0:T(1,128)S(1)}, u32[]{:S(2)}, u32[]{:S(2)}) collective-permute-start(f32[4,2,4,1,256]{4,3,2,1,0:T(1,128)S(1)} %pad_maximum_fusion.8), channel_id=1, source_target_pairs={{8,0},{16,8},{24,16},{32,24},{40,32},{48,40},{56,48},{0,56},{9,1},... | collective-permute-start | bytes 98312 | tf_op jit(solution)/shard_map/ppermute | solution.py:438
  10.2 11.9 %collective-permute-start.2 = (f32[4,2,4,64,1]{3,2,4,1,0:T(4,128)S(1)}, f32[4,2,4,64,1]{3,2,4,1,0:T(4,128)S(1)}, u32[]{:S(2)}, u32[]{:S(2)}) collective-permute-start(f32[4,2,4,64,1]{3,2,4,1,0:T(4,128)S(1)} %pad_maximum_fusion.12), channel_id=1, source_target_pairs={{1,0},{2,1},{3,2},{4,3},{5,4},{6,5},{7,6},{0,7},{9,8},{10,9},{11,1... | collective-permute-start | bytes 24584 | tf_op jit(solution)/shard_map/ppermute | solution.py:440
  15.4 8.1 %collective-permute-start.3 = (f32[4,2,4,64,1]{3,2,4,1,0:T(4,128)S(1)}, f32[4,2,4,64,1]{3,2,4,1,0:T(4,128)S(1)}, u32[]{:S(2)}, u32[]{:S(2)}) collective-permute-start(f32[4,2,4,64,1]{3,2,4,1,0:T(4,128)S(1)} %pad_maximum_fusion.13), channel_id=1, source_target_pairs={{0,1},{1,2},{2,3},{3,4},{4,5},{5,6},{6,7},{7,0},{8,9},{9,10},{10,1... | collective-permute-start | bytes 24584 | tf_op jit(solution)/shard_map/ppermute | solution.py:441
  26.9 5.0 %copy-start.16 = (f32[2,64,256]{2,1,0:T(8,128)S(1)}, f32[2,64,256]{2,1,0:T(8,128)}, u32[]{:S(2)}) copy-start(f32[2,64,256]{2,1,0:T(8,128)} %param.15) | copy-start | bytes 393220
  31.9 47.7 %copy-start.2 = (f32[64,256]{1,0:T(8,128)S(1)}, f32[64,256]{1,0:T(8,128)}, u32[]{:S(2)}) copy-start(f32[64,256]{1,0:T(8,128)} %convert_element_type.35.ocean_ref) | copy-start | bytes 196612
  31.9 47.7 %copy-start.13 = (f32[2,4,64,256]{3,2,1,0:T(8,128)S(1)}, f32[2,4,64,256]{3,2,1,0:T(8,128)}, u32[]{:S(2)}) copy-start(f32[2,4,64,256]{3,2,1,0:T(8,128)} %get-tuple-element.47) | copy-start | bytes 1572868
  31.9 47.7 %copy-start.14 = (f32[2,4,64,256]{3,2,1,0:T(8,128)S(1)}, f32[2,4,64,256]{3,2,1,0:T(8,128)}, u32[]{:S(2)}) copy-start(f32[2,4,64,256]{3,2,1,0:T(8,128)} %get-tuple-element.50) | copy-start | bytes 1572868
  78.5 2.0 copy-start.5
  79.6 1.3 copy-start.6
  79.8 11.6 %copy-start = (f32[2,4,64,256]{3,2,1,0:T(8,128)}, f32[2,4,64,256]{3,2,1,0:T(8,128)S(1)}, u32[]{:S(2)}) copy-start(f32[2,4,64,256]{3,2,1,0:T(8,128)S(1)} %get-tuple-element.119.vvel_ref) | copy-start | bytes 1572868
  79.8 11.6 %copy-start.1 = (f32[2,4,64,256]{3,2,1,0:T(8,128)}, f32[2,4,64,256]{3,2,1,0:T(8,128)S(1)}, u32[]{:S(2)}) copy-start(f32[2,4,64,256]{3,2,1,0:T(8,128)S(1)} %get-tuple-element.120.uvel_ref) | copy-start | bytes 1572868
  81.3 7.3 %collective-permute-start.7 = (f32[4,2,4,64,1]{3,2,4,1,0:T(4,128)S(1)}, f32[4,2,4,64,1]{3,2,4,1,0:T(4,128)S(1)}, u32[]{:S(2)}, u32[]{:S(2)}) collective-permute-start(f32[4,2,4,64,1]{3,2,4,1,0:T(4,128)S(1)} %pad_maximum_fusion.15), channel_id=1, source_target_pairs={{0,1},{1,2},{2,3},{3,4},{4,5},{5,6},{6,7},{7,0},{8,9},{9,10},{10,1... | collective-permute-start | bytes 24584 | tf_op jit(solution)/shard_map/ppermute | solution.py:441
  82.0 8.0 %collective-permute-start.6 = (f32[4,2,4,64,1]{3,2,4,1,0:T(4,128)S(1)}, f32[4,2,4,64,1]{3,2,4,1,0:T(4,128)S(1)}, u32[]{:S(2)}, u32[]{:S(2)}) collective-permute-start(f32[4,2,4,64,1]{3,2,4,1,0:T(4,128)S(1)} %pad_maximum_fusion.14), channel_id=1, source_target_pairs={{1,0},{2,1},{3,2},{4,3},{5,4},{6,5},{7,6},{0,7},{9,8},{10,9},{11,1... | collective-permute-start | bytes 24584 | tf_op jit(solution)/shard_map/ppermute | solution.py:440
  85.5 5.9 %collective-permute-start.5 = (f32[4,2,4,1,256]{4,3,2,1,0:T(1,128)S(1)}, f32[4,2,4,1,256]{4,3,2,1,0:T(1,128)S(1)}, u32[]{:S(2)}, u32[]{:S(2)}) collective-permute-start(f32[4,2,4,1,256]{4,3,2,1,0:T(1,128)S(1)} %pad_maximum_fusion.11), channel_id=1, source_target_pairs={{0,8},{8,16},{16,24},{24,32},{32,40},{40,48},{48,56},{56,0},{1,9},... | collective-permute-start | bytes 98312 | tf_op jit(solution)/shard_map/ppermute | solution.py:439
  85.6 6.4 %collective-permute-start.4 = (f32[4,2,4,1,256]{4,3,2,1,0:T(1,128)S(1)}, f32[4,2,4,1,256]{4,3,2,1,0:T(1,128)S(1)}, u32[]{:S(2)}, u32[]{:S(2)}) collective-permute-start(f32[4,2,4,1,256]{4,3,2,1,0:T(1,128)S(1)} %pad_maximum_fusion.10), channel_id=1, source_target_pairs={{8,0},{16,8},{24,16},{32,24},{40,32},{48,40},{56,48},{0,56},{9,1},... | collective-permute-start | bytes 98312 | tf_op jit(solution)/shard_map/ppermute | solution.py:438
  102.4 91.0 %copy-start.3 = (f32[64,256]{1,0:T(8,128)S(1)}, f32[64,256]{1,0:T(8,128)}, u32[]{:S(2)}) copy-start(f32[64,256]{1,0:T(8,128)} %convert_element_type.35.ocean_ref) | copy-start | bytes 196612
  102.4 91.0 %copy-start.11 = (f32[2,4,64,256]{3,2,1,0:T(8,128)S(1)}, f32[2,4,64,256]{3,2,1,0:T(8,128)}, u32[]{:S(2)}) copy-start(f32[2,4,64,256]{3,2,1,0:T(8,128)} %get-tuple-element.56) | copy-start | bytes 1572868
  189.7 23.4 %copy-start.7 = (f32[4,2,4,64,256]{4,3,2,1,0:T(8,128)S(1)}, f32[4,2,4,64,256]{4,3,2,1,0:T(8,128)}, u32[]{:S(2)}) copy-start(f32[4,2,4,64,256]{4,3,2,1,0:T(8,128)} %get-tuple-element.57) | copy-start | bytes 6291460
  208.2 7.9 %copy-start.9 = (f32[2,4,64,256]{3,2,1,0:T(8,128)S(1)}, f32[2,4,64,256]{3,2,1,0:T(8,128)}, u32[]{:S(2)}) copy-start(f32[2,4,64,256]{3,2,1,0:T(8,128)} %get-tuple-element.51) | copy-start | bytes 1572868
  210.1 14.7 %collective-permute-start.8 = (f32[2,4,64,256]{3,2,1,0:T(8,128)}, f32[2,4,64,256]{3,2,1,0:T(8,128)}, u32[]{:S(2)}, u32[]{:S(2)}) collective-permute-start(f32[2,4,64,256]{3,2,1,0:T(8,128)} %select_maximum_fusion), channel_id=1, source_target_pairs={{0,64},{64,0},{1,65},{65,1},{2,66},{66,2},{3,67},{67,3},{4,68},{68... | collective-permute-start | bytes 1572872 | tf_op jit(solution)/shard_map/ppermute | solution.py:615
  213.0 1.0 copy-start.10
  218.2 12.8 %copy-start.8 = (f32[2,4,64,256]{3,2,1,0:T(8,128)S(1)}, f32[2,4,64,256]{3,2,1,0:T(8,128)}, u32[]{:S(2)}) copy-start(f32[2,4,64,256]{3,2,1,0:T(8,128)} %get-tuple-element.55) | copy-start | bytes 1572868
  220.2 9.0 %copy-start.15 = (f32[1,2,64,256]{3,2,1,0:T(8,128)S(1)}, f32[1,2,64,256]{3,2,1,0:T(8,128)}, u32[]{:S(2)}) copy-start(f32[1,2,64,256]{3,2,1,0:T(8,128)} %get-tuple-element.110) | copy-start | bytes 393220
  220.2 10.9 %copy-start.12 = (f32[2,64,256]{2,1,0:T(8,128)S(1)}, f32[2,64,256]{2,1,0:T(8,128)}, u32[]{:S(2)}) copy-start(f32[2,64,256]{2,1,0:T(8,128)} %get-tuple-element.112) | copy-start | bytes 393220

commit v8 on v7

--- a/solution.py
+++ b/solution.py
@@ -179,12 +179,18 @@
         partner = (lax.axis_index("member") + 1) % 2
         pl.semaphore_signal(barrier, 1, device_id=(partner, my, mx), device_id_type=mesh_id)
     pl.semaphore_wait(barrier, (ny - 1) + (nx - 1) + 4 + (1 if carry else 0))
+    cargo_copies = []
     if carry:
-        cargo_copy = pltpu.make_async_remote_copy(
-            src_ref=cargo_ref, dst_ref=cargo_out, send_sem=csem.at[0], recv_sem=csem.at[1],
-            device_id=(partner, my, mx), device_id_type=mesh_id,
-        )
-        cargo_copy.start()
+        for part in range(cargo_ref.shape[0]):
+            for half in range(cargo_ref.shape[1]):
+                piece = part * cargo_ref.shape[1] + half
+                copy = pltpu.make_async_remote_copy(
+                    src_ref=cargo_ref.at[part, half], dst_ref=cargo_out.at[part, half],
+                    send_sem=csem.at[0, piece], recv_sem=csem.at[1, piece],
+                    device_id=(partner, my, mx), device_id_type=mesh_id,
+                )
+                copy.start()
+                cargo_copies.append(copy)
 
     def halo_copies(first, moves):
         started = []
@@ -287,8 +293,8 @@
         out_ref[0, m] = x[0:rows, 0:cols]
         out_ref[1, m] = (east(x) - west(x))[0:rows, 0:cols]
         out_ref[2, m] = (north(x) - south(x))[0:rows, 0:cols]
-    if carry:
-        cargo_copy.wait()
+    for copy in cargo_copies:
+        copy.wait()
 
 
 def surface_kernel_solve(surf, inside, own, cargo=None):
@@ -310,7 +316,7 @@
             pltpu.SemaphoreType.DMA((8,)),
             pltpu.SemaphoreType.DMA((8,)),
         ]
-        + ([pltpu.SemaphoreType.DMA((2,))] if carry else [])
+        + ([pltpu.SemaphoreType.DMA((2, cargo.shape[0] * cargo.shape[1]))] if carry else [])
         + [
             pltpu.VMEM((ITERS, 8, 128), jnp.float32),
             pltpu.VMEM((ITERS, ny, 8, 128), jnp.float32),

time: 236 us -> 237 us (level)
  no operation moved by 1% of the time
where the time goes in v8:
time: 237 us; the launch traced here: 236 us
  Pallas kernels  154 us (65%)
  other arithmetic  34.7 us (15%)
  local copies, waits for them, and re-layouts  20.7 us (9%)
  starting transfers between devices  18.2 us (8%)
  between operations  5.69 us (2%)
    pallas_call x2, Pallas kernels, surface_kernel_solve(): pl.pallas_call(functools.partial(solve_kernel, ny, nx, carry), out_shape=...  132 us
    pallas_call x1, Pallas kernels, grid_sum(): pl.pallas_call(functools.partial(gather_sum_kernel, ny, nx), out_shape=ja...  12.2 us
    pallas_call x2, Pallas kernels, volume_step(): pl.pallas_call(volume_kernel, grid=(members,), in_specs=[field] * 4 + [pl...  9.91 us
    ppermute x2, starting transfers between devices, exchange_fields(): lax.ppermute(jnp.stack([f[..., :, :1] for f in fields]), 'gridx', bwd_x)  8.68 us
    select_n x5, other arithmetic, pick(): chosen.append(jnp.where(here[place], from_here, from_other))  8.02 us
    another operation x5, other arithmetic, pick(): return jnp.stack(chosen)  6.05 us
    ppermute x2, starting transfers between devices, exchange_fields(): lax.ppermute(jnp.stack([f[..., :1, :] for f in fields]), 'gridy', bwd_y)  5.89 us
    slice x8, local copies, waits for them, and re-layouts, exchange_fields(): f[..., :, -1:]  5.8 us
  transfers between devices with their start and end apart: 9, of which 1 were waited for; matrix products, arithmetic and copies ran while one was open for 10% of the time, Pallas kernels for 0%

profile of v8, /device:TPU:0, one launch (start us, length us, event | category | flops | bytes accessed | tf_op | source)
XLA Modules:
  0.0 235.7 jit_solution(17471639671048193855)
XLA Ops:
  2.8 2.9 %collective-permute-start = (f32[4,2,4,1,256]{4,3,2,1,0:T(1,128)S(1)}, f32[4,2,4,1,256]{4,3,2,1,0:T(1,128)S(1)}, u32[]{:S(2)}, u32[]{:S(2)}) collective-permute-start(f32[4,2,4,1,256]{4,3,2,1,0:T(1,128)S(1)} %pad_maximum_fusion.8), channel_id=1, source_target_pairs={{8,0},{16,8},{24,16},{32,24},{40,32},{48,40},{56,48},{0,56},{9,1},... | collective-permute-start | bytes 98312 | tf_op jit(solution)/shard_map/ppermute | solution.py:444
  5.7 1.4 slice_reduce_fusion.10
  7.1 1.4 slice_reduce_fusion.9
  8.5 1.4 slice_reduce_fusion.8
  10.2 5.2 %collective-permute-start.2 = (f32[4,2,4,64,1]{3,2,4,1,0:T(4,128)S(1)}, f32[4,2,4,64,1]{3,2,4,1,0:T(4,128)S(1)}, u32[]{:S(2)}, u32[]{:S(2)}) collective-permute-start(f32[4,2,4,64,1]{3,2,4,1,0:T(4,128)S(1)} %pad_maximum_fusion.12), channel_id=1, source_target_pairs={{1,0},{2,1},{3,2},{4,3},{5,4},{6,5},{7,6},{0,7},{9,8},{10,9},{11,1... | collective-permute-start | bytes 24584 | tf_op jit(solution)/shard_map/ppermute | solution.py:446
  22.1 1.4 copy.143.e_ref
  23.5 1.4 copy.144.w_ref
  26.9 5.0 %shard_map.126 = (f32[2,4,64,256]{3,2,1,0:T(8,128)}, f32[2,4,64,256]{3,2,1,0:T(8,128)}, f32[2,4,64,256]{3,2,1,0:T(8,128)}, f32[2,4,64,256]{3,2,1,0:T(8,128)}, f3...) custom-call(f32[2,4,64,256]{3,2,1,0:T(8,128)} %temp_ref.1, f32[2,4,64,256]{3,2,1,0:T(8,128)} %salt_ref.1, ...), custom_call_target="tpu_custom_call" | custom-call | tf_op jit(solution)/shard_map/pallas_call | solution.py:413
  31.9 1.8 pad_maximum_fusion.5.refs_0_
  33.8 44.7 %shard_map.127 = f32[3,2,64,256]{3,2,1,0:T(8,128)} custom-call(f32[3,2,64,256]{3,2,1,0:T(8,128)} %pad_maximum_fusion.5.refs_0_, f32[80,512]{1,0:T(8,128)} %get-tuple-element.133.refs_1_, f32[80,512]{1,0:T(8,128)} %get-tuple-element.134.refs_2_), custom_call_target="tpu_custom_call" | custom-call | tf_op jit(solution)/shard_map/pallas_call | solution.py:309
  78.5 1.1 multiply_bitcast_fusion.2
  82.0 3.5 %collective-permute-start.6 = (f32[4,2,4,64,1]{3,2,4,1,0:T(4,128)S(1)}, f32[4,2,4,64,1]{3,2,4,1,0:T(4,128)S(1)}, u32[]{:S(2)}, u32[]{:S(2)}) collective-permute-start(f32[4,2,4,64,1]{3,2,4,1,0:T(4,128)S(1)} %pad_maximum_fusion.14), channel_id=1, source_target_pairs={{1,0},{2,1},{3,2},{4,3},{5,4},{6,5},{7,6},{0,7},{9,8},{10,9},{11,1... | collective-permute-start | bytes 24584 | tf_op jit(solution)/shard_map/ppermute | solution.py:446
  85.6 2.9 %collective-permute-start.4 = (f32[4,2,4,1,256]{4,3,2,1,0:T(1,128)S(1)}, f32[4,2,4,1,256]{4,3,2,1,0:T(1,128)S(1)}, u32[]{:S(2)}, u32[]{:S(2)}) collective-permute-start(f32[4,2,4,1,256]{4,3,2,1,0:T(1,128)S(1)} %pad_maximum_fusion.10), channel_id=1, source_target_pairs={{8,0},{16,8},{24,16},{32,24},{40,32},{48,40},{56,48},{0,56},{9,1},... | collective-permute-start | bytes 98312 | tf_op jit(solution)/shard_map/ppermute | solution.py:444
  88.5 1.4 copy.156.w_ref
  90.0 1.4 copy.155.e_ref
  92.6 5.0 %shard_map.128 = (f32[2,4,64,256]{3,2,1,0:T(8,128)}, f32[2,4,64,256]{3,2,1,0:T(8,128)}, f32[2,4,64,256]{3,2,1,0:T(8,128)}, f32[2,4,64,256]{3,2,1,0:T(8,128)}, f3...) custom-call(f32[2,4,64,256]{3,2,1,0:T(8,128)} %get-tuple-element.45.temp_ref, f32[2,4,64,256]{3,2,1,0:T(8,128)} %get-tuple-element.46.salt_ref, ...), custom_call_target="tpu_custom_call" | custom-call | tf_op jit(solution)/shard_map/pallas_call | solution.py:413
  97.6 1.7 pad_maximum_fusion.6.refs_0_
  99.3 3.0 %pad_maximum_fusion.refs_3_ = f32[4,2,4,64,256]{4,3,2,1,0:T(8,128)} fusion(f32[1,2,4,64,256]{4,3,2,1,0:T(8,128)} %bitcast.136, f32[1,2,4,64,256]{4,3,2,1,0:T(8,128)} %bitcast.133, f32[1,2,4,64,256]{4,3,2,1,0:T(8,128)} %bitcast.135, f32[1,2,4,64,256]{4,3,2,1,0:T(8,128)} %bitcast.134), kind=kLoop, calls=%fused_computation.1 | loop fusion | flops 1572864 | bytes 4194304 | tf_op jit(solution)/shard_map/stack | solution.py:591
  102.4 87.4 %shard_map.129 = (f32[3,2,64,256]{3,2,1,0:T(8,128)}, f32[4,2,4,64,256]{4,3,2,1,0:T(8,128)}) custom-call(f32[3,2,64,256]{3,2,1,0:T(8,128)} %pad_maximum_fusion.6.refs_0_, f32[80,512]{1,0:T(8,128)} %get-tuple-element.133.refs_1_, f32[80,512]{1,0:T(8,128)} %get-tuple-element.134.refs_2_, f32[4,2,4,64,256]{4,3,2,1,0:T(8,128)} %pad_maximum_fusion.refs_3_), custom_call_target="tpu_custom_call" | custom-call | tf_op jit(solution)/shard_map/pallas_call | solution.py:309
  189.8 1.9 fusion.17
  191.7 1.8 copy.160
  194.6 12.2 %shard_map.130 = f32[40,128]{1,0:T(8,128)} custom-call(f32[40,128]{1,0:T(8,128)} %select_maximum_fusion.1.x_ref), custom_call_target="tpu_custom_call" | custom-call | tf_op jit(solution)/shard_map/pallas_call | solution.py:90
  208.3 1.9 select_maximum_fusion
  210.2 2.9 %collective-permute-start.8 = (f32[2,4,64,256]{3,2,1,0:T(8,128)}, f32[2,4,64,256]{3,2,1,0:T(8,128)}, u32[]{:S(2)}, u32[]{:S(2)}) collective-permute-start(f32[2,4,64,256]{3,2,1,0:T(8,128)} %select_maximum_fusion), channel_id=1, source_target_pairs={{0,64},{64,0},{1,65},{65,1},{2,66},{66,2},{3,67},{67,3},{4,68},{68... | collective-permute-start | bytes 1572872 | tf_op jit(solution)/shard_map/ppermute | solution.py:621
  214.2 2.0 bitcast_select_fusion.1
  216.3 2.1 bitcast_select_fusion.3
  218.5 1.8 pad_maximum_fusion.2
  220.3 1.9 pad_maximum_fusion.1
  222.8 2.1 collective-permute-done.8
  229.3 1.3 select_bitcast_fusion.1
  231.4 1.3 dynamic-slice_select_fusion.1
  233.5 1.3 dynamic-slice_select_fusion.3
  (112 shorter events, 21.4 us)
Async XLA Ops:
  0.6 9.2 %copy-start.4 = (f32[2,4,64,256]{3,2,1,0:T(8,128)S(1)}, f32[2,4,64,256]{3,2,1,0:T(8,128)}, u32[]{:S(2)}) copy-start(f32[2,4,64,256]{3,2,1,0:T(8,128)} %temp_ref.1) | copy-start | bytes 1572868
  0.6 14.9 %copy-start.18 = (s32[2]{0:T(128)S(1)}, s32[2]{0:T(128)}, u32[]{:S(2)}) copy-start(s32[2]{0:T(128)} %param.17) | copy-start | bytes 28
  0.7 19.5 %copy-start.17 = (s32[64,256]{1,0:T(8,128)S(1)}, s32[64,256]{1,0:T(8,128)}, u32[]{:S(2)}) copy-start(s32[64,256]{1,0:T(8,128)} %param.16) | copy-start | bytes 196612
  2.7 22.3 %collective-permute-start.1 = (f32[4,2,4,1,256]{4,3,2,1,0:T(1,128)S(1)}, f32[4,2,4,1,256]{4,3,2,1,0:T(1,128)S(1)}, u32[]{:S(2)}, u32[]{:S(2)}) collective-permute-start(f32[4,2,4,1,256]{4,3,2,1,0:T(1,128)S(1)} %pad_maximum_fusion.9), channel_id=1, source_target_pairs={{0,8},{8,16},{16,24},{24,32},{32,40},{40,48},{48,56},{56,0},{1,9},... | collective-permute-start | bytes 98312 | tf_op jit(solution)/shard_map/ppermute | solution.py:445
  2.8 22.8 %collective-permute-start = (f32[4,2,4,1,256]{4,3,2,1,0:T(1,128)S(1)}, f32[4,2,4,1,256]{4,3,2,1,0:T(1,128)S(1)}, u32[]{:S(2)}, u32[]{:S(2)}) collective-permute-start(f32[4,2,4,1,256]{4,3,2,1,0:T(1,128)S(1)} %pad_maximum_fusion.8), channel_id=1, source_target_pairs={{8,0},{16,8},{24,16},{32,24},{40,32},{48,40},{56,48},{0,56},{9,1},... | collective-permute-start | bytes 98312 | tf_op jit(solution)/shard_map/ppermute | solution.py:444
  10.2 11.9 %collective-permute-start.2 = (f32[4,2,4,64,1]{3,2,4,1,0:T(4,128)S(1)}, f32[4,2,4,64,1]{3,2,4,1,0:T(4,128)S(1)}, u32[]{:S(2)}, u32[]{:S(2)}) collective-permute-start(f32[4,2,4,64,1]{3,2,4,1,0:T(4,128)S(1)} %pad_maximum_fusion.12), channel_id=1, source_target_pairs={{1,0},{2,1},{3,2},{4,3},{5,4},{6,5},{7,6},{0,7},{9,8},{10,9},{11,1... | collective-permute-start | bytes 24584 | tf_op jit(solution)/shard_map/ppermute | solution.py:446
  15.4 8.1 %collective-permute-start.3 = (f32[4,2,4,64,1]{3,2,4,1,0:T(4,128)S(1)}, f32[4,2,4,64,1]{3,2,4,1,0:T(4,128)S(1)}, u32[]{:S(2)}, u32[]{:S(2)}) collective-permute-start(f32[4,2,4,64,1]{3,2,4,1,0:T(4,128)S(1)} %pad_maximum_fusion.13), channel_id=1, source_target_pairs={{0,1},{1,2},{2,3},{3,4},{4,5},{5,6},{6,7},{7,0},{8,9},{9,10},{10,1... | collective-permute-start | bytes 24584 | tf_op jit(solution)/shard_map/ppermute | solution.py:447
  26.9 5.0 %copy-start.16 = (f32[2,64,256]{2,1,0:T(8,128)S(1)}, f32[2,64,256]{2,1,0:T(8,128)}, u32[]{:S(2)}) copy-start(f32[2,64,256]{2,1,0:T(8,128)} %param.15) | copy-start | bytes 393220
  31.9 47.7 %copy-start.2 = (f32[64,256]{1,0:T(8,128)S(1)}, f32[64,256]{1,0:T(8,128)}, u32[]{:S(2)}) copy-start(f32[64,256]{1,0:T(8,128)} %convert_element_type.35.ocean_ref) | copy-start | bytes 196612
  31.9 47.7 %copy-start.13 = (f32[2,4,64,256]{3,2,1,0:T(8,128)S(1)}, f32[2,4,64,256]{3,2,1,0:T(8,128)}, u32[]{:S(2)}) copy-start(f32[2,4,64,256]{3,2,1,0:T(8,128)} %get-tuple-element.47) | copy-start | bytes 1572868
  31.9 47.7 %copy-start.14 = (f32[2,4,64,256]{3,2,1,0:T(8,128)S(1)}, f32[2,4,64,256]{3,2,1,0:T(8,128)}, u32[]{:S(2)}) copy-start(f32[2,4,64,256]{3,2,1,0:T(8,128)} %get-tuple-element.50) | copy-start | bytes 1572868
  78.5 2.0 copy-start.5
  79.6 1.3 copy-start.6
  79.8 11.6 %copy-start = (f32[2,4,64,256]{3,2,1,0:T(8,128)}, f32[2,4,64,256]{3,2,1,0:T(8,128)S(1)}, u32[]{:S(2)}) copy-start(f32[2,4,64,256]{3,2,1,0:T(8,128)S(1)} %get-tuple-element.119.vvel_ref) | copy-start | bytes 1572868
  79.8 11.6 %copy-start.1 = (f32[2,4,64,256]{3,2,1,0:T(8,128)}, f32[2,4,64,256]{3,2,1,0:T(8,128)S(1)}, u32[]{:S(2)}) copy-start(f32[2,4,64,256]{3,2,1,0:T(8,128)S(1)} %get-tuple-element.120.uvel_ref) | copy-start | bytes 1572868
  81.3 7.3 %collective-permute-start.7 = (f32[4,2,4,64,1]{3,2,4,1,0:T(4,128)S(1)}, f32[4,2,4,64,1]{3,2,4,1,0:T(4,128)S(1)}, u32[]{:S(2)}, u32[]{:S(2)}) collective-permute-start(f32[4,2,4,64,1]{3,2,4,1,0:T(4,128)S(1)} %pad_maximum_fusion.15), channel_id=1, source_target_pairs={{0,1},{1,2},{2,3},{3,4},{4,5},{5,6},{6,7},{7,0},{8,9},{9,10},{10,1... | collective-permute-start | bytes 24584 | tf_op jit(solution)/shard_map/ppermute | solution.py:447
  82.0 8.0 %collective-permute-start.6 = (f32[4,2,4,64,1]{3,2,4,1,0:T(4,128)S(1)}, f32[4,2,4,64,1]{3,2,4,1,0:T(4,128)S(1)}, u32[]{:S(2)}, u32[]{:S(2)}) collective-permute-start(f32[4,2,4,64,1]{3,2,4,1,0:T(4,128)S(1)} %pad_maximum_fusion.14), channel_id=1, source_target_pairs={{1,0},{2,1},{3,2},{4,3},{5,4},{6,5},{7,6},{0,7},{9,8},{10,9},{11,1... | collective-permute-start | bytes 24584 | tf_op jit(solution)/shard_map/ppermute | solution.py:446
  85.5 5.9 %collective-permute-start.5 = (f32[4,2,4,1,256]{4,3,2,1,0:T(1,128)S(1)}, f32[4,2,4,1,256]{4,3,2,1,0:T(1,128)S(1)}, u32[]{:S(2)}, u32[]{:S(2)}) collective-permute-start(f32[4,2,4,1,256]{4,3,2,1,0:T(1,128)S(1)} %pad_maximum_fusion.11), channel_id=1, source_target_pairs={{0,8},{8,16},{16,24},{24,32},{32,40},{40,48},{48,56},{56,0},{1,9},... | collective-permute-start | bytes 98312 | tf_op jit(solution)/shard_map/ppermute | solution.py:445
  85.6 6.4 %collective-permute-start.4 = (f32[4,2,4,1,256]{4,3,2,1,0:T(1,128)S(1)}, f32[4,2,4,1,256]{4,3,2,1,0:T(1,128)S(1)}, u32[]{:S(2)}, u32[]{:S(2)}) collective-permute-start(f32[4,2,4,1,256]{4,3,2,1,0:T(1,128)S(1)} %pad_maximum_fusion.10), channel_id=1, source_target_pairs={{8,0},{16,8},{24,16},{32,24},{40,32},{48,40},{56,48},{0,56},{9,1},... | collective-permute-start | bytes 98312 | tf_op jit(solution)/shard_map/ppermute | solution.py:444
  102.4 91.1 %copy-start.3 = (f32[64,256]{1,0:T(8,128)S(1)}, f32[64,256]{1,0:T(8,128)}, u32[]{:S(2)}) copy-start(f32[64,256]{1,0:T(8,128)} %convert_element_type.35.ocean_ref) | copy-start | bytes 196612
  102.4 91.1 %copy-start.11 = (f32[2,4,64,256]{3,2,1,0:T(8,128)S(1)}, f32[2,4,64,256]{3,2,1,0:T(8,128)}, u32[]{:S(2)}) copy-start(f32[2,4,64,256]{3,2,1,0:T(8,128)} %get-tuple-element.56) | copy-start | bytes 1572868
  189.8 23.4 %copy-start.7 = (f32[4,2,4,64,256]{4,3,2,1,0:T(8,128)S(1)}, f32[4,2,4,64,256]{4,3,2,1,0:T(8,128)}, u32[]{:S(2)}) copy-start(f32[4,2,4,64,256]{4,3,2,1,0:T(8,128)} %get-tuple-element.57) | copy-start | bytes 6291460
  208.3 7.9 %copy-start.9 = (f32[2,4,64,256]{3,2,1,0:T(8,128)S(1)}, f32[2,4,64,256]{3,2,1,0:T(8,128)}, u32[]{:S(2)}) copy-start(f32[2,4,64,256]{3,2,1,0:T(8,128)} %get-tuple-element.51) | copy-start | bytes 1572868
  210.2 14.7 %collective-permute-start.8 = (f32[2,4,64,256]{3,2,1,0:T(8,128)}, f32[2,4,64,256]{3,2,1,0:T(8,128)}, u32[]{:S(2)}, u32[]{:S(2)}) collective-permute-start(f32[2,4,64,256]{3,2,1,0:T(8,128)} %select_maximum_fusion), channel_id=1, source_target_pairs={{0,64},{64,0},{1,65},{65,1},{2,66},{66,2},{3,67},{67,3},{4,68},{68... | collective-permute-start | bytes 1572872 | tf_op jit(solution)/shard_map/ppermute | solution.py:621
  213.2 1.0 copy-start.10
  218.4 12.9 %copy-start.8 = (f32[2,4,64,256]{3,2,1,0:T(8,128)S(1)}, f32[2,4,64,256]{3,2,1,0:T(8,128)}, u32[]{:S(2)}) copy-start(f32[2,4,64,256]{3,2,1,0:T(8,128)} %get-tuple-element.55) | copy-start | bytes 1572868
  220.3 9.0 %copy-start.15 = (f32[1,2,64,256]{3,2,1,0:T(8,128)S(1)}, f32[1,2,64,256]{3,2,1,0:T(8,128)}, u32[]{:S(2)}) copy-start(f32[1,2,64,256]{3,2,1,0:T(8,128)} %get-tuple-element.110) | copy-start | bytes 393220
  220.3 10.9 %copy-start.12 = (f32[2,64,256]{2,1,0:T(8,128)S(1)}, f32[2,64,256]{2,1,0:T(8,128)}, u32[]{:S(2)}) copy-start(f32[2,64,256]{2,1,0:T(8,128)} %get-tuple-element.112) | copy-start | bytes 393220

commit v9 on v6

--- a/solution.py
+++ b/solution.py
@@ -106,45 +106,41 @@
 
 
 def exchange_sum(k, vec, ny, nx, bufs, device_ids):
-    send_y, recv_y, send_x, recv_x, sy, ry, sx, rx = bufs
-    my, mx, along_y, along_x = device_ids
+    send_buf, recv, send_sem, recv_sem = bufs
+    me, device = device_ids
+    count = ny * nx
     mesh_id = pl.DeviceIdType.MESH
-
-    def phase(value, send_buf, recv, send_sem, recv_sem, count, me, device):
-        send_buf[k] = value
-        recv[k, me] = value
-        sent = []
-        for d in range(1, count):
-            peer = (me + d) % count
-            copy = pltpu.make_async_remote_copy(
-                src_ref=send_buf.at[k],
-                dst_ref=recv.at[k, me],
-                send_sem=send_sem.at[k, peer],
-                recv_sem=recv_sem.at[k, me],
-                device_id=device(peer),
-                device_id_type=mesh_id,
-            )
-            copy.start()
-            sent.append(copy)
-        for d in range(1, count):
-            peer = (me + d) % count
-            pltpu.make_async_remote_copy(
-                src_ref=send_buf.at[k],
-                dst_ref=recv.at[k, peer],
-                send_sem=send_sem.at[k, peer],
-                recv_sem=recv_sem.at[k, peer],
-                device_id=device(peer),
-                device_id_type=mesh_id,
-            ).wait_recv()
-        for copy in sent:
-            copy.wait_send()
-        total = recv[k, 0]
-        for j in range(1, count):
-            total = total + recv[k, j]
-        return total
-
-    partial = phase(vec, send_y, recv_y, sy, ry, ny, my, along_y)
-    return phase(partial, send_x, recv_x, sx, rx, nx, mx, along_x)
+    send_buf[k] = vec
+    recv[k, me] = vec
+    sent = []
+    for d in range(1, count):
+        peer = (me + d) % count
+        copy = pltpu.make_async_remote_copy(
+            src_ref=send_buf.at[k],
+            dst_ref=recv.at[k, me],
+            send_sem=send_sem.at[k, peer],
+            recv_sem=recv_sem.at[k, me],
+            device_id=device(peer),
+            device_id_type=mesh_id,
+        )
+        copy.start()
+        sent.append(copy)
+    for d in range(1, count):
+        peer = (me + d) % count
+        pltpu.make_async_remote_copy(
+            src_ref=send_buf.at[k],
+            dst_ref=recv.at[k, peer],
+            send_sem=send_sem.at[k, peer],
+            recv_sem=recv_sem.at[k, peer],
+            device_id=device(peer),
+            device_id_type=mesh_id,
+        ).wait_recv()
+    for copy in sent:
+        copy.wait_send()
+    total = recv[k, 0]
+    for j in range(1, count):
+        total = total + recv[k, j]
+    return total
 
 
 def solve_kernel(ny, nx, surf_ref, inside_ref, own_ref, out_ref, frame, hsend, hrecv, *bufs):
@@ -154,22 +150,18 @@
     mx = lax.axis_index("gridx")
     along_y = lambda p: (member, p, mx)
     along_x = lambda p: (member, my, p)
+    group_size = ny * nx
+    me = my * nx + mx
+    group = lambda q: (member, q // nx, q % nx)
     barrier = pltpu.get_barrier_semaphore()
-    for d in range(1, ny):
-        pl.semaphore_signal(barrier, 1, device_id=along_y((my + d) % ny), device_id_type=mesh_id)
-    for d in range(1, nx):
-        pl.semaphore_signal(barrier, 1, device_id=along_x((mx + d) % nx), device_id_type=mesh_id)
-    for dy in (1, ny - 1):
-        for dx in (1, nx - 1):
-            pl.semaphore_signal(
-                barrier, 1, device_id=(member, (my + dy) % ny, (mx + dx) % nx), device_id_type=mesh_id
-            )
+    for d in range(1, group_size):
+        pl.semaphore_signal(barrier, 1, device_id=group((me + d) % group_size), device_id_type=mesh_id)
     rows, cols = surf_ref.shape[2], surf_ref.shape[3]
     wide_rows, wide_cols = frame.shape[2], frame.shape[3]
     band = (wide_rows - rows) // 2
     block = (wide_cols - cols) // 2
     frame[:, :, 0:rows, 0:cols] = surf_ref[...]
-    pl.semaphore_wait(barrier, (ny - 1) + (nx - 1) + 4)
+    pl.semaphore_wait(barrier, group_size - 1)
 
     def halo_copies(first, moves):
         started = []
@@ -248,7 +240,7 @@
         for m in range(members):
             vec = jnp.where(lane == 2 * m, total(residual[m] * residual[m]), vec)
             vec = jnp.where(lane == 2 * m + 1, total(residual[m] * image_res[m]), vec)
-        sums = exchange_sum(count, vec, ny, nx, bufs, (my, mx, along_y, along_x))
+        sums = exchange_sum(count, vec, ny, nx, bufs, (me, group))
         for m in range(members):
             gamma = sums[0:1, 2 * m : 2 * m + 1]
             delta = sums[0:1, 2 * m + 1 : 2 * m + 2]
@@ -288,13 +280,9 @@
             pltpu.SemaphoreType.DMA((8,)),
             pltpu.SemaphoreType.DMA((8,)),
             pltpu.VMEM((ITERS, 8, 128), jnp.float32),
-            pltpu.VMEM((ITERS, ny, 8, 128), jnp.float32),
-            pltpu.VMEM((ITERS, 8, 128), jnp.float32),
-            pltpu.VMEM((ITERS, nx, 8, 128), jnp.float32),
-            pltpu.SemaphoreType.DMA((ITERS, ny)),
-            pltpu.SemaphoreType.DMA((ITERS, ny)),
-            pltpu.SemaphoreType.DMA((ITERS, nx)),
-            pltpu.SemaphoreType.DMA((ITERS, nx)),
+            pltpu.VMEM((ITERS, ny * nx, 8, 128), jnp.float32),
+            pltpu.SemaphoreType.DMA((ITERS, ny * nx)),
+            pltpu.SemaphoreType.DMA((ITERS, ny * nx)),
         ],
         compiler_params=pltpu.CompilerParams(collective_id=1, has_side_effects=True),
     )(surf, inside, own)

time: 216 us -> 224 us (1.037)
  Pallas kernels: 122 us -> 129 us
    pallas_call x2, Pallas kernels: 86.8 us -> 91.4 us  [surface_kernel_solve(): pl.pallas_call(functools.partial(solve_kernel, ny, nx), out_shape=jax.Sha...]
where the time goes in v9:
time: 224 us; the launch traced here: 223 us
  Pallas kernels  129 us (58%)
  other arithmetic  26.6 us (12%)
  local copies, waits for them, and re-layouts  21.4 us (10%)
  starting transfers between devices  20.2 us (9%)
  waiting for transfers between devices  19.9 us (9%)
  between operations  5.75 us (3%)
    pallas_call x2, Pallas kernels, surface_kernel_solve(): pl.pallas_call(functools.partial(solve_kernel, ny, nx), out_shape=jax.Sha...  91.4 us
    pallas_call x1, Pallas kernels, grid_sum(): pl.pallas_call(functools.partial(gather_sum_kernel, ny, nx), out_shape=ja...  27.7 us
    ppermute x1, waiting for transfers between devices, shards(): flows_other = lax.ppermute(flows, 'member', swap)  19.9 us
    pallas_call x2, Pallas kernels, volume_step(): pl.pallas_call(volume_kernel, grid=(members,), in_specs=[field] * 4 + [pl...  9.92 us
    ppermute x2, starting transfers between devices, exchange_fields(): lax.ppermute(jnp.stack([f[..., :, :1] for f in fields]), 'gridx', bwd_x)  8.6 us
    ppermute x2, starting transfers between devices, exchange_fields(): lax.ppermute(jnp.stack([f[..., :1, :] for f in fields]), 'gridy', bwd_y)  5.89 us
    slice x8, local copies, waits for them, and re-layouts, exchange_fields(): f[..., :, -1:]  4.77 us
  transfers between devices with their start and end apart: 10, of which 1 were waited for; matrix products, arithmetic and copies ran while one was open for 12% of the time, Pallas kernels for 12%

profile of v9, /device:TPU:0, one launch (start us, length us, event | category | flops | bytes accessed | tf_op | source)
XLA Modules:
  0.0 222.8 jit_solution(3112103472534537554)
XLA Ops:
  0.7 1.0 slice_bitcast_fusion.11
  2.8 2.9 %collective-permute-start = (f32[4,2,4,1,256]{4,3,2,1,0:T(1,128)S(1)}, f32[4,2,4,1,256]{4,3,2,1,0:T(1,128)S(1)}, u32[]{:S(2)}, u32[]{:S(2)}) collective-permute-start(f32[4,2,4,1,256]{4,3,2,1,0:T(1,128)S(1)} %pad_maximum_fusion.7), channel_id=1, source_target_pairs={{8,0},{16,8},{24,16},{32,24},{40,32},{48,40},{56,48},{0,56},{9,1},... | collective-permute-start | bytes 98312 | tf_op jit(solution)/shard_map/ppermute | solution.py:400
  5.8 1.4 slice_reduce_fusion.10
  7.1 1.4 slice_reduce_fusion.9
  9.2 5.2 %collective-permute-start.2 = (f32[4,2,4,64,1]{3,2,4,1,0:T(4,128)S(1)}, f32[4,2,4,64,1]{3,2,4,1,0:T(4,128)S(1)}, u32[]{:S(2)}, u32[]{:S(2)}) collective-permute-start(f32[4,2,4,64,1]{3,2,4,1,0:T(4,128)S(1)} %pad_maximum_fusion.11), channel_id=1, source_target_pairs={{1,0},{2,1},{3,2},{4,3},{5,4},{6,5},{7,6},{0,7},{9,8},{10,9},{11,1... | collective-permute-start | bytes 24584 | tf_op jit(solution)/shard_map/ppermute | solution.py:402
  21.7 1.4 copy.225.e_ref
  23.1 1.4 copy.226.w_ref
  26.5 5.0 %shard_map.126 = (f32[2,4,64,256]{3,2,1,0:T(8,128)}, f32[2,4,64,256]{3,2,1,0:T(8,128)}, f32[2,4,64,256]{3,2,1,0:T(8,128)}, f32[2,4,64,256]{3,2,1,0:T(8,128)}, f3...) custom-call(f32[2,4,64,256]{3,2,1,0:T(8,128)} %temp_ref.1, f32[2,4,64,256]{3,2,1,0:T(8,128)} %salt_ref.1, ...), custom_call_target="tpu_custom_call" | custom-call | tf_op jit(solution)/shard_map/pallas_call | solution.py:369
  31.5 1.8 pad_maximum_fusion.4.surf_ref
  33.3 46.8 %shard_map.127 = f32[3,2,64,256]{3,2,1,0:T(8,128)} custom-call(f32[3,2,64,256]{3,2,1,0:T(8,128)} %pad_maximum_fusion.4.surf_ref, f32[80,512]{1,0:T(8,128)} %get-tuple-element.150.inside_ref, f32[80,512]{1,0:T(8,128)} %get-tuple-element.151.own_ref), custom_call_target="tpu_custom_call" | custom-call | tf_op jit(solution)/shard_map/pallas_call | solution.py:273
  80.1 1.1 fusion.15
  84.0 3.4 %collective-permute-start.6 = (f32[4,2,4,64,1]{3,2,4,1,0:T(4,128)S(1)}, f32[4,2,4,64,1]{3,2,4,1,0:T(4,128)S(1)}, u32[]{:S(2)}, u32[]{:S(2)}) collective-permute-start(f32[4,2,4,64,1]{3,2,4,1,0:T(4,128)S(1)} %pad_maximum_fusion.13), channel_id=1, source_target_pairs={{1,0},{2,1},{3,2},{4,3},{5,4},{6,5},{7,6},{0,7},{9,8},{10,9},{11,1... | collective-permute-start | bytes 24584 | tf_op jit(solution)/shard_map/ppermute | solution.py:402
  87.5 2.9 %collective-permute-start.4 = (f32[4,2,4,1,256]{4,3,2,1,0:T(1,128)S(1)}, f32[4,2,4,1,256]{4,3,2,1,0:T(1,128)S(1)}, u32[]{:S(2)}, u32[]{:S(2)}) collective-permute-start(f32[4,2,4,1,256]{4,3,2,1,0:T(1,128)S(1)} %pad_maximum_fusion.9), channel_id=1, source_target_pairs={{8,0},{16,8},{24,16},{32,24},{40,32},{48,40},{56,48},{0,56},{9,1},... | collective-permute-start | bytes 98312 | tf_op jit(solution)/shard_map/ppermute | solution.py:400
  90.5 1.4 copy.240.w_ref
  91.9 1.4 copy.239.e_ref
  94.6 5.0 %shard_map.128 = (f32[2,4,64,256]{3,2,1,0:T(8,128)}, f32[2,4,64,256]{3,2,1,0:T(8,128)}, f32[2,4,64,256]{3,2,1,0:T(8,128)}, f32[2,4,64,256]{3,2,1,0:T(8,128)}, f3...) custom-call(f32[2,4,64,256]{3,2,1,0:T(8,128)} %get-tuple-element.43.temp_ref, f32[2,4,64,256]{3,2,1,0:T(8,128)} %get-tuple-element.44.salt_ref, ...), custom_call_target="tpu_custom_call" | custom-call | tf_op jit(solution)/shard_map/pallas_call | solution.py:369
  99.6 1.8 pad_maximum_fusion.5.surf_ref
  101.4 44.6 %shard_map.129 = f32[3,2,64,256]{3,2,1,0:T(8,128)} custom-call(f32[3,2,64,256]{3,2,1,0:T(8,128)} %pad_maximum_fusion.5.surf_ref, f32[80,512]{1,0:T(8,128)} %get-tuple-element.150.inside_ref, f32[80,512]{1,0:T(8,128)} %get-tuple-element.151.own_ref), custom_call_target="tpu_custom_call" | custom-call | tf_op jit(solution)/shard_map/pallas_call | solution.py:273
  146.0 1.1 multiply_bitcast_fusion.1
  148.3 1.1 pad_maximum_fusion.1
  149.4 2.9 %collective-permute-start.8 = (f32[2,2,4,64,256]{4,3,2,1,0:T(8,128)}, f32[2,2,4,64,256]{4,3,2,1,0:T(8,128)}, u32[]{:S(2)}, u32[]{:S(2)}) collective-permute-start(f32[2,2,4,64,256]{4,3,2,1,0:T(8,128)} %pad_maximum_fusion.1), channel_id=1, source_target_pairs={{0,64},{64,0},{1,65},{65,1},{2,66},{66,2},{3,67},{67,3},{4,68},{68... | collective-permute-start | bytes 3145736 | tf_op jit(solution)/shard_map/ppermute | solution.py:553
  153.1 27.7 %shard_map.130 = f32[40,128]{1,0:T(8,128)} custom-call(f32[40,128]{1,0:T(8,128)} %select_maximum_fusion.1.x_ref), custom_call_target="tpu_custom_call" | custom-call | tf_op jit(solution)/shard_map/pallas_call | solution.py:90
  180.8 1.3 fusion.10
  183.5 1.9 collective-permute-start.9
  185.4 1.3 pad_clamp_fusion
  189.0 1.3 fusion.14
  190.3 1.4 bitcast_select_fusion.1
  191.7 1.4 bitcast_select_fusion.3
  194.8 19.9 %collective-permute-done.9 = f32[2,10,64,256]{3,2,1,0:T(8,128)} collective-permute-done((f32[2,10,64,256]{3,2,1,0:T(8,128)S(1)}, f32[2,10,64,256]{3,2,1,0:T(8,128)}, u32[]{:S(2)}, u32[]{:S(2)}) %collective-permute-start.9) | collective-permute-done | bytes 1310752 | tf_op jit(solution)/shard_map/ppermute | solution.py:575
  214.7 1.3 slice.272
  216.1 1.6 dynamic-slice_select_fusion
  218.3 1.0 fusion
  (113 shorter events, 21.8 us)
Async XLA Ops:
  0.6 8.2 %copy-start.2 = (f32[2,4,64,256]{3,2,1,0:T(8,128)S(1)}, f32[2,4,64,256]{3,2,1,0:T(8,128)}, u32[]{:S(2)}) copy-start(f32[2,4,64,256]{3,2,1,0:T(8,128)} %temp_ref.1) | copy-start | bytes 1572868
  0.6 7.9 %copy-start.3 = (f32[2,4,64,256]{3,2,1,0:T(8,128)S(1)}, f32[2,4,64,256]{3,2,1,0:T(8,128)}, u32[]{:S(2)}) copy-start(f32[2,4,64,256]{3,2,1,0:T(8,128)} %vvel_ref.1) | copy-start | bytes 1572868
  0.7 13.9 %copy-start.18 = (s32[2]{0:T(128)S(1)}, s32[2]{0:T(128)}, u32[]{:S(2)}) copy-start(s32[2]{0:T(128)} %param.17) | copy-start | bytes 28
  2.7 21.8 %collective-permute-start.1 = (f32[4,2,4,1,256]{4,3,2,1,0:T(1,128)S(1)}, f32[4,2,4,1,256]{4,3,2,1,0:T(1,128)S(1)}, u32[]{:S(2)}, u32[]{:S(2)}) collective-permute-start(f32[4,2,4,1,256]{4,3,2,1,0:T(1,128)S(1)} %pad_maximum_fusion.8), channel_id=1, source_target_pairs={{0,8},{8,16},{16,24},{24,32},{32,40},{40,48},{48,56},{56,0},{1,9},... | collective-permute-start | bytes 98312 | tf_op jit(solution)/shard_map/ppermute | solution.py:401
  2.8 16.9 %copy-start.15 = (s32[64,256]{1,0:T(8,128)S(1)}, s32[64,256]{1,0:T(8,128)}, u32[]{:S(2)}) copy-start(s32[64,256]{1,0:T(8,128)} %param.16) | copy-start | bytes 196612
  2.8 22.4 %collective-permute-start = (f32[4,2,4,1,256]{4,3,2,1,0:T(1,128)S(1)}, f32[4,2,4,1,256]{4,3,2,1,0:T(1,128)S(1)}, u32[]{:S(2)}, u32[]{:S(2)}) collective-permute-start(f32[4,2,4,1,256]{4,3,2,1,0:T(1,128)S(1)} %pad_maximum_fusion.7), channel_id=1, source_target_pairs={{8,0},{16,8},{24,16},{32,24},{40,32},{48,40},{56,48},{0,56},{9,1},... | collective-permute-start | bytes 98312 | tf_op jit(solution)/shard_map/ppermute | solution.py:400
  9.2 12.5 %collective-permute-start.2 = (f32[4,2,4,64,1]{3,2,4,1,0:T(4,128)S(1)}, f32[4,2,4,64,1]{3,2,4,1,0:T(4,128)S(1)}, u32[]{:S(2)}, u32[]{:S(2)}) collective-permute-start(f32[4,2,4,64,1]{3,2,4,1,0:T(4,128)S(1)} %pad_maximum_fusion.11), channel_id=1, source_target_pairs={{1,0},{2,1},{3,2},{4,3},{5,4},{6,5},{7,6},{0,7},{9,8},{10,9},{11,1... | collective-permute-start | bytes 24584 | tf_op jit(solution)/shard_map/ppermute | solution.py:402
  14.4 8.7 %collective-permute-start.3 = (f32[4,2,4,64,1]{3,2,4,1,0:T(4,128)S(1)}, f32[4,2,4,64,1]{3,2,4,1,0:T(4,128)S(1)}, u32[]{:S(2)}, u32[]{:S(2)}) collective-permute-start(f32[4,2,4,64,1]{3,2,4,1,0:T(4,128)S(1)} %pad_maximum_fusion.12), channel_id=1, source_target_pairs={{0,1},{1,2},{2,3},{3,4},{4,5},{5,6},{6,7},{7,0},{8,9},{9,10},{10,1... | collective-permute-start | bytes 24584 | tf_op jit(solution)/shard_map/ppermute | solution.py:403
  14.5 132.8 %copy-start.16 = (pred[8]{0:T(512)(128)(4,1)}, pred[8]{0:T(512)(128)(4,1)S(1)}, u32[]{:S(2)}) copy-start(pred[8]{0:T(512)(128)(4,1)S(1)} %iota_compare_fusion.4) | copy-start | bytes 28
  26.5 5.0 %copy-start.14 = (f32[2,64,256]{2,1,0:T(8,128)S(1)}, f32[2,64,256]{2,1,0:T(8,128)}, u32[]{:S(2)}) copy-start(f32[2,64,256]{2,1,0:T(8,128)} %param.15) | copy-start | bytes 393220
  31.5 49.7 %copy-start.8 = (f32[64,256]{1,0:T(8,128)S(1)}, f32[64,256]{1,0:T(8,128)}, u32[]{:S(2)}) copy-start(f32[64,256]{1,0:T(8,128)} %convert_element_type.35.ocean_ref) | copy-start | bytes 196612
  31.5 49.7 %copy-start.12 = (f32[2,4,64,256]{3,2,1,0:T(8,128)S(1)}, f32[2,4,64,256]{3,2,1,0:T(8,128)}, u32[]{:S(2)}) copy-start(f32[2,4,64,256]{3,2,1,0:T(8,128)} %get-tuple-element.45) | copy-start | bytes 1572868
  31.5 49.7 %copy-start.13 = (f32[2,4,64,256]{3,2,1,0:T(8,128)S(1)}, f32[2,4,64,256]{3,2,1,0:T(8,128)}, u32[]{:S(2)}) copy-start(f32[2,4,64,256]{3,2,1,0:T(8,128)} %get-tuple-element.48) | copy-start | bytes 1572868
  81.2 1.1 copy-start.4
  81.3 10.6 %copy-start = (f32[2,4,64,256]{3,2,1,0:T(8,128)}, f32[2,4,64,256]{3,2,1,0:T(8,128)S(1)}, u32[]{:S(2)}) copy-start(f32[2,4,64,256]{3,2,1,0:T(8,128)S(1)} %get-tuple-element.136.vvel_ref) | copy-start | bytes 1572868
  81.4 10.6 %copy-start.1 = (f32[2,4,64,256]{3,2,1,0:T(8,128)}, f32[2,4,64,256]{3,2,1,0:T(8,128)S(1)}, u32[]{:S(2)}) copy-start(f32[2,4,64,256]{3,2,1,0:T(8,128)S(1)} %get-tuple-element.137.uvel_ref) | copy-start | bytes 1572868
  81.4 1.5 copy-start.5
  83.2 7.3 %collective-permute-start.7 = (f32[4,2,4,64,1]{3,2,4,1,0:T(4,128)S(1)}, f32[4,2,4,64,1]{3,2,4,1,0:T(4,128)S(1)}, u32[]{:S(2)}, u32[]{:S(2)}) collective-permute-start(f32[4,2,4,64,1]{3,2,4,1,0:T(4,128)S(1)} %pad_maximum_fusion.14), channel_id=1, source_target_pairs={{0,1},{1,2},{2,3},{3,4},{4,5},{5,6},{6,7},{7,0},{8,9},{9,10},{10,1... | collective-permute-start | bytes 24584 | tf_op jit(solution)/shard_map/ppermute | solution.py:403
  84.0 7.9 %collective-permute-start.6 = (f32[4,2,4,64,1]{3,2,4,1,0:T(4,128)S(1)}, f32[4,2,4,64,1]{3,2,4,1,0:T(4,128)S(1)}, u32[]{:S(2)}, u32[]{:S(2)}) collective-permute-start(f32[4,2,4,64,1]{3,2,4,1,0:T(4,128)S(1)} %pad_maximum_fusion.13), channel_id=1, source_target_pairs={{1,0},{2,1},{3,2},{4,3},{5,4},{6,5},{7,6},{0,7},{9,8},{10,9},{11,1... | collective-permute-start | bytes 24584 | tf_op jit(solution)/shard_map/ppermute | solution.py:402
  87.5 5.9 %collective-permute-start.5 = (f32[4,2,4,1,256]{4,3,2,1,0:T(1,128)S(1)}, f32[4,2,4,1,256]{4,3,2,1,0:T(1,128)S(1)}, u32[]{:S(2)}, u32[]{:S(2)}) collective-permute-start(f32[4,2,4,1,256]{4,3,2,1,0:T(1,128)S(1)} %pad_maximum_fusion.10), channel_id=1, source_target_pairs={{0,8},{8,16},{16,24},{24,32},{32,40},{40,48},{48,56},{56,0},{1,9},... | collective-permute-start | bytes 98312 | tf_op jit(solution)/shard_map/ppermute | solution.py:401
  87.5 6.4 %collective-permute-start.4 = (f32[4,2,4,1,256]{4,3,2,1,0:T(1,128)S(1)}, f32[4,2,4,1,256]{4,3,2,1,0:T(1,128)S(1)}, u32[]{:S(2)}, u32[]{:S(2)}) collective-permute-start(f32[4,2,4,1,256]{4,3,2,1,0:T(1,128)S(1)} %pad_maximum_fusion.9), channel_id=1, source_target_pairs={{8,0},{16,8},{24,16},{32,24},{40,32},{48,40},{56,48},{0,56},{9,1},... | collective-permute-start | bytes 98312 | tf_op jit(solution)/shard_map/ppermute | solution.py:400
  99.5 47.6 %copy-start.9 = (f32[64,256]{1,0:T(8,128)S(1)}, f32[64,256]{1,0:T(8,128)}, u32[]{:S(2)}) copy-start(f32[64,256]{1,0:T(8,128)} %convert_element_type.35.ocean_ref) | copy-start | bytes 196612
  99.6 47.6 %copy-start.10 = (f32[2,4,64,256]{3,2,1,0:T(8,128)S(1)}, f32[2,4,64,256]{3,2,1,0:T(8,128)}, u32[]{:S(2)}) copy-start(f32[2,4,64,256]{3,2,1,0:T(8,128)} %get-tuple-element.51) | copy-start | bytes 1572868
  99.6 47.6 %copy-start.11 = (f32[2,4,64,256]{3,2,1,0:T(8,128)S(1)}, f32[2,4,64,256]{3,2,1,0:T(8,128)}, u32[]{:S(2)}) copy-start(f32[2,4,64,256]{3,2,1,0:T(8,128)} %get-tuple-element.54) | copy-start | bytes 1572868
  147.1 1.0 copy-start.6
  147.1 1.2 copy-start.7
  149.4 39.6 %collective-permute-start.8 = (f32[2,2,4,64,256]{4,3,2,1,0:T(8,128)}, f32[2,2,4,64,256]{4,3,2,1,0:T(8,128)}, u32[]{:S(2)}, u32[]{:S(2)}) collective-permute-start(f32[2,2,4,64,256]{4,3,2,1,0:T(8,128)} %pad_maximum_fusion.1), channel_id=1, source_target_pairs={{0,64},{64,0},{1,65},{65,1},{2,66},{66,2},{3,67},{67,3},{4,68},{68... | collective-permute-start | bytes 3145736 | tf_op jit(solution)/shard_map/ppermute | solution.py:553
  180.8 5.9 %slice-start = ((f32[40,128]{1,0:T(8,128)}), f32[32,128]{1,0:T(8,128)S(1)}, s32[]{:S(2)}) async-start(f32[40,128]{1,0:T(8,128)} %shard_map.130), calls=%async_computation | async-start | bytes 32768 | tf_op jit(solution)/shard_map/slice | solution.py:567
  183.5 31.2 %collective-permute-start.9 = (f32[2,10,64,256]{3,2,1,0:T(8,128)S(1)}, f32[2,10,64,256]{3,2,1,0:T(8,128)}, u32[]{:S(2)}, u32[]{:S(2)}) collective-permute-start(f32[2,10,64,256]{3,2,1,0:T(8,128)S(1)} %select_maximum_fusion), channel_id=1, source_target_pairs={{0,64},{64,0},{1,65},{65,1},{2,66},{66,2},{3,67},{67,3},{4,68},{68... | collective-permute-start | bytes 3932168 | tf_op jit(solution)/shard_map/ppermute | solution.py:575
  218.3 1.9 copy-start.17
  218.3 3.9 %copy-start.19 = (s32[2]{0:T(128)S(1)}, s32[2]{0:T(128)}, u32[]{:S(2)}) copy-start(s32[2]{0:T(128)} %param.17) | copy-start | bytes 28

commit v10 on v8

--- a/solution.py
+++ b/solution.py
@@ -303,14 +303,13 @@
     fields, members, rows, cols = surf.shape
     carry = cargo is not None
     vmem = pl.BlockSpec(memory_space=pltpu.VMEM)
-    anywhere = pl.BlockSpec(memory_space=pl.ANY)
     solved_shape = jax.ShapeDtypeStruct((3, members, rows, cols), jnp.float32)
     operands = (surf, inside, own) + ((cargo,) if carry else ())
     results = pl.pallas_call(
         functools.partial(solve_kernel, ny, nx, carry),
         out_shape=[solved_shape] + ([jax.ShapeDtypeStruct(cargo.shape, cargo.dtype)] if carry else []),
-        in_specs=[vmem] * 3 + ([anywhere] if carry else []),
-        out_specs=[vmem] + ([anywhere] if carry else []),
+        in_specs=[vmem] * 3 + ([vmem] if carry else []),
+        out_specs=[vmem] + ([vmem] if carry else []),
         scratch_shapes=[
             pltpu.VMEM((fields, members) + inside.shape, jnp.float32),
             pltpu.SemaphoreType.DMA((8,)),

time: 237 us -> 238 us (level)
  no operation moved by 1% of the time
where the time goes in v10:
time: 238 us; the launch traced here: 237 us
  Pallas kernels  156 us (66%)
  other arithmetic  34.7 us (15%)
  local copies, waits for them, and re-layouts  20.7 us (9%)
  starting transfers between devices  18.2 us (8%)
  between operations  5.69 us (2%)
    pallas_call x2, Pallas kernels, surface_kernel_solve(): pl.pallas_call(functools.partial(solve_kernel, ny, nx, carry), out_shape=...  133 us
    pallas_call x1, Pallas kernels, grid_sum(): pl.pallas_call(functools.partial(gather_sum_kernel, ny, nx), out_shape=ja...  12.4 us
    pallas_call x2, Pallas kernels, volume_step(): pl.pallas_call(volume_kernel, grid=(members,), in_specs=[field] * 4 + [pl...  9.91 us
    ppermute x2, starting transfers between devices, exchange_fields(): lax.ppermute(jnp.stack([f[..., :, :1] for f in fields]), 'gridx', bwd_x)  8.68 us
    select_n x5, other arithmetic, pick(): chosen.append(jnp.where(here[place], from_here, from_other))  8.02 us
    another operation x5, other arithmetic, pick(): return jnp.stack(chosen)  6.05 us
    ppermute x2, starting transfers between devices, exchange_fields(): lax.ppermute(jnp.stack([f[..., :1, :] for f in fields]), 'gridy', bwd_y)  5.89 us
    slice x8, local copies, waits for them, and re-layouts, exchange_fields(): f[..., :, -1:]  5.8 us
  transfers between devices with their start and end apart: 9, of which 1 were waited for; matrix products, arithmetic and copies ran while one was open for 10% of the time, Pallas kernels for 0%

profile of v10, /device:TPU:0, one launch (start us, length us, event | category | flops | bytes accessed | tf_op | source)
XLA Modules:
  0.0 237.2 jit_solution(3912301933420213795)
XLA Ops:
  2.8 2.9 %collective-permute-start = (f32[4,2,4,1,256]{4,3,2,1,0:T(1,128)S(1)}, f32[4,2,4,1,256]{4,3,2,1,0:T(1,128)S(1)}, u32[]{:S(2)}, u32[]{:S(2)}) collective-permute-start(f32[4,2,4,1,256]{4,3,2,1,0:T(1,128)S(1)} %pad_maximum_fusion.8), channel_id=1, source_target_pairs={{8,0},{16,8},{24,16},{32,24},{40,32},{48,40},{56,48},{0,56},{9,1},... | collective-permute-start | bytes 98312 | tf_op jit(solution)/shard_map/ppermute | solution.py:443
  5.7 1.4 slice_reduce_fusion.10
  7.1 1.4 slice_reduce_fusion.9
  8.5 1.4 slice_reduce_fusion.8
  10.2 5.2 %collective-permute-start.2 = (f32[4,2,4,64,1]{3,2,4,1,0:T(4,128)S(1)}, f32[4,2,4,64,1]{3,2,4,1,0:T(4,128)S(1)}, u32[]{:S(2)}, u32[]{:S(2)}) collective-permute-start(f32[4,2,4,64,1]{3,2,4,1,0:T(4,128)S(1)} %pad_maximum_fusion.12), channel_id=1, source_target_pairs={{1,0},{2,1},{3,2},{4,3},{5,4},{6,5},{7,6},{0,7},{9,8},{10,9},{11,1... | collective-permute-start | bytes 24584 | tf_op jit(solution)/shard_map/ppermute | solution.py:445
  22.1 1.4 copy.143.e_ref
  23.5 1.4 copy.144.w_ref
  26.9 5.0 %shard_map.126 = (f32[2,4,64,256]{3,2,1,0:T(8,128)}, f32[2,4,64,256]{3,2,1,0:T(8,128)}, f32[2,4,64,256]{3,2,1,0:T(8,128)}, f32[2,4,64,256]{3,2,1,0:T(8,128)}, f3...) custom-call(f32[2,4,64,256]{3,2,1,0:T(8,128)} %temp_ref.1, f32[2,4,64,256]{3,2,1,0:T(8,128)} %salt_ref.1, ...), custom_call_target="tpu_custom_call" | custom-call | tf_op jit(solution)/shard_map/pallas_call | solution.py:412
  31.9 1.8 pad_maximum_fusion.5.refs_0_
  33.8 44.7 %shard_map.127 = f32[3,2,64,256]{3,2,1,0:T(8,128)} custom-call(f32[3,2,64,256]{3,2,1,0:T(8,128)} %pad_maximum_fusion.5.refs_0_, f32[80,512]{1,0:T(8,128)} %get-tuple-element.133.refs_1_, f32[80,512]{1,0:T(8,128)} %get-tuple-element.134.refs_2_), custom_call_target="tpu_custom_call" | custom-call | tf_op jit(solution)/shard_map/pallas_call | solution.py:308
  78.5 1.1 multiply_bitcast_fusion.2
  82.0 3.5 %collective-permute-start.6 = (f32[4,2,4,64,1]{3,2,4,1,0:T(4,128)S(1)}, f32[4,2,4,64,1]{3,2,4,1,0:T(4,128)S(1)}, u32[]{:S(2)}, u32[]{:S(2)}) collective-permute-start(f32[4,2,4,64,1]{3,2,4,1,0:T(4,128)S(1)} %pad_maximum_fusion.14), channel_id=1, source_target_pairs={{1,0},{2,1},{3,2},{4,3},{5,4},{6,5},{7,6},{0,7},{9,8},{10,9},{11,1... | collective-permute-start | bytes 24584 | tf_op jit(solution)/shard_map/ppermute | solution.py:445
  85.6 2.9 %collective-permute-start.4 = (f32[4,2,4,1,256]{4,3,2,1,0:T(1,128)S(1)}, f32[4,2,4,1,256]{4,3,2,1,0:T(1,128)S(1)}, u32[]{:S(2)}, u32[]{:S(2)}) collective-permute-start(f32[4,2,4,1,256]{4,3,2,1,0:T(1,128)S(1)} %pad_maximum_fusion.10), channel_id=1, source_target_pairs={{8,0},{16,8},{24,16},{32,24},{40,32},{48,40},{56,48},{0,56},{9,1},... | collective-permute-start | bytes 98312 | tf_op jit(solution)/shard_map/ppermute | solution.py:443
  88.5 1.4 copy.156.w_ref
  90.0 1.4 copy.155.e_ref
  92.6 5.0 %shard_map.128 = (f32[2,4,64,256]{3,2,1,0:T(8,128)}, f32[2,4,64,256]{3,2,1,0:T(8,128)}, f32[2,4,64,256]{3,2,1,0:T(8,128)}, f32[2,4,64,256]{3,2,1,0:T(8,128)}, f3...) custom-call(f32[2,4,64,256]{3,2,1,0:T(8,128)} %get-tuple-element.45.temp_ref, f32[2,4,64,256]{3,2,1,0:T(8,128)} %get-tuple-element.46.salt_ref, ...), custom_call_target="tpu_custom_call" | custom-call | tf_op jit(solution)/shard_map/pallas_call | solution.py:412
  97.6 1.7 pad_maximum_fusion.6.refs_0_
  99.3 3.0 %pad_maximum_fusion.refs_3_ = f32[4,2,4,64,256]{4,3,2,1,0:T(8,128)} fusion(f32[1,2,4,64,256]{4,3,2,1,0:T(8,128)} %bitcast.136, f32[1,2,4,64,256]{4,3,2,1,0:T(8,128)} %bitcast.133, f32[1,2,4,64,256]{4,3,2,1,0:T(8,128)} %bitcast.135, f32[1,2,4,64,256]{4,3,2,1,0:T(8,128)} %bitcast.134), kind=kLoop, calls=%fused_computation.1 | loop fusion | flops 1572864 | bytes 4194304 | tf_op jit(solution)/shard_map/stack | solution.py:590
  102.4 88.7 %shard_map.129 = (f32[3,2,64,256]{3,2,1,0:T(8,128)}, f32[4,2,4,64,256]{4,3,2,1,0:T(8,128)}) custom-call(f32[3,2,64,256]{3,2,1,0:T(8,128)} %pad_maximum_fusion.6.refs_0_, f32[80,512]{1,0:T(8,128)} %get-tuple-element.133.refs_1_, f32[80,512]{1,0:T(8,128)} %get-tuple-element.134.refs_2_, f32[4,2,4,64,256]{4,3,2,1,0:T(8,128)} %pad_maximum_fusion.refs_3_), custom_call_target="tpu_custom_call" | custom-call | tf_op jit(solution)/shard_map/pallas_call | solution.py:308
  191.1 1.9 fusion.17
  193.0 1.8 copy.160
  195.9 12.4 %shard_map.130 = f32[40,128]{1,0:T(8,128)} custom-call(f32[40,128]{1,0:T(8,128)} %select_maximum_fusion.1.x_ref), custom_call_target="tpu_custom_call" | custom-call | tf_op jit(solution)/shard_map/pallas_call | solution.py:90
  209.8 1.9 select_maximum_fusion
  211.7 2.9 %collective-permute-start.8 = (f32[2,4,64,256]{3,2,1,0:T(8,128)}, f32[2,4,64,256]{3,2,1,0:T(8,128)}, u32[]{:S(2)}, u32[]{:S(2)}) collective-permute-start(f32[2,4,64,256]{3,2,1,0:T(8,128)} %select_maximum_fusion), channel_id=1, source_target_pairs={{0,64},{64,0},{1,65},{65,1},{2,66},{66,2},{3,67},{67,3},{4,68},{68... | collective-permute-start | bytes 1572872 | tf_op jit(solution)/shard_map/ppermute | solution.py:620
  215.7 2.0 bitcast_select_fusion.1
  217.7 2.1 bitcast_select_fusion.3
  219.9 1.8 pad_maximum_fusion.2
  221.8 1.9 pad_maximum_fusion.1
  224.3 2.2 collective-permute-done.8
  230.8 1.3 select_bitcast_fusion.1
  232.9 1.3 dynamic-slice_select_fusion.1
  235.1 1.3 dynamic-slice_select_fusion.3
  (112 shorter events, 21.4 us)
Async XLA Ops:
  0.6 9.2 %copy-start.4 = (f32[2,4,64,256]{3,2,1,0:T(8,128)S(1)}, f32[2,4,64,256]{3,2,1,0:T(8,128)}, u32[]{:S(2)}) copy-start(f32[2,4,64,256]{3,2,1,0:T(8,128)} %temp_ref.1) | copy-start | bytes 1572868
  0.6 14.9 %copy-start.18 = (s32[2]{0:T(128)S(1)}, s32[2]{0:T(128)}, u32[]{:S(2)}) copy-start(s32[2]{0:T(128)} %param.17) | copy-start | bytes 28
  0.7 19.5 %copy-start.17 = (s32[64,256]{1,0:T(8,128)S(1)}, s32[64,256]{1,0:T(8,128)}, u32[]{:S(2)}) copy-start(s32[64,256]{1,0:T(8,128)} %param.16) | copy-start | bytes 196612
  2.7 22.3 %collective-permute-start.1 = (f32[4,2,4,1,256]{4,3,2,1,0:T(1,128)S(1)}, f32[4,2,4,1,256]{4,3,2,1,0:T(1,128)S(1)}, u32[]{:S(2)}, u32[]{:S(2)}) collective-permute-start(f32[4,2,4,1,256]{4,3,2,1,0:T(1,128)S(1)} %pad_maximum_fusion.9), channel_id=1, source_target_pairs={{0,8},{8,16},{16,24},{24,32},{32,40},{40,48},{48,56},{56,0},{1,9},... | collective-permute-start | bytes 98312 | tf_op jit(solution)/shard_map/ppermute | solution.py:444
  2.8 22.8 %collective-permute-start = (f32[4,2,4,1,256]{4,3,2,1,0:T(1,128)S(1)}, f32[4,2,4,1,256]{4,3,2,1,0:T(1,128)S(1)}, u32[]{:S(2)}, u32[]{:S(2)}) collective-permute-start(f32[4,2,4,1,256]{4,3,2,1,0:T(1,128)S(1)} %pad_maximum_fusion.8), channel_id=1, source_target_pairs={{8,0},{16,8},{24,16},{32,24},{40,32},{48,40},{56,48},{0,56},{9,1},... | collective-permute-start | bytes 98312 | tf_op jit(solution)/shard_map/ppermute | solution.py:443
  10.2 11.9 %collective-permute-start.2 = (f32[4,2,4,64,1]{3,2,4,1,0:T(4,128)S(1)}, f32[4,2,4,64,1]{3,2,4,1,0:T(4,128)S(1)}, u32[]{:S(2)}, u32[]{:S(2)}) collective-permute-start(f32[4,2,4,64,1]{3,2,4,1,0:T(4,128)S(1)} %pad_maximum_fusion.12), channel_id=1, source_target_pairs={{1,0},{2,1},{3,2},{4,3},{5,4},{6,5},{7,6},{0,7},{9,8},{10,9},{11,1... | collective-permute-start | bytes 24584 | tf_op jit(solution)/shard_map/ppermute | solution.py:445
  15.4 8.1 %collective-permute-start.3 = (f32[4,2,4,64,1]{3,2,4,1,0:T(4,128)S(1)}, f32[4,2,4,64,1]{3,2,4,1,0:T(4,128)S(1)}, u32[]{:S(2)}, u32[]{:S(2)}) collective-permute-start(f32[4,2,4,64,1]{3,2,4,1,0:T(4,128)S(1)} %pad_maximum_fusion.13), channel_id=1, source_target_pairs={{0,1},{1,2},{2,3},{3,4},{4,5},{5,6},{6,7},{7,0},{8,9},{9,10},{10,1... | collective-permute-start | bytes 24584 | tf_op jit(solution)/shard_map/ppermute | solution.py:446
  26.9 5.0 %copy-start.16 = (f32[2,64,256]{2,1,0:T(8,128)S(1)}, f32[2,64,256]{2,1,0:T(8,128)}, u32[]{:S(2)}) copy-start(f32[2,64,256]{2,1,0:T(8,128)} %param.15) | copy-start | bytes 393220
  31.9 47.7 %copy-start.2 = (f32[64,256]{1,0:T(8,128)S(1)}, f32[64,256]{1,0:T(8,128)}, u32[]{:S(2)}) copy-start(f32[64,256]{1,0:T(8,128)} %convert_element_type.35.ocean_ref) | copy-start | bytes 196612
  31.9 47.7 %copy-start.13 = (f32[2,4,64,256]{3,2,1,0:T(8,128)S(1)}, f32[2,4,64,256]{3,2,1,0:T(8,128)}, u32[]{:S(2)}) copy-start(f32[2,4,64,256]{3,2,1,0:T(8,128)} %get-tuple-element.47) | copy-start | bytes 1572868
  31.9 47.7 %copy-start.14 = (f32[2,4,64,256]{3,2,1,0:T(8,128)S(1)}, f32[2,4,64,256]{3,2,1,0:T(8,128)}, u32[]{:S(2)}) copy-start(f32[2,4,64,256]{3,2,1,0:T(8,128)} %get-tuple-element.50) | copy-start | bytes 1572868
  78.5 2.0 copy-start.5
  79.6 1.3 copy-start.6
  79.8 11.6 %copy-start = (f32[2,4,64,256]{3,2,1,0:T(8,128)}, f32[2,4,64,256]{3,2,1,0:T(8,128)S(1)}, u32[]{:S(2)}) copy-start(f32[2,4,64,256]{3,2,1,0:T(8,128)S(1)} %get-tuple-element.119.vvel_ref) | copy-start | bytes 1572868
  79.8 11.6 %copy-start.1 = (f32[2,4,64,256]{3,2,1,0:T(8,128)}, f32[2,4,64,256]{3,2,1,0:T(8,128)S(1)}, u32[]{:S(2)}) copy-start(f32[2,4,64,256]{3,2,1,0:T(8,128)S(1)} %get-tuple-element.120.uvel_ref) | copy-start | bytes 1572868
  81.3 7.3 %collective-permute-start.7 = (f32[4,2,4,64,1]{3,2,4,1,0:T(4,128)S(1)}, f32[4,2,4,64,1]{3,2,4,1,0:T(4,128)S(1)}, u32[]{:S(2)}, u32[]{:S(2)}) collective-permute-start(f32[4,2,4,64,1]{3,2,4,1,0:T(4,128)S(1)} %pad_maximum_fusion.15), channel_id=1, source_target_pairs={{0,1},{1,2},{2,3},{3,4},{4,5},{5,6},{6,7},{7,0},{8,9},{9,10},{10,1... | collective-permute-start | bytes 24584 | tf_op jit(solution)/shard_map/ppermute | solution.py:446
  82.0 8.0 %collective-permute-start.6 = (f32[4,2,4,64,1]{3,2,4,1,0:T(4,128)S(1)}, f32[4,2,4,64,1]{3,2,4,1,0:T(4,128)S(1)}, u32[]{:S(2)}, u32[]{:S(2)}) collective-permute-start(f32[4,2,4,64,1]{3,2,4,1,0:T(4,128)S(1)} %pad_maximum_fusion.14), channel_id=1, source_target_pairs={{1,0},{2,1},{3,2},{4,3},{5,4},{6,5},{7,6},{0,7},{9,8},{10,9},{11,1... | collective-permute-start | bytes 24584 | tf_op jit(solution)/shard_map/ppermute | solution.py:445
  85.5 5.9 %collective-permute-start.5 = (f32[4,2,4,1,256]{4,3,2,1,0:T(1,128)S(1)}, f32[4,2,4,1,256]{4,3,2,1,0:T(1,128)S(1)}, u32[]{:S(2)}, u32[]{:S(2)}) collective-permute-start(f32[4,2,4,1,256]{4,3,2,1,0:T(1,128)S(1)} %pad_maximum_fusion.11), channel_id=1, source_target_pairs={{0,8},{8,16},{16,24},{24,32},{32,40},{40,48},{48,56},{56,0},{1,9},... | collective-permute-start | bytes 98312 | tf_op jit(solution)/shard_map/ppermute | solution.py:444
  85.6 6.4 %collective-permute-start.4 = (f32[4,2,4,1,256]{4,3,2,1,0:T(1,128)S(1)}, f32[4,2,4,1,256]{4,3,2,1,0:T(1,128)S(1)}, u32[]{:S(2)}, u32[]{:S(2)}) collective-permute-start(f32[4,2,4,1,256]{4,3,2,1,0:T(1,128)S(1)} %pad_maximum_fusion.10), channel_id=1, source_target_pairs={{8,0},{16,8},{24,16},{32,24},{40,32},{48,40},{56,48},{0,56},{9,1},... | collective-permute-start | bytes 98312 | tf_op jit(solution)/shard_map/ppermute | solution.py:443
  102.4 92.4 %copy-start.3 = (f32[64,256]{1,0:T(8,128)S(1)}, f32[64,256]{1,0:T(8,128)}, u32[]{:S(2)}) copy-start(f32[64,256]{1,0:T(8,128)} %convert_element_type.35.ocean_ref) | copy-start | bytes 196612
  102.4 92.4 %copy-start.11 = (f32[2,4,64,256]{3,2,1,0:T(8,128)S(1)}, f32[2,4,64,256]{3,2,1,0:T(8,128)}, u32[]{:S(2)}) copy-start(f32[2,4,64,256]{3,2,1,0:T(8,128)} %get-tuple-element.56) | copy-start | bytes 1572868
  191.1 23.5 %copy-start.7 = (f32[4,2,4,64,256]{4,3,2,1,0:T(8,128)S(1)}, f32[4,2,4,64,256]{4,3,2,1,0:T(8,128)}, u32[]{:S(2)}) copy-start(f32[4,2,4,64,256]{4,3,2,1,0:T(8,128)} %get-tuple-element.57) | copy-start | bytes 6291460
  209.8 7.9 %copy-start.9 = (f32[2,4,64,256]{3,2,1,0:T(8,128)S(1)}, f32[2,4,64,256]{3,2,1,0:T(8,128)}, u32[]{:S(2)}) copy-start(f32[2,4,64,256]{3,2,1,0:T(8,128)} %get-tuple-element.51) | copy-start | bytes 1572868
  211.7 14.8 %collective-permute-start.8 = (f32[2,4,64,256]{3,2,1,0:T(8,128)}, f32[2,4,64,256]{3,2,1,0:T(8,128)}, u32[]{:S(2)}, u32[]{:S(2)}) collective-permute-start(f32[2,4,64,256]{3,2,1,0:T(8,128)} %select_maximum_fusion), channel_id=1, source_target_pairs={{0,64},{64,0},{1,65},{65,1},{2,66},{66,2},{3,67},{67,3},{4,68},{68... | collective-permute-start | bytes 1572872 | tf_op jit(solution)/shard_map/ppermute | solution.py:620
  214.6 1.0 copy-start.10
  219.8 12.9 %copy-start.8 = (f32[2,4,64,256]{3,2,1,0:T(8,128)S(1)}, f32[2,4,64,256]{3,2,1,0:T(8,128)}, u32[]{:S(2)}) copy-start(f32[2,4,64,256]{3,2,1,0:T(8,128)} %get-tuple-element.55) | copy-start | bytes 1572868
  221.8 9.0 %copy-start.15 = (f32[1,2,64,256]{3,2,1,0:T(8,128)S(1)}, f32[1,2,64,256]{3,2,1,0:T(8,128)}, u32[]{:S(2)}) copy-start(f32[1,2,64,256]{3,2,1,0:T(8,128)} %get-tuple-element.110) | copy-start | bytes 393220
  221.8 11.0 %copy-start.12 = (f32[2,64,256]{2,1,0:T(8,128)S(1)}, f32[2,64,256]{2,1,0:T(8,128)}, u32[]{:S(2)}) copy-start(f32[2,64,256]{2,1,0:T(8,128)} %get-tuple-element.112) | copy-start | bytes 393220

commit v11 on v6

--- a/solution.py
+++ b/solution.py
@@ -226,7 +226,7 @@
         return ((1.0 + 4.0 * SURF_C) * f - SURF_C * (east(f) + west(f) + north(f) + south(f))) * inside
 
     def total(f):
-        return jnp.sum(jnp.where(own, f, 0.0), axis=(0, 1), keepdims=True)
+        return jnp.sum(f[0:rows, 0:cols], axis=(0, 1), keepdims=True)
 
     residual = []
     for m in range(members):

time: 216 us -> 215 us (level)
  no operation moved by 1% of the time
where the time goes in v11:
time: 215 us; the launch traced here: 214 us
  Pallas kernels  122 us (57%)
  other arithmetic  26.6 us (12%)
  local copies, waits for them, and re-layouts  21.4 us (10%)
  starting transfers between devices  20.2 us (9%)
  waiting for transfers between devices  18.7 us (9%)
  between operations  5.75 us (3%)
    pallas_call x2, Pallas kernels, surface_kernel_solve(): pl.pallas_call(functools.partial(solve_kernel, ny, nx), out_shape=jax.Sha...  86.2 us
    pallas_call x1, Pallas kernels, grid_sum(): pl.pallas_call(functools.partial(gather_sum_kernel, ny, nx), out_shape=ja...  25.7 us
    ppermute x1, waiting for transfers between devices, shards(): flows_other = lax.ppermute(flows, 'member', swap)  18.7 us
    pallas_call x2, Pallas kernels, volume_step(): pl.pallas_call(volume_kernel, grid=(members,), in_specs=[field] * 4 + [pl...  9.92 us
    ppermute x2, starting transfers between devices, exchange_fields(): lax.ppermute(jnp.stack([f[..., :, :1] for f in fields]), 'gridx', bwd_x)  8.68 us
    ppermute x2, starting transfers between devices, exchange_fields(): lax.ppermute(jnp.stack([f[..., :1, :] for f in fields]), 'gridy', bwd_y)  5.89 us
    slice x8, local copies, waits for them, and re-layouts, exchange_fields(): f[..., :, -1:]  4.77 us
    select_n x3, other arithmetic, pick(): chosen.append(jnp.where(here[place], from_here, from_other))  4.44 us
  transfers between devices with their start and end apart: 10, of which 1 were waited for; matrix products, arithmetic and copies ran while one was open for 12% of the time, Pallas kernels for 12%

profile of v11, /device:TPU:0, one launch (start us, length us, event | category | flops | bytes accessed | tf_op | source)
XLA Modules:
  0.0 214.4 jit_solution(5676850311986781655)
XLA Ops:
  0.7 1.0 slice_bitcast_fusion.11
  2.8 2.9 %collective-permute-start = (f32[4,2,4,1,256]{4,3,2,1,0:T(1,128)S(1)}, f32[4,2,4,1,256]{4,3,2,1,0:T(1,128)S(1)}, u32[]{:S(2)}, u32[]{:S(2)}) collective-permute-start(f32[4,2,4,1,256]{4,3,2,1,0:T(1,128)S(1)} %pad_maximum_fusion.7), channel_id=1, source_target_pairs={{8,0},{16,8},{24,16},{32,24},{40,32},{48,40},{56,48},{0,56},{9,1},... | collective-permute-start | bytes 98312 | tf_op jit(solution)/shard_map/ppermute | solution.py:412
  5.8 1.4 slice_reduce_fusion.10
  7.1 1.4 slice_reduce_fusion.9
  9.2 5.2 %collective-permute-start.2 = (f32[4,2,4,64,1]{3,2,4,1,0:T(4,128)S(1)}, f32[4,2,4,64,1]{3,2,4,1,0:T(4,128)S(1)}, u32[]{:S(2)}, u32[]{:S(2)}) collective-permute-start(f32[4,2,4,64,1]{3,2,4,1,0:T(4,128)S(1)} %pad_maximum_fusion.11), channel_id=1, source_target_pairs={{1,0},{2,1},{3,2},{4,3},{5,4},{6,5},{7,6},{0,7},{9,8},{10,9},{11,1... | collective-permute-start | bytes 24584 | tf_op jit(solution)/shard_map/ppermute | solution.py:414
  21.7 1.4 copy.225.e_ref
  23.1 1.4 copy.226.w_ref
  26.5 5.0 %shard_map.126 = (f32[2,4,64,256]{3,2,1,0:T(8,128)}, f32[2,4,64,256]{3,2,1,0:T(8,128)}, f32[2,4,64,256]{3,2,1,0:T(8,128)}, f32[2,4,64,256]{3,2,1,0:T(8,128)}, f3...) custom-call(f32[2,4,64,256]{3,2,1,0:T(8,128)} %temp_ref.1, f32[2,4,64,256]{3,2,1,0:T(8,128)} %salt_ref.1, ...), custom_call_target="tpu_custom_call" | custom-call | tf_op jit(solution)/shard_map/pallas_call | solution.py:381
  31.5 1.8 pad_maximum_fusion.4.surf_ref
  33.3 44.4 %shard_map.127 = f32[3,2,64,256]{3,2,1,0:T(8,128)} custom-call(f32[3,2,64,256]{3,2,1,0:T(8,128)} %pad_maximum_fusion.4.surf_ref, f32[80,512]{1,0:T(8,128)} %get-tuple-element.150.inside_ref, f32[80,512]{1,0:T(8,128)} %get-tuple-element.151.own_ref), custom_call_target="tpu_custom_call" | custom-call | tf_op jit(solution)/shard_map/pallas_call | solution.py:281
  77.7 1.1 fusion.15
  81.6 3.5 %collective-permute-start.6 = (f32[4,2,4,64,1]{3,2,4,1,0:T(4,128)S(1)}, f32[4,2,4,64,1]{3,2,4,1,0:T(4,128)S(1)}, u32[]{:S(2)}, u32[]{:S(2)}) collective-permute-start(f32[4,2,4,64,1]{3,2,4,1,0:T(4,128)S(1)} %pad_maximum_fusion.13), channel_id=1, source_target_pairs={{1,0},{2,1},{3,2},{4,3},{5,4},{6,5},{7,6},{0,7},{9,8},{10,9},{11,1... | collective-permute-start | bytes 24584 | tf_op jit(solution)/shard_map/ppermute | solution.py:414
  85.1 2.9 %collective-permute-start.4 = (f32[4,2,4,1,256]{4,3,2,1,0:T(1,128)S(1)}, f32[4,2,4,1,256]{4,3,2,1,0:T(1,128)S(1)}, u32[]{:S(2)}, u32[]{:S(2)}) collective-permute-start(f32[4,2,4,1,256]{4,3,2,1,0:T(1,128)S(1)} %pad_maximum_fusion.9), channel_id=1, source_target_pairs={{8,0},{16,8},{24,16},{32,24},{40,32},{48,40},{56,48},{0,56},{9,1},... | collective-permute-start | bytes 98312 | tf_op jit(solution)/shard_map/ppermute | solution.py:412
  88.1 1.4 copy.240.w_ref
  89.6 1.4 copy.239.e_ref
  92.2 5.0 %shard_map.128 = (f32[2,4,64,256]{3,2,1,0:T(8,128)}, f32[2,4,64,256]{3,2,1,0:T(8,128)}, f32[2,4,64,256]{3,2,1,0:T(8,128)}, f32[2,4,64,256]{3,2,1,0:T(8,128)}, f3...) custom-call(f32[2,4,64,256]{3,2,1,0:T(8,128)} %get-tuple-element.43.temp_ref, f32[2,4,64,256]{3,2,1,0:T(8,128)} %get-tuple-element.44.salt_ref, ...), custom_call_target="tpu_custom_call" | custom-call | tf_op jit(solution)/shard_map/pallas_call | solution.py:381
  97.2 1.8 pad_maximum_fusion.5.surf_ref
  99.0 41.8 %shard_map.129 = f32[3,2,64,256]{3,2,1,0:T(8,128)} custom-call(f32[3,2,64,256]{3,2,1,0:T(8,128)} %pad_maximum_fusion.5.surf_ref, f32[80,512]{1,0:T(8,128)} %get-tuple-element.150.inside_ref, f32[80,512]{1,0:T(8,128)} %get-tuple-element.151.own_ref), custom_call_target="tpu_custom_call" | custom-call | tf_op jit(solution)/shard_map/pallas_call | solution.py:281
  140.8 1.1 multiply_bitcast_fusion.1
  143.1 1.1 pad_maximum_fusion.1
  144.2 2.9 %collective-permute-start.8 = (f32[2,2,4,64,256]{4,3,2,1,0:T(8,128)}, f32[2,2,4,64,256]{4,3,2,1,0:T(8,128)}, u32[]{:S(2)}, u32[]{:S(2)}) collective-permute-start(f32[2,2,4,64,256]{4,3,2,1,0:T(8,128)} %pad_maximum_fusion.1), channel_id=1, source_target_pairs={{0,64},{64,0},{1,65},{65,1},{2,66},{66,2},{3,67},{67,3},{4,68},{68... | collective-permute-start | bytes 3145736 | tf_op jit(solution)/shard_map/ppermute | solution.py:565
  147.9 25.7 %shard_map.130 = f32[40,128]{1,0:T(8,128)} custom-call(f32[40,128]{1,0:T(8,128)} %select_maximum_fusion.1.x_ref), custom_call_target="tpu_custom_call" | custom-call | tf_op jit(solution)/shard_map/pallas_call | solution.py:90
  173.6 1.3 fusion.10
  176.3 1.9 collective-permute-start.9
  178.2 1.3 pad_clamp_fusion
  181.7 1.3 fusion.14
  183.0 1.4 bitcast_select_fusion.1
  184.5 1.4 bitcast_select_fusion.3
  187.6 18.7 %collective-permute-done.9 = f32[2,10,64,256]{3,2,1,0:T(8,128)} collective-permute-done((f32[2,10,64,256]{3,2,1,0:T(8,128)S(1)}, f32[2,10,64,256]{3,2,1,0:T(8,128)}, u32[]{:S(2)}, u32[]{:S(2)}) %collective-permute-start.9) | collective-permute-done | bytes 1310752 | tf_op jit(solution)/shard_map/ppermute | solution.py:587
  206.3 1.3 slice.272
  207.7 1.6 dynamic-slice_select_fusion
  209.9 1.0 fusion
  (113 shorter events, 21.8 us)
Async XLA Ops:
  0.6 8.2 %copy-start.2 = (f32[2,4,64,256]{3,2,1,0:T(8,128)S(1)}, f32[2,4,64,256]{3,2,1,0:T(8,128)}, u32[]{:S(2)}) copy-start(f32[2,4,64,256]{3,2,1,0:T(8,128)} %temp_ref.1) | copy-start | bytes 1572868
  0.6 7.9 %copy-start.3 = (f32[2,4,64,256]{3,2,1,0:T(8,128)S(1)}, f32[2,4,64,256]{3,2,1,0:T(8,128)}, u32[]{:S(2)}) copy-start(f32[2,4,64,256]{3,2,1,0:T(8,128)} %vvel_ref.1) | copy-start | bytes 1572868
  0.7 13.9 %copy-start.18 = (s32[2]{0:T(128)S(1)}, s32[2]{0:T(128)}, u32[]{:S(2)}) copy-start(s32[2]{0:T(128)} %param.17) | copy-start | bytes 28
  2.7 21.8 %collective-permute-start.1 = (f32[4,2,4,1,256]{4,3,2,1,0:T(1,128)S(1)}, f32[4,2,4,1,256]{4,3,2,1,0:T(1,128)S(1)}, u32[]{:S(2)}, u32[]{:S(2)}) collective-permute-start(f32[4,2,4,1,256]{4,3,2,1,0:T(1,128)S(1)} %pad_maximum_fusion.8), channel_id=1, source_target_pairs={{0,8},{8,16},{16,24},{24,32},{32,40},{40,48},{48,56},{56,0},{1,9},... | collective-permute-start | bytes 98312 | tf_op jit(solution)/shard_map/ppermute | solution.py:413
  2.8 16.9 %copy-start.15 = (s32[64,256]{1,0:T(8,128)S(1)}, s32[64,256]{1,0:T(8,128)}, u32[]{:S(2)}) copy-start(s32[64,256]{1,0:T(8,128)} %param.16) | copy-start | bytes 196612
  2.8 22.4 %collective-permute-start = (f32[4,2,4,1,256]{4,3,2,1,0:T(1,128)S(1)}, f32[4,2,4,1,256]{4,3,2,1,0:T(1,128)S(1)}, u32[]{:S(2)}, u32[]{:S(2)}) collective-permute-start(f32[4,2,4,1,256]{4,3,2,1,0:T(1,128)S(1)} %pad_maximum_fusion.7), channel_id=1, source_target_pairs={{8,0},{16,8},{24,16},{32,24},{40,32},{48,40},{56,48},{0,56},{9,1},... | collective-permute-start | bytes 98312 | tf_op jit(solution)/shard_map/ppermute | solution.py:412
  9.2 12.5 %collective-permute-start.2 = (f32[4,2,4,64,1]{3,2,4,1,0:T(4,128)S(1)}, f32[4,2,4,64,1]{3,2,4,1,0:T(4,128)S(1)}, u32[]{:S(2)}, u32[]{:S(2)}) collective-permute-start(f32[4,2,4,64,1]{3,2,4,1,0:T(4,128)S(1)} %pad_maximum_fusion.11), channel_id=1, source_target_pairs={{1,0},{2,1},{3,2},{4,3},{5,4},{6,5},{7,6},{0,7},{9,8},{10,9},{11,1... | collective-permute-start | bytes 24584 | tf_op jit(solution)/shard_map/ppermute | solution.py:414
  14.4 8.7 %collective-permute-start.3 = (f32[4,2,4,64,1]{3,2,4,1,0:T(4,128)S(1)}, f32[4,2,4,64,1]{3,2,4,1,0:T(4,128)S(1)}, u32[]{:S(2)}, u32[]{:S(2)}) collective-permute-start(f32[4,2,4,64,1]{3,2,4,1,0:T(4,128)S(1)} %pad_maximum_fusion.12), channel_id=1, source_target_pairs={{0,1},{1,2},{2,3},{3,4},{4,5},{5,6},{6,7},{7,0},{8,9},{9,10},{10,1... | collective-permute-start | bytes 24584 | tf_op jit(solution)/shard_map/ppermute | solution.py:415
  14.5 127.6 %copy-start.16 = (pred[8]{0:T(512)(128)(4,1)}, pred[8]{0:T(512)(128)(4,1)S(1)}, u32[]{:S(2)}) copy-start(pred[8]{0:T(512)(128)(4,1)S(1)} %iota_compare_fusion.4) | copy-start | bytes 28
  26.5 5.0 %copy-start.14 = (f32[2,64,256]{2,1,0:T(8,128)S(1)}, f32[2,64,256]{2,1,0:T(8,128)}, u32[]{:S(2)}) copy-start(f32[2,64,256]{2,1,0:T(8,128)} %param.15) | copy-start | bytes 393220
  31.5 47.4 %copy-start.8 = (f32[64,256]{1,0:T(8,128)S(1)}, f32[64,256]{1,0:T(8,128)}, u32[]{:S(2)}) copy-start(f32[64,256]{1,0:T(8,128)} %convert_element_type.35.ocean_ref) | copy-start | bytes 196612
  31.5 47.4 %copy-start.12 = (f32[2,4,64,256]{3,2,1,0:T(8,128)S(1)}, f32[2,4,64,256]{3,2,1,0:T(8,128)}, u32[]{:S(2)}) copy-start(f32[2,4,64,256]{3,2,1,0:T(8,128)} %get-tuple-element.45) | copy-start | bytes 1572868
  31.5 47.4 %copy-start.13 = (f32[2,4,64,256]{3,2,1,0:T(8,128)S(1)}, f32[2,4,64,256]{3,2,1,0:T(8,128)}, u32[]{:S(2)}) copy-start(f32[2,4,64,256]{3,2,1,0:T(8,128)} %get-tuple-element.48) | copy-start | bytes 1572868
  78.8 1.1 copy-start.4
  79.0 10.6 %copy-start = (f32[2,4,64,256]{3,2,1,0:T(8,128)}, f32[2,4,64,256]{3,2,1,0:T(8,128)S(1)}, u32[]{:S(2)}) copy-start(f32[2,4,64,256]{3,2,1,0:T(8,128)S(1)} %get-tuple-element.136.vvel_ref) | copy-start | bytes 1572868
  79.0 10.6 %copy-start.1 = (f32[2,4,64,256]{3,2,1,0:T(8,128)}, f32[2,4,64,256]{3,2,1,0:T(8,128)S(1)}, u32[]{:S(2)}) copy-start(f32[2,4,64,256]{3,2,1,0:T(8,128)S(1)} %get-tuple-element.137.uvel_ref) | copy-start | bytes 1572868
  79.0 1.5 copy-start.5
  80.8 7.3 %collective-permute-start.7 = (f32[4,2,4,64,1]{3,2,4,1,0:T(4,128)S(1)}, f32[4,2,4,64,1]{3,2,4,1,0:T(4,128)S(1)}, u32[]{:S(2)}, u32[]{:S(2)}) collective-permute-start(f32[4,2,4,64,1]{3,2,4,1,0:T(4,128)S(1)} %pad_maximum_fusion.14), channel_id=1, source_target_pairs={{0,1},{1,2},{2,3},{3,4},{4,5},{5,6},{6,7},{7,0},{8,9},{9,10},{10,1... | collective-permute-start | bytes 24584 | tf_op jit(solution)/shard_map/ppermute | solution.py:415
  81.6 8.0 %collective-permute-start.6 = (f32[4,2,4,64,1]{3,2,4,1,0:T(4,128)S(1)}, f32[4,2,4,64,1]{3,2,4,1,0:T(4,128)S(1)}, u32[]{:S(2)}, u32[]{:S(2)}) collective-permute-start(f32[4,2,4,64,1]{3,2,4,1,0:T(4,128)S(1)} %pad_maximum_fusion.13), channel_id=1, source_target_pairs={{1,0},{2,1},{3,2},{4,3},{5,4},{6,5},{7,6},{0,7},{9,8},{10,9},{11,1... | collective-permute-start | bytes 24584 | tf_op jit(solution)/shard_map/ppermute | solution.py:414
  85.1 5.9 %collective-permute-start.5 = (f32[4,2,4,1,256]{4,3,2,1,0:T(1,128)S(1)}, f32[4,2,4,1,256]{4,3,2,1,0:T(1,128)S(1)}, u32[]{:S(2)}, u32[]{:S(2)}) collective-permute-start(f32[4,2,4,1,256]{4,3,2,1,0:T(1,128)S(1)} %pad_maximum_fusion.10), channel_id=1, source_target_pairs={{0,8},{8,16},{16,24},{24,32},{32,40},{40,48},{48,56},{56,0},{1,9},... | collective-permute-start | bytes 98312 | tf_op jit(solution)/shard_map/ppermute | solution.py:413
  85.1 6.4 %collective-permute-start.4 = (f32[4,2,4,1,256]{4,3,2,1,0:T(1,128)S(1)}, f32[4,2,4,1,256]{4,3,2,1,0:T(1,128)S(1)}, u32[]{:S(2)}, u32[]{:S(2)}) collective-permute-start(f32[4,2,4,1,256]{4,3,2,1,0:T(1,128)S(1)} %pad_maximum_fusion.9), channel_id=1, source_target_pairs={{8,0},{16,8},{24,16},{32,24},{40,32},{48,40},{56,48},{0,56},{9,1},... | collective-permute-start | bytes 98312 | tf_op jit(solution)/shard_map/ppermute | solution.py:412
  97.2 44.7 %copy-start.9 = (f32[64,256]{1,0:T(8,128)S(1)}, f32[64,256]{1,0:T(8,128)}, u32[]{:S(2)}) copy-start(f32[64,256]{1,0:T(8,128)} %convert_element_type.35.ocean_ref) | copy-start | bytes 196612
  97.2 44.7 %copy-start.10 = (f32[2,4,64,256]{3,2,1,0:T(8,128)S(1)}, f32[2,4,64,256]{3,2,1,0:T(8,128)}, u32[]{:S(2)}) copy-start(f32[2,4,64,256]{3,2,1,0:T(8,128)} %get-tuple-element.51) | copy-start | bytes 1572868
  97.2 44.7 %copy-start.11 = (f32[2,4,64,256]{3,2,1,0:T(8,128)S(1)}, f32[2,4,64,256]{3,2,1,0:T(8,128)}, u32[]{:S(2)}) copy-start(f32[2,4,64,256]{3,2,1,0:T(8,128)} %get-tuple-element.54) | copy-start | bytes 1572868
  141.9 1.0 copy-start.6
  141.9 1.2 copy-start.7
  144.2 37.6 %collective-permute-start.8 = (f32[2,2,4,64,256]{4,3,2,1,0:T(8,128)}, f32[2,2,4,64,256]{4,3,2,1,0:T(8,128)}, u32[]{:S(2)}, u32[]{:S(2)}) collective-permute-start(f32[2,2,4,64,256]{4,3,2,1,0:T(8,128)} %pad_maximum_fusion.1), channel_id=1, source_target_pairs={{0,64},{64,0},{1,65},{65,1},{2,66},{66,2},{3,67},{67,3},{4,68},{68... | collective-permute-start | bytes 3145736 | tf_op jit(solution)/shard_map/ppermute | solution.py:565
  173.6 5.9 %slice-start = ((f32[40,128]{1,0:T(8,128)}), f32[32,128]{1,0:T(8,128)S(1)}, s32[]{:S(2)}) async-start(f32[40,128]{1,0:T(8,128)} %shard_map.130), calls=%async_computation | async-start | bytes 32768 | tf_op jit(solution)/shard_map/slice | solution.py:579
  176.3 30.0 %collective-permute-start.9 = (f32[2,10,64,256]{3,2,1,0:T(8,128)S(1)}, f32[2,10,64,256]{3,2,1,0:T(8,128)}, u32[]{:S(2)}, u32[]{:S(2)}) collective-permute-start(f32[2,10,64,256]{3,2,1,0:T(8,128)S(1)} %select_maximum_fusion), channel_id=1, source_target_pairs={{0,64},{64,0},{1,65},{65,1},{2,66},{66,2},{3,67},{67,3},{4,68},{68... | collective-permute-start | bytes 3932168 | tf_op jit(solution)/shard_map/ppermute | solution.py:587
  209.9 1.9 copy-start.17
  209.9 3.9 %copy-start.19 = (s32[2]{0:T(128)S(1)}, s32[2]{0:T(128)}, u32[]{:S(2)}) copy-start(s32[2]{0:T(128)} %param.17) | copy-start | bytes 28

commit v12 on v11

--- a/solution.py
+++ b/solution.py
@@ -147,7 +147,7 @@
     return phase(partial, send_x, recv_x, sx, rx, nx, mx, along_x)
 
 
-def solve_kernel(ny, nx, surf_ref, inside_ref, own_ref, out_ref, frame, hsend, hrecv, *bufs):
+def solve_kernel(ny, nx, tu_ref, tv_ref, eta_ref, inside_ref, own_ref, out_ref, frame, hsend, hrecv, *bufs):
     mesh_id = pl.DeviceIdType.MESH
     member = lax.axis_index("member")
     my = lax.axis_index("gridy")
@@ -164,11 +164,13 @@
             pl.semaphore_signal(
                 barrier, 1, device_id=(member, (my + dy) % ny, (mx + dx) % nx), device_id_type=mesh_id
             )
-    rows, cols = surf_ref.shape[2], surf_ref.shape[3]
+    rows, cols = eta_ref.shape[1], eta_ref.shape[2]
     wide_rows, wide_cols = frame.shape[2], frame.shape[3]
     band = (wide_rows - rows) // 2
     block = (wide_cols - cols) // 2
-    frame[:, :, 0:rows, 0:cols] = surf_ref[...]
+    frame[0, :, 0:rows, 0:cols] = tu_ref[...]
+    frame[1, :, 0:rows, 0:cols] = tv_ref[...]
+    frame[2, :, 0:rows, 0:cols] = eta_ref[...]
     pl.semaphore_wait(barrier, (ny - 1) + (nx - 1) + 4)
 
     def halo_copies(first, moves):
@@ -206,7 +208,7 @@
         (frame.at[:, :, low_rows, east_part], frame.at[:, :, south_halo, west_halo], (member, up, right)),
     ])
 
-    members = surf_ref.shape[1]
+    members = eta_ref.shape[0]
     inside = inside_ref[...]
     own = own_ref[...] > 0.5
 
@@ -274,14 +276,15 @@
         out_ref[2, m] = (north(x) - south(x))[0:rows, 0:cols]
 
 
-def surface_kernel_solve(surf, inside, own):
+def surface_kernel_solve(trans_u, trans_v, eta, inside, own):
     ny = lax.axis_size("gridy")
     nx = lax.axis_size("gridx")
-    fields, members, rows, cols = surf.shape
+    members, rows, cols = eta.shape
+    fields = 3
     return pl.pallas_call(
         functools.partial(solve_kernel, ny, nx),
         out_shape=jax.ShapeDtypeStruct((3, members, rows, cols), jnp.float32),
-        in_specs=[pl.BlockSpec(memory_space=pltpu.VMEM)] * 3,
+        in_specs=[pl.BlockSpec(memory_space=pltpu.VMEM)] * 5,
         out_specs=pl.BlockSpec(memory_space=pltpu.VMEM),
         scratch_shapes=[
             pltpu.VMEM((fields, members) + inside.shape, jnp.float32),
@@ -297,7 +300,7 @@
             pltpu.SemaphoreType.DMA((ITERS, nx)),
         ],
         compiler_params=pltpu.CompilerParams(collective_id=1, has_side_effects=True),
-    )(surf, inside, own)
+    )(trans_u, trans_v, eta, inside, own)
 
 
 def volume_kernel(temp_ref, salt_ref, uvel_ref, vvel_ref, ocean_ref, cor_ref, n_ref, s_ref, e_ref, w_ref,
@@ -555,7 +558,7 @@
         temp_next, salt_next, ustar, vstar, trans_u, trans_v = volume_step(
             temp, salt, uvel, vvel, ocean, cor_tile, rims
         )
-        solved = surface_kernel_solve(jnp.stack((trans_u, trans_v, eta)), wide_inside, own_mask)
+        solved = surface_kernel_solve(trans_u, trans_v, eta, wide_inside, own_mask)
         eta = solved[0]
         east_west = solved[1]
         north_south = solved[2]

time: 215 us -> 213 us (level)
  other arithmetic: 26.6 us -> 23.2 us
    another operation x2 -> x0, other arithmetic: 3.66 us -> none  [shards(): jnp.stack((trans_u, trans_v, eta))]
where the time goes in v12:
time: 213 us; the launch traced here: 212 us
  Pallas kernels  122 us (57%)
  other arithmetic  23.2 us (11%)
  local copies, waits for them, and re-layouts  21.4 us (10%)
  starting transfers between devices  20.2 us (9%)
  waiting for transfers between devices  19 us (9%)
  between operations  5.71 us (3%)
    pallas_call x2, Pallas kernels, surface_kernel_solve(): pl.pallas_call(functools.partial(solve_kernel, ny, nx), out_shape=jax.Sha...  86.6 us
    pallas_call x1, Pallas kernels, grid_sum(): pl.pallas_call(functools.partial(gather_sum_kernel, ny, nx), out_shape=ja...  25.7 us
    ppermute x1, waiting for transfers between devices, shards(): flows_other = lax.ppermute(flows, 'member', swap)  19 us
    pallas_call x2, Pallas kernels, volume_step(): pl.pallas_call(volume_kernel, grid=(members,), in_specs=[field] * 4 + [pl...  9.92 us
    ppermute x2, starting transfers between devices, exchange_fields(): lax.ppermute(jnp.stack([f[..., :, :1] for f in fields]), 'gridx', bwd_x)  8.68 us
    ppermute x2, starting transfers between devices, exchange_fields(): lax.ppermute(jnp.stack([f[..., :1, :] for f in fields]), 'gridy', bwd_y)  5.89 us
    slice x8, local copies, waits for them, and re-layouts, exchange_fields(): f[..., :, -1:]  4.77 us
  transfers between devices with their start and end apart: 10, of which 1 were waited for; matrix products, arithmetic and copies ran while one was open for 12% of the time, Pallas kernels for 12%

profile of v12, /device:TPU:0, one launch (start us, length us, event | category | flops | bytes accessed | tf_op | source)
XLA Modules:
  0.0 211.6 jit_solution(3584756721749791884)
XLA Ops:
  0.7 1.0 slice_bitcast_fusion.12
  1.7 1.0 slice_bitcast_fusion.10
  2.8 2.9 %collective-permute-start = (f32[4,2,4,1,256]{4,3,2,1,0:T(1,128)S(1)}, f32[4,2,4,1,256]{4,3,2,1,0:T(1,128)S(1)}, u32[]{:S(2)}, u32[]{:S(2)}) collective-permute-start(f32[4,2,4,1,256]{4,3,2,1,0:T(1,128)S(1)} %pad_maximum_fusion.5), channel_id=1, source_target_pairs={{8,0},{16,8},{24,16},{32,24},{40,32},{48,40},{56,48},{0,56},{9,1},... | collective-permute-start | bytes 98312 | tf_op jit(solution)/shard_map/ppermute | solution.py:415
  5.8 1.4 slice_reduce_fusion.10
  7.1 1.4 slice_reduce_fusion.9
  9.2 5.2 %collective-permute-start.2 = (f32[4,2,4,64,1]{3,2,4,1,0:T(4,128)S(1)}, f32[4,2,4,64,1]{3,2,4,1,0:T(4,128)S(1)}, u32[]{:S(2)}, u32[]{:S(2)}) collective-permute-start(f32[4,2,4,64,1]{3,2,4,1,0:T(4,128)S(1)} %pad_maximum_fusion.9), channel_id=1, source_target_pairs={{1,0},{2,1},{3,2},{4,3},{5,4},{6,5},{7,6},{0,7},{9,8},{10,9},{11,1... | collective-permute-start | bytes 24584 | tf_op jit(solution)/shard_map/ppermute | solution.py:417
  21.7 1.4 copy.225.e_ref
  23.1 1.4 copy.226.w_ref
  26.5 4.9 %shard_map.126 = (f32[2,4,64,256]{3,2,1,0:T(8,128)}, f32[2,4,64,256]{3,2,1,0:T(8,128)}, f32[2,4,64,256]{3,2,1,0:T(8,128)}, f32[2,4,64,256]{3,2,1,0:T(8,128)}, f3...) custom-call(f32[2,4,64,256]{3,2,1,0:T(8,128)} %temp_ref.1, f32[2,4,64,256]{3,2,1,0:T(8,128)} %salt_ref.1, ...), custom_call_target="tpu_custom_call" | custom-call | tf_op jit(solution)/shard_map/pallas_call | solution.py:384
  31.4 44.6 %shard_map.127 = f32[3,2,64,256]{3,2,1,0:T(8,128)} custom-call(f32[2,64,256]{2,1,0:T(8,128)} %get-tuple-element.46.tu_ref, f32[2,64,256]{2,1,0:T(8,128)} %get-tuple-element.47.tv_ref, f32[2,64,256]{2,1,0:T(8,128)} %eta_ref.1, f32[80,512]{1,0:T(8,128)} %get-tuple-element.150.inside_ref, f32[80,512]{1,0:T(8,128)} %get-tuple-element.151.own_ref), custom_call_target="tpu_custom_call" | custom-call | tf_op jit(solution)/shard_map/pallas_call | solution.py:284
  76.1 1.7 slice_bitcast_fusion.1
  80.5 3.5 %collective-permute-start.6 = (f32[4,2,4,64,1]{3,2,4,1,0:T(4,128)S(1)}, f32[4,2,4,64,1]{3,2,4,1,0:T(4,128)S(1)}, u32[]{:S(2)}, u32[]{:S(2)}) collective-permute-start(f32[4,2,4,64,1]{3,2,4,1,0:T(4,128)S(1)} %pad_maximum_fusion.11), channel_id=1, source_target_pairs={{1,0},{2,1},{3,2},{4,3},{5,4},{6,5},{7,6},{0,7},{9,8},{10,9},{11,1... | collective-permute-start | bytes 24584 | tf_op jit(solution)/shard_map/ppermute | solution.py:417
  84.1 2.9 %collective-permute-start.4 = (f32[4,2,4,1,256]{4,3,2,1,0:T(1,128)S(1)}, f32[4,2,4,1,256]{4,3,2,1,0:T(1,128)S(1)}, u32[]{:S(2)}, u32[]{:S(2)}) collective-permute-start(f32[4,2,4,1,256]{4,3,2,1,0:T(1,128)S(1)} %pad_maximum_fusion.7), channel_id=1, source_target_pairs={{8,0},{16,8},{24,16},{32,24},{40,32},{48,40},{56,48},{0,56},{9,1},... | collective-permute-start | bytes 98312 | tf_op jit(solution)/shard_map/ppermute | solution.py:415
  87.0 1.4 copy.240.w_ref
  88.5 1.4 copy.239.e_ref
  91.2 5.0 %shard_map.128 = (f32[2,4,64,256]{3,2,1,0:T(8,128)}, f32[2,4,64,256]{3,2,1,0:T(8,128)}, f32[2,4,64,256]{3,2,1,0:T(8,128)}, f32[2,4,64,256]{3,2,1,0:T(8,128)}, f3...) custom-call(f32[2,4,64,256]{3,2,1,0:T(8,128)} %get-tuple-element.43.temp_ref, f32[2,4,64,256]{3,2,1,0:T(8,128)} %get-tuple-element.44.salt_ref, ...), custom_call_target="tpu_custom_call" | custom-call | tf_op jit(solution)/shard_map/pallas_call | solution.py:384
  96.2 42.0 %shard_map.129 = f32[3,2,64,256]{3,2,1,0:T(8,128)} custom-call(f32[2,64,256]{2,1,0:T(8,128)} %get-tuple-element.52.tu_ref, f32[2,64,256]{2,1,0:T(8,128)} %get-tuple-element.53.tv_ref, f32[2,64,256]{2,1,0:T(8,128)} %get-tuple-element.132.eta_ref, f32[80,512]{1,0:T(8,128)} %get-tuple-element.150.inside_ref, f32[80,512]{1,0:T(8,128)} %get-tuple-element.151.own_ref), custom_call_target="tpu_custom_call" | custom-call | tf_op jit(solution)/shard_map/pallas_call | solution.py:284
  138.2 1.1 multiply_bitcast_fusion.1
  140.4 1.1 pad_maximum_fusion.1
  141.5 2.9 %collective-permute-start.8 = (f32[2,2,4,64,256]{4,3,2,1,0:T(8,128)}, f32[2,2,4,64,256]{4,3,2,1,0:T(8,128)}, u32[]{:S(2)}, u32[]{:S(2)}) collective-permute-start(f32[2,2,4,64,256]{4,3,2,1,0:T(8,128)} %pad_maximum_fusion.1), channel_id=1, source_target_pairs={{0,64},{64,0},{1,65},{65,1},{2,66},{66,2},{3,67},{67,3},{4,68},{68... | collective-permute-start | bytes 3145736 | tf_op jit(solution)/shard_map/ppermute | solution.py:568
  145.2 25.7 %shard_map.130 = f32[40,128]{1,0:T(8,128)} custom-call(f32[40,128]{1,0:T(8,128)} %select_maximum_fusion.1.x_ref), custom_call_target="tpu_custom_call" | custom-call | tf_op jit(solution)/shard_map/pallas_call | solution.py:90
  170.9 1.3 fusion.10
  173.6 1.9 collective-permute-start.9
  175.6 1.3 pad_clamp_fusion
  179.1 1.3 fusion.14
  180.4 1.3 bitcast_select_fusion.1
  181.7 1.3 bitcast_select_fusion.3
  183.9 0.8 pad_maximum_fusion.2
  184.7 19.0 %collective-permute-done.9 = f32[2,10,64,256]{3,2,1,0:T(8,128)} collective-permute-done((f32[2,10,64,256]{3,2,1,0:T(8,128)S(1)}, f32[2,10,64,256]{3,2,1,0:T(8,128)}, u32[]{:S(2)}, u32[]{:S(2)}) %collective-permute-start.9) | collective-permute-done | bytes 1310752 | tf_op jit(solution)/shard_map/ppermute | solution.py:590
  203.7 1.3 slice.272
  205.0 1.4 dynamic-slice_select_fusion
  207.1 1.0 fusion
  (109 shorter events, 19.9 us)
Async XLA Ops:
  0.6 8.2 %copy-start.2 = (f32[2,4,64,256]{3,2,1,0:T(8,128)S(1)}, f32[2,4,64,256]{3,2,1,0:T(8,128)}, u32[]{:S(2)}) copy-start(f32[2,4,64,256]{3,2,1,0:T(8,128)} %temp_ref.1) | copy-start | bytes 1572868
  0.6 7.9 %copy-start.3 = (f32[2,4,64,256]{3,2,1,0:T(8,128)S(1)}, f32[2,4,64,256]{3,2,1,0:T(8,128)}, u32[]{:S(2)}) copy-start(f32[2,4,64,256]{3,2,1,0:T(8,128)} %vvel_ref.1) | copy-start | bytes 1572868
  0.7 13.9 %copy-start.17 = (s32[2]{0:T(128)S(1)}, s32[2]{0:T(128)}, u32[]{:S(2)}) copy-start(s32[2]{0:T(128)} %param.17) | copy-start | bytes 28
  2.7 21.8 %collective-permute-start.1 = (f32[4,2,4,1,256]{4,3,2,1,0:T(1,128)S(1)}, f32[4,2,4,1,256]{4,3,2,1,0:T(1,128)S(1)}, u32[]{:S(2)}, u32[]{:S(2)}) collective-permute-start(f32[4,2,4,1,256]{4,3,2,1,0:T(1,128)S(1)} %pad_maximum_fusion.6), channel_id=1, source_target_pairs={{0,8},{8,16},{16,24},{24,32},{32,40},{40,48},{48,56},{56,0},{1,9},... | collective-permute-start | bytes 98312 | tf_op jit(solution)/shard_map/ppermute | solution.py:416
  2.8 16.9 %copy-start.14 = (s32[64,256]{1,0:T(8,128)S(1)}, s32[64,256]{1,0:T(8,128)}, u32[]{:S(2)}) copy-start(s32[64,256]{1,0:T(8,128)} %param.16) | copy-start | bytes 196612
  2.8 22.3 %collective-permute-start = (f32[4,2,4,1,256]{4,3,2,1,0:T(1,128)S(1)}, f32[4,2,4,1,256]{4,3,2,1,0:T(1,128)S(1)}, u32[]{:S(2)}, u32[]{:S(2)}) collective-permute-start(f32[4,2,4,1,256]{4,3,2,1,0:T(1,128)S(1)} %pad_maximum_fusion.5), channel_id=1, source_target_pairs={{8,0},{16,8},{24,16},{32,24},{40,32},{48,40},{56,48},{0,56},{9,1},... | collective-permute-start | bytes 98312 | tf_op jit(solution)/shard_map/ppermute | solution.py:415
  9.2 12.4 %collective-permute-start.2 = (f32[4,2,4,64,1]{3,2,4,1,0:T(4,128)S(1)}, f32[4,2,4,64,1]{3,2,4,1,0:T(4,128)S(1)}, u32[]{:S(2)}, u32[]{:S(2)}) collective-permute-start(f32[4,2,4,64,1]{3,2,4,1,0:T(4,128)S(1)} %pad_maximum_fusion.9), channel_id=1, source_target_pairs={{1,0},{2,1},{3,2},{4,3},{5,4},{6,5},{7,6},{0,7},{9,8},{10,9},{11,1... | collective-permute-start | bytes 24584 | tf_op jit(solution)/shard_map/ppermute | solution.py:417
  14.4 8.7 %collective-permute-start.3 = (f32[4,2,4,64,1]{3,2,4,1,0:T(4,128)S(1)}, f32[4,2,4,64,1]{3,2,4,1,0:T(4,128)S(1)}, u32[]{:S(2)}, u32[]{:S(2)}) collective-permute-start(f32[4,2,4,64,1]{3,2,4,1,0:T(4,128)S(1)} %pad_maximum_fusion.10), channel_id=1, source_target_pairs={{0,1},{1,2},{2,3},{3,4},{4,5},{5,6},{6,7},{7,0},{8,9},{9,10},{10,1... | collective-permute-start | bytes 24584 | tf_op jit(solution)/shard_map/ppermute | solution.py:418
  14.5 125.0 %copy-start.15 = (pred[8]{0:T(512)(128)(4,1)}, pred[8]{0:T(512)(128)(4,1)S(1)}, u32[]{:S(2)}) copy-start(pred[8]{0:T(512)(128)(4,1)S(1)} %iota_compare_fusion.4) | copy-start | bytes 28
  31.4 46.4 %copy-start.8 = (f32[64,256]{1,0:T(8,128)S(1)}, f32[64,256]{1,0:T(8,128)}, u32[]{:S(2)}) copy-start(f32[64,256]{1,0:T(8,128)} %convert_element_type.35.ocean_ref) | copy-start | bytes 196612
  31.4 46.4 %copy-start.12 = (f32[2,4,64,256]{3,2,1,0:T(8,128)S(1)}, f32[2,4,64,256]{3,2,1,0:T(8,128)}, u32[]{:S(2)}) copy-start(f32[2,4,64,256]{3,2,1,0:T(8,128)} %get-tuple-element.45) | copy-start | bytes 1572868
  31.4 46.4 %copy-start.13 = (f32[2,4,64,256]{3,2,1,0:T(8,128)S(1)}, f32[2,4,64,256]{3,2,1,0:T(8,128)}, u32[]{:S(2)}) copy-start(f32[2,4,64,256]{3,2,1,0:T(8,128)} %get-tuple-element.48) | copy-start | bytes 1572868
  77.8 1.1 copy-start.4
  77.9 10.6 %copy-start = (f32[2,4,64,256]{3,2,1,0:T(8,128)}, f32[2,4,64,256]{3,2,1,0:T(8,128)S(1)}, u32[]{:S(2)}) copy-start(f32[2,4,64,256]{3,2,1,0:T(8,128)S(1)} %get-tuple-element.136.vvel_ref) | copy-start | bytes 1572868
  77.9 10.6 %copy-start.1 = (f32[2,4,64,256]{3,2,1,0:T(8,128)}, f32[2,4,64,256]{3,2,1,0:T(8,128)S(1)}, u32[]{:S(2)}) copy-start(f32[2,4,64,256]{3,2,1,0:T(8,128)S(1)} %get-tuple-element.137.uvel_ref) | copy-start | bytes 1572868
  77.9 1.5 copy-start.5
  79.8 7.3 %collective-permute-start.7 = (f32[4,2,4,64,1]{3,2,4,1,0:T(4,128)S(1)}, f32[4,2,4,64,1]{3,2,4,1,0:T(4,128)S(1)}, u32[]{:S(2)}, u32[]{:S(2)}) collective-permute-start(f32[4,2,4,64,1]{3,2,4,1,0:T(4,128)S(1)} %pad_maximum_fusion.12), channel_id=1, source_target_pairs={{0,1},{1,2},{2,3},{3,4},{4,5},{5,6},{6,7},{7,0},{8,9},{9,10},{10,1... | collective-permute-start | bytes 24584 | tf_op jit(solution)/shard_map/ppermute | solution.py:418
  80.5 8.0 %collective-permute-start.6 = (f32[4,2,4,64,1]{3,2,4,1,0:T(4,128)S(1)}, f32[4,2,4,64,1]{3,2,4,1,0:T(4,128)S(1)}, u32[]{:S(2)}, u32[]{:S(2)}) collective-permute-start(f32[4,2,4,64,1]{3,2,4,1,0:T(4,128)S(1)} %pad_maximum_fusion.11), channel_id=1, source_target_pairs={{1,0},{2,1},{3,2},{4,3},{5,4},{6,5},{7,6},{0,7},{9,8},{10,9},{11,1... | collective-permute-start | bytes 24584 | tf_op jit(solution)/shard_map/ppermute | solution.py:417
  84.0 5.9 %collective-permute-start.5 = (f32[4,2,4,1,256]{4,3,2,1,0:T(1,128)S(1)}, f32[4,2,4,1,256]{4,3,2,1,0:T(1,128)S(1)}, u32[]{:S(2)}, u32[]{:S(2)}) collective-permute-start(f32[4,2,4,1,256]{4,3,2,1,0:T(1,128)S(1)} %pad_maximum_fusion.8), channel_id=1, source_target_pairs={{0,8},{8,16},{16,24},{24,32},{32,40},{40,48},{48,56},{56,0},{1,9},... | collective-permute-start | bytes 98312 | tf_op jit(solution)/shard_map/ppermute | solution.py:416
  84.1 6.4 %collective-permute-start.4 = (f32[4,2,4,1,256]{4,3,2,1,0:T(1,128)S(1)}, f32[4,2,4,1,256]{4,3,2,1,0:T(1,128)S(1)}, u32[]{:S(2)}, u32[]{:S(2)}) collective-permute-start(f32[4,2,4,1,256]{4,3,2,1,0:T(1,128)S(1)} %pad_maximum_fusion.7), channel_id=1, source_target_pairs={{8,0},{16,8},{24,16},{32,24},{40,32},{48,40},{56,48},{0,56},{9,1},... | collective-permute-start | bytes 98312 | tf_op jit(solution)/shard_map/ppermute | solution.py:415
  96.1 43.1 %copy-start.9 = (f32[64,256]{1,0:T(8,128)S(1)}, f32[64,256]{1,0:T(8,128)}, u32[]{:S(2)}) copy-start(f32[64,256]{1,0:T(8,128)} %convert_element_type.35.ocean_ref) | copy-start | bytes 196612
  96.2 43.1 %copy-start.10 = (f32[2,4,64,256]{3,2,1,0:T(8,128)S(1)}, f32[2,4,64,256]{3,2,1,0:T(8,128)}, u32[]{:S(2)}) copy-start(f32[2,4,64,256]{3,2,1,0:T(8,128)} %get-tuple-element.51) | copy-start | bytes 1572868
  96.2 43.1 %copy-start.11 = (f32[2,4,64,256]{3,2,1,0:T(8,128)S(1)}, f32[2,4,64,256]{3,2,1,0:T(8,128)}, u32[]{:S(2)}) copy-start(f32[2,4,64,256]{3,2,1,0:T(8,128)} %get-tuple-element.54) | copy-start | bytes 1572868
  139.2 1.0 copy-start.6
  139.2 1.2 copy-start.7
  141.5 37.6 %collective-permute-start.8 = (f32[2,2,4,64,256]{4,3,2,1,0:T(8,128)}, f32[2,2,4,64,256]{4,3,2,1,0:T(8,128)}, u32[]{:S(2)}, u32[]{:S(2)}) collective-permute-start(f32[2,2,4,64,256]{4,3,2,1,0:T(8,128)} %pad_maximum_fusion.1), channel_id=1, source_target_pairs={{0,64},{64,0},{1,65},{65,1},{2,66},{66,2},{3,67},{67,3},{4,68},{68... | collective-permute-start | bytes 3145736 | tf_op jit(solution)/shard_map/ppermute | solution.py:568
  170.9 5.9 %slice-start = ((f32[40,128]{1,0:T(8,128)}), f32[32,128]{1,0:T(8,128)S(1)}, s32[]{:S(2)}) async-start(f32[40,128]{1,0:T(8,128)} %shard_map.130), calls=%async_computation | async-start | bytes 32768 | tf_op jit(solution)/shard_map/slice | solution.py:582
  173.6 30.0 %collective-permute-start.9 = (f32[2,10,64,256]{3,2,1,0:T(8,128)S(1)}, f32[2,10,64,256]{3,2,1,0:T(8,128)}, u32[]{:S(2)}, u32[]{:S(2)}) collective-permute-start(f32[2,10,64,256]{3,2,1,0:T(8,128)S(1)} %select_maximum_fusion), channel_id=1, source_target_pairs={{0,64},{64,0},{1,65},{65,1},{2,66},{66,2},{3,67},{67,3},{4,68},{68... | collective-permute-start | bytes 3932168 | tf_op jit(solution)/shard_map/ppermute | solution.py:590
  207.1 1.9 copy-start.16
  207.1 3.9 %copy-start.18 = (s32[2]{0:T(128)S(1)}, s32[2]{0:T(128)}, u32[]{:S(2)}) copy-start(s32[2]{0:T(128)} %param.17) | copy-start | bytes 28

commit v13 on v12

--- a/solution.py
+++ b/solution.py
@@ -303,17 +303,21 @@
     )(trans_u, trans_v, eta, inside, own)
 
 
-def volume_kernel(temp_ref, salt_ref, uvel_ref, vvel_ref, ocean_ref, cor_ref, n_ref, s_ref, e_ref, w_ref,
+def volume_kernel(ny, temp_ref, salt_ref, uvel_ref, vvel_ref, land_ref, n_ref, s_ref, e_ref, w_ref,
                   tn_ref, sn_ref, us_ref, vs_ref, tu_ref, tv_ref):
     levels, rows, cols = temp_ref.shape[1], temp_ref.shape[2], temp_ref.shape[3]
     row = lax.broadcasted_iota(jnp.int32, (rows, cols), 0)
     col = lax.broadcasted_iota(jnp.int32, (rows, cols), 1)
+    tile_row = lax.axis_index("gridy")
+    north_keep = jnp.where(tile_row < ny - 1, 1.0, 0.0)
+    south_keep = jnp.where(tile_row > 0, 1.0, 0.0)
+    latitude = (tile_row * rows + row).astype(jnp.float32) + 0.5
     top = row == rows - 1
     bottom = row == 0
     right = col == cols - 1
     left = col == 0
-    ocean = ocean_ref[...]
-    cor = cor_ref[...]
+    ocean = land_ref[...].astype(jnp.float32)
+    cor = CORI_K * (2.0 * latitude / (rows * ny) - 1.0)
 
     def around(f, rims):
         n, s, e, w = rims
@@ -325,7 +329,7 @@
         )
 
     def rims_of(k, l):
-        return (n_ref[k, 0, l], s_ref[k, 0, l], e_ref[k, 0, l], w_ref[k, 0, l])
+        return (n_ref[k, 0, l] * north_keep, s_ref[k, 0, l] * south_keep, e_ref[k, 0, l], w_ref[k, 0, l])
 
     running = None
     running_rims = None
@@ -371,7 +375,7 @@
     tv_ref[0] = tv
 
 
-def volume_step(temp, salt, uvel, vvel, ocean, cor_tile, rims):
+def volume_step(temp, salt, uvel, vvel, land_mask, rims):
     members, levels, rows, cols = temp.shape
     field = pl.BlockSpec((1, levels, rows, cols), lambda m: (m, 0, 0, 0))
     plane = pl.BlockSpec((rows, cols), lambda m: (0, 0))
@@ -382,12 +386,12 @@
     volume_shape = jax.ShapeDtypeStruct(temp.shape, jnp.float32)
     surface_shape = jax.ShapeDtypeStruct((members, rows, cols), jnp.float32)
     return pl.pallas_call(
-        volume_kernel,
+        functools.partial(volume_kernel, lax.axis_size("gridy")),
         grid=(members,),
-        in_specs=[field] * 4 + [plane, plane, row_rim, row_rim, col_rim, col_rim],
+        in_specs=[field] * 4 + [plane, row_rim, row_rim, col_rim, col_rim],
         out_specs=[field] * 4 + [surface] * 2,
         out_shape=[volume_shape] * 4 + [surface_shape] * 2,
-    )(temp, salt, uvel, vvel, ocean, cor_tile, north, south, east, west)
+    )(temp, salt, uvel, vvel, land_mask, north, south, east, west)
 
 
 def ring(axis):
@@ -412,8 +416,8 @@
 def exchange_fields(fields, south_keep, north_keep):
     fwd_y, bwd_y = ring("gridy")
     fwd_x, bwd_x = ring("gridx")
-    north = lax.ppermute(jnp.stack([f[..., :1, :] for f in fields]), "gridy", bwd_y) * north_keep
-    south = lax.ppermute(jnp.stack([f[..., -1:, :] for f in fields]), "gridy", fwd_y) * south_keep
+    north = lax.ppermute(jnp.stack([f[..., :1, :] for f in fields]), "gridy", bwd_y)
+    south = lax.ppermute(jnp.stack([f[..., -1:, :] for f in fields]), "gridy", fwd_y)
     east = lax.ppermute(jnp.stack([f[..., :, :1] for f in fields]), "gridx", bwd_x)
     west = lax.ppermute(jnp.stack([f[..., :, -1:] for f in fields]), "gridx", fwd_x)
     return (north, south, east, west)
@@ -556,7 +560,7 @@
         fields = (temp, salt, uvel, vvel)
         rims = exchange_fields(fields, south_keep, north_keep)
         temp_next, salt_next, ustar, vstar, trans_u, trans_v = volume_step(
-            temp, salt, uvel, vvel, ocean, cor_tile, rims
+            temp, salt, uvel, vvel, land_mask, rims
         )
         solved = surface_kernel_solve(trans_u, trans_v, eta, wide_inside, own_mask)
         eta = solved[0]

time: 213 us -> 211 us (level)
  other arithmetic: 23.2 us -> 20.4 us
    pallas_call x2, Pallas kernels: 86.6 us -> 84.1 us  [surface_kernel_solve(): pl.pallas_call(functools.partial(solve_kernel, ny, nx), out_shape=jax.Sha...]
    mul x4 -> x0, other arithmetic: 2.51 us -> none  [the longest x2 1.26 us: exchange_fields(): lax.ppermute(jnp.stack([f[..., -1:, :] for f in fields]), 'gridy', fwd_y)]
    unnamed x38 -> x42, local copies, waits for them, and re-layouts: 1.26 us -> 3.66 us
  transfers between devices with their start and end apart: 10 -> 10, of which waited for: 1 -> 2; matrix products, arithmetic and copies ran while one was open for 12% -> 12% of each run, Pallas kernels for 12% -> 12%
where the time goes in v13:
time: 211 us; the launch traced here: 210 us
  Pallas kernels  120 us (57%)
  local copies, waits for them, and re-layouts  23.1 us (11%)
  other arithmetic  20.4 us (10%)
  waiting for transfers between devices  20.3 us (10%)
  starting transfers between devices  20.2 us (10%)
  between operations  5.62 us (3%)
    pallas_call x2, Pallas kernels, surface_kernel_solve(): pl.pallas_call(functools.partial(solve_kernel, ny, nx), out_shape=jax.Sha...  84.1 us
    pallas_call x1, Pallas kernels, grid_sum(): pl.pallas_call(functools.partial(gather_sum_kernel, ny, nx), out_shape=ja...  26.1 us
    ppermute x1, waiting for transfers between devices, shards(): flows_other = lax.ppermute(flows, 'member', swap)  18.6 us
    pallas_call x2, Pallas kernels, volume_step(): pl.pallas_call(functools.partial(volume_kernel, lax.axis_size('gridy')),...  9.9 us
    ppermute x2, starting transfers between devices, exchange_fields(): lax.ppermute(jnp.stack([f[..., :, :1] for f in fields]), 'gridx', bwd_x)  8.5 us
    ppermute x2, starting transfers between devices, exchange_fields(): lax.ppermute(jnp.stack([f[..., :1, :] for f in fields]), 'gridy', bwd_y)  5.89 us
    slice x8, local copies, waits for them, and re-layouts, exchange_fields(): f[..., :, -1:]  4.77 us
    select_n x3, other arithmetic, pick(): chosen.append(jnp.where(here[place], from_here, from_other))  4.44 us
  transfers between devices with their start and end apart: 10, of which 2 were waited for; matrix products, arithmetic and copies ran while one was open for 12% of the time, Pallas kernels for 12%

profile of v13, /device:TPU:0, one launch (start us, length us, event | category | flops | bytes accessed | tf_op | source)
XLA Modules:
  0.0 209.8 jit_solution(13958524343648279417)
XLA Ops:
  0.7 1.0 slice_bitcast_fusion.12
  1.7 1.0 slice_bitcast_fusion.10
  2.8 2.9 %collective-permute-start = (f32[4,2,4,1,256]{4,3,2,1,0:T(1,128)S(1)}, f32[4,2,4,1,256]{4,3,2,1,0:T(1,128)S(1)}, u32[]{:S(2)}, u32[]{:S(2)}) collective-permute-start(f32[4,2,4,1,256]{4,3,2,1,0:T(1,128)S(1)} %pad_maximum_fusion.5), channel_id=1, source_target_pairs={{8,0},{16,8},{24,16},{32,24},{40,32},{48,40},{56,48},{0,56},{9,1},... | collective-permute-start | bytes 98312 | tf_op jit(solution)/shard_map/ppermute | solution.py:419
  5.8 1.4 slice_reduce_fusion.10
  7.1 1.4 slice_reduce_fusion.9
  9.2 5.2 %collective-permute-start.2 = (f32[4,2,4,64,1]{3,2,4,1,0:T(4,128)S(1)}, f32[4,2,4,64,1]{3,2,4,1,0:T(4,128)S(1)}, u32[]{:S(2)}, u32[]{:S(2)}) collective-permute-start(f32[4,2,4,64,1]{3,2,4,1,0:T(4,128)S(1)} %pad_maximum_fusion.9), channel_id=1, source_target_pairs={{1,0},{2,1},{3,2},{4,3},{5,4},{6,5},{7,6},{0,7},{9,8},{10,9},{11,1... | collective-permute-start | bytes 24584 | tf_op jit(solution)/shard_map/ppermute | solution.py:421
  17.2 1.4 copy.205.e_ref
  18.6 1.7 collective-permute-done.3
  20.3 1.4 copy.206.w_ref
  22.9 4.9 %shard_map.126 = (f32[2,4,64,256]{3,2,1,0:T(8,128)}, f32[2,4,64,256]{3,2,1,0:T(8,128)}, f32[2,4,64,256]{3,2,1,0:T(8,128)}, f32[2,4,64,256]{3,2,1,0:T(8,128)}, f3...) custom-call(f32[2,4,64,256]{3,2,1,0:T(8,128)} %temp_ref.1, f32[2,4,64,256]{3,2,1,0:T(8,128)} %salt_ref.1, ...), custom_call_target="tpu_custom_call" | custom-call | tf_op jit(solution)/shard_map/pallas_call | solution.py:388
  27.9 42.9 %shard_map.127 = f32[3,2,64,256]{3,2,1,0:T(8,128)} custom-call(f32[2,64,256]{2,1,0:T(8,128)} %get-tuple-element.46.tu_ref, f32[2,64,256]{2,1,0:T(8,128)} %get-tuple-element.47.tv_ref, f32[2,64,256]{2,1,0:T(8,128)} %eta_ref.1, f32[80,512]{1,0:T(8,128)} %get-tuple-element.150.inside_ref, f32[80,512]{1,0:T(8,128)} %get-tuple-element.151.own_ref), custom_call_target="tpu_custom_call" | custom-call | tf_op jit(solution)/shard_map/pallas_call | solution.py:284
  70.8 1.7 slice_bitcast_fusion.1
  75.4 3.3 %collective-permute-start.6 = (f32[4,2,4,64,1]{3,2,4,1,0:T(4,128)S(1)}, f32[4,2,4,64,1]{3,2,4,1,0:T(4,128)S(1)}, u32[]{:S(2)}, u32[]{:S(2)}) collective-permute-start(f32[4,2,4,64,1]{3,2,4,1,0:T(4,128)S(1)} %pad_maximum_fusion.11), channel_id=1, source_target_pairs={{1,0},{2,1},{3,2},{4,3},{5,4},{6,5},{7,6},{0,7},{9,8},{10,9},{11,1... | collective-permute-start | bytes 24584 | tf_op jit(solution)/shard_map/ppermute | solution.py:421
  78.8 2.9 %collective-permute-start.4 = (f32[4,2,4,1,256]{4,3,2,1,0:T(1,128)S(1)}, f32[4,2,4,1,256]{4,3,2,1,0:T(1,128)S(1)}, u32[]{:S(2)}, u32[]{:S(2)}) collective-permute-start(f32[4,2,4,1,256]{4,3,2,1,0:T(1,128)S(1)} %pad_maximum_fusion.7), channel_id=1, source_target_pairs={{8,0},{16,8},{24,16},{32,24},{40,32},{48,40},{56,48},{0,56},{9,1},... | collective-permute-start | bytes 98312 | tf_op jit(solution)/shard_map/ppermute | solution.py:419
  85.6 1.4 copy.220.w_ref
  87.1 1.4 copy.219.e_ref
  89.7 5.0 %shard_map.128 = (f32[2,4,64,256]{3,2,1,0:T(8,128)}, f32[2,4,64,256]{3,2,1,0:T(8,128)}, f32[2,4,64,256]{3,2,1,0:T(8,128)}, f32[2,4,64,256]{3,2,1,0:T(8,128)}, f3...) custom-call(f32[2,4,64,256]{3,2,1,0:T(8,128)} %get-tuple-element.43.temp_ref, f32[2,4,64,256]{3,2,1,0:T(8,128)} %get-tuple-element.44.salt_ref, ...), custom_call_target="tpu_custom_call" | custom-call | tf_op jit(solution)/shard_map/pallas_call | solution.py:388
  94.7 41.2 %shard_map.129 = f32[3,2,64,256]{3,2,1,0:T(8,128)} custom-call(f32[2,64,256]{2,1,0:T(8,128)} %get-tuple-element.52.tu_ref, f32[2,64,256]{2,1,0:T(8,128)} %get-tuple-element.53.tv_ref, f32[2,64,256]{2,1,0:T(8,128)} %get-tuple-element.132.eta_ref, f32[80,512]{1,0:T(8,128)} %get-tuple-element.150.inside_ref, f32[80,512]{1,0:T(8,128)} %get-tuple-element.151.own_ref), custom_call_target="tpu_custom_call" | custom-call | tf_op jit(solution)/shard_map/pallas_call | solution.py:284
  135.9 1.1 multiply_bitcast_fusion.1
  138.1 1.1 pad_maximum_fusion.1
  139.2 2.9 %collective-permute-start.8 = (f32[2,2,4,64,256]{4,3,2,1,0:T(8,128)}, f32[2,2,4,64,256]{4,3,2,1,0:T(8,128)}, u32[]{:S(2)}, u32[]{:S(2)}) collective-permute-start(f32[2,2,4,64,256]{4,3,2,1,0:T(8,128)} %pad_maximum_fusion.1), channel_id=1, source_target_pairs={{0,64},{64,0},{1,65},{65,1},{2,66},{66,2},{3,67},{67,3},{4,68},{68... | collective-permute-start | bytes 3145736 | tf_op jit(solution)/shard_map/ppermute | solution.py:572
  142.9 26.1 %shard_map.130 = f32[40,128]{1,0:T(8,128)} custom-call(f32[40,128]{1,0:T(8,128)} %select_maximum_fusion.1.x_ref), custom_call_target="tpu_custom_call" | custom-call | tf_op jit(solution)/shard_map/pallas_call | solution.py:90
  169.1 1.3 fusion.9
  171.8 1.9 collective-permute-start.9
  173.7 1.3 pad_clamp_fusion
  177.2 1.3 fusion.13
  178.5 1.4 bitcast_select_fusion.1
  180.0 1.4 bitcast_select_fusion.3
  183.1 18.6 %collective-permute-done.9 = f32[2,10,64,256]{3,2,1,0:T(8,128)} collective-permute-done((f32[2,10,64,256]{3,2,1,0:T(8,128)S(1)}, f32[2,10,64,256]{3,2,1,0:T(8,128)}, u32[]{:S(2)}, u32[]{:S(2)}) %collective-permute-start.9) | collective-permute-done | bytes 1310752 | tf_op jit(solution)/shard_map/ppermute | solution.py:594
  201.7 1.3 slice.272
  203.1 1.6 dynamic-slice_select_fusion
  205.3 1.0 fusion
  (107 shorter events, 19.6 us)
Async XLA Ops:
  0.6 8.2 %copy-start.2 = (f32[2,4,64,256]{3,2,1,0:T(8,128)S(1)}, f32[2,4,64,256]{3,2,1,0:T(8,128)}, u32[]{:S(2)}) copy-start(f32[2,4,64,256]{3,2,1,0:T(8,128)} %temp_ref.1) | copy-start | bytes 1572868
  0.6 7.9 %copy-start.3 = (f32[2,4,64,256]{3,2,1,0:T(8,128)S(1)}, f32[2,4,64,256]{3,2,1,0:T(8,128)}, u32[]{:S(2)}) copy-start(f32[2,4,64,256]{3,2,1,0:T(8,128)} %vvel_ref.1) | copy-start | bytes 1572868
  0.7 13.9 %copy-start.19 = (s32[2]{0:T(128)S(1)}, s32[2]{0:T(128)}, u32[]{:S(2)}) copy-start(s32[2]{0:T(128)} %param.17) | copy-start | bytes 28
  2.7 19.0 %collective-permute-start.1 = (f32[4,2,4,1,256]{4,3,2,1,0:T(1,128)S(1)}, f32[4,2,4,1,256]{4,3,2,1,0:T(1,128)S(1)}, u32[]{:S(2)}, u32[]{:S(2)}) collective-permute-start(f32[4,2,4,1,256]{4,3,2,1,0:T(1,128)S(1)} %pad_maximum_fusion.6), channel_id=1, source_target_pairs={{0,8},{8,16},{16,24},{24,32},{32,40},{40,48},{48,56},{56,0},{1,9},... | collective-permute-start | bytes 98312 | tf_op jit(solution)/shard_map/ppermute | solution.py:420
  2.8 14.3 %copy-start.8 = (s32[64,256]{1,0:T(8,128)S(1)}, s32[64,256]{1,0:T(8,128)}, u32[]{:S(2)}) copy-start(s32[64,256]{1,0:T(8,128)} %land_ref.3) | copy-start | bytes 196612
  2.8 18.9 %collective-permute-start = (f32[4,2,4,1,256]{4,3,2,1,0:T(1,128)S(1)}, f32[4,2,4,1,256]{4,3,2,1,0:T(1,128)S(1)}, u32[]{:S(2)}, u32[]{:S(2)}) collective-permute-start(f32[4,2,4,1,256]{4,3,2,1,0:T(1,128)S(1)} %pad_maximum_fusion.5), channel_id=1, source_target_pairs={{8,0},{16,8},{24,16},{32,24},{40,32},{48,40},{56,48},{0,56},{9,1},... | collective-permute-start | bytes 98312 | tf_op jit(solution)/shard_map/ppermute | solution.py:419
  9.2 7.9 %collective-permute-start.2 = (f32[4,2,4,64,1]{3,2,4,1,0:T(4,128)S(1)}, f32[4,2,4,64,1]{3,2,4,1,0:T(4,128)S(1)}, u32[]{:S(2)}, u32[]{:S(2)}) collective-permute-start(f32[4,2,4,64,1]{3,2,4,1,0:T(4,128)S(1)} %pad_maximum_fusion.9), channel_id=1, source_target_pairs={{1,0},{2,1},{3,2},{4,3},{5,4},{6,5},{7,6},{0,7},{9,8},{10,9},{11,1... | collective-permute-start | bytes 24584 | tf_op jit(solution)/shard_map/ppermute | solution.py:421
  14.4 5.8 %collective-permute-start.3 = (f32[4,2,4,64,1]{3,2,4,1,0:T(4,128)S(1)}, f32[4,2,4,64,1]{3,2,4,1,0:T(4,128)S(1)}, u32[]{:S(2)}, u32[]{:S(2)}) collective-permute-start(f32[4,2,4,64,1]{3,2,4,1,0:T(4,128)S(1)} %pad_maximum_fusion.10), channel_id=1, source_target_pairs={{0,1},{1,2},{2,3},{3,4},{4,5},{5,6},{6,7},{7,0},{8,9},{9,10},{10,1... | collective-permute-start | bytes 24584 | tf_op jit(solution)/shard_map/ppermute | solution.py:422
  14.5 122.7 %copy-start.17 = (pred[8]{0:T(512)(128)(4,1)}, pred[8]{0:T(512)(128)(4,1)S(1)}, u32[]{:S(2)}) copy-start(pred[8]{0:T(512)(128)(4,1)S(1)} %iota_compare_fusion.4) | copy-start | bytes 28
  21.7 0.6 copy-start.13
  22.3 0.6 copy-start.14
  27.8 44.7 %copy-start.11 = (f32[2,4,64,256]{3,2,1,0:T(8,128)S(1)}, f32[2,4,64,256]{3,2,1,0:T(8,128)}, u32[]{:S(2)}) copy-start(f32[2,4,64,256]{3,2,1,0:T(8,128)} %get-tuple-element.45) | copy-start | bytes 1572868
  27.9 44.7 %copy-start.12 = (f32[2,4,64,256]{3,2,1,0:T(8,128)S(1)}, f32[2,4,64,256]{3,2,1,0:T(8,128)}, u32[]{:S(2)}) copy-start(f32[2,4,64,256]{3,2,1,0:T(8,128)} %get-tuple-element.48) | copy-start | bytes 1572868
  72.5 1.1 copy-start.4
  72.6 14.4 %copy-start = (f32[2,4,64,256]{3,2,1,0:T(8,128)}, f32[2,4,64,256]{3,2,1,0:T(8,128)S(1)}, u32[]{:S(2)}) copy-start(f32[2,4,64,256]{3,2,1,0:T(8,128)S(1)} %get-tuple-element.136.vvel_ref) | copy-start | bytes 1572868
  72.7 14.4 %copy-start.1 = (f32[2,4,64,256]{3,2,1,0:T(8,128)}, f32[2,4,64,256]{3,2,1,0:T(8,128)S(1)}, u32[]{:S(2)}) copy-start(f32[2,4,64,256]{3,2,1,0:T(8,128)S(1)} %get-tuple-element.137.uvel_ref) | copy-start | bytes 1572868
  72.7 1.5 copy-start.5
  74.5 11.1 %collective-permute-start.7 = (f32[4,2,4,64,1]{3,2,4,1,0:T(4,128)S(1)}, f32[4,2,4,64,1]{3,2,4,1,0:T(4,128)S(1)}, u32[]{:S(2)}, u32[]{:S(2)}) collective-permute-start(f32[4,2,4,64,1]{3,2,4,1,0:T(4,128)S(1)} %pad_maximum_fusion.12), channel_id=1, source_target_pairs={{0,1},{1,2},{2,3},{3,4},{4,5},{5,6},{6,7},{7,0},{8,9},{9,10},{10,1... | collective-permute-start | bytes 24584 | tf_op jit(solution)/shard_map/ppermute | solution.py:422
  75.4 11.7 %collective-permute-start.6 = (f32[4,2,4,64,1]{3,2,4,1,0:T(4,128)S(1)}, f32[4,2,4,64,1]{3,2,4,1,0:T(4,128)S(1)}, u32[]{:S(2)}, u32[]{:S(2)}) collective-permute-start(f32[4,2,4,64,1]{3,2,4,1,0:T(4,128)S(1)} %pad_maximum_fusion.11), channel_id=1, source_target_pairs={{1,0},{2,1},{3,2},{4,3},{5,4},{6,5},{7,6},{0,7},{9,8},{10,9},{11,1... | collective-permute-start | bytes 24584 | tf_op jit(solution)/shard_map/ppermute | solution.py:421
  78.8 9.7 %collective-permute-start.5 = (f32[4,2,4,1,256]{4,3,2,1,0:T(1,128)S(1)}, f32[4,2,4,1,256]{4,3,2,1,0:T(1,128)S(1)}, u32[]{:S(2)}, u32[]{:S(2)}) collective-permute-start(f32[4,2,4,1,256]{4,3,2,1,0:T(1,128)S(1)} %pad_maximum_fusion.8), channel_id=1, source_target_pairs={{0,8},{8,16},{16,24},{24,32},{32,40},{40,48},{48,56},{56,0},{1,9},... | collective-permute-start | bytes 98312 | tf_op jit(solution)/shard_map/ppermute | solution.py:420
  78.8 9.7 %collective-permute-start.4 = (f32[4,2,4,1,256]{4,3,2,1,0:T(1,128)S(1)}, f32[4,2,4,1,256]{4,3,2,1,0:T(1,128)S(1)}, u32[]{:S(2)}, u32[]{:S(2)}) collective-permute-start(f32[4,2,4,1,256]{4,3,2,1,0:T(1,128)S(1)} %pad_maximum_fusion.7), channel_id=1, source_target_pairs={{8,0},{16,8},{24,16},{32,24},{40,32},{48,40},{56,48},{0,56},{9,1},... | collective-permute-start | bytes 98312 | tf_op jit(solution)/shard_map/ppermute | solution.py:419
  88.5 0.6 copy-start.15
  89.1 0.6 copy-start.16
  94.7 42.3 %copy-start.9 = (f32[2,4,64,256]{3,2,1,0:T(8,128)S(1)}, f32[2,4,64,256]{3,2,1,0:T(8,128)}, u32[]{:S(2)}) copy-start(f32[2,4,64,256]{3,2,1,0:T(8,128)} %get-tuple-element.51) | copy-start | bytes 1572868
  94.7 42.3 %copy-start.10 = (f32[2,4,64,256]{3,2,1,0:T(8,128)S(1)}, f32[2,4,64,256]{3,2,1,0:T(8,128)}, u32[]{:S(2)}) copy-start(f32[2,4,64,256]{3,2,1,0:T(8,128)} %get-tuple-element.54) | copy-start | bytes 1572868
  136.9 1.0 copy-start.6
  136.9 1.2 copy-start.7
  139.2 38.0 %collective-permute-start.8 = (f32[2,2,4,64,256]{4,3,2,1,0:T(8,128)}, f32[2,2,4,64,256]{4,3,2,1,0:T(8,128)}, u32[]{:S(2)}, u32[]{:S(2)}) collective-permute-start(f32[2,2,4,64,256]{4,3,2,1,0:T(8,128)} %pad_maximum_fusion.1), channel_id=1, source_target_pairs={{0,64},{64,0},{1,65},{65,1},{2,66},{66,2},{3,67},{67,3},{4,68},{68... | collective-permute-start | bytes 3145736 | tf_op jit(solution)/shard_map/ppermute | solution.py:572
  169.1 5.9 %slice-start = ((f32[40,128]{1,0:T(8,128)}), f32[32,128]{1,0:T(8,128)S(1)}, s32[]{:S(2)}) async-start(f32[40,128]{1,0:T(8,128)} %shard_map.130), calls=%async_computation | async-start | bytes 32768 | tf_op jit(solution)/shard_map/slice | solution.py:586
  171.8 30.0 %collective-permute-start.9 = (f32[2,10,64,256]{3,2,1,0:T(8,128)S(1)}, f32[2,10,64,256]{3,2,1,0:T(8,128)}, u32[]{:S(2)}, u32[]{:S(2)}) collective-permute-start(f32[2,10,64,256]{3,2,1,0:T(8,128)S(1)} %select_maximum_fusion), channel_id=1, source_target_pairs={{0,64},{64,0},{1,65},{65,1},{2,66},{66,2},{3,67},{67,3},{4,68},{68... | collective-permute-start | bytes 3932168 | tf_op jit(solution)/shard_map/ppermute | solution.py:594
  205.3 1.9 copy-start.18
  205.3 3.9 %copy-start.20 = (s32[2]{0:T(128)S(1)}, s32[2]{0:T(128)}, u32[]{:S(2)}) copy-start(s32[2]{0:T(128)} %param.17) | copy-start | bytes 28

commit v14 on v13

--- a/solution.py
+++ b/solution.py
@@ -589,10 +589,10 @@
     score = summed[zonal_slots.shape[0], :members] * (zonal_scale * score_scale)
     swap = [(0, 1), (1, 0)]
     mine = lax.axis_index("member")
-    score_slab = jnp.zeros((members, 1) + eta.shape[1:], jnp.float32).at[:, 0, 0, 0].set(score)
-    flows = jnp.concatenate([uvel, vvel, eta[:, None], score_slab], axis=1)
+    after_score = eta + 0.0 * jnp.sum(score)
+    flows = jnp.concatenate([uvel, vvel, after_score[:, None]], axis=1)
     flows_other = lax.ppermute(flows, "member", swap)
-    score_other = flows_other[:, 2 * levels + 1, 0, 0]
+    score_other = lax.ppermute(score, "member", swap)
     every_score = jnp.where(
         mine == 0, jnp.concatenate([score, score_other]), jnp.concatenate([score_other, score])
     )

time: 211 us -> 212 us (level)
  waiting for transfers between devices: 20.3 us -> 40.7 us
  Pallas kernels: 120 us -> 106 us
  local copies, waits for them, and re-layouts: 23.1 us -> 18.7 us
  other arithmetic: 20.4 us -> 17.2 us
    ppermute x1, waiting for transfers between devices: 0.01 us -> 20.8 us  [shards(): lax.ppermute(jnp.stack((temp_next, salt_next)), 'member', [(0, 1), (1, 0)])]
    pallas_call x1, Pallas kernels: 26.1 us -> 13 us  [grid_sum(): pl.pallas_call(functools.partial(gather_sum_kernel, ny, nx), out_shape=ja...]
    ppermute x0 -> x1, starting transfers between devices: none -> 2.9 us  [shards(): score_other = lax.ppermute(score, 'member', swap)]
    ppermute x1, starting transfers between devices: 2.9 us -> 0.63 us  [shards(): lax.ppermute(jnp.stack((temp_next, salt_next)), 'member', [(0, 1), (1, 0)])]
    slice x2 -> x0, local copies, waits for them, and re-layouts: 2.17 us -> none  [the longest x1 1.35 us: shards(): new_flows = pick(flows[:, :2 * levels + 1], flows_other[:, :2 * levels + 1])]
  transfers between devices with their start and end apart: 10 -> 11, of which waited for: 2 -> 3; matrix products, arithmetic and copies ran while one was open for 12% -> 10% of each run, Pallas kernels for 12% -> 0%
where the time goes in v14:
time: 212 us; the launch traced here: 211 us
  Pallas kernels  106 us (50%)
  waiting for transfers between devices  40.7 us (19%)
  starting transfers between devices  22.1 us (10%)
  local copies, waits for them, and re-layouts  18.7 us (9%)
  other arithmetic  17.2 us (8%)
  between operations  6.33 us (3%)
    pallas_call x2, Pallas kernels, surface_kernel_solve(): pl.pallas_call(functools.partial(solve_kernel, ny, nx), out_shape=jax.Sha...  83.6 us
    ppermute x1, waiting for transfers between devices, shards(): lax.ppermute(jnp.stack((temp_next, salt_next)), 'member', [(0, 1), (1, 0)])  20.8 us
    ppermute x1, waiting for transfers between devices, shards(): flows_other = lax.ppermute(flows, 'member', swap)  17.6 us
    pallas_call x1, Pallas kernels, grid_sum(): pl.pallas_call(functools.partial(gather_sum_kernel, ny, nx), out_shape=ja...  13 us
    pallas_call x2, Pallas kernels, volume_step(): pl.pallas_call(functools.partial(volume_kernel, lax.axis_size('gridy')),...  9.89 us
    ppermute x2, starting transfers between devices, exchange_fields(): lax.ppermute(jnp.stack([f[..., :, :1] for f in fields]), 'gridx', bwd_x)  8.23 us
    ppermute x2, starting transfers between devices, exchange_fields(): lax.ppermute(jnp.stack([f[..., :1, :] for f in fields]), 'gridy', bwd_y)  5.89 us
    slice x8, local copies, waits for them, and re-layouts, exchange_fields(): f[..., :, -1:]  4.77 us
  transfers between devices with their start and end apart: 11, of which 3 were waited for; matrix products, arithmetic and copies ran while one was open for 10% of the time, Pallas kernels for 0%

profile of v14, /device:TPU:0, one launch (start us, length us, event | category | flops | bytes accessed | tf_op | source)
XLA Modules:
  0.0 211.5 jit_solution(3714553202597983378)
XLA Ops:
  0.7 1.1 slice_bitcast_fusion.11
  1.7 1.0 slice_bitcast_fusion.9
  2.8 2.9 %collective-permute-start = (f32[4,2,4,1,256]{4,3,2,1,0:T(1,128)S(1)}, f32[4,2,4,1,256]{4,3,2,1,0:T(1,128)S(1)}, u32[]{:S(2)}, u32[]{:S(2)}) collective-permute-start(f32[4,2,4,1,256]{4,3,2,1,0:T(1,128)S(1)} %pad_maximum_fusion.5), channel_id=1, source_target_pairs={{8,0},{16,8},{24,16},{32,24},{40,32},{48,40},{56,48},{0,56},{9,1},... | collective-permute-start | bytes 98312 | tf_op jit(solution)/shard_map/ppermute | solution.py:419
  5.8 1.4 slice_reduce_fusion.10
  7.1 1.4 slice_reduce_fusion.9
  9.2 5.2 %collective-permute-start.2 = (f32[4,2,4,64,1]{3,2,4,1,0:T(4,128)S(1)}, f32[4,2,4,64,1]{3,2,4,1,0:T(4,128)S(1)}, u32[]{:S(2)}, u32[]{:S(2)}) collective-permute-start(f32[4,2,4,64,1]{3,2,4,1,0:T(4,128)S(1)} %pad_maximum_fusion.9), channel_id=1, source_target_pairs={{1,0},{2,1},{3,2},{4,3},{5,4},{6,5},{7,6},{0,7},{9,8},{10,9},{11,1... | collective-permute-start | bytes 24584 | tf_op jit(solution)/shard_map/ppermute | solution.py:421
  16.6 1.4 copy.195.e_ref
  18.0 2.2 %collective-permute-done.3 = f32[4,2,4,64,1]{3,2,4,1,0:T(4,128)S(1)} collective-permute-done((f32[4,2,4,64,1]{3,2,4,1,0:T(4,128)S(1)}, f32[4,2,4,64,1]{3,2,4,1,0:T(4,128)S(1)}, u32[]{:S(2)}, u32[]{:S(2)}) %collective-permute-start.3) | collective-permute-done | bytes 8224 | tf_op jit(solution)/shard_map/ppermute | solution.py:422
  20.3 1.4 copy.196.w_ref
  22.9 4.9 %shard_map.126 = (f32[2,4,64,256]{3,2,1,0:T(8,128)}, f32[2,4,64,256]{3,2,1,0:T(8,128)}, f32[2,4,64,256]{3,2,1,0:T(8,128)}, f32[2,4,64,256]{3,2,1,0:T(8,128)}, f3...) custom-call(f32[2,4,64,256]{3,2,1,0:T(8,128)} %temp_ref.1, f32[2,4,64,256]{3,2,1,0:T(8,128)} %salt_ref.1, ...), custom_call_target="tpu_custom_call" | custom-call | tf_op jit(solution)/shard_map/pallas_call | solution.py:388
  27.9 42.4 %shard_map.127 = f32[3,2,64,256]{3,2,1,0:T(8,128)} custom-call(f32[2,64,256]{2,1,0:T(8,128)} %get-tuple-element.34.tu_ref, f32[2,64,256]{2,1,0:T(8,128)} %get-tuple-element.35.tv_ref, f32[2,64,256]{2,1,0:T(8,128)} %eta_ref.1, f32[80,512]{1,0:T(8,128)} %get-tuple-element.136.inside_ref, f32[80,512]{1,0:T(8,128)} %get-tuple-element.137.own_ref), custom_call_target="tpu_custom_call" | custom-call | tf_op jit(solution)/shard_map/pallas_call | solution.py:284
  70.3 1.7 slice_bitcast_fusion
  74.0 1.4 collective-permute-start.7
  75.4 3.0 %collective-permute-start.6 = (f32[4,2,4,64,1]{3,2,4,1,0:T(4,128)S(1)}, f32[4,2,4,64,1]{3,2,4,1,0:T(4,128)S(1)}, u32[]{:S(2)}, u32[]{:S(2)}) collective-permute-start(f32[4,2,4,64,1]{3,2,4,1,0:T(4,128)S(1)} %pad_maximum_fusion.11), channel_id=1, source_target_pairs={{1,0},{2,1},{3,2},{4,3},{5,4},{6,5},{7,6},{0,7},{9,8},{10,9},{11,1... | collective-permute-start | bytes 24584 | tf_op jit(solution)/shard_map/ppermute | solution.py:421
  78.6 2.9 %collective-permute-start.4 = (f32[4,2,4,1,256]{4,3,2,1,0:T(1,128)S(1)}, f32[4,2,4,1,256]{4,3,2,1,0:T(1,128)S(1)}, u32[]{:S(2)}, u32[]{:S(2)}) collective-permute-start(f32[4,2,4,1,256]{4,3,2,1,0:T(1,128)S(1)} %pad_maximum_fusion.7), channel_id=1, source_target_pairs={{8,0},{16,8},{24,16},{32,24},{40,32},{48,40},{56,48},{0,56},{9,1},... | collective-permute-start | bytes 98312 | tf_op jit(solution)/shard_map/ppermute | solution.py:419
  85.4 1.4 copy.210.w_ref
  86.9 1.4 copy.209.e_ref
  89.5 5.0 %shard_map.128 = (f32[2,4,64,256]{3,2,1,0:T(8,128)}, f32[2,4,64,256]{3,2,1,0:T(8,128)}, f32[2,4,64,256]{3,2,1,0:T(8,128)}, f32[2,4,64,256]{3,2,1,0:T(8,128)}, f3...) custom-call(f32[2,4,64,256]{3,2,1,0:T(8,128)} %get-tuple-element.31.temp_ref, f32[2,4,64,256]{3,2,1,0:T(8,128)} %get-tuple-element.32.salt_ref, ...), custom_call_target="tpu_custom_call" | custom-call | tf_op jit(solution)/shard_map/pallas_call | solution.py:388
  94.5 41.2 %shard_map.129 = f32[3,2,64,256]{3,2,1,0:T(8,128)} custom-call(f32[2,64,256]{2,1,0:T(8,128)} %get-tuple-element.40.tu_ref, f32[2,64,256]{2,1,0:T(8,128)} %get-tuple-element.41.tv_ref, f32[2,64,256]{2,1,0:T(8,128)} %get-tuple-element.119.eta_ref, f32[80,512]{1,0:T(8,128)} %get-tuple-element.136.inside_ref, f32[80,512]{1,0:T(8,128)} %get-tuple-element.137.own_ref), custom_call_target="tpu_custom_call" | custom-call | tf_op jit(solution)/shard_map/pallas_call | solution.py:284
  135.7 1.0 multiply_bitcast_fusion
  137.8 13.0 %shard_map.130 = f32[40,128]{1,0:T(8,128)} custom-call(f32[40,128]{1,0:T(8,128)} %select_maximum_fusion.x_ref), custom_call_target="tpu_custom_call" | custom-call | tf_op jit(solution)/shard_map/pallas_call | solution.py:90
  150.8 1.3 fusion.9
  152.1 2.9 %collective-permute-start.10 = (f32[2]{0:T(128)S(1)}, f32[2]{0:T(128)S(1)}, u32[]{:S(2)}, u32[]{:S(2)}) collective-permute-start(f32[2]{0:T(128)S(1)} %get-tuple-element.124), channel_id=1, source_target_pairs={{0,64},{64,0},{1,65},{65,1},{2,66},{66,2},{3,67},{67,3},{4,68},{68... | collective-permute-start | bytes 32 | tf_op jit(solution)/shard_map/ppermute | solution.py:595
  155.7 1.1 pad_maximum_fusion.1
  157.6 3.0 %collective-permute-start.9 = (f32[2,9,64,256]{3,2,1,0:T(8,128)S(1)}, f32[2,9,64,256]{3,2,1,0:T(8,128)S(1)}, u32[]{:S(2)}, u32[]{:S(2)}) collective-permute-start(f32[2,9,64,256]{3,2,1,0:T(8,128)S(1)} %pad_maximum_fusion), channel_id=1, source_target_pairs={{0,64},{64,0},{1,65},{65,1},{2,66},{66,2},{3,67},{67,3},{4,68},{68... | collective-permute-start | bytes 3538952 | tf_op jit(solution)/shard_map/ppermute | solution.py:594
  163.9 20.8 %collective-permute-done.8 = f32[2,2,4,64,256]{4,3,2,1,0:T(8,128)} collective-permute-done((f32[2,2,4,64,256]{4,3,2,1,0:T(8,128)}, f32[2,2,4,64,256]{4,3,2,1,0:T(8,128)}, u32[]{:S(2)}, u32[]{:S(2)}) %collective-permute-start.8) | collective-permute-done | bytes 1048608 | tf_op jit(solution)/shard_map/ppermute | solution.py:572
  184.8 1.3 fusion.13
  186.1 1.4 bitcast_select_fusion.1
  187.5 1.4 bitcast_select_fusion.3
  190.6 17.6 %collective-permute-done.9 = f32[2,9,64,256]{3,2,1,0:T(8,128)S(1)} collective-permute-done((f32[2,9,64,256]{3,2,1,0:T(8,128)S(1)}, f32[2,9,64,256]{3,2,1,0:T(8,128)S(1)}, u32[]{:S(2)}, u32[]{:S(2)}) %collective-permute-start.9) | collective-permute-done | bytes 1179680 | tf_op jit(solution)/shard_map/ppermute | solution.py:594
  208.3 1.5 dynamic-slice_select_fusion
  210.5 1.0 fusion
  (103 shorter events, 14.3 us)
Async XLA Ops:
  0.6 8.2 %copy-start.2 = (f32[2,4,64,256]{3,2,1,0:T(8,128)S(1)}, f32[2,4,64,256]{3,2,1,0:T(8,128)}, u32[]{:S(2)}) copy-start(f32[2,4,64,256]{3,2,1,0:T(8,128)} %temp_ref.1) | copy-start | bytes 1572868
  0.6 7.9 %copy-start.3 = (f32[2,4,64,256]{3,2,1,0:T(8,128)S(1)}, f32[2,4,64,256]{3,2,1,0:T(8,128)}, u32[]{:S(2)}) copy-start(f32[2,4,64,256]{3,2,1,0:T(8,128)} %vvel_ref.1) | copy-start | bytes 1572868
  2.7 11.8 %copy-start.18 = (s32[2]{0:T(128)S(1)}, s32[2]{0:T(128)}, u32[]{:S(2)}) copy-start(s32[2]{0:T(128)} %param.15) | copy-start | bytes 28
  2.7 19.0 %collective-permute-start.1 = (f32[4,2,4,1,256]{4,3,2,1,0:T(1,128)S(1)}, f32[4,2,4,1,256]{4,3,2,1,0:T(1,128)S(1)}, u32[]{:S(2)}, u32[]{:S(2)}) collective-permute-start(f32[4,2,4,1,256]{4,3,2,1,0:T(1,128)S(1)} %pad_maximum_fusion.6), channel_id=1, source_target_pairs={{0,8},{8,16},{16,24},{24,32},{32,40},{40,48},{48,56},{56,0},{1,9},... | collective-permute-start | bytes 98312 | tf_op jit(solution)/shard_map/ppermute | solution.py:420
  2.8 13.8 %copy-start.9 = (s32[64,256]{1,0:T(8,128)S(1)}, s32[64,256]{1,0:T(8,128)}, u32[]{:S(2)}) copy-start(s32[64,256]{1,0:T(8,128)} %land_ref.3) | copy-start | bytes 196612
  2.8 18.9 %collective-permute-start = (f32[4,2,4,1,256]{4,3,2,1,0:T(1,128)S(1)}, f32[4,2,4,1,256]{4,3,2,1,0:T(1,128)S(1)}, u32[]{:S(2)}, u32[]{:S(2)}) collective-permute-start(f32[4,2,4,1,256]{4,3,2,1,0:T(1,128)S(1)} %pad_maximum_fusion.5), channel_id=1, source_target_pairs={{8,0},{16,8},{24,16},{32,24},{40,32},{48,40},{56,48},{0,56},{9,1},... | collective-permute-start | bytes 98312 | tf_op jit(solution)/shard_map/ppermute | solution.py:419
  9.2 7.4 %collective-permute-start.2 = (f32[4,2,4,64,1]{3,2,4,1,0:T(4,128)S(1)}, f32[4,2,4,64,1]{3,2,4,1,0:T(4,128)S(1)}, u32[]{:S(2)}, u32[]{:S(2)}) collective-permute-start(f32[4,2,4,64,1]{3,2,4,1,0:T(4,128)S(1)} %pad_maximum_fusion.9), channel_id=1, source_target_pairs={{1,0},{2,1},{3,2},{4,3},{5,4},{6,5},{7,6},{0,7},{9,8},{10,9},{11,1... | collective-permute-start | bytes 24584 | tf_op jit(solution)/shard_map/ppermute | solution.py:421
  14.4 5.8 %collective-permute-start.3 = (f32[4,2,4,64,1]{3,2,4,1,0:T(4,128)S(1)}, f32[4,2,4,64,1]{3,2,4,1,0:T(4,128)S(1)}, u32[]{:S(2)}, u32[]{:S(2)}) collective-permute-start(f32[4,2,4,64,1]{3,2,4,1,0:T(4,128)S(1)} %pad_maximum_fusion.10), channel_id=1, source_target_pairs={{0,1},{1,2},{2,3},{3,4},{4,5},{5,6},{6,7},{7,0},{8,9},{9,10},{10,1... | collective-permute-start | bytes 24584 | tf_op jit(solution)/shard_map/ppermute | solution.py:422
  21.7 0.6 copy-start.14
  22.3 0.6 copy-start.15
  27.9 44.2 %copy-start.10 = (f32[2,4,64,256]{3,2,1,0:T(8,128)S(1)}, f32[2,4,64,256]{3,2,1,0:T(8,128)}, u32[]{:S(2)}) copy-start(f32[2,4,64,256]{3,2,1,0:T(8,128)} %get-tuple-element.33) | copy-start | bytes 1572868
  27.9 44.1 %copy-start.11 = (f32[2,4,64,256]{3,2,1,0:T(8,128)S(1)}, f32[2,4,64,256]{3,2,1,0:T(8,128)}, u32[]{:S(2)}) copy-start(f32[2,4,64,256]{3,2,1,0:T(8,128)} %get-tuple-element.36) | copy-start | bytes 1572868
  72.0 1.1 copy-start.4
  72.1 3.3 %copy-start = (f32[2,4,64,256]{3,2,1,0:T(8,128)}, f32[2,4,64,256]{3,2,1,0:T(8,128)S(1)}, u32[]{:S(2)}) copy-start(f32[2,4,64,256]{3,2,1,0:T(8,128)S(1)} %get-tuple-element.122.vvel_ref) | copy-start | bytes 1572868
  72.1 3.3 %copy-start.1 = (f32[2,4,64,256]{3,2,1,0:T(8,128)}, f32[2,4,64,256]{3,2,1,0:T(8,128)S(1)}, u32[]{:S(2)}) copy-start(f32[2,4,64,256]{3,2,1,0:T(8,128)S(1)} %get-tuple-element.123.uvel_ref) | copy-start | bytes 1572868
  72.1 1.5 copy-start.5
  74.0 11.4 %collective-permute-start.7 = (f32[4,2,4,64,1]{3,2,4,1,0:T(4,128)S(1)}, f32[4,2,4,64,1]{3,2,4,1,0:T(4,128)S(1)}, u32[]{:S(2)}, u32[]{:S(2)}) collective-permute-start(f32[4,2,4,64,1]{3,2,4,1,0:T(4,128)S(1)} %pad_maximum_fusion.12), channel_id=1, source_target_pairs={{0,1},{1,2},{2,3},{3,4},{4,5},{5,6},{6,7},{7,0},{8,9},{9,10},{10,1... | collective-permute-start | bytes 24584 | tf_op jit(solution)/shard_map/ppermute | solution.py:422
  75.4 11.4 %collective-permute-start.6 = (f32[4,2,4,64,1]{3,2,4,1,0:T(4,128)S(1)}, f32[4,2,4,64,1]{3,2,4,1,0:T(4,128)S(1)}, u32[]{:S(2)}, u32[]{:S(2)}) collective-permute-start(f32[4,2,4,64,1]{3,2,4,1,0:T(4,128)S(1)} %pad_maximum_fusion.11), channel_id=1, source_target_pairs={{1,0},{2,1},{3,2},{4,3},{5,4},{6,5},{7,6},{0,7},{9,8},{10,9},{11,1... | collective-permute-start | bytes 24584 | tf_op jit(solution)/shard_map/ppermute | solution.py:421
  78.5 9.8 %collective-permute-start.5 = (f32[4,2,4,1,256]{4,3,2,1,0:T(1,128)S(1)}, f32[4,2,4,1,256]{4,3,2,1,0:T(1,128)S(1)}, u32[]{:S(2)}, u32[]{:S(2)}) collective-permute-start(f32[4,2,4,1,256]{4,3,2,1,0:T(1,128)S(1)} %pad_maximum_fusion.8), channel_id=1, source_target_pairs={{0,8},{8,16},{16,24},{24,32},{32,40},{40,48},{48,56},{56,0},{1,9},... | collective-permute-start | bytes 98312 | tf_op jit(solution)/shard_map/ppermute | solution.py:420
  78.6 9.7 %collective-permute-start.4 = (f32[4,2,4,1,256]{4,3,2,1,0:T(1,128)S(1)}, f32[4,2,4,1,256]{4,3,2,1,0:T(1,128)S(1)}, u32[]{:S(2)}, u32[]{:S(2)}) collective-permute-start(f32[4,2,4,1,256]{4,3,2,1,0:T(1,128)S(1)} %pad_maximum_fusion.7), channel_id=1, source_target_pairs={{8,0},{16,8},{24,16},{32,24},{40,32},{48,40},{56,48},{0,56},{9,1},... | collective-permute-start | bytes 98312 | tf_op jit(solution)/shard_map/ppermute | solution.py:419
  88.3 0.6 copy-start.16
  88.9 0.6 copy-start.17
  94.4 42.2 %copy-start.13 = (f32[2,4,64,256]{3,2,1,0:T(8,128)S(1)}, f32[2,4,64,256]{3,2,1,0:T(8,128)}, u32[]{:S(2)}) copy-start(f32[2,4,64,256]{3,2,1,0:T(8,128)} %get-tuple-element.42) | copy-start | bytes 1572868
  135.6 20.1 %copy-start.8 = (f32[3,2,64,256]{3,2,1,0:T(8,128)S(1)}, f32[3,2,64,256]{3,2,1,0:T(8,128)}, u32[]{:S(2)}) copy-start(f32[3,2,64,256]{3,2,1,0:T(8,128)} %shard_map.129) | copy-start | bytes 1179652
  135.6 20.1 %copy-start.6 = (f32[2,4,64,256]{3,2,1,0:T(8,128)S(1)}, f32[2,4,64,256]{3,2,1,0:T(8,128)}, u32[]{:S(2)}) copy-start(f32[2,4,64,256]{3,2,1,0:T(8,128)} %get-tuple-element.37) | copy-start | bytes 1572868
  135.6 20.1 %copy-start.7 = (f32[2,4,64,256]{3,2,1,0:T(8,128)S(1)}, f32[2,4,64,256]{3,2,1,0:T(8,128)}, u32[]{:S(2)}) copy-start(f32[2,4,64,256]{3,2,1,0:T(8,128)} %get-tuple-element.38) | copy-start | bytes 1572868
  152.1 9.3 %collective-permute-start.10 = (f32[2]{0:T(128)S(1)}, f32[2]{0:T(128)S(1)}, u32[]{:S(2)}, u32[]{:S(2)}) collective-permute-start(f32[2]{0:T(128)S(1)} %get-tuple-element.124), channel_id=1, source_target_pairs={{0,64},{64,0},{1,65},{65,1},{2,66},{66,2},{3,67},{67,3},{4,68},{68... | collective-permute-start | bytes 32 | tf_op jit(solution)/shard_map/ppermute | solution.py:595
  155.7 1.8 copy-start.12
  156.8 27.9 %collective-permute-start.8 = (f32[2,2,4,64,256]{4,3,2,1,0:T(8,128)}, f32[2,2,4,64,256]{4,3,2,1,0:T(8,128)}, u32[]{:S(2)}, u32[]{:S(2)}) collective-permute-start(f32[2,2,4,64,256]{4,3,2,1,0:T(8,128)} %pad_maximum_fusion.1), channel_id=1, source_target_pairs={{0,64},{64,0},{1,65},{65,1},{2,66},{66,2},{3,67},{67,3},{4,68},{68... | collective-permute-start | bytes 3145736 | tf_op jit(solution)/shard_map/ppermute | solution.py:572
  157.5 3.1 %slice-start = ((f32[40,128]{1,0:T(8,128)}), f32[32,128]{1,0:T(8,128)S(1)}, s32[]{:S(2)}) async-start(f32[40,128]{1,0:T(8,128)} %shard_map.130), calls=%async_computation | async-start | bytes 32768 | tf_op jit(solution)/shard_map/slice | solution.py:586
  157.6 50.6 %collective-permute-start.9 = (f32[2,9,64,256]{3,2,1,0:T(8,128)S(1)}, f32[2,9,64,256]{3,2,1,0:T(8,128)S(1)}, u32[]{:S(2)}, u32[]{:S(2)}) collective-permute-start(f32[2,9,64,256]{3,2,1,0:T(8,128)S(1)} %pad_maximum_fusion), channel_id=1, source_target_pairs={{0,64},{64,0},{1,65},{65,1},{2,66},{66,2},{3,67},{67,3},{4,68},{68... | collective-permute-start | bytes 3538952 | tf_op jit(solution)/shard_map/ppermute | solution.py:594

commit v15 on v13

--- a/solution.py
+++ b/solution.py
@@ -328,8 +328,16 @@
             jnp.where(bottom, s, pltpu.roll(f, 1, 0)),
         )
 
+    east_cols = [e_ref[k, 0].T for k in range(4)]
+    west_cols = [w_ref[k, 0].T for k in range(4)]
+
     def rims_of(k, l):
-        return (n_ref[k, 0, l] * north_keep, s_ref[k, 0, l] * south_keep, e_ref[k, 0, l], w_ref[k, 0, l])
+        return (
+            n_ref[k, 0, l] * north_keep,
+            s_ref[k, 0, l] * south_keep,
+            east_cols[k][:, l : l + 1],
+            west_cols[k][:, l : l + 1],
+        )
 
     running = None
     running_rims = None
@@ -381,7 +389,7 @@
     plane = pl.BlockSpec((rows, cols), lambda m: (0, 0))
     north, south, east, west = rims
     row_rim = pl.BlockSpec((4, 1, levels, 1, cols), lambda m: (0, m, 0, 0, 0))
-    col_rim = pl.BlockSpec((4, 1, levels, rows, 1), lambda m: (0, m, 0, 0, 0))
+    col_rim = pl.BlockSpec((4, 1, levels, rows), lambda m: (0, m, 0, 0))
     surface = pl.BlockSpec((1, rows, cols), lambda m: (m, 0, 0))
     volume_shape = jax.ShapeDtypeStruct(temp.shape, jnp.float32)
     surface_shape = jax.ShapeDtypeStruct((members, rows, cols), jnp.float32)
@@ -418,8 +426,8 @@
     fwd_x, bwd_x = ring("gridx")
     north = lax.ppermute(jnp.stack([f[..., :1, :] for f in fields]), "gridy", bwd_y)
     south = lax.ppermute(jnp.stack([f[..., -1:, :] for f in fields]), "gridy", fwd_y)
-    east = lax.ppermute(jnp.stack([f[..., :, :1] for f in fields]), "gridx", bwd_x)
-    west = lax.ppermute(jnp.stack([f[..., :, -1:] for f in fields]), "gridx", fwd_x)
+    east = lax.ppermute(jnp.stack([f[..., :, 0] for f in fields]), "gridx", bwd_x)
+    west = lax.ppermute(jnp.stack([f[..., :, -1] for f in fields]), "gridx", fwd_x)
     return (north, south, east, west)
 
 

time: 211 us -> 231 us (1.095)
  local copies, waits for them, and re-layouts: 23.1 us -> 37.3 us
  waiting for transfers between devices: 20.3 us -> 26.4 us
    pallas_call x0 -> x4, local copies, waits for them, and re-layouts: none -> 6.6 us  [volume_step(): pl.pallas_call(functools.partial(volume_kernel, lax.axis_size('gridy')),...]
    ppermute x4 -> x0, local copies, waits for them, and re-layouts: 5.69 us -> none  [the longest x2 2.89 us: exchange_fields(): lax.ppermute(jnp.stack([f[..., :, -1:] for f in fields]), 'gridx', fwd_x)]
    slice x8 -> x10, local copies, waits for them, and re-layouts: 4.77 us -> 10.4 us  [the longest x4 6.82 us: exchange_fields(): f[..., -1:, :]]
    mul x1 -> x6, local copies, waits for them, and re-layouts: 0.65 us -> 5.59 us  [the longest x3 3.03 us: shards(): uvel = ocean * (ustar - GRAV_K * 0.5 * east_west[:, None])]
    ppermute x1, waiting for transfers between devices: 18.6 us -> 22.9 us  [shards(): flows_other = lax.ppermute(flows, 'member', swap)]
  transfers between devices with their start and end apart: 10 -> 10, of which waited for: 2 -> 2; matrix products, arithmetic and copies ran while one was open for 12% -> 9% of each run, Pallas kernels for 12% -> 11%
where the time goes in v15:
time: 231 us; the launch traced here: 230 us
  Pallas kernels  120 us (52%)
  local copies, waits for them, and re-layouts  37.3 us (16%)
  waiting for transfers between devices  26.4 us (11%)
  other arithmetic  20.7 us (9%)
  starting transfers between devices  20.2 us (9%)
  between operations  5.74 us (2%)
    pallas_call x2, Pallas kernels, surface_kernel_solve(): pl.pallas_call(functools.partial(solve_kernel, ny, nx), out_shape=jax.Sha...  83.5 us
    pallas_call x1, Pallas kernels, grid_sum(): pl.pallas_call(functools.partial(gather_sum_kernel, ny, nx), out_shape=ja...  25.9 us
    ppermute x1, waiting for transfers between devices, shards(): flows_other = lax.ppermute(flows, 'member', swap)  22.9 us
    pallas_call x2, Pallas kernels, volume_step(): pl.pallas_call(functools.partial(volume_kernel, lax.axis_size('gridy')),...  10.3 us
    ppermute x2, starting transfers between devices, exchange_fields(): lax.ppermute(jnp.stack([f[..., :, 0] for f in fields]), 'gridx', bwd_x)  7.92 us
    slice x4, local copies, waits for them, and re-layouts, exchange_fields(): f[..., -1:, :]  6.82 us
    pallas_call x4, local copies, waits for them, and re-layouts, volume_step(): pl.pallas_call(functools.partial(volume_kernel, lax.axis_size('gridy')),...  6.6 us
    ppermute x2, starting transfers between devices, exchange_fields(): lax.ppermute(jnp.stack([f[..., :1, :] for f in fields]), 'gridy', bwd_y)  5.9 us
  transfers between devices with their start and end apart: 10, of which 2 were waited for; matrix products, arithmetic and copies ran while one was open for 9% of the time, Pallas kernels for 11%

profile of v15, /device:TPU:0, one launch (start us, length us, event | category | flops | bytes accessed | tf_op | source)
XLA Modules:
  0.0 230.0 jit_solution(6076426504240005382)
XLA Ops:
  2.8 2.9 %collective-permute-start = (f32[4,2,4,1,256]{4,3,2,1,0:T(1,128)S(1)}, f32[4,2,4,1,256]{4,3,2,1,0:T(1,128)S(1)}, u32[]{:S(2)}, u32[]{:S(2)}) collective-permute-start(f32[4,2,4,1,256]{4,3,2,1,0:T(1,128)S(1)} %pad_maximum_fusion.5), channel_id=1, source_target_pairs={{8,0},{16,8},{24,16},{32,24},{40,32},{48,40},{56,48},{0,56},{9,1},... | collective-permute-start | bytes 98312 | tf_op jit(solution)/shard_map/ppermute | solution.py:427
  7.9 5.2 %collective-permute-start.2 = (f32[4,2,4,64]{3,2,1,0:T(4,128)S(1)}, f32[4,2,4,64]{3,2,1,0:T(4,128)S(1)}, u32[]{:S(2)}, u32[]{:S(2)}) collective-permute-start(f32[4,2,4,64]{3,2,1,0:T(4,128)S(1)} %pad_maximum_fusion.9), channel_id=1, source_target_pairs={{1,0},{2,1},{3,2},{4,3},{5,4},{6,5},{7,6},{0,7},{9,8},{10,9},{11,1... | collective-permute-start | bytes 24584 | tf_op jit(solution)/shard_map/ppermute | solution.py:429
  16.1 3.5 %collective-permute-done.3.w_ref = f32[4,2,4,64]{3,2,1,0:T(4,128)S(1)} collective-permute-done((f32[4,2,4,64]{3,2,1,0:T(4,128)S(1)}, f32[4,2,4,64]{3,2,1,0:T(4,128)S(1)}, u32[]{:S(2)}, u32[]{:S(2)}) %collective-permute-start.3) | collective-permute-done | bytes 8224 | tf_op jit(solution)/shard_map/ppermute | solution.py:430
  20.8 5.1 %shard_map.126 = (f32[2,4,64,256]{3,2,1,0:T(8,128)}, f32[2,4,64,256]{3,2,1,0:T(8,128)}, f32[2,4,64,256]{3,2,1,0:T(8,128)}, f32[2,4,64,256]{3,2,1,0:T(8,128)}, f3...) custom-call(f32[2,4,64,256]{3,2,1,0:T(8,128)} %temp_ref.1, f32[2,4,64,256]{3,2,1,0:T(8,128)} %salt_ref.1, ...), custom_call_target="tpu_custom_call" | custom-call | tf_op jit(solution)/shard_map/pallas_call | solution.py:396
  25.9 42.3 %shard_map.127 = f32[3,2,64,256]{3,2,1,0:T(8,128)} custom-call(f32[2,64,256]{2,1,0:T(8,128)} %get-tuple-element.46.tu_ref, f32[2,64,256]{2,1,0:T(8,128)} %get-tuple-element.47.tv_ref, f32[2,64,256]{2,1,0:T(8,128)} %eta_ref.1, f32[80,512]{1,0:T(8,128)} %get-tuple-element.143.inside_ref, f32[80,512]{1,0:T(8,128)} %get-tuple-element.144.own_ref), custom_call_target="tpu_custom_call" | custom-call | tf_op jit(solution)/shard_map/pallas_call | solution.py:284
  68.3 1.7 slice_bitcast_fusion.1
  71.5 1.3 copy.177
  72.8 1.9 subtract_multiply_fusion
  74.8 1.7 fusion.14
  76.4 2.1 fusion.15
  78.5 2.4 %copy.186 = f32[2,4,64,256]{2,1,0,3:T(4,128)} copy(f32[2,4,64,256]{3,2,1,0:T(8,128)} %get-tuple-element.43.temp_ref) | data formatting | bytes 1048576 | tf_op jit(solution)/shard_map/pallas_call | solution.py:396
  81.8 2.4 %copy.187 = f32[2,4,64,256]{2,1,0,3:T(4,128)} copy(f32[2,4,64,256]{3,2,1,0:T(8,128)} %get-tuple-element.44.salt_ref) | data formatting | bytes 1048576 | tf_op jit(solution)/shard_map/pallas_call | solution.py:396
  86.4 1.5 collective-permute-start.7
  87.9 2.7 %collective-permute-start.6 = (f32[4,2,4,64]{3,2,1,0:T(4,128)S(1)}, f32[4,2,4,64]{3,2,1,0:T(4,128)S(1)}, u32[]{:S(2)}, u32[]{:S(2)}) collective-permute-start(f32[4,2,4,64]{3,2,1,0:T(4,128)S(1)} %pad_maximum_fusion.11), channel_id=1, source_target_pairs={{1,0},{2,1},{3,2},{4,3},{5,4},{6,5},{7,6},{0,7},{9,8},{10,9},{11,1... | collective-permute-start | bytes 24584 | tf_op jit(solution)/shard_map/ppermute | solution.py:429
  90.6 1.5 copy.182
  92.2 1.5 copy.183
  94.3 1.5 copy.179
  96.0 3.0 %collective-permute-start.4 = (f32[4,2,4,1,256]{4,3,2,1,0:T(1,128)S(1)}, f32[4,2,4,1,256]{4,3,2,1,0:T(1,128)S(1)}, u32[]{:S(2)}, u32[]{:S(2)}) collective-permute-start(f32[4,2,4,1,256]{4,3,2,1,0:T(1,128)S(1)} %pad_maximum_fusion.7), channel_id=1, source_target_pairs={{8,0},{16,8},{24,16},{32,24},{40,32},{48,40},{56,48},{0,56},{9,1},... | collective-permute-start | bytes 98312 | tf_op jit(solution)/shard_map/ppermute | solution.py:427
  102.8 1.3 copy.190.uvel_ref
  104.1 1.3 copy.191.vvel_ref
  106.6 5.2 %shard_map.128 = (f32[2,4,64,256]{3,2,1,0:T(8,128)}, f32[2,4,64,256]{3,2,1,0:T(8,128)}, f32[2,4,64,256]{3,2,1,0:T(8,128)}, f32[2,4,64,256]{3,2,1,0:T(8,128)}, f3...) custom-call(f32[2,4,64,256]{3,2,1,0:T(8,128)} %get-tuple-element.43.temp_ref, f32[2,4,64,256]{3,2,1,0:T(8,128)} %get-tuple-element.44.salt_ref, ...), custom_call_target="tpu_custom_call" | custom-call | tf_op jit(solution)/shard_map/pallas_call | solution.py:396
  111.7 41.2 %shard_map.129 = f32[3,2,64,256]{3,2,1,0:T(8,128)} custom-call(f32[2,64,256]{2,1,0:T(8,128)} %get-tuple-element.52.tu_ref, f32[2,64,256]{2,1,0:T(8,128)} %get-tuple-element.53.tv_ref, f32[2,64,256]{2,1,0:T(8,128)} %get-tuple-element.125.eta_ref, f32[80,512]{1,0:T(8,128)} %get-tuple-element.143.inside_ref, f32[80,512]{1,0:T(8,128)} %get-tuple-element.144.own_ref), custom_call_target="tpu_custom_call" | custom-call | tf_op jit(solution)/shard_map/pallas_call | solution.py:284
  155.7 1.5 fusion.12
  157.2 1.6 copy.194
  160.6 2.9 %collective-permute-start.8 = (f32[2,2,4,64,256]{4,3,2,1,0:T(8,128)}, f32[2,2,4,64,256]{4,3,2,1,0:T(8,128)S(1)}, u32[]{:S(2)}, u32[]{:S(2)}) collective-permute-start(f32[2,2,4,64,256]{4,3,2,1,0:T(8,128)} %pad_maximum_fusion.1), channel_id=1, source_target_pairs={{0,64},{64,0},{1,65},{65,1},{2,66},{66,2},{3,67},{67,3},{4,68},{68... | collective-permute-start | bytes 3145736 | tf_op jit(solution)/shard_map/ppermute | solution.py:580
  164.2 25.9 %shard_map.130 = f32[40,128]{1,0:T(8,128)} custom-call(f32[40,128]{1,0:T(8,128)} %select_maximum_fusion.1.x_ref), custom_call_target="tpu_custom_call" | custom-call | tf_op jit(solution)/shard_map/pallas_call | solution.py:90
  192.2 1.8 collective-permute-start.9
  195.0 1.3 bitcast_select_fusion.1
  196.4 1.3 bitcast_select_fusion.3
  199.4 22.9 %collective-permute-done.9 = f32[2,10,64,256]{3,2,1,0:T(8,128)} collective-permute-done((f32[2,10,64,256]{3,2,1,0:T(8,128)}, f32[2,10,64,256]{3,2,1,0:T(8,128)}, u32[]{:S(2)}, u32[]{:S(2)}) %collective-permute-start.9) | collective-permute-done | bytes 1310752 | tf_op jit(solution)/shard_map/ppermute | solution.py:602
  222.3 1.3 slice.276
  223.6 1.4 dynamic-slice_select_fusion
  (130 shorter events, 29.0 us)
Async XLA Ops:
  0.6 6.3 %copy-start.1 = (f32[2,4,64,256]{3,2,1,0:T(8,128)S(1)}, f32[2,4,64,256]{3,2,1,0:T(8,128)}, u32[]{:S(2)}) copy-start(f32[2,4,64,256]{3,2,1,0:T(8,128)} %uvel_ref.1) | copy-start | bytes 1572868
  0.6 6.4 %copy-start.2 = (f32[2,4,64,256]{3,2,1,0:T(8,128)S(1)}, f32[2,4,64,256]{3,2,1,0:T(8,128)}, u32[]{:S(2)}) copy-start(f32[2,4,64,256]{3,2,1,0:T(8,128)} %vvel_ref.1) | copy-start | bytes 1572868
  2.7 16.9 %collective-permute-start.1 = (f32[4,2,4,1,256]{4,3,2,1,0:T(1,128)S(1)}, f32[4,2,4,1,256]{4,3,2,1,0:T(1,128)S(1)}, u32[]{:S(2)}, u32[]{:S(2)}) collective-permute-start(f32[4,2,4,1,256]{4,3,2,1,0:T(1,128)S(1)} %pad_maximum_fusion.6), channel_id=1, source_target_pairs={{0,8},{8,16},{16,24},{24,32},{32,40},{40,48},{48,56},{56,0},{1,9},... | collective-permute-start | bytes 98312 | tf_op jit(solution)/shard_map/ppermute | solution.py:428
  2.8 4.4 %copy-start = (f32[2,4,64,256]{3,2,1,0:T(8,128)S(1)}, f32[2,4,64,256]{3,2,1,0:T(8,128)}, u32[]{:S(2)}) copy-start(f32[2,4,64,256]{3,2,1,0:T(8,128)} %temp_ref.1) | copy-start | bytes 1572868
  2.8 16.8 %collective-permute-start = (f32[4,2,4,1,256]{4,3,2,1,0:T(1,128)S(1)}, f32[4,2,4,1,256]{4,3,2,1,0:T(1,128)S(1)}, u32[]{:S(2)}, u32[]{:S(2)}) collective-permute-start(f32[4,2,4,1,256]{4,3,2,1,0:T(1,128)S(1)} %pad_maximum_fusion.5), channel_id=1, source_target_pairs={{8,0},{16,8},{24,16},{32,24},{40,32},{48,40},{56,48},{0,56},{9,1},... | collective-permute-start | bytes 98312 | tf_op jit(solution)/shard_map/ppermute | solution.py:427
  7.3 6.5 %copy-start.18 = (s32[2]{0:T(128)S(1)}, s32[2]{0:T(128)}, u32[]{:S(2)}) copy-start(s32[2]{0:T(128)} %param.17) | copy-start | bytes 28
  7.3 8.6 %copy-start.5 = (s32[64,256]{1,0:T(8,128)S(1)}, s32[64,256]{1,0:T(8,128)}, u32[]{:S(2)}) copy-start(s32[64,256]{1,0:T(8,128)} %land_ref.3) | copy-start | bytes 196612
  7.9 8.1 %collective-permute-start.2 = (f32[4,2,4,64]{3,2,1,0:T(4,128)S(1)}, f32[4,2,4,64]{3,2,1,0:T(4,128)S(1)}, u32[]{:S(2)}, u32[]{:S(2)}) collective-permute-start(f32[4,2,4,64]{3,2,1,0:T(4,128)S(1)} %pad_maximum_fusion.9), channel_id=1, source_target_pairs={{1,0},{2,1},{3,2},{4,3},{5,4},{6,5},{7,6},{0,7},{9,8},{10,9},{11,1... | collective-permute-start | bytes 24584 | tf_op jit(solution)/shard_map/ppermute | solution.py:429
  13.7 5.9 %collective-permute-start.3 = (f32[4,2,4,64]{3,2,1,0:T(4,128)S(1)}, f32[4,2,4,64]{3,2,1,0:T(4,128)S(1)}, u32[]{:S(2)}, u32[]{:S(2)}) collective-permute-start(f32[4,2,4,64]{3,2,1,0:T(4,128)S(1)} %pad_maximum_fusion.10), channel_id=1, source_target_pairs={{0,1},{1,2},{2,3},{3,4},{4,5},{5,6},{6,7},{7,0},{8,9},{9,10},{10,1... | collective-permute-start | bytes 24584 | tf_op jit(solution)/shard_map/ppermute | solution.py:430
  16.1 3.5 %copy-start.15 = (f32[4,2,4,64]{3,2,1,0:T(4,128)}, f32[4,2,4,64]{3,2,1,0:T(4,128)S(1)}, u32[]{:S(2)}) copy-start(f32[4,2,4,64]{3,2,1,0:T(4,128)S(1)} %collective-permute-done.2.e_ref) | copy-start | bytes 24580
  19.6 0.6 copy-start.17
  19.6 0.6 copy-start.10
  20.2 0.6 copy-start.11
  25.9 45.1 %copy-start.7 = (f32[2,4,64,256]{3,2,1,0:T(8,128)S(1)}, f32[2,4,64,256]{3,2,1,0:T(8,128)}, u32[]{:S(2)}) copy-start(f32[2,4,64,256]{3,2,1,0:T(8,128)} %get-tuple-element.45) | copy-start | bytes 1572868
  70.0 1.5 copy-start.6
  86.4 18.9 %collective-permute-start.7 = (f32[4,2,4,64]{3,2,1,0:T(4,128)S(1)}, f32[4,2,4,64]{3,2,1,0:T(4,128)S(1)}, u32[]{:S(2)}, u32[]{:S(2)}) collective-permute-start(f32[4,2,4,64]{3,2,1,0:T(4,128)S(1)} %pad_maximum_fusion.12), channel_id=1, source_target_pairs={{0,1},{1,2},{2,3},{3,4},{4,5},{5,6},{6,7},{7,0},{8,9},{9,10},{10,1... | collective-permute-start | bytes 24584 | tf_op jit(solution)/shard_map/ppermute | solution.py:430
  87.9 17.4 %collective-permute-start.6 = (f32[4,2,4,64]{3,2,1,0:T(4,128)S(1)}, f32[4,2,4,64]{3,2,1,0:T(4,128)S(1)}, u32[]{:S(2)}, u32[]{:S(2)}) collective-permute-start(f32[4,2,4,64]{3,2,1,0:T(4,128)S(1)} %pad_maximum_fusion.11), channel_id=1, source_target_pairs={{1,0},{2,1},{3,2},{4,3},{5,4},{6,5},{7,6},{0,7},{9,8},{10,9},{11,1... | collective-permute-start | bytes 24584 | tf_op jit(solution)/shard_map/ppermute | solution.py:429
  93.8 11.5 %collective-permute-start.5 = (f32[4,2,4,1,256]{4,3,2,1,0:T(1,128)S(1)}, f32[4,2,4,1,256]{4,3,2,1,0:T(1,128)S(1)}, u32[]{:S(2)}, u32[]{:S(2)}) collective-permute-start(f32[4,2,4,1,256]{4,3,2,1,0:T(1,128)S(1)} %pad_maximum_fusion.8), channel_id=1, source_target_pairs={{0,8},{8,16},{16,24},{24,32},{32,40},{40,48},{48,56},{56,0},{1,9},... | collective-permute-start | bytes 98312 | tf_op jit(solution)/shard_map/ppermute | solution.py:428
  96.0 9.4 %collective-permute-start.4 = (f32[4,2,4,1,256]{4,3,2,1,0:T(1,128)S(1)}, f32[4,2,4,1,256]{4,3,2,1,0:T(1,128)S(1)}, u32[]{:S(2)}, u32[]{:S(2)}) collective-permute-start(f32[4,2,4,1,256]{4,3,2,1,0:T(1,128)S(1)} %pad_maximum_fusion.7), channel_id=1, source_target_pairs={{8,0},{16,8},{24,16},{32,24},{40,32},{48,40},{56,48},{0,56},{9,1},... | collective-permute-start | bytes 98312 | tf_op jit(solution)/shard_map/ppermute | solution.py:427
  105.3 0.6 copy-start.14
  105.3 0.6 copy-start.16
  105.3 0.6 copy-start.12
  106.0 0.6 copy-start.13
  111.7 42.3 %copy-start.9 = (f32[2,4,64,256]{3,2,1,0:T(8,128)S(1)}, f32[2,4,64,256]{3,2,1,0:T(8,128)}, u32[]{:S(2)}) copy-start(f32[2,4,64,256]{3,2,1,0:T(8,128)} %get-tuple-element.51) | copy-start | bytes 1572868
  154.0 1.0 copy-start.8
  157.2 2.3 copy-start.3
  157.2 2.3 copy-start.4
  160.6 34.4 %collective-permute-start.8 = (f32[2,2,4,64,256]{4,3,2,1,0:T(8,128)}, f32[2,2,4,64,256]{4,3,2,1,0:T(8,128)S(1)}, u32[]{:S(2)}, u32[]{:S(2)}) collective-permute-start(f32[2,2,4,64,256]{4,3,2,1,0:T(8,128)} %pad_maximum_fusion.1), channel_id=1, source_target_pairs={{0,64},{64,0},{1,65},{65,1},{2,66},{66,2},{3,67},{67,3},{4,68},{68... | collective-permute-start | bytes 3145736 | tf_op jit(solution)/shard_map/ppermute | solution.py:580
  190.1 3.9 %slice-start = ((f32[40,128]{1,0:T(8,128)}), f32[32,128]{1,0:T(8,128)S(1)}, s32[]{:S(2)}) async-start(f32[40,128]{1,0:T(8,128)} %shard_map.130), calls=%async_computation | async-start | bytes 32768 | tf_op jit(solution)/shard_map/slice | solution.py:594
  192.2 30.1 %collective-permute-start.9 = (f32[2,10,64,256]{3,2,1,0:T(8,128)}, f32[2,10,64,256]{3,2,1,0:T(8,128)}, u32[]{:S(2)}, u32[]{:S(2)}) collective-permute-start(f32[2,10,64,256]{3,2,1,0:T(8,128)} %select_maximum_fusion), channel_id=1, source_target_pairs={{0,64},{64,0},{1,65},{65,1},{2,66},{66,2},{3,67},{67,3},{4,68},{68... | collective-permute-start | bytes 3932168 | tf_op jit(solution)/shard_map/ppermute | solution.py:602

commit v16 on v13

--- a/solution.py
+++ b/solution.py
@@ -328,51 +328,52 @@
             jnp.where(bottom, s, pltpu.roll(f, 1, 0)),
         )
 
-    def rims_of(k, l):
-        return (n_ref[k, 0, l] * north_keep, s_ref[k, 0, l] * south_keep, e_ref[k, 0, l], w_ref[k, 0, l])
-
-    running = None
-    running_rims = None
-    tu = None
-    tv = None
-    for l in range(levels):
-        t = temp_ref[0, l]
-        s = salt_ref[0, l]
-        u = uvel_ref[0, l]
-        v = vvel_ref[0, l]
-        rt, rs, ru, rv = rims_of(0, l), rims_of(1, l), rims_of(2, l), rims_of(3, l)
-        layer = BETA_S * s - ALPHA_T * t
-        layer_rims = tuple(BETA_S * b - ALPHA_T * a for a, b in zip(rt, rs))
-        if running is None:
-            running, running_rims = layer, layer_rims
-        else:
-            running = running + layer
-            running_rims = tuple(a + b for a, b in zip(running_rims, layer_rims))
-        press = PRESS_K * running
-        press_rims = tuple(PRESS_K * a for a in running_rims)
-        te, tw, tn, ts = around(t, rt)
-        se, sw, sn, ss = around(s, rs)
-        ue, uw, un, us = around(u, ru)
-        ve, vw, vn, vs = around(v, rv)
-        pe, pw, pn, ps = around(press, press_rims)
-        tn_ref[0, l] = ocean * (
-            t - STEP_DT * 0.5 * (u * (te - tw) + v * (tn - ts)) + KAPPA * (te + tw + tn + ts - 4.0 * t)
-        )
-        sn_ref[0, l] = ocean * (
-            s - STEP_DT * 0.5 * (u * (se - sw) + v * (sn - ss)) + KAPPA * (se + sw + sn + ss - 4.0 * s)
-        )
-        ustar = ocean * (
-            u + STEP_DT * (cor * v - 0.5 * (pe - pw) - DRAG_K * u) + VISCOSITY * (ue + uw + un + us - 4.0 * u)
-        )
-        vstar = ocean * (
-            v + STEP_DT * (-cor * u - 0.5 * (pn - ps) - DRAG_K * v) + VISCOSITY * (ve + vw + vn + vs - 4.0 * v)
-        )
-        us_ref[0, l] = ustar
-        vs_ref[0, l] = vstar
-        tu = ustar if tu is None else tu + ustar
-        tv = vstar if tv is None else tv + vstar
-    tu_ref[0] = tu
-    tv_ref[0] = tv
+    def rims_of(k, l, m):
+        return (n_ref[k, m, l] * north_keep, s_ref[k, m, l] * south_keep, e_ref[k, m, l], w_ref[k, m, l])
+
+    for m in range(temp_ref.shape[0]):
+        running = None
+        running_rims = None
+        tu = None
+        tv = None
+        for l in range(levels):
+            t = temp_ref[m, l]
+            s = salt_ref[m, l]
+            u = uvel_ref[m, l]
+            v = vvel_ref[m, l]
+            rt, rs, ru, rv = rims_of(0, l, m), rims_of(1, l, m), rims_of(2, l, m), rims_of(3, l, m)
+            layer = BETA_S * s - ALPHA_T * t
+            layer_rims = tuple(BETA_S * b - ALPHA_T * a for a, b in zip(rt, rs))
+            if running is None:
+                running, running_rims = layer, layer_rims
+            else:
+                running = running + layer
+                running_rims = tuple(a + b for a, b in zip(running_rims, layer_rims))
+            press = PRESS_K * running
+            press_rims = tuple(PRESS_K * a for a in running_rims)
+            te, tw, tn, ts = around(t, rt)
+            se, sw, sn, ss = around(s, rs)
+            ue, uw, un, us = around(u, ru)
+            ve, vw, vn, vs = around(v, rv)
+            pe, pw, pn, ps = around(press, press_rims)
+            tn_ref[m, l] = ocean * (
+                t - STEP_DT * 0.5 * (u * (te - tw) + v * (tn - ts)) + KAPPA * (te + tw + tn + ts - 4.0 * t)
+            )
+            sn_ref[m, l] = ocean * (
+                s - STEP_DT * 0.5 * (u * (se - sw) + v * (sn - ss)) + KAPPA * (se + sw + sn + ss - 4.0 * s)
+            )
+            ustar = ocean * (
+                u + STEP_DT * (cor * v - 0.5 * (pe - pw) - DRAG_K * u) + VISCOSITY * (ue + uw + un + us - 4.0 * u)
+            )
+            vstar = ocean * (
+                v + STEP_DT * (-cor * u - 0.5 * (pn - ps) - DRAG_K * v) + VISCOSITY * (ve + vw + vn + vs - 4.0 * v)
+            )
+            us_ref[m, l] = ustar
+            vs_ref[m, l] = vstar
+            tu = ustar if tu is None else tu + ustar
+            tv = vstar if tv is None else tv + vstar
+        tu_ref[m] = tu
+        tv_ref[m] = tv
 
 
 def volume_step(temp, salt, uvel, vvel, land_mask, rims):
@@ -385,11 +386,11 @@
     surface = pl.BlockSpec((1, rows, cols), lambda m: (m, 0, 0))
     volume_shape = jax.ShapeDtypeStruct(temp.shape, jnp.float32)
     surface_shape = jax.ShapeDtypeStruct((members, rows, cols), jnp.float32)
+    vmem = pl.BlockSpec(memory_space=pltpu.VMEM)
     return pl.pallas_call(
         functools.partial(volume_kernel, lax.axis_size("gridy")),
-        grid=(members,),
-        in_specs=[field] * 4 + [plane, row_rim, row_rim, col_rim, col_rim],
-        out_specs=[field] * 4 + [surface] * 2,
+        in_specs=[vmem] * 9,
+        out_specs=[vmem] * 6,
         out_shape=[volume_shape] * 4 + [surface_shape] * 2,
     )(temp, salt, uvel, vvel, land_mask, north, south, east, west)
 

time: 211 us -> 212 us (level)
  no operation moved by 1% of the time
where the time goes in v16:
time: 212 us
  Pallas kernels  122 us (58%)
  local copies, waits for them, and re-layouts  23.1 us (11%)
  other arithmetic  20.4 us (10%)
  waiting for transfers between devices  20.3 us (10%)
  starting transfers between devices  20.2 us (10%)
  between operations  5.59 us (3%)
    pallas_call x2, Pallas kernels, surface_kernel_solve(): pl.pallas_call(functools.partial(solve_kernel, ny, nx), out_shape=jax.Sha...  84.1 us
    pallas_call x1, Pallas kernels, grid_sum(): pl.pallas_call(functools.partial(gather_sum_kernel, ny, nx), out_shape=ja...  26.1 us
    ppermute x1, waiting for transfers between devices, shards(): flows_other = lax.ppermute(flows, 'member', swap)  18.6 us
    pallas_call x2, Pallas kernels, volume_step(): pl.pallas_call(functools.partial(volume_kernel, lax.axis_size('gridy')),...  11.7 us
    ppermute x2, starting transfers between devices, exchange_fields(): lax.ppermute(jnp.stack([f[..., :, :1] for f in fields]), 'gridx', bwd_x)  8.5 us
    ppermute x2, starting transfers between devices, exchange_fields(): lax.ppermute(jnp.stack([f[..., :1, :] for f in fields]), 'gridy', bwd_y)  5.89 us
    slice x8, local copies, waits for them, and re-layouts, exchange_fields(): f[..., :, -1:]  4.77 us
    select_n x3, other arithmetic, pick(): chosen.append(jnp.where(here[place], from_here, from_other))  4.44 us
  transfers between devices with their start and end apart: 10, of which 2 were waited for; matrix products, arithmetic and copies ran while one was open for 12% of the time, Pallas kernels for 12%

profile of v16, /device:TPU:0, one launch (start us, length us, event | category | flops | bytes accessed | tf_op | source)
XLA Modules:
  0.0 211.5 jit_solution(10448767986725257641)
XLA Ops:
  0.7 1.0 slice_bitcast_fusion.12
  1.7 1.0 slice_bitcast_fusion.10
  2.8 2.9 %collective-permute-start = (f32[4,2,4,1,256]{4,3,2,1,0:T(1,128)S(1)}, f32[4,2,4,1,256]{4,3,2,1,0:T(1,128)S(1)}, u32[]{:S(2)}, u32[]{:S(2)}) collective-permute-start(f32[4,2,4,1,256]{4,3,2,1,0:T(1,128)S(1)} %pad_maximum_fusion.5), channel_id=1, source_target_pairs={{8,0},{16,8},{24,16},{32,24},{40,32},{48,40},{56,48},{0,56},{9,1},... | collective-permute-start | bytes 98312 | tf_op jit(solution)/shard_map/ppermute | solution.py:420
  5.8 1.4 slice_reduce_fusion.10
  7.1 1.4 slice_reduce_fusion.9
  9.2 5.2 %collective-permute-start.2 = (f32[4,2,4,64,1]{3,2,4,1,0:T(4,128)S(1)}, f32[4,2,4,64,1]{3,2,4,1,0:T(4,128)S(1)}, u32[]{:S(2)}, u32[]{:S(2)}) collective-permute-start(f32[4,2,4,64,1]{3,2,4,1,0:T(4,128)S(1)} %pad_maximum_fusion.9), channel_id=1, source_target_pairs={{1,0},{2,1},{3,2},{4,3},{5,4},{6,5},{7,6},{0,7},{9,8},{10,9},{11,1... | collective-permute-start | bytes 24584 | tf_op jit(solution)/shard_map/ppermute | solution.py:422
  17.2 1.4 copy.205.e_ref
  18.6 1.7 collective-permute-done.3
  20.3 1.4 copy.206.w_ref
  22.9 5.8 %shard_map.126 = (f32[2,4,64,256]{3,2,1,0:T(8,128)}, f32[2,4,64,256]{3,2,1,0:T(8,128)}, f32[2,4,64,256]{3,2,1,0:T(8,128)}, f32[2,4,64,256]{3,2,1,0:T(8,128)}, f3...) custom-call(f32[2,4,64,256]{3,2,1,0:T(8,128)} %temp_ref.1, f32[2,4,64,256]{3,2,1,0:T(8,128)} %salt_ref.1, ...), custom_call_target="tpu_custom_call" | custom-call | tf_op jit(solution)/shard_map/pallas_call | solution.py:390
  28.7 42.9 %shard_map.127 = f32[3,2,64,256]{3,2,1,0:T(8,128)} custom-call(f32[2,64,256]{2,1,0:T(8,128)} %get-tuple-element.46.tu_ref, f32[2,64,256]{2,1,0:T(8,128)} %get-tuple-element.47.tv_ref, f32[2,64,256]{2,1,0:T(8,128)} %eta_ref.1, f32[80,512]{1,0:T(8,128)} %get-tuple-element.150.inside_ref, f32[80,512]{1,0:T(8,128)} %get-tuple-element.151.own_ref), custom_call_target="tpu_custom_call" | custom-call | tf_op jit(solution)/shard_map/pallas_call | solution.py:284
  71.7 1.7 slice_bitcast_fusion.1
  76.3 3.3 %collective-permute-start.6 = (f32[4,2,4,64,1]{3,2,4,1,0:T(4,128)S(1)}, f32[4,2,4,64,1]{3,2,4,1,0:T(4,128)S(1)}, u32[]{:S(2)}, u32[]{:S(2)}) collective-permute-start(f32[4,2,4,64,1]{3,2,4,1,0:T(4,128)S(1)} %pad_maximum_fusion.11), channel_id=1, source_target_pairs={{1,0},{2,1},{3,2},{4,3},{5,4},{6,5},{7,6},{0,7},{9,8},{10,9},{11,1... | collective-permute-start | bytes 24584 | tf_op jit(solution)/shard_map/ppermute | solution.py:422
  79.7 2.9 %collective-permute-start.4 = (f32[4,2,4,1,256]{4,3,2,1,0:T(1,128)S(1)}, f32[4,2,4,1,256]{4,3,2,1,0:T(1,128)S(1)}, u32[]{:S(2)}, u32[]{:S(2)}) collective-permute-start(f32[4,2,4,1,256]{4,3,2,1,0:T(1,128)S(1)} %pad_maximum_fusion.7), channel_id=1, source_target_pairs={{8,0},{16,8},{24,16},{32,24},{40,32},{48,40},{56,48},{0,56},{9,1},... | collective-permute-start | bytes 98312 | tf_op jit(solution)/shard_map/ppermute | solution.py:420
  86.5 1.4 copy.220.w_ref
  88.0 1.4 copy.219.e_ref
  90.6 5.8 %shard_map.128 = (f32[2,4,64,256]{3,2,1,0:T(8,128)}, f32[2,4,64,256]{3,2,1,0:T(8,128)}, f32[2,4,64,256]{3,2,1,0:T(8,128)}, f32[2,4,64,256]{3,2,1,0:T(8,128)}, f3...) custom-call(f32[2,4,64,256]{3,2,1,0:T(8,128)} %get-tuple-element.43.temp_ref, f32[2,4,64,256]{3,2,1,0:T(8,128)} %get-tuple-element.44.salt_ref, ...), custom_call_target="tpu_custom_call" | custom-call | tf_op jit(solution)/shard_map/pallas_call | solution.py:390
  96.4 41.2 %shard_map.129 = f32[3,2,64,256]{3,2,1,0:T(8,128)} custom-call(f32[2,64,256]{2,1,0:T(8,128)} %get-tuple-element.52.tu_ref, f32[2,64,256]{2,1,0:T(8,128)} %get-tuple-element.53.tv_ref, f32[2,64,256]{2,1,0:T(8,128)} %get-tuple-element.132.eta_ref, f32[80,512]{1,0:T(8,128)} %get-tuple-element.150.inside_ref, f32[80,512]{1,0:T(8,128)} %get-tuple-element.151.own_ref), custom_call_target="tpu_custom_call" | custom-call | tf_op jit(solution)/shard_map/pallas_call | solution.py:284
  137.6 1.1 multiply_bitcast_fusion.1
  139.9 1.1 pad_maximum_fusion.1
  141.0 2.9 %collective-permute-start.8 = (f32[2,2,4,64,256]{4,3,2,1,0:T(8,128)}, f32[2,2,4,64,256]{4,3,2,1,0:T(8,128)}, u32[]{:S(2)}, u32[]{:S(2)}) collective-permute-start(f32[2,2,4,64,256]{4,3,2,1,0:T(8,128)} %pad_maximum_fusion.1), channel_id=1, source_target_pairs={{0,64},{64,0},{1,65},{65,1},{2,66},{66,2},{3,67},{67,3},{4,68},{68... | collective-permute-start | bytes 3145736 | tf_op jit(solution)/shard_map/ppermute | solution.py:573
  144.6 26.1 %shard_map.130 = f32[40,128]{1,0:T(8,128)} custom-call(f32[40,128]{1,0:T(8,128)} %select_maximum_fusion.1.x_ref), custom_call_target="tpu_custom_call" | custom-call | tf_op jit(solution)/shard_map/pallas_call | solution.py:90
  170.8 1.3 fusion.9
  173.5 1.9 collective-permute-start.9
  175.4 1.3 pad_clamp_fusion
  179.0 1.3 fusion.13
  180.3 1.4 bitcast_select_fusion.1
  181.7 1.4 bitcast_select_fusion.3
  184.9 18.6 %collective-permute-done.9 = f32[2,10,64,256]{3,2,1,0:T(8,128)} collective-permute-done((f32[2,10,64,256]{3,2,1,0:T(8,128)S(1)}, f32[2,10,64,256]{3,2,1,0:T(8,128)}, u32[]{:S(2)}, u32[]{:S(2)}) %collective-permute-start.9) | collective-permute-done | bytes 1310752 | tf_op jit(solution)/shard_map/ppermute | solution.py:595
  203.5 1.3 slice.272
  204.8 1.6 dynamic-slice_select_fusion
  207.1 1.0 fusion
  (107 shorter events, 19.6 us)
Async XLA Ops:
  0.6 8.2 %copy-start.2 = (f32[2,4,64,256]{3,2,1,0:T(8,128)S(1)}, f32[2,4,64,256]{3,2,1,0:T(8,128)}, u32[]{:S(2)}) copy-start(f32[2,4,64,256]{3,2,1,0:T(8,128)} %temp_ref.1) | copy-start | bytes 1572868
  0.6 7.9 %copy-start.3 = (f32[2,4,64,256]{3,2,1,0:T(8,128)S(1)}, f32[2,4,64,256]{3,2,1,0:T(8,128)}, u32[]{:S(2)}) copy-start(f32[2,4,64,256]{3,2,1,0:T(8,128)} %vvel_ref.1) | copy-start | bytes 1572868
  0.7 13.9 %copy-start.19 = (s32[2]{0:T(128)S(1)}, s32[2]{0:T(128)}, u32[]{:S(2)}) copy-start(s32[2]{0:T(128)} %param.17) | copy-start | bytes 28
  2.7 19.0 %collective-permute-start.1 = (f32[4,2,4,1,256]{4,3,2,1,0:T(1,128)S(1)}, f32[4,2,4,1,256]{4,3,2,1,0:T(1,128)S(1)}, u32[]{:S(2)}, u32[]{:S(2)}) collective-permute-start(f32[4,2,4,1,256]{4,3,2,1,0:T(1,128)S(1)} %pad_maximum_fusion.6), channel_id=1, source_target_pairs={{0,8},{8,16},{16,24},{24,32},{32,40},{40,48},{48,56},{56,0},{1,9},... | collective-permute-start | bytes 98312 | tf_op jit(solution)/shard_map/ppermute | solution.py:421
  2.8 14.3 %copy-start.8 = (s32[64,256]{1,0:T(8,128)S(1)}, s32[64,256]{1,0:T(8,128)}, u32[]{:S(2)}) copy-start(s32[64,256]{1,0:T(8,128)} %land_ref.3) | copy-start | bytes 196612
  2.8 18.9 %collective-permute-start = (f32[4,2,4,1,256]{4,3,2,1,0:T(1,128)S(1)}, f32[4,2,4,1,256]{4,3,2,1,0:T(1,128)S(1)}, u32[]{:S(2)}, u32[]{:S(2)}) collective-permute-start(f32[4,2,4,1,256]{4,3,2,1,0:T(1,128)S(1)} %pad_maximum_fusion.5), channel_id=1, source_target_pairs={{8,0},{16,8},{24,16},{32,24},{40,32},{48,40},{56,48},{0,56},{9,1},... | collective-permute-start | bytes 98312 | tf_op jit(solution)/shard_map/ppermute | solution.py:420
  9.2 7.9 %collective-permute-start.2 = (f32[4,2,4,64,1]{3,2,4,1,0:T(4,128)S(1)}, f32[4,2,4,64,1]{3,2,4,1,0:T(4,128)S(1)}, u32[]{:S(2)}, u32[]{:S(2)}) collective-permute-start(f32[4,2,4,64,1]{3,2,4,1,0:T(4,128)S(1)} %pad_maximum_fusion.9), channel_id=1, source_target_pairs={{1,0},{2,1},{3,2},{4,3},{5,4},{6,5},{7,6},{0,7},{9,8},{10,9},{11,1... | collective-permute-start | bytes 24584 | tf_op jit(solution)/shard_map/ppermute | solution.py:422
  14.4 5.8 %collective-permute-start.3 = (f32[4,2,4,64,1]{3,2,4,1,0:T(4,128)S(1)}, f32[4,2,4,64,1]{3,2,4,1,0:T(4,128)S(1)}, u32[]{:S(2)}, u32[]{:S(2)}) collective-permute-start(f32[4,2,4,64,1]{3,2,4,1,0:T(4,128)S(1)} %pad_maximum_fusion.10), channel_id=1, source_target_pairs={{0,1},{1,2},{2,3},{3,4},{4,5},{5,6},{6,7},{7,0},{8,9},{9,10},{10,1... | collective-permute-start | bytes 24584 | tf_op jit(solution)/shard_map/ppermute | solution.py:423
  14.5 124.4 %copy-start.17 = (pred[8]{0:T(512)(128)(4,1)}, pred[8]{0:T(512)(128)(4,1)S(1)}, u32[]{:S(2)}) copy-start(pred[8]{0:T(512)(128)(4,1)S(1)} %iota_compare_fusion.4) | copy-start | bytes 28
  21.7 0.6 copy-start.13
  22.3 0.6 copy-start.14
  28.7 44.7 %copy-start.11 = (f32[2,4,64,256]{3,2,1,0:T(8,128)S(1)}, f32[2,4,64,256]{3,2,1,0:T(8,128)}, u32[]{:S(2)}) copy-start(f32[2,4,64,256]{3,2,1,0:T(8,128)} %get-tuple-element.45) | copy-start | bytes 1572868
  28.7 44.7 %copy-start.12 = (f32[2,4,64,256]{3,2,1,0:T(8,128)S(1)}, f32[2,4,64,256]{3,2,1,0:T(8,128)}, u32[]{:S(2)}) copy-start(f32[2,4,64,256]{3,2,1,0:T(8,128)} %get-tuple-element.48) | copy-start | bytes 1572868
  73.4 1.1 copy-start.4
  73.5 14.4 %copy-start = (f32[2,4,64,256]{3,2,1,0:T(8,128)}, f32[2,4,64,256]{3,2,1,0:T(8,128)S(1)}, u32[]{:S(2)}) copy-start(f32[2,4,64,256]{3,2,1,0:T(8,128)S(1)} %get-tuple-element.136.vvel_ref) | copy-start | bytes 1572868
  73.5 14.4 %copy-start.1 = (f32[2,4,64,256]{3,2,1,0:T(8,128)}, f32[2,4,64,256]{3,2,1,0:T(8,128)S(1)}, u32[]{:S(2)}) copy-start(f32[2,4,64,256]{3,2,1,0:T(8,128)S(1)} %get-tuple-element.137.uvel_ref) | copy-start | bytes 1572868
  73.5 1.5 copy-start.5
  75.4 11.1 %collective-permute-start.7 = (f32[4,2,4,64,1]{3,2,4,1,0:T(4,128)S(1)}, f32[4,2,4,64,1]{3,2,4,1,0:T(4,128)S(1)}, u32[]{:S(2)}, u32[]{:S(2)}) collective-permute-start(f32[4,2,4,64,1]{3,2,4,1,0:T(4,128)S(1)} %pad_maximum_fusion.12), channel_id=1, source_target_pairs={{0,1},{1,2},{2,3},{3,4},{4,5},{5,6},{6,7},{7,0},{8,9},{9,10},{10,1... | collective-permute-start | bytes 24584 | tf_op jit(solution)/shard_map/ppermute | solution.py:423
  76.3 11.7 %collective-permute-start.6 = (f32[4,2,4,64,1]{3,2,4,1,0:T(4,128)S(1)}, f32[4,2,4,64,1]{3,2,4,1,0:T(4,128)S(1)}, u32[]{:S(2)}, u32[]{:S(2)}) collective-permute-start(f32[4,2,4,64,1]{3,2,4,1,0:T(4,128)S(1)} %pad_maximum_fusion.11), channel_id=1, source_target_pairs={{1,0},{2,1},{3,2},{4,3},{5,4},{6,5},{7,6},{0,7},{9,8},{10,9},{11,1... | collective-permute-start | bytes 24584 | tf_op jit(solution)/shard_map/ppermute | solution.py:422
  79.6 9.7 %collective-permute-start.5 = (f32[4,2,4,1,256]{4,3,2,1,0:T(1,128)S(1)}, f32[4,2,4,1,256]{4,3,2,1,0:T(1,128)S(1)}, u32[]{:S(2)}, u32[]{:S(2)}) collective-permute-start(f32[4,2,4,1,256]{4,3,2,1,0:T(1,128)S(1)} %pad_maximum_fusion.8), channel_id=1, source_target_pairs={{0,8},{8,16},{16,24},{24,32},{32,40},{40,48},{48,56},{56,0},{1,9},... | collective-permute-start | bytes 98312 | tf_op jit(solution)/shard_map/ppermute | solution.py:421
  79.7 9.7 %collective-permute-start.4 = (f32[4,2,4,1,256]{4,3,2,1,0:T(1,128)S(1)}, f32[4,2,4,1,256]{4,3,2,1,0:T(1,128)S(1)}, u32[]{:S(2)}, u32[]{:S(2)}) collective-permute-start(f32[4,2,4,1,256]{4,3,2,1,0:T(1,128)S(1)} %pad_maximum_fusion.7), channel_id=1, source_target_pairs={{8,0},{16,8},{24,16},{32,24},{40,32},{48,40},{56,48},{0,56},{9,1},... | collective-permute-start | bytes 98312 | tf_op jit(solution)/shard_map/ppermute | solution.py:420
  89.4 0.6 copy-start.15
  90.0 0.6 copy-start.16
  96.4 42.3 %copy-start.9 = (f32[2,4,64,256]{3,2,1,0:T(8,128)S(1)}, f32[2,4,64,256]{3,2,1,0:T(8,128)}, u32[]{:S(2)}) copy-start(f32[2,4,64,256]{3,2,1,0:T(8,128)} %get-tuple-element.51) | copy-start | bytes 1572868
  96.4 42.3 %copy-start.10 = (f32[2,4,64,256]{3,2,1,0:T(8,128)S(1)}, f32[2,4,64,256]{3,2,1,0:T(8,128)}, u32[]{:S(2)}) copy-start(f32[2,4,64,256]{3,2,1,0:T(8,128)} %get-tuple-element.54) | copy-start | bytes 1572868
  138.7 1.0 copy-start.6
  138.7 1.2 copy-start.7
  141.0 38.0 %collective-permute-start.8 = (f32[2,2,4,64,256]{4,3,2,1,0:T(8,128)}, f32[2,2,4,64,256]{4,3,2,1,0:T(8,128)}, u32[]{:S(2)}, u32[]{:S(2)}) collective-permute-start(f32[2,2,4,64,256]{4,3,2,1,0:T(8,128)} %pad_maximum_fusion.1), channel_id=1, source_target_pairs={{0,64},{64,0},{1,65},{65,1},{2,66},{66,2},{3,67},{67,3},{4,68},{68... | collective-permute-start | bytes 3145736 | tf_op jit(solution)/shard_map/ppermute | solution.py:573
  170.8 5.9 %slice-start = ((f32[40,128]{1,0:T(8,128)}), f32[32,128]{1,0:T(8,128)S(1)}, s32[]{:S(2)}) async-start(f32[40,128]{1,0:T(8,128)} %shard_map.130), calls=%async_computation | async-start | bytes 32768 | tf_op jit(solution)/shard_map/slice | solution.py:587
  173.5 30.0 %collective-permute-start.9 = (f32[2,10,64,256]{3,2,1,0:T(8,128)S(1)}, f32[2,10,64,256]{3,2,1,0:T(8,128)}, u32[]{:S(2)}, u32[]{:S(2)}) collective-permute-start(f32[2,10,64,256]{3,2,1,0:T(8,128)S(1)} %select_maximum_fusion), channel_id=1, source_target_pairs={{0,64},{64,0},{1,65},{65,1},{2,66},{66,2},{3,67},{67,3},{4,68},{68... | collective-permute-start | bytes 3932168 | tf_op jit(solution)/shard_map/ppermute | solution.py:595
  207.1 1.9 copy-start.18
  207.1 3.9 %copy-start.20 = (s32[2]{0:T(128)S(1)}, s32[2]{0:T(128)}, u32[]{:S(2)}) copy-start(s32[2]{0:T(128)} %param.17) | copy-start | bytes 28

commit v17 on v13

--- a/solution.py
+++ b/solution.py
@@ -147,7 +147,7 @@
     return phase(partial, send_x, recv_x, sx, rx, nx, mx, along_x)
 
 
-def solve_kernel(ny, nx, tu_ref, tv_ref, eta_ref, inside_ref, own_ref, out_ref, frame, hsend, hrecv, *bufs):
+def solve_kernel(ny, nx, tu_ref, tv_ref, eta_ref, inside_ref, out_ref, frame, hsend, hrecv, *bufs):
     mesh_id = pl.DeviceIdType.MESH
     member = lax.axis_index("member")
     my = lax.axis_index("gridy")
@@ -210,7 +210,6 @@
 
     members = eta_ref.shape[0]
     inside = inside_ref[...]
-    own = own_ref[...] > 0.5
 
     def east(f):
         return pltpu.roll(f, wide_cols - 1, 1)
@@ -276,7 +275,7 @@
         out_ref[2, m] = (north(x) - south(x))[0:rows, 0:cols]
 
 
-def surface_kernel_solve(trans_u, trans_v, eta, inside, own):
+def surface_kernel_solve(trans_u, trans_v, eta, inside):
     ny = lax.axis_size("gridy")
     nx = lax.axis_size("gridx")
     members, rows, cols = eta.shape
@@ -284,7 +283,7 @@
     return pl.pallas_call(
         functools.partial(solve_kernel, ny, nx),
         out_shape=jax.ShapeDtypeStruct((3, members, rows, cols), jnp.float32),
-        in_specs=[pl.BlockSpec(memory_space=pltpu.VMEM)] * 5,
+        in_specs=[pl.BlockSpec(memory_space=pltpu.VMEM)] * 4,
         out_specs=pl.BlockSpec(memory_space=pltpu.VMEM),
         scratch_shapes=[
             pltpu.VMEM((fields, members) + inside.shape, jnp.float32),
@@ -300,7 +299,7 @@
             pltpu.SemaphoreType.DMA((ITERS, nx)),
         ],
         compiler_params=pltpu.CompilerParams(collective_id=1, has_side_effects=True),
-    )(trans_u, trans_v, eta, inside, own)
+    )(trans_u, trans_v, eta, inside)
 
 
 def volume_kernel(ny, temp_ref, salt_ref, uvel_ref, vvel_ref, land_ref, n_ref, s_ref, e_ref, w_ref,
@@ -562,7 +561,7 @@
         temp_next, salt_next, ustar, vstar, trans_u, trans_v = volume_step(
             temp, salt, uvel, vvel, land_mask, rims
         )
-        solved = surface_kernel_solve(trans_u, trans_v, eta, wide_inside, own_mask)
+        solved = surface_kernel_solve(trans_u, trans_v, eta, wide_inside)
         eta = solved[0]
         east_west = solved[1]
         north_south = solved[2]

time: 211 us -> 210 us (level)
  transfers between devices with their start and end apart: 10 -> 10, of which waited for: 2 -> 2; matrix products, arithmetic and copies ran while one was open for 12% -> 12% of each run, Pallas kernels for 12% -> 13%
where the time goes in v17:
time: 210 us; the launch traced here: 209 us
  Pallas kernels  120 us (57%)
  local copies, waits for them, and re-layouts  23 us (11%)
  waiting for transfers between devices  20.8 us (10%)
  starting transfers between devices  20.2 us (10%)
  other arithmetic  20 us (10%)
  between operations  5.38 us (3%)
    pallas_call x2, Pallas kernels, surface_kernel_solve(): pl.pallas_call(functools.partial(solve_kernel, ny, nx), out_shape=jax.Sha...  83.7 us
    pallas_call x1, Pallas kernels, grid_sum(): pl.pallas_call(functools.partial(gather_sum_kernel, ny, nx), out_shape=ja...  26.1 us
    ppermute x1, waiting for transfers between devices, shards(): flows_other = lax.ppermute(flows, 'member', swap)  18.9 us
    pallas_call x2, Pallas kernels, volume_step(): pl.pallas_call(functools.partial(volume_kernel, lax.axis_size('gridy')),...  9.9 us
    ppermute x2, starting transfers between devices, exchange_fields(): lax.ppermute(jnp.stack([f[..., :, :1] for f in fields]), 'gridx', bwd_x)  8.29 us
    ppermute x2, starting transfers between devices, exchange_fields(): lax.ppermute(jnp.stack([f[..., :1, :] for f in fields]), 'gridy', bwd_y)  5.89 us
    slice x8, local copies, waits for them, and re-layouts, exchange_fields(): f[..., :, -1:]  4.77 us
  transfers between devices with their start and end apart: 10, of which 2 were waited for; matrix products, arithmetic and copies ran while one was open for 12% of the time, Pallas kernels for 13%

profile of v17, /device:TPU:0, one launch (start us, length us, event | category | flops | bytes accessed | tf_op | source)
XLA Modules:
  0.0 209.1 jit_solution(13047663897068020012)
XLA Ops:
  0.7 1.0 slice_bitcast_fusion.12
  2.8 2.9 %collective-permute-start = (f32[4,2,4,1,256]{4,3,2,1,0:T(1,128)S(1)}, f32[4,2,4,1,256]{4,3,2,1,0:T(1,128)S(1)}, u32[]{:S(2)}, u32[]{:S(2)}) collective-permute-start(f32[4,2,4,1,256]{4,3,2,1,0:T(1,128)S(1)} %pad_maximum_fusion.5), channel_id=1, source_target_pairs={{8,0},{16,8},{24,16},{32,24},{40,32},{48,40},{56,48},{0,56},{9,1},... | collective-permute-start | bytes 98312 | tf_op jit(solution)/shard_map/ppermute | solution.py:418
  5.8 1.4 slice_reduce_fusion.10
  7.1 1.4 slice_reduce_fusion.9
  9.2 5.2 %collective-permute-start.2 = (f32[4,2,4,64,1]{3,2,4,1,0:T(4,128)S(1)}, f32[4,2,4,64,1]{3,2,4,1,0:T(4,128)S(1)}, u32[]{:S(2)}, u32[]{:S(2)}) collective-permute-start(f32[4,2,4,64,1]{3,2,4,1,0:T(4,128)S(1)} %pad_maximum_fusion.9), channel_id=1, source_target_pairs={{1,0},{2,1},{3,2},{4,3},{5,4},{6,5},{7,6},{0,7},{9,8},{10,9},{11,1... | collective-permute-start | bytes 24584 | tf_op jit(solution)/shard_map/ppermute | solution.py:420
  17.0 1.4 copy.205.e_ref
  18.4 1.9 collective-permute-done.3
  20.3 1.4 copy.206.w_ref
  22.9 4.9 %shard_map.126 = (f32[2,4,64,256]{3,2,1,0:T(8,128)}, f32[2,4,64,256]{3,2,1,0:T(8,128)}, f32[2,4,64,256]{3,2,1,0:T(8,128)}, f32[2,4,64,256]{3,2,1,0:T(8,128)}, f3...) custom-call(f32[2,4,64,256]{3,2,1,0:T(8,128)} %temp_ref.1, f32[2,4,64,256]{3,2,1,0:T(8,128)} %salt_ref.1, ...), custom_call_target="tpu_custom_call" | custom-call | tf_op jit(solution)/shard_map/pallas_call | solution.py:387
  27.9 42.6 %shard_map.127 = f32[3,2,64,256]{3,2,1,0:T(8,128)} custom-call(f32[2,64,256]{2,1,0:T(8,128)} %get-tuple-element.46.tu_ref, f32[2,64,256]{2,1,0:T(8,128)} %get-tuple-element.47.tv_ref, f32[2,64,256]{2,1,0:T(8,128)} %eta_ref.1, f32[80,512]{1,0:T(8,128)} %fusion.5.inside_ref), custom_call_target="tpu_custom_call" | custom-call | tf_op jit(solution)/shard_map/pallas_call | solution.py:283
  70.5 1.7 slice_bitcast_fusion.1
  74.2 1.1 collective-permute-start.7
  75.4 3.1 %collective-permute-start.6 = (f32[4,2,4,64,1]{3,2,4,1,0:T(4,128)S(1)}, f32[4,2,4,64,1]{3,2,4,1,0:T(4,128)S(1)}, u32[]{:S(2)}, u32[]{:S(2)}) collective-permute-start(f32[4,2,4,64,1]{3,2,4,1,0:T(4,128)S(1)} %pad_maximum_fusion.11), channel_id=1, source_target_pairs={{1,0},{2,1},{3,2},{4,3},{5,4},{6,5},{7,6},{0,7},{9,8},{10,9},{11,1... | collective-permute-start | bytes 24584 | tf_op jit(solution)/shard_map/ppermute | solution.py:420
  78.6 2.9 %collective-permute-start.4 = (f32[4,2,4,1,256]{4,3,2,1,0:T(1,128)S(1)}, f32[4,2,4,1,256]{4,3,2,1,0:T(1,128)S(1)}, u32[]{:S(2)}, u32[]{:S(2)}) collective-permute-start(f32[4,2,4,1,256]{4,3,2,1,0:T(1,128)S(1)} %pad_maximum_fusion.7), channel_id=1, source_target_pairs={{8,0},{16,8},{24,16},{32,24},{40,32},{48,40},{56,48},{0,56},{9,1},... | collective-permute-start | bytes 98312 | tf_op jit(solution)/shard_map/ppermute | solution.py:418
  85.1 1.4 copy.220.w_ref
  86.6 1.4 copy.219.e_ref
  89.2 5.0 %shard_map.128 = (f32[2,4,64,256]{3,2,1,0:T(8,128)}, f32[2,4,64,256]{3,2,1,0:T(8,128)}, f32[2,4,64,256]{3,2,1,0:T(8,128)}, f32[2,4,64,256]{3,2,1,0:T(8,128)}, f3...) custom-call(f32[2,4,64,256]{3,2,1,0:T(8,128)} %get-tuple-element.43.temp_ref, f32[2,4,64,256]{3,2,1,0:T(8,128)} %get-tuple-element.44.salt_ref, ...), custom_call_target="tpu_custom_call" | custom-call | tf_op jit(solution)/shard_map/pallas_call | solution.py:387
  94.2 41.1 %shard_map.129 = f32[3,2,64,256]{3,2,1,0:T(8,128)} custom-call(f32[2,64,256]{2,1,0:T(8,128)} %get-tuple-element.52.tu_ref, f32[2,64,256]{2,1,0:T(8,128)} %get-tuple-element.53.tv_ref, f32[2,64,256]{2,1,0:T(8,128)} %get-tuple-element.132.eta_ref, f32[80,512]{1,0:T(8,128)} %fusion.5.inside_ref), custom_call_target="tpu_custom_call" | custom-call | tf_op jit(solution)/shard_map/pallas_call | solution.py:283
  135.3 1.1 multiply_bitcast_fusion.1
  137.6 1.1 pad_maximum_fusion.1
  138.7 2.9 %collective-permute-start.8 = (f32[2,2,4,64,256]{4,3,2,1,0:T(8,128)}, f32[2,2,4,64,256]{4,3,2,1,0:T(8,128)}, u32[]{:S(2)}, u32[]{:S(2)}) collective-permute-start(f32[2,2,4,64,256]{4,3,2,1,0:T(8,128)} %pad_maximum_fusion.1), channel_id=1, source_target_pairs={{0,64},{64,0},{1,65},{65,1},{2,66},{66,2},{3,67},{67,3},{4,68},{68... | collective-permute-start | bytes 3145736 | tf_op jit(solution)/shard_map/ppermute | solution.py:571
  142.3 26.1 %shard_map.130 = f32[40,128]{1,0:T(8,128)} custom-call(f32[40,128]{1,0:T(8,128)} %select_maximum_fusion.1.x_ref), custom_call_target="tpu_custom_call" | custom-call | tf_op jit(solution)/shard_map/pallas_call | solution.py:90
  168.5 1.3 fusion.9
  171.2 1.9 collective-permute-start.9
  173.1 1.3 pad_clamp_fusion
  176.7 1.3 fusion.13
  178.0 1.3 bitcast_select_fusion.1
  179.3 1.3 bitcast_select_fusion.3
  182.3 18.9 %collective-permute-done.9 = f32[2,10,64,256]{3,2,1,0:T(8,128)} collective-permute-done((f32[2,10,64,256]{3,2,1,0:T(8,128)S(1)}, f32[2,10,64,256]{3,2,1,0:T(8,128)}, u32[]{:S(2)}, u32[]{:S(2)}) %collective-permute-start.9) | collective-permute-done | bytes 1310752 | tf_op jit(solution)/shard_map/ppermute | solution.py:593
  201.2 1.3 slice.272
  202.5 1.4 dynamic-slice_select_fusion
  204.6 1.0 fusion
  (105 shorter events, 19.5 us)
Async XLA Ops:
  0.6 8.2 %copy-start.2 = (f32[2,4,64,256]{3,2,1,0:T(8,128)S(1)}, f32[2,4,64,256]{3,2,1,0:T(8,128)}, u32[]{:S(2)}) copy-start(f32[2,4,64,256]{3,2,1,0:T(8,128)} %temp_ref.1) | copy-start | bytes 1572868
  0.6 7.9 %copy-start.3 = (f32[2,4,64,256]{3,2,1,0:T(8,128)S(1)}, f32[2,4,64,256]{3,2,1,0:T(8,128)}, u32[]{:S(2)}) copy-start(f32[2,4,64,256]{3,2,1,0:T(8,128)} %vvel_ref.1) | copy-start | bytes 1572868
  0.7 13.9 %copy-start.19 = (s32[2]{0:T(128)S(1)}, s32[2]{0:T(128)}, u32[]{:S(2)}) copy-start(s32[2]{0:T(128)} %param.17) | copy-start | bytes 28
  1.7 15.3 %copy-start.8 = (s32[64,256]{1,0:T(8,128)S(1)}, s32[64,256]{1,0:T(8,128)}, u32[]{:S(2)}) copy-start(s32[64,256]{1,0:T(8,128)} %land_ref.3) | copy-start | bytes 196612
  2.8 19.0 %collective-permute-start.1 = (f32[4,2,4,1,256]{4,3,2,1,0:T(1,128)S(1)}, f32[4,2,4,1,256]{4,3,2,1,0:T(1,128)S(1)}, u32[]{:S(2)}, u32[]{:S(2)}) collective-permute-start(f32[4,2,4,1,256]{4,3,2,1,0:T(1,128)S(1)} %pad_maximum_fusion.6), channel_id=1, source_target_pairs={{0,8},{8,16},{16,24},{24,32},{32,40},{40,48},{48,56},{56,0},{1,9},... | collective-permute-start | bytes 98312 | tf_op jit(solution)/shard_map/ppermute | solution.py:419
  2.8 18.9 %collective-permute-start = (f32[4,2,4,1,256]{4,3,2,1,0:T(1,128)S(1)}, f32[4,2,4,1,256]{4,3,2,1,0:T(1,128)S(1)}, u32[]{:S(2)}, u32[]{:S(2)}) collective-permute-start(f32[4,2,4,1,256]{4,3,2,1,0:T(1,128)S(1)} %pad_maximum_fusion.5), channel_id=1, source_target_pairs={{8,0},{16,8},{24,16},{32,24},{40,32},{48,40},{56,48},{0,56},{9,1},... | collective-permute-start | bytes 98312 | tf_op jit(solution)/shard_map/ppermute | solution.py:418
  9.2 7.7 %collective-permute-start.2 = (f32[4,2,4,64,1]{3,2,4,1,0:T(4,128)S(1)}, f32[4,2,4,64,1]{3,2,4,1,0:T(4,128)S(1)}, u32[]{:S(2)}, u32[]{:S(2)}) collective-permute-start(f32[4,2,4,64,1]{3,2,4,1,0:T(4,128)S(1)} %pad_maximum_fusion.9), channel_id=1, source_target_pairs={{1,0},{2,1},{3,2},{4,3},{5,4},{6,5},{7,6},{0,7},{9,8},{10,9},{11,1... | collective-permute-start | bytes 24584 | tf_op jit(solution)/shard_map/ppermute | solution.py:420
  14.4 5.8 %collective-permute-start.3 = (f32[4,2,4,64,1]{3,2,4,1,0:T(4,128)S(1)}, f32[4,2,4,64,1]{3,2,4,1,0:T(4,128)S(1)}, u32[]{:S(2)}, u32[]{:S(2)}) collective-permute-start(f32[4,2,4,64,1]{3,2,4,1,0:T(4,128)S(1)} %pad_maximum_fusion.10), channel_id=1, source_target_pairs={{0,1},{1,2},{2,3},{3,4},{4,5},{5,6},{6,7},{7,0},{8,9},{9,10},{10,1... | collective-permute-start | bytes 24584 | tf_op jit(solution)/shard_map/ppermute | solution.py:421
  14.5 122.1 %copy-start.17 = (pred[8]{0:T(512)(128)(4,1)}, pred[8]{0:T(512)(128)(4,1)S(1)}, u32[]{:S(2)}) copy-start(pred[8]{0:T(512)(128)(4,1)S(1)} %iota_compare_fusion.3) | copy-start | bytes 28
  21.7 0.6 copy-start.13
  22.3 0.6 copy-start.14
  27.9 44.4 %copy-start.11 = (f32[2,4,64,256]{3,2,1,0:T(8,128)S(1)}, f32[2,4,64,256]{3,2,1,0:T(8,128)}, u32[]{:S(2)}) copy-start(f32[2,4,64,256]{3,2,1,0:T(8,128)} %get-tuple-element.45) | copy-start | bytes 1572868
  27.9 44.4 %copy-start.12 = (f32[2,4,64,256]{3,2,1,0:T(8,128)S(1)}, f32[2,4,64,256]{3,2,1,0:T(8,128)}, u32[]{:S(2)}) copy-start(f32[2,4,64,256]{3,2,1,0:T(8,128)} %get-tuple-element.48) | copy-start | bytes 1572868
  72.3 1.1 copy-start.4
  72.4 14.2 %copy-start = (f32[2,4,64,256]{3,2,1,0:T(8,128)}, f32[2,4,64,256]{3,2,1,0:T(8,128)S(1)}, u32[]{:S(2)}) copy-start(f32[2,4,64,256]{3,2,1,0:T(8,128)S(1)} %get-tuple-element.136.vvel_ref) | copy-start | bytes 1572868
  72.4 14.2 %copy-start.1 = (f32[2,4,64,256]{3,2,1,0:T(8,128)}, f32[2,4,64,256]{3,2,1,0:T(8,128)S(1)}, u32[]{:S(2)}) copy-start(f32[2,4,64,256]{3,2,1,0:T(8,128)S(1)} %get-tuple-element.137.uvel_ref) | copy-start | bytes 1572868
  72.4 1.5 copy-start.5
  74.2 10.9 %collective-permute-start.7 = (f32[4,2,4,64,1]{3,2,4,1,0:T(4,128)S(1)}, f32[4,2,4,64,1]{3,2,4,1,0:T(4,128)S(1)}, u32[]{:S(2)}, u32[]{:S(2)}) collective-permute-start(f32[4,2,4,64,1]{3,2,4,1,0:T(4,128)S(1)} %pad_maximum_fusion.12), channel_id=1, source_target_pairs={{0,1},{1,2},{2,3},{3,4},{4,5},{5,6},{6,7},{7,0},{8,9},{9,10},{10,1... | collective-permute-start | bytes 24584 | tf_op jit(solution)/shard_map/ppermute | solution.py:421
  75.4 11.2 %collective-permute-start.6 = (f32[4,2,4,64,1]{3,2,4,1,0:T(4,128)S(1)}, f32[4,2,4,64,1]{3,2,4,1,0:T(4,128)S(1)}, u32[]{:S(2)}, u32[]{:S(2)}) collective-permute-start(f32[4,2,4,64,1]{3,2,4,1,0:T(4,128)S(1)} %pad_maximum_fusion.11), channel_id=1, source_target_pairs={{1,0},{2,1},{3,2},{4,3},{5,4},{6,5},{7,6},{0,7},{9,8},{10,9},{11,1... | collective-permute-start | bytes 24584 | tf_op jit(solution)/shard_map/ppermute | solution.py:420
  78.5 9.5 %collective-permute-start.5 = (f32[4,2,4,1,256]{4,3,2,1,0:T(1,128)S(1)}, f32[4,2,4,1,256]{4,3,2,1,0:T(1,128)S(1)}, u32[]{:S(2)}, u32[]{:S(2)}) collective-permute-start(f32[4,2,4,1,256]{4,3,2,1,0:T(1,128)S(1)} %pad_maximum_fusion.8), channel_id=1, source_target_pairs={{0,8},{8,16},{16,24},{24,32},{32,40},{40,48},{48,56},{56,0},{1,9},... | collective-permute-start | bytes 98312 | tf_op jit(solution)/shard_map/ppermute | solution.py:419
  78.6 9.4 %collective-permute-start.4 = (f32[4,2,4,1,256]{4,3,2,1,0:T(1,128)S(1)}, f32[4,2,4,1,256]{4,3,2,1,0:T(1,128)S(1)}, u32[]{:S(2)}, u32[]{:S(2)}) collective-permute-start(f32[4,2,4,1,256]{4,3,2,1,0:T(1,128)S(1)} %pad_maximum_fusion.7), channel_id=1, source_target_pairs={{8,0},{16,8},{24,16},{32,24},{40,32},{48,40},{56,48},{0,56},{9,1},... | collective-permute-start | bytes 98312 | tf_op jit(solution)/shard_map/ppermute | solution.py:418
  88.0 0.6 copy-start.15
  88.6 0.6 copy-start.16
  94.2 42.2 %copy-start.9 = (f32[2,4,64,256]{3,2,1,0:T(8,128)S(1)}, f32[2,4,64,256]{3,2,1,0:T(8,128)}, u32[]{:S(2)}) copy-start(f32[2,4,64,256]{3,2,1,0:T(8,128)} %get-tuple-element.51) | copy-start | bytes 1572868
  94.2 42.2 %copy-start.10 = (f32[2,4,64,256]{3,2,1,0:T(8,128)S(1)}, f32[2,4,64,256]{3,2,1,0:T(8,128)}, u32[]{:S(2)}) copy-start(f32[2,4,64,256]{3,2,1,0:T(8,128)} %get-tuple-element.54) | copy-start | bytes 1572868
  136.4 1.0 copy-start.6
  136.4 1.2 copy-start.7
  138.7 38.0 %collective-permute-start.8 = (f32[2,2,4,64,256]{4,3,2,1,0:T(8,128)}, f32[2,2,4,64,256]{4,3,2,1,0:T(8,128)}, u32[]{:S(2)}, u32[]{:S(2)}) collective-permute-start(f32[2,2,4,64,256]{4,3,2,1,0:T(8,128)} %pad_maximum_fusion.1), channel_id=1, source_target_pairs={{0,64},{64,0},{1,65},{65,1},{2,66},{66,2},{3,67},{67,3},{4,68},{68... | collective-permute-start | bytes 3145736 | tf_op jit(solution)/shard_map/ppermute | solution.py:571
  168.5 5.9 %slice-start = ((f32[40,128]{1,0:T(8,128)}), f32[32,128]{1,0:T(8,128)S(1)}, s32[]{:S(2)}) async-start(f32[40,128]{1,0:T(8,128)} %shard_map.130), calls=%async_computation | async-start | bytes 32768 | tf_op jit(solution)/shard_map/slice | solution.py:585
  171.2 30.0 %collective-permute-start.9 = (f32[2,10,64,256]{3,2,1,0:T(8,128)S(1)}, f32[2,10,64,256]{3,2,1,0:T(8,128)}, u32[]{:S(2)}, u32[]{:S(2)}) collective-permute-start(f32[2,10,64,256]{3,2,1,0:T(8,128)S(1)} %select_maximum_fusion), channel_id=1, source_target_pairs={{0,64},{64,0},{1,65},{65,1},{2,66},{66,2},{3,67},{67,3},{4,68},{68... | collective-permute-start | bytes 3932168 | tf_op jit(solution)/shard_map/ppermute | solution.py:593
  204.6 1.9 copy-start.18
  204.6 3.9 %copy-start.20 = (s32[2]{0:T(128)S(1)}, s32[2]{0:T(128)}, u32[]{:S(2)}) copy-start(s32[2]{0:T(128)} %param.17) | copy-start | bytes 28

commit v18 on v17

--- a/solution.py
+++ b/solution.py
@@ -147,7 +147,7 @@
     return phase(partial, send_x, recv_x, sx, rx, nx, mx, along_x)
 
 
-def solve_kernel(ny, nx, tu_ref, tv_ref, eta_ref, inside_ref, out_ref, frame, hsend, hrecv, *bufs):
+def solve_kernel(ny, nx, tu_ref, tv_ref, eta_ref, out_ref, frame, hsend, hrecv, *bufs):
     mesh_id = pl.DeviceIdType.MESH
     member = lax.axis_index("member")
     my = lax.axis_index("gridy")
@@ -209,7 +209,9 @@
     ])
 
     members = eta_ref.shape[0]
-    inside = inside_ref[...]
+    frame_row = lax.broadcasted_iota(jnp.int32, (wide_rows, wide_cols), 0)
+    global_row = my * rows + jnp.where(frame_row < rows + band, frame_row, frame_row - wide_rows)
+    inside = ((global_row >= 0) & (global_row < rows * ny)).astype(jnp.float32)
 
     def east(f):
         return pltpu.roll(f, wide_cols - 1, 1)
@@ -275,7 +277,7 @@
         out_ref[2, m] = (north(x) - south(x))[0:rows, 0:cols]
 
 
-def surface_kernel_solve(trans_u, trans_v, eta, inside):
+def surface_kernel_solve(trans_u, trans_v, eta, inside_shape):
     ny = lax.axis_size("gridy")
     nx = lax.axis_size("gridx")
     members, rows, cols = eta.shape
@@ -283,10 +285,10 @@
     return pl.pallas_call(
         functools.partial(solve_kernel, ny, nx),
         out_shape=jax.ShapeDtypeStruct((3, members, rows, cols), jnp.float32),
-        in_specs=[pl.BlockSpec(memory_space=pltpu.VMEM)] * 4,
+        in_specs=[pl.BlockSpec(memory_space=pltpu.VMEM)] * 3,
         out_specs=pl.BlockSpec(memory_space=pltpu.VMEM),
         scratch_shapes=[
-            pltpu.VMEM((fields, members) + inside.shape, jnp.float32),
+            pltpu.VMEM((fields, members) + inside_shape, jnp.float32),
             pltpu.SemaphoreType.DMA((8,)),
             pltpu.SemaphoreType.DMA((8,)),
             pltpu.VMEM((ITERS, 8, 128), jnp.float32),
@@ -299,7 +301,7 @@
             pltpu.SemaphoreType.DMA((ITERS, nx)),
         ],
         compiler_params=pltpu.CompilerParams(collective_id=1, has_side_effects=True),
-    )(trans_u, trans_v, eta, inside)
+    )(trans_u, trans_v, eta)
 
 
 def volume_kernel(ny, temp_ref, salt_ref, uvel_ref, vvel_ref, land_ref, n_ref, s_ref, e_ref, w_ref,
@@ -561,7 +563,7 @@
         temp_next, salt_next, ustar, vstar, trans_u, trans_v = volume_step(
             temp, salt, uvel, vvel, land_mask, rims
         )
-        solved = surface_kernel_solve(trans_u, trans_v, eta, wide_inside)
+        solved = surface_kernel_solve(trans_u, trans_v, eta, wide_inside.shape)
         eta = solved[0]
         east_west = solved[1]
         north_south = solved[2]

time: 210 us -> 210 us (level)
  transfers between devices with their start and end apart: 10 -> 10, of which waited for: 2 -> 2; matrix products, arithmetic and copies ran while one was open for 12% -> 11% of each run, Pallas kernels for 13% -> 12%
where the time goes in v18:
time: 210 us; the launch traced here: 209 us
  Pallas kernels  119 us (57%)
  local copies, waits for them, and re-layouts  23.1 us (11%)
  waiting for transfers between devices  21.4 us (10%)
  starting transfers between devices  20.2 us (10%)
  other arithmetic  19.3 us (9%)
  between operations  5.72 us (3%)
    pallas_call x2, Pallas kernels, surface_kernel_solve(): pl.pallas_call(functools.partial(solve_kernel, ny, nx), out_shape=jax.Sha...  83.3 us
    pallas_call x1, Pallas kernels, grid_sum(): pl.pallas_call(functools.partial(gather_sum_kernel, ny, nx), out_shape=ja...  25.9 us
    ppermute x1, waiting for transfers between devices, shards(): flows_other = lax.ppermute(flows, 'member', swap)  18.8 us
    pallas_call x2, Pallas kernels, volume_step(): pl.pallas_call(functools.partial(volume_kernel, lax.axis_size('gridy')),...  9.89 us
    ppermute x2, starting transfers between devices, exchange_fields(): lax.ppermute(jnp.stack([f[..., :, :1] for f in fields]), 'gridx', bwd_x)  7.92 us
    ppermute x2, starting transfers between devices, exchange_fields(): lax.ppermute(jnp.stack([f[..., :1, :] for f in fields]), 'gridy', bwd_y)  5.89 us
    slice x8, local copies, waits for them, and re-layouts, exchange_fields(): f[..., :, -1:]  4.77 us
  transfers between devices with their start and end apart: 10, of which 2 were waited for; matrix products, arithmetic and copies ran while one was open for 11% of the time, Pallas kernels for 12%

profile of v18, /device:TPU:0, one launch (start us, length us, event | category | flops | bytes accessed | tf_op | source)
XLA Modules:
  0.0 208.8 jit_solution(2728366887274285395)
XLA Ops:
  0.7 1.0 slice_bitcast_fusion.12
  2.8 2.9 %collective-permute-start = (f32[4,2,4,1,256]{4,3,2,1,0:T(1,128)S(1)}, f32[4,2,4,1,256]{4,3,2,1,0:T(1,128)S(1)}, u32[]{:S(2)}, u32[]{:S(2)}) collective-permute-start(f32[4,2,4,1,256]{4,3,2,1,0:T(1,128)S(1)} %pad_maximum_fusion.5), channel_id=1, source_target_pairs={{8,0},{16,8},{24,16},{32,24},{40,32},{48,40},{56,48},{0,56},{9,1},... | collective-permute-start | bytes 98312 | tf_op jit(solution)/shard_map/ppermute | solution.py:420
  5.8 1.4 slice_reduce_fusion.10
  7.1 1.4 slice_reduce_fusion.9
  9.2 5.2 %collective-permute-start.2 = (f32[4,2,4,64,1]{3,2,4,1,0:T(4,128)S(1)}, f32[4,2,4,64,1]{3,2,4,1,0:T(4,128)S(1)}, u32[]{:S(2)}, u32[]{:S(2)}) collective-permute-start(f32[4,2,4,64,1]{3,2,4,1,0:T(4,128)S(1)} %pad_maximum_fusion.9), channel_id=1, source_target_pairs={{1,0},{2,1},{3,2},{4,3},{5,4},{6,5},{7,6},{0,7},{9,8},{10,9},{11,1... | collective-permute-start | bytes 24584 | tf_op jit(solution)/shard_map/ppermute | solution.py:422
  16.3 1.4 copy.205.e_ref
  17.7 2.5 %collective-permute-done.3 = f32[4,2,4,64,1]{3,2,4,1,0:T(4,128)S(1)} collective-permute-done((f32[4,2,4,64,1]{3,2,4,1,0:T(4,128)S(1)}, f32[4,2,4,64,1]{3,2,4,1,0:T(4,128)S(1)}, u32[]{:S(2)}, u32[]{:S(2)}) %collective-permute-start.3) | collective-permute-done | bytes 8224 | tf_op jit(solution)/shard_map/ppermute | solution.py:423
  20.3 1.4 copy.206.w_ref
  22.9 4.9 %shard_map.126 = (f32[2,4,64,256]{3,2,1,0:T(8,128)}, f32[2,4,64,256]{3,2,1,0:T(8,128)}, f32[2,4,64,256]{3,2,1,0:T(8,128)}, f32[2,4,64,256]{3,2,1,0:T(8,128)}, f3...) custom-call(f32[2,4,64,256]{3,2,1,0:T(8,128)} %temp_ref.1, f32[2,4,64,256]{3,2,1,0:T(8,128)} %salt_ref.1, ...), custom_call_target="tpu_custom_call" | custom-call | tf_op jit(solution)/shard_map/pallas_call | solution.py:389
  27.9 42.2 %shard_map.127 = f32[3,2,64,256]{3,2,1,0:T(8,128)} custom-call(f32[2,64,256]{2,1,0:T(8,128)} %get-tuple-element.46.tu_ref, f32[2,64,256]{2,1,0:T(8,128)} %get-tuple-element.47.tv_ref, f32[2,64,256]{2,1,0:T(8,128)} %eta_ref.1), custom_call_target="tpu_custom_call" | custom-call | tf_op jit(solution)/shard_map/pallas_call | solution.py:285
  70.1 1.7 slice_bitcast_fusion.1
  73.8 1.5 collective-permute-start.7
  75.3 2.7 %collective-permute-start.6 = (f32[4,2,4,64,1]{3,2,4,1,0:T(4,128)S(1)}, f32[4,2,4,64,1]{3,2,4,1,0:T(4,128)S(1)}, u32[]{:S(2)}, u32[]{:S(2)}) collective-permute-start(f32[4,2,4,64,1]{3,2,4,1,0:T(4,128)S(1)} %pad_maximum_fusion.11), channel_id=1, source_target_pairs={{1,0},{2,1},{3,2},{4,3},{5,4},{6,5},{7,6},{0,7},{9,8},{10,9},{11,1... | collective-permute-start | bytes 24584 | tf_op jit(solution)/shard_map/ppermute | solution.py:422
  78.1 2.9 %collective-permute-start.4 = (f32[4,2,4,1,256]{4,3,2,1,0:T(1,128)S(1)}, f32[4,2,4,1,256]{4,3,2,1,0:T(1,128)S(1)}, u32[]{:S(2)}, u32[]{:S(2)}) collective-permute-start(f32[4,2,4,1,256]{4,3,2,1,0:T(1,128)S(1)} %pad_maximum_fusion.7), channel_id=1, source_target_pairs={{8,0},{16,8},{24,16},{32,24},{40,32},{48,40},{56,48},{0,56},{9,1},... | collective-permute-start | bytes 98312 | tf_op jit(solution)/shard_map/ppermute | solution.py:420
  85.0 1.4 copy.220.w_ref
  86.5 1.4 copy.219.e_ref
  89.1 5.0 %shard_map.128 = (f32[2,4,64,256]{3,2,1,0:T(8,128)}, f32[2,4,64,256]{3,2,1,0:T(8,128)}, f32[2,4,64,256]{3,2,1,0:T(8,128)}, f32[2,4,64,256]{3,2,1,0:T(8,128)}, f3...) custom-call(f32[2,4,64,256]{3,2,1,0:T(8,128)} %get-tuple-element.43.temp_ref, f32[2,4,64,256]{3,2,1,0:T(8,128)} %get-tuple-element.44.salt_ref, ...), custom_call_target="tpu_custom_call" | custom-call | tf_op jit(solution)/shard_map/pallas_call | solution.py:389
  94.1 41.1 %shard_map.129 = f32[3,2,64,256]{3,2,1,0:T(8,128)} custom-call(f32[2,64,256]{2,1,0:T(8,128)} %get-tuple-element.52.tu_ref, f32[2,64,256]{2,1,0:T(8,128)} %get-tuple-element.53.tv_ref, f32[2,64,256]{2,1,0:T(8,128)} %get-tuple-element.132.eta_ref), custom_call_target="tpu_custom_call" | custom-call | tf_op jit(solution)/shard_map/pallas_call | solution.py:285
  135.2 1.1 multiply_bitcast_fusion.1
  137.4 1.1 pad_maximum_fusion.1
  138.5 2.9 %collective-permute-start.8 = (f32[2,2,4,64,256]{4,3,2,1,0:T(8,128)}, f32[2,2,4,64,256]{4,3,2,1,0:T(8,128)}, u32[]{:S(2)}, u32[]{:S(2)}) collective-permute-start(f32[2,2,4,64,256]{4,3,2,1,0:T(8,128)} %pad_maximum_fusion.1), channel_id=1, source_target_pairs={{0,64},{64,0},{1,65},{65,1},{2,66},{66,2},{3,67},{67,3},{4,68},{68... | collective-permute-start | bytes 3145736 | tf_op jit(solution)/shard_map/ppermute | solution.py:573
  142.2 25.9 %shard_map.130 = f32[40,128]{1,0:T(8,128)} custom-call(f32[40,128]{1,0:T(8,128)} %select_maximum_fusion.1.x_ref), custom_call_target="tpu_custom_call" | custom-call | tf_op jit(solution)/shard_map/pallas_call | solution.py:90
  168.1 1.3 fusion.5
  170.8 1.9 collective-permute-start.9
  172.8 1.3 pad_clamp_fusion
  176.3 1.3 fusion.9
  177.6 1.3 bitcast_select_fusion.1
  178.9 1.3 bitcast_select_fusion.3
  182.0 18.8 %collective-permute-done.9 = f32[2,10,64,256]{3,2,1,0:T(8,128)} collective-permute-done((f32[2,10,64,256]{3,2,1,0:T(8,128)S(1)}, f32[2,10,64,256]{3,2,1,0:T(8,128)}, u32[]{:S(2)}, u32[]{:S(2)}) %collective-permute-start.9) | collective-permute-done | bytes 1310752 | tf_op jit(solution)/shard_map/ppermute | solution.py:595
  200.8 1.3 slice.272
  202.2 1.5 dynamic-slice_select_fusion
  204.3 1.0 fusion
  (102 shorter events, 18.8 us)
Async XLA Ops:
  0.6 8.2 %copy-start.2 = (f32[2,4,64,256]{3,2,1,0:T(8,128)S(1)}, f32[2,4,64,256]{3,2,1,0:T(8,128)}, u32[]{:S(2)}) copy-start(f32[2,4,64,256]{3,2,1,0:T(8,128)} %temp_ref.1) | copy-start | bytes 1572868
  0.6 7.9 %copy-start.3 = (f32[2,4,64,256]{3,2,1,0:T(8,128)S(1)}, f32[2,4,64,256]{3,2,1,0:T(8,128)}, u32[]{:S(2)}) copy-start(f32[2,4,64,256]{3,2,1,0:T(8,128)} %vvel_ref.1) | copy-start | bytes 1572868
  0.7 13.8 %copy-start.19 = (s32[2]{0:T(128)S(1)}, s32[2]{0:T(128)}, u32[]{:S(2)}) copy-start(s32[2]{0:T(128)} %param.17) | copy-start | bytes 28
  0.7 15.6 %copy-start.8 = (s32[64,256]{1,0:T(8,128)S(1)}, s32[64,256]{1,0:T(8,128)}, u32[]{:S(2)}) copy-start(s32[64,256]{1,0:T(8,128)} %land_ref.3) | copy-start | bytes 196612
  2.7 19.0 %collective-permute-start.1 = (f32[4,2,4,1,256]{4,3,2,1,0:T(1,128)S(1)}, f32[4,2,4,1,256]{4,3,2,1,0:T(1,128)S(1)}, u32[]{:S(2)}, u32[]{:S(2)}) collective-permute-start(f32[4,2,4,1,256]{4,3,2,1,0:T(1,128)S(1)} %pad_maximum_fusion.6), channel_id=1, source_target_pairs={{0,8},{8,16},{16,24},{24,32},{32,40},{40,48},{48,56},{56,0},{1,9},... | collective-permute-start | bytes 98312 | tf_op jit(solution)/shard_map/ppermute | solution.py:421
  2.8 18.9 %collective-permute-start = (f32[4,2,4,1,256]{4,3,2,1,0:T(1,128)S(1)}, f32[4,2,4,1,256]{4,3,2,1,0:T(1,128)S(1)}, u32[]{:S(2)}, u32[]{:S(2)}) collective-permute-start(f32[4,2,4,1,256]{4,3,2,1,0:T(1,128)S(1)} %pad_maximum_fusion.5), channel_id=1, source_target_pairs={{8,0},{16,8},{24,16},{32,24},{40,32},{48,40},{56,48},{0,56},{9,1},... | collective-permute-start | bytes 98312 | tf_op jit(solution)/shard_map/ppermute | solution.py:420
  9.2 7.1 %collective-permute-start.2 = (f32[4,2,4,64,1]{3,2,4,1,0:T(4,128)S(1)}, f32[4,2,4,64,1]{3,2,4,1,0:T(4,128)S(1)}, u32[]{:S(2)}, u32[]{:S(2)}) collective-permute-start(f32[4,2,4,64,1]{3,2,4,1,0:T(4,128)S(1)} %pad_maximum_fusion.9), channel_id=1, source_target_pairs={{1,0},{2,1},{3,2},{4,3},{5,4},{6,5},{7,6},{0,7},{9,8},{10,9},{11,1... | collective-permute-start | bytes 24584 | tf_op jit(solution)/shard_map/ppermute | solution.py:422
  14.4 5.8 %collective-permute-start.3 = (f32[4,2,4,64,1]{3,2,4,1,0:T(4,128)S(1)}, f32[4,2,4,64,1]{3,2,4,1,0:T(4,128)S(1)}, u32[]{:S(2)}, u32[]{:S(2)}) collective-permute-start(f32[4,2,4,64,1]{3,2,4,1,0:T(4,128)S(1)} %pad_maximum_fusion.10), channel_id=1, source_target_pairs={{0,1},{1,2},{2,3},{3,4},{4,5},{5,6},{6,7},{7,0},{8,9},{9,10},{10,1... | collective-permute-start | bytes 24584 | tf_op jit(solution)/shard_map/ppermute | solution.py:423
  16.3 120.1 %copy-start.17 = (pred[8]{0:T(512)(128)(4,1)}, pred[8]{0:T(512)(128)(4,1)S(1)}, u32[]{:S(2)}) copy-start(pred[8]{0:T(512)(128)(4,1)S(1)} %iota_compare_fusion.2) | copy-start | bytes 28
  21.7 0.6 copy-start.13
  22.3 0.6 copy-start.14
  27.8 43.9 %copy-start.11 = (f32[2,4,64,256]{3,2,1,0:T(8,128)S(1)}, f32[2,4,64,256]{3,2,1,0:T(8,128)}, u32[]{:S(2)}) copy-start(f32[2,4,64,256]{3,2,1,0:T(8,128)} %get-tuple-element.45) | copy-start | bytes 1572868
  27.9 43.9 %copy-start.12 = (f32[2,4,64,256]{3,2,1,0:T(8,128)S(1)}, f32[2,4,64,256]{3,2,1,0:T(8,128)}, u32[]{:S(2)}) copy-start(f32[2,4,64,256]{3,2,1,0:T(8,128)} %get-tuple-element.48) | copy-start | bytes 1572868
  71.8 1.1 copy-start.4
  71.9 14.6 %copy-start = (f32[2,4,64,256]{3,2,1,0:T(8,128)}, f32[2,4,64,256]{3,2,1,0:T(8,128)S(1)}, u32[]{:S(2)}) copy-start(f32[2,4,64,256]{3,2,1,0:T(8,128)S(1)} %get-tuple-element.136.vvel_ref) | copy-start | bytes 1572868
  71.9 14.6 %copy-start.1 = (f32[2,4,64,256]{3,2,1,0:T(8,128)}, f32[2,4,64,256]{3,2,1,0:T(8,128)S(1)}, u32[]{:S(2)}) copy-start(f32[2,4,64,256]{3,2,1,0:T(8,128)S(1)} %get-tuple-element.137.uvel_ref) | copy-start | bytes 1572868
  71.9 1.5 copy-start.5
  73.8 11.2 %collective-permute-start.7 = (f32[4,2,4,64,1]{3,2,4,1,0:T(4,128)S(1)}, f32[4,2,4,64,1]{3,2,4,1,0:T(4,128)S(1)}, u32[]{:S(2)}, u32[]{:S(2)}) collective-permute-start(f32[4,2,4,64,1]{3,2,4,1,0:T(4,128)S(1)} %pad_maximum_fusion.12), channel_id=1, source_target_pairs={{0,1},{1,2},{2,3},{3,4},{4,5},{5,6},{6,7},{7,0},{8,9},{9,10},{10,1... | collective-permute-start | bytes 24584 | tf_op jit(solution)/shard_map/ppermute | solution.py:423
  75.3 11.2 %collective-permute-start.6 = (f32[4,2,4,64,1]{3,2,4,1,0:T(4,128)S(1)}, f32[4,2,4,64,1]{3,2,4,1,0:T(4,128)S(1)}, u32[]{:S(2)}, u32[]{:S(2)}) collective-permute-start(f32[4,2,4,64,1]{3,2,4,1,0:T(4,128)S(1)} %pad_maximum_fusion.11), channel_id=1, source_target_pairs={{1,0},{2,1},{3,2},{4,3},{5,4},{6,5},{7,6},{0,7},{9,8},{10,9},{11,1... | collective-permute-start | bytes 24584 | tf_op jit(solution)/shard_map/ppermute | solution.py:422
  78.0 9.9 %collective-permute-start.5 = (f32[4,2,4,1,256]{4,3,2,1,0:T(1,128)S(1)}, f32[4,2,4,1,256]{4,3,2,1,0:T(1,128)S(1)}, u32[]{:S(2)}, u32[]{:S(2)}) collective-permute-start(f32[4,2,4,1,256]{4,3,2,1,0:T(1,128)S(1)} %pad_maximum_fusion.8), channel_id=1, source_target_pairs={{0,8},{8,16},{16,24},{24,32},{32,40},{40,48},{48,56},{56,0},{1,9},... | collective-permute-start | bytes 98312 | tf_op jit(solution)/shard_map/ppermute | solution.py:421
  78.1 9.8 %collective-permute-start.4 = (f32[4,2,4,1,256]{4,3,2,1,0:T(1,128)S(1)}, f32[4,2,4,1,256]{4,3,2,1,0:T(1,128)S(1)}, u32[]{:S(2)}, u32[]{:S(2)}) collective-permute-start(f32[4,2,4,1,256]{4,3,2,1,0:T(1,128)S(1)} %pad_maximum_fusion.7), channel_id=1, source_target_pairs={{8,0},{16,8},{24,16},{32,24},{40,32},{48,40},{56,48},{0,56},{9,1},... | collective-permute-start | bytes 98312 | tf_op jit(solution)/shard_map/ppermute | solution.py:420
  87.9 0.6 copy-start.15
  88.5 0.6 copy-start.16
  94.1 42.2 %copy-start.9 = (f32[2,4,64,256]{3,2,1,0:T(8,128)S(1)}, f32[2,4,64,256]{3,2,1,0:T(8,128)}, u32[]{:S(2)}) copy-start(f32[2,4,64,256]{3,2,1,0:T(8,128)} %get-tuple-element.51) | copy-start | bytes 1572868
  94.1 42.2 %copy-start.10 = (f32[2,4,64,256]{3,2,1,0:T(8,128)S(1)}, f32[2,4,64,256]{3,2,1,0:T(8,128)}, u32[]{:S(2)}) copy-start(f32[2,4,64,256]{3,2,1,0:T(8,128)} %get-tuple-element.54) | copy-start | bytes 1572868
  136.2 1.0 copy-start.6
  136.2 1.2 copy-start.7
  138.5 37.8 %collective-permute-start.8 = (f32[2,2,4,64,256]{4,3,2,1,0:T(8,128)}, f32[2,2,4,64,256]{4,3,2,1,0:T(8,128)}, u32[]{:S(2)}, u32[]{:S(2)}) collective-permute-start(f32[2,2,4,64,256]{4,3,2,1,0:T(8,128)} %pad_maximum_fusion.1), channel_id=1, source_target_pairs={{0,64},{64,0},{1,65},{65,1},{2,66},{66,2},{3,67},{67,3},{4,68},{68... | collective-permute-start | bytes 3145736 | tf_op jit(solution)/shard_map/ppermute | solution.py:573
  168.1 5.9 %slice-start = ((f32[40,128]{1,0:T(8,128)}), f32[32,128]{1,0:T(8,128)S(1)}, s32[]{:S(2)}) async-start(f32[40,128]{1,0:T(8,128)} %shard_map.130), calls=%async_computation | async-start | bytes 32768 | tf_op jit(solution)/shard_map/slice | solution.py:587
  170.8 30.0 %collective-permute-start.9 = (f32[2,10,64,256]{3,2,1,0:T(8,128)S(1)}, f32[2,10,64,256]{3,2,1,0:T(8,128)}, u32[]{:S(2)}, u32[]{:S(2)}) collective-permute-start(f32[2,10,64,256]{3,2,1,0:T(8,128)S(1)} %select_maximum_fusion), channel_id=1, source_target_pairs={{0,64},{64,0},{1,65},{65,1},{2,66},{66,2},{3,67},{67,3},{4,68},{68... | collective-permute-start | bytes 3932168 | tf_op jit(solution)/shard_map/ppermute | solution.py:595
  204.3 1.9 copy-start.18
  204.3 3.9 %copy-start.20 = (s32[2]{0:T(128)S(1)}, s32[2]{0:T(128)}, u32[]{:S(2)}) copy-start(s32[2]{0:T(128)} %param.17) | copy-start | bytes 28
